TPU v7x, 32 devices: a whole 2x2x4 slice. The times are simulated.
32 devices in a mesh: groups: 2 (over y), sess: 4 (over z), inner: 2 (over x), rep: 2 (over core).
Axes of the slice: x: 2, y: 2, z: 4, core: 2. Of those that a mesh axis runs over, the one named last changes fastest.
Arguments:
- thinker_rows: bfloat16 [4096, 3584], P(('groups', 'sess', 'rep'), 'inner'), parts along dimension 0, may hold values from -6 to 6
- row_session: int32 [4096, 1], P(('groups', 'sess', 'rep')), parts along dimension 0, may hold values from 0 to 31; in each aligned block of 256 rows (0 to 255, 256 to 511, ...) at most 12 rows name the same one
- speaker_of: int32 [64], P('groups'), parts along dimension 0, may hold values from 0 to 7
- prompt_slot: int32 [16], P('groups'), parts along dimension 0, may hold values from 0 to 7, each once
- prompt_cache: bfloat16 [16, 1024, 1024], P(('groups', 'sess'), ('inner', 'rep')), parts along dimension 0, may hold values from -64 to 64
- proj_weight: bfloat16 [3584, 896], P('inner'), may hold values from -0.09375 to 0.09375
- attn_gain: bfloat16 [896], replicated, may hold values from 0.5 to 1.5
- q_weight: bfloat16 [896, 1536], replicated, may hold values from -0.1875 to 0.1875
- k_weight: bfloat16 [896, 512], replicated, may hold values from -0.625 to 0.625
- v_weight: bfloat16 [896, 512], replicated, may hold values from -0.1875 to 0.1875
- o_weight: bfloat16 [1536, 896], replicated, may hold values from -0.15625 to 0.15625
Outputs:
- voice_states: bfloat16 [64, 96, 896], P(('groups', 'sess', 'inner', 'rep')), parts along dimension 0
There are 2 independent parts, one for each index of `groups`. A program takes and returns all parts, laid end to end along the dimension named above; an argument that names none is the same for every part. Nothing has to cross between parts.
Inputs may be any that keep to these rules, and one draw needn't show every extreme that they name: `row_session`: column 0 names the session of the row. Within each block of 256 rows (rows b * 256 to (b + 1) * 256 - 1, the rows of one index of sess+rep) no session is named by more than 12 rows, a bound that some block reaches; every session is named by some row. `prompt_slot`: each slot holds exactly one speaker's prompt.
All inputs are finite; a program needn't handle non-finite values.
Results may differ from a plain program's by a relative error of at most 0.0071.
Values may be sent and summed in bfloat16 or wider, within the bound.
No kernel may reach another device: no remote copies, remote signals or barrier semaphores. Data moves between devices by JAX's collectives and lax.ppermute only.
A program may use at most 128 MiB of HBM per device.

v0:
```python
import jax
import jax.numpy as jnp
from jax import lax
from jax.sharding import PartitionSpec as P

H = 12
KVH = 4
HD = 128
PROMPT = 1024
SLOTS = 96


EPSILON = 1e-06
ROPE_BASE = 1000000.0


def rms_scale(states, gain):
    widened = states.astype(jnp.float32)
    factor = lax.rsqrt(jnp.mean(widened * widened, axis=-1, keepdims=True) + EPSILON)
    return (widened * factor * gain.astype(jnp.float32)).astype(jnp.bfloat16)


def rope_tables(slot_total):
    half_width = HD // 2
    inverse = ROPE_BASE ** (-(jnp.arange(half_width, dtype=jnp.float32) * 2.0) / HD)
    angles = (PROMPT + jnp.arange(slot_total)).astype(jnp.float32)[:, None] * inverse[None, :]
    cosine = jnp.concatenate([jnp.cos(angles), jnp.cos(angles)], axis=1)[:, None, :]
    sine_table = jnp.concatenate([jnp.sin(angles), jnp.sin(angles)], axis=1)[:, None, :]
    return (cosine, sine_table)


def rotate(vectors, cosine, sine_table):
    half_width = vectors.shape[-1] // 2
    turned = jnp.concatenate([-vectors[..., half_width:], vectors[..., :half_width]], axis=-1)
    return vectors * cosine + turned * sine_table


def attend(states, lengths, prompts, attn_gain, q_weight, k_weight, v_weight, o_weight):
    session_total, slot_total, model_width = states.shape
    flat_rows = states.reshape(session_total * slot_total, model_width)
    normed = rms_scale(flat_rows, attn_gain)
    cosine, sine_table = rope_tables(slot_total)
    query = rotate(
        jnp.dot(normed, q_weight, preferred_element_type=jnp.float32).reshape(
            session_total, slot_total, H, HD
        ),
        cosine,
        sine_table,
    ).astype(jnp.bfloat16)
    own_keys = rotate(
        jnp.dot(normed, k_weight, preferred_element_type=jnp.float32).reshape(
            session_total, slot_total, KVH, HD
        ),
        cosine,
        sine_table,
    ).astype(jnp.bfloat16)
    own_values = (
        jnp.dot(normed, v_weight, preferred_element_type=jnp.float32)
        .reshape(session_total, slot_total, KVH, HD)
        .astype(jnp.bfloat16)
    )
    prompt_keys = prompts[:, :, : KVH * HD].reshape(session_total, PROMPT, KVH, HD)
    prompt_values = prompts[:, :, KVH * HD :].reshape(session_total, PROMPT, KVH, HD)
    all_keys = jnp.concatenate([prompt_keys, own_keys], axis=1)
    all_values = jnp.concatenate([prompt_values, own_values], axis=1)
    key_place = jnp.arange(PROMPT + slot_total) - PROMPT
    query_place = jnp.arange(slot_total)
    allowed = (key_place[None, None, :] < 0) | (
        key_place[None, None, :] <= query_place[None, :, None]
    ) & (key_place[None, None, :] < lengths[:, None, None])
    per_group = H // KVH
    outputs = []
    for kv_head in range(KVH):
        query_group = query[:, :, kv_head * per_group : (kv_head + 1) * per_group]
        scores = jnp.einsum(
            "cqhd,ckd->chqk",
            query_group,
            all_keys[:, :, kv_head],
            preferred_element_type=jnp.float32,
        ) * HD ** (-0.5)
        scores = jnp.where(allowed[:, None], scores, -1e30)
        highest = jnp.max(scores, axis=-1, keepdims=True)
        powers = jnp.exp(scores - highest)
        weights = (powers / jnp.sum(powers, axis=-1, keepdims=True)).astype(jnp.bfloat16)
        outputs.append(
            jnp.einsum(
                "chqk,ckd->cqhd",
                weights,
                all_values[:, :, kv_head],
                preferred_element_type=jnp.float32,
            )
        )
    attended = (
        jnp.concatenate(outputs, axis=2)
        .reshape(session_total * slot_total, H * HD)
        .astype(jnp.bfloat16)
    )
    return flat_rows.astype(jnp.float32) + jnp.dot(
        attended, o_weight, preferred_element_type=jnp.float32
    )


def body(
    thinker_rows,
    row_session,
    speaker_of,
    prompt_slot,
    prompt_cache,
    proj_weight,
    attn_gain,
    q_weight,
    k_weight,
    v_weight,
    o_weight,
):
    sess_count = lax.axis_size("sess")
    inner_count = lax.axis_size("inner")
    rep_count = lax.axis_size("rep")
    owner_count = sess_count * rep_count
    session_all = speaker_of.shape[0]
    per_device = session_all // (owner_count * inner_count)
    per_owner = per_device * inner_count
    slot_cap = SLOTS // owner_count
    inner_place = lax.axis_index("inner")
    shard_place = lax.axis_index("sess")
    row_owner = row_session[:, 0]
    device_of = row_owner // per_device
    target = (
        (device_of // (inner_count * rep_count) * rep_count + device_of % rep_count) * per_owner
        + device_of // rep_count % inner_count * per_device
        + row_owner % per_device
    )
    row_order = jnp.arange(row_owner.shape[0])
    earlier = jnp.sum(
        (
            (row_owner[:, None] == row_owner[None, :]) & (row_order[None, :] < row_order[:, None])
        ).astype(jnp.int32),
        axis=1,
    )
    slot_place = target * slot_cap + earlier
    counts = jnp.sum(
        (target[:, None] == jnp.arange(owner_count * per_owner)[None, :]).astype(jnp.int32), axis=0
    ).reshape(owner_count, per_owner)
    partial_sum = jnp.dot(thinker_rows, proj_weight, preferred_element_type=jnp.float32)
    own_columns = lax.psum_scatter(partial_sum, "inner", scatter_dimension=1, tiled=True).astype(
        jnp.bfloat16
    )
    buffer = (
        jnp.zeros((owner_count * per_owner * slot_cap, own_columns.shape[1]), own_columns.dtype)
        .at[slot_place]
        .set(own_columns)
    )
    arrived = lax.all_to_all(
        buffer.reshape(owner_count, per_owner * slot_cap, own_columns.shape[1]),
        ("sess", "rep"),
        split_axis=0,
        concat_axis=0,
        tiled=True,
    )
    counts_in = lax.all_to_all(counts, ("sess", "rep"), split_axis=0, concat_axis=0, tiled=True)
    arrived_rows = arrived.reshape(owner_count, per_owner, slot_cap, arrived.shape[2])
    regrouped = lax.all_to_all(arrived_rows, "inner", split_axis=1, concat_axis=3, tiled=True)
    projected = jnp.transpose(regrouped, (1, 0, 2, 3)).reshape(
        per_device, owner_count * slot_cap, regrouped.shape[3]
    )
    own_counts = lax.dynamic_slice_in_dim(counts_in, inner_place * per_device, per_device, 1)
    offsets = jnp.cumsum(own_counts, axis=0) - own_counts
    lengths = jnp.sum(own_counts, axis=0)
    within = jnp.arange(slot_cap)
    position = jnp.transpose(offsets)[:, :, None] + within[None, None, :]
    live_slot = within[None, None, :] < jnp.transpose(own_counts)[:, :, None]
    position = jnp.where(live_slot, position, SLOTS).reshape(per_device, owner_count * slot_cap)
    session_rows = jnp.broadcast_to(jnp.arange(per_device)[:, None], position.shape)
    compact = (
        jnp.zeros((per_device, SLOTS, projected.shape[2]), jnp.bfloat16)
        .at[session_rows, position]
        .set(projected, mode="drop")
    )
    shard_sessions = per_device * inner_count * rep_count
    wanted_speaker = lax.dynamic_slice_in_dim(
        speaker_of, shard_place * shard_sessions, shard_sessions
    )
    speaker_table = jnp.arange(prompt_slot.shape[0])
    wanted_slot = jnp.sum(
        jnp.where(wanted_speaker[:, None] == speaker_table[None, :], prompt_slot[None, :], 0),
        axis=1,
    )
    piece = lax.all_gather(prompt_cache, "sess", axis=0, tiled=True)
    matching = (wanted_slot[:, None] == jnp.arange(piece.shape[0])[None, :]).astype(jnp.bfloat16)
    chosen = jnp.einsum("sp,ptc->stc", matching, piece, preferred_element_type=jnp.float32)
    prompts = lax.all_to_all(
        chosen.astype(jnp.bfloat16), ("inner", "rep"), split_axis=0, concat_axis=1, tiled=True
    )
    summed = attend(compact, lengths, prompts, attn_gain, q_weight, k_weight, v_weight, o_weight)
    live_rows = (jnp.arange(SLOTS)[None, :] < lengths[:, None]).reshape(-1, 1)
    return (
        jnp.where(live_rows, summed, 0.0)
        .astype(jnp.bfloat16)
        .reshape(per_device, SLOTS, summed.shape[1])
    )


def solution(mesh):
    in_specs = (
        P(("groups", "sess", "rep"), "inner"),
        P(("groups", "sess", "rep"), None),
        P("groups"),
        P("groups"),
        P(("groups", "sess"), ("inner", "rep"), None),
        P("inner", None),
        P(),
        P(),
        P(),
        P(),
        P(),
    )
    out_specs = P(("groups", "sess", "inner", "rep"), None, None)
    return jax.shard_map(body, mesh=mesh, in_specs=in_specs, out_specs=out_specs, check_vma=False)
```

profile of v0, /device:TPU:0, one launch (start us, length us, event | category | flops | bytes accessed | tf_op | source)
XLA Modules:
  0.0 214.4 jit_solution(5181493876565836849)
XLA Ops:
  9.3 3.5 %fusion.175 = f32[256,896]{0,1:T(8,128)} fusion(bf16[256,1792]{1,0:T(8,128)(2,1)} %param.11, bf16[1792,896]{1,0:T(8,128)(2,1)S(1)} %copy-done), kind=kOutput, calls=%fused_computation.189 | convolution fusion | flops 822083584 | bytes 5046272 | tf_op jit(solution)/shard_map/dot_general | solution.py:144
  14.4 6.3 %all-to-all-start = ((s32[8,1,4]{2,1,0:T(1,128)}), s32[8,1,4]{2,1,0:T(1,128)S(1)}, u32[]{:S(2)}, u32[]{:S(2)}) async-start(s32[8,1,4]{2,1,0:T(1,128)} %bitcast.1), calls=%async_computation | async-start | bytes 8192 | tf_op jit(solution)/shard_map/all_to_all | solution.py:160
  20.7 4.9 %copy.90 = bf16[896,1536]{0,1:T(8,128)(2,1)} copy(bf16[896,1536]{1,0:T(8,128)(2,1)} %param.18) | data formatting | bytes 5505024 | tf_op args[7]
  29.3 5.2 %reduce-scatter.2.cloned.1.call-done = f32[256,448]{0,1:T(8,128)} async-done(((f32[256,896]{0,1:T(8,128)}), f32[256,448]{0,1:T(8,128)}) %reduce-scatter.2.cloned.1.call-update) | async-done | bytes 458768 | tf_op jit(solution)/shard_map/reduce_scatter | solution.py:145
  38.0 4.6 %all-to-all-start.1 = ((bf16[8,48,448]{2,1,0:T(8,128)(2,1)}), bf16[8,48,448]{2,1,0:T(8,128)(2,1)S(1)}, u32[]{:S(2)}, u32[]{:S(2)}) async-start(bf16[8,48,448]{2,1,0:T(8,128)(2,1)} %bitcast.8), calls=%async_computation.2 | async-start | bytes 786432 | tf_op jit(solution)/shard_map/all_to_all | solution.py:153
  43.7 24.4 %all-to-all-done.1 = bf16[8,48,448]{2,1,0:T(8,128)(2,1)S(1)} async-done(((bf16[8,48,448]{2,1,0:T(8,128)(2,1)}), bf16[8,48,448]{2,1,0:T(8,128)(2,1)S(1)}, u32[]{:S(2)}, u32[]{:S(2)}) %all-to-all-start.1) | async-done | bytes 344096 | tf_op jit(solution)/shard_map/all_to_all | solution.py:153
  69.1 3.5 %all-to-all-start.2 = ((bf16[8,4,12,448]{3,0,2,1:T(8,128)(2,1)}), bf16[8,4,12,448]{3,0,2,1:T(8,128)(2,1)S(1)}, u32[]{:S(2)}, u32[]{:S(2)}) async-start(bf16[8,4,12,448]{3,0,2,1:T(8,128)(2,1)} %bitcast.9), calls=%async_computation.3 | async-start | bytes 786432 | tf_op jit(solution)/shard_map/all_to_all | solution.py:162
  72.5 33.9 %all-gather.2.cloned.1.call-done = bf16[8,256,1024]{2,1,0:T(8,128)(2,1)} async-done(((bf16[2,256,1024]{2,1,0:T(8,128)(2,1)}), bf16[8,256,1024]{2,1,0:T(8,128)(2,1)}) %all-gather.2.cloned.1.call-update) | async-done | bytes 4194320 | tf_op jit(solution)/shard_map/all_gather | solution.py:188
  106.4 4.7 %fusion.22 = bf16[8,256,1024]{2,0,1:T(8,128)(2,1)S(1)} fusion(bf16[8,256,1024]{2,1,0:T(8,128)(2,1)} %all-gather.2.cloned.1.call-done, s32[8]{0:T(128)S(1)} %select_reduce_fusion), kind=kOutput, calls=%fused_computation.34 | convolution fusion | flops 35651648 | bytes 8388640 | tf_op jit(solution)/shard_map/sp,ptc->stc/dot_general | solution.py:190
  111.2 4.3 %copy.80 = bf16[8,256,1024]{2,1,0:T(8,128)(2,1)} copy(bf16[8,256,1024]{2,0,1:T(8,128)(2,1)S(1)} %fusion.22) | data formatting | bytes 8388608 | tf_op jit(solution)/shard_map/convert_element_type | solution.py:192
  115.4 5.0 %all-to-all-start.3 = ((bf16[8,256,1024]{2,1,0:T(8,128)(2,1)}), bf16[8,256,1024]{2,1,0:T(8,128)(2,1)}, u32[]{:S(2)}, u32[]{:S(2)}) async-start(bf16[8,256,1024]{2,1,0:T(8,128)(2,1)} %copy.80), calls=%async_computation.4 | async-start | bytes 8388608 | tf_op jit(solution)/shard_map/all_to_all | solution.py:191
  122.3 13.1 %scatter_fusion = bf16[2,96,896]{2,1,0:T(8,128)(2,1)S(1)} fusion(bf16[2,96,896]{2,1,0:T(8,128)(2,1)S(1)} %broadcast_in_dim.55, s32[192]{0:T(256)S(1)} %reshape.305, bf16[192,896]{1,0:T(8,128)(2,1)S(1)} %reshape.307), kind=kCustom, calls=%fused_computation.1 | custom fusion | bytes 1033728 | tf_op jit(solution)/shard_map/scatter | solution.py:177
  140.3 28.3 %all-to-all-done.3 = bf16[8,256,1024]{2,1,0:T(8,128)(2,1)} async-done(((bf16[8,256,1024]{2,1,0:T(8,128)(2,1)}), bf16[8,256,1024]{2,1,0:T(8,128)(2,1)}, u32[]{:S(2)}, u32[]{:S(2)}) %all-to-all-start.3) | async-done | bytes 4194336 | tf_op jit(solution)/shard_map/all_to_all | solution.py:191
  168.5 2.6 %copy.81 = bf16[2,4,256,1024]{3,2,1,0:T(8,128)(2,1)S(1)} copy(bf16[2,4,256,1024]{3,2,0,1:T(8,128)(2,1)} %bitcast.16) | data formatting | bytes 8388608 | tf_op jit(solution)/shard_map/all_to_all | solution.py:191
  171.1 2.5 %fusion.154 = (bf16[2,1024,512]{2,1,0:T(8,128)(2,1)}, bf16[2,1024,512]{2,1,0:T(8,128)(2,1)}) fusion(bf16[2,1024,1024]{2,1,0:T(8,128)(2,1)S(1)} %bitcast.185), kind=kLoop, calls=%fused_computation.184 | loop fusion | bytes 8388608 | tf_op jit(solution)/shard_map/slice | solution.py:63
  173.6 3.0 %copy.86 = bf16[2,1024,512]{1,2,0:T(8,128)(2,1)S(1)} copy(bf16[2,1024,512]{2,1,0:T(8,128)(2,1)} %get-tuple-element.10) | data formatting | bytes 4194304 | tf_op jit(solution)/shard_map/slice | solution.py:62
  176.7 2.5 %copy.88 = bf16[2,1024,4,128]{3,1,0,2:T(8,128)(2,1)} copy(bf16[2,1024,4,128]{1,3,2,0:T(8,128)(2,1)S(1)} %bitcast.187) | data formatting | bytes 4194304 | tf_op jit(solution)/shard_map/reshape | solution.py:62
  179.2 3.8 %fusion.155 = (f32[2,3,96]{2,1,0:T(4,128)S(1)}, f32[2,3,96,1120]{3,2,1,0:T(8,128)}) fusion(pred[2,96,1120]{2,1,0:T(8,128)(4,1)S(1)} %copy-done.9, bf16[2,1024,4,128]{3,1,0,2:T(8,128)(2,1)} %copy.88, bf16[2,96,12,128]{3,1,2,0:T(8,128)(2,1)S(1)} %fusion.32, bf16[2,96,4,128]{3,1,2,0:T(8,128)(2,1)S(1)} %copy-done.10), kind=kOutput, calls=%fused_computation.185 | convolution fusion | flops 168879200 | bytes 5245184 | tf_op jit(solution)/shard_map/sub | solution.py:83
  183.0 2.6 %fusion.160 = (f32[2,3,96]{2,1,0:T(4,128)S(1)}, f32[2,3,96,1120]{3,2,1,0:T(8,128)}) fusion(pred[2,96,1120]{2,1,0:T(8,128)(4,1)S(1)} %copy-done.9, bf16[2,1024,4,128]{3,1,0,2:T(8,128)(2,1)S(1)} %copy-done.4, bf16[2,96,12,128]{3,1,2,0:T(8,128)(2,1)S(1)} %fusion.32, bf16[2,96,4,128]{3,1,2,0:T(8,128)(2,1)S(1)} %copy-done.10), kind=kOutput, calls=%fused_computation.186 | convolution fusion | flops 168879200 | bytes 5245184 | tf_op jit(solution)/shard_map/sub | solution.py:83
  185.7 2.6 %fusion.165 = (f32[2,3,96]{2,1,0:T(4,128)S(1)}, f32[2,3,96,1120]{3,2,1,0:T(8,128)}) fusion(pred[2,96,1120]{2,1,0:T(8,128)(4,1)S(1)} %copy-done.9, bf16[2,1024,4,128]{3,1,0,2:T(8,128)(2,1)S(1)} %copy-done.4, bf16[2,96,12,128]{3,1,2,0:T(8,128)(2,1)S(1)} %fusion.32, bf16[2,96,4,128]{3,1,2,0:T(8,128)(2,1)S(1)} %copy-done.10), kind=kOutput, calls=%fused_computation.187 | convolution fusion | flops 168879200 | bytes 5245184 | tf_op jit(solution)/shard_map/sub | solution.py:83
  188.3 2.7 %fusion.170 = (f32[2,3,96]{2,1,0:T(4,128)S(1)}, f32[2,3,96,1120]{3,2,1,0:T(8,128)}) fusion(pred[2,96,1120]{2,1,0:T(8,128)(4,1)S(1)} %copy-done.9, bf16[2,1024,4,128]{3,1,0,2:T(8,128)(2,1)S(1)} %copy-done.4, bf16[2,96,12,128]{3,1,2,0:T(8,128)(2,1)S(1)} %fusion.32, bf16[2,96,4,128]{3,1,2,0:T(8,128)(2,1)S(1)} %copy-done.10), kind=kOutput, calls=%fused_computation.188 | convolution fusion | flops 168879200 | bytes 5245184 | tf_op jit(solution)/shard_map/sub | solution.py:83
  190.9 3.0 %copy.82 = bf16[2,1024,512]{1,2,0:T(8,128)(2,1)S(1)} copy(bf16[2,1024,512]{2,1,0:T(8,128)(2,1)} %get-tuple-element.9) | data formatting | bytes 4194304 | tf_op jit(solution)/shard_map/slice | solution.py:63
  193.9 2.9 %copy.84 = bf16[2,1024,4,128]{3,1,0,2:T(8,128)(2,1)} copy(bf16[2,1024,4,128]{1,3,2,0:T(8,128)(2,1)S(1)} %bitcast.188) | data formatting | bytes 4194304 | tf_op jit(solution)/shard_map/reshape | solution.py:63
  196.8 2.6 %fusion.40 = bf16[2,96,3,128]{3,1,2,0:T(8,128)(2,1)S(1)} fusion(f32[2,3,96,1120]{3,2,1,0:T(8,128)} %get-tuple-element.18, f32[2,3,96]{2,1,0:T(4,128)S(1)} %get-tuple-element.17, bf16[2,1024,4,128]{3,1,0,2:T(8,128)(2,1)} %copy.84, bf16[2,96,4,128]{3,1,2,0:T(8,128)(2,1)S(1)} %copy-done.17), kind=kOutput, calls=%fused_computation.64 | convolution fusion | flops 167661568 | bytes 5024000 | tf_op jit(solution)/shard_map/chqk,ckd->cqhd/dot_general | solution.py:86
  (104 shorter events, 26.7 us)
Async XLA Ops:
  7.4 1.9 copy-start
  7.4 6.0 %copy-start.11 = (s32[256,1]{0,1:T(1,128)S(1)}, s32[256,1]{0,1:T(1,128)}, u32[]{:S(2)}) copy-start(s32[256,1]{0,1:T(1,128)} %param.12) | copy-start | bytes 3076
  7.4 27.1 %reduce-scatter.2.cloned.1.call-start = ((), (), s32[]{:S(2)}) async-start(), calls=%async_computation.5 | async-start | bytes 1376256 | tf_op jit(solution)/shard_map/reduce_scatter | solution.py:145
  12.8 93.7 %all-gather.2.cloned.1.call-start = ((), (), s32[]{:S(2)}) async-start(), calls=%async_computation.6 | async-start | bytes 5242880 | tf_op jit(solution)/shard_map/all_gather | solution.py:188
  14.4 14.6 %all-to-all-start = ((s32[8,1,4]{2,1,0:T(1,128)}), s32[8,1,4]{2,1,0:T(1,128)S(1)}, u32[]{:S(2)}, u32[]{:S(2)}) async-start(s32[8,1,4]{2,1,0:T(1,128)} %bitcast.1), calls=%async_computation | async-start | bytes 8192 | tf_op jit(solution)/shard_map/all_to_all | solution.py:160
  20.7 5.0 %copy-start.12 = (bf16[896]{0:T(1024)(128)(2,1)S(1)}, bf16[896]{0:T(1024)(128)(2,1)}, u32[]{:S(2)}) copy-start(bf16[896]{0:T(1024)(128)(2,1)} %param.17) | copy-start | bytes 5380
  20.7 5.0 %copy-start.5 = (bf16[896,512]{1,0:T(8,128)(2,1)S(1)}, bf16[896,512]{1,0:T(8,128)(2,1)}, u32[]{:S(2)}) copy-start(bf16[896,512]{1,0:T(8,128)(2,1)} %param.19) | copy-start | bytes 2752516
  20.7 5.6 %copy-start.14 = (s32[32]{0:T(128)S(1)}, s32[32]{0:T(128)}, u32[]{:S(2)}) copy-start(s32[32]{0:T(128)} %param.13) | copy-start | bytes 388
  20.7 5.7 %copy-start.15 = (s32[8]{0:T(128)S(1)}, s32[8]{0:T(128)}, u32[]{:S(2)}) copy-start(s32[8]{0:T(128)} %param.14) | copy-start | bytes 100
  25.6 2.1 copy-start.6
  38.0 30.1 %all-to-all-start.1 = ((bf16[8,48,448]{2,1,0:T(8,128)(2,1)}), bf16[8,48,448]{2,1,0:T(8,128)(2,1)S(1)}, u32[]{:S(2)}, u32[]{:S(2)}) async-start(bf16[8,48,448]{2,1,0:T(8,128)(2,1)} %bitcast.8), calls=%async_computation.2 | async-start | bytes 786432 | tf_op jit(solution)/shard_map/all_to_all | solution.py:153
  69.1 46.4 %all-to-all-start.2 = ((bf16[8,4,12,448]{3,0,2,1:T(8,128)(2,1)}), bf16[8,4,12,448]{3,0,2,1:T(8,128)(2,1)S(1)}, u32[]{:S(2)}, u32[]{:S(2)}) async-start(bf16[8,4,12,448]{3,0,2,1:T(8,128)(2,1)} %bitcast.9), calls=%async_computation.3 | async-start | bytes 786432 | tf_op jit(solution)/shard_map/all_to_all | solution.py:162
  115.4 53.1 %all-to-all-start.3 = ((bf16[8,256,1024]{2,1,0:T(8,128)(2,1)}), bf16[8,256,1024]{2,1,0:T(8,128)(2,1)}, u32[]{:S(2)}, u32[]{:S(2)}) async-start(bf16[8,256,1024]{2,1,0:T(8,128)(2,1)} %copy.80), calls=%async_computation.4 | async-start | bytes 8388608 | tf_op jit(solution)/shard_map/all_to_all | solution.py:191
  136.0 2.2 %copy-start.2 = (bf16[896,1536]{0,1:T(8,128)(2,1)S(1)}, bf16[896,1536]{0,1:T(8,128)(2,1)}, u32[]{:S(2)}) copy-start(bf16[896,1536]{0,1:T(8,128)(2,1)} %copy.90) | copy-start | bytes 8257540
  176.6 2.6 %copy-start.9 = (pred[2,96,1120]{2,1,0:T(8,128)(4,1)S(1)}, pred[2,96,1120]{2,1,0:T(8,128)(4,1)}, u32[]{:S(2)}) copy-start(pred[2,96,1120]{2,1,0:T(8,128)(4,1)} %and_or_fusion) | copy-start | bytes 645124
  176.6 2.6 %copy-start.10 = (bf16[2,96,4,128]{3,1,2,0:T(8,128)(2,1)S(1)}, bf16[2,96,4,128]{3,1,2,0:T(8,128)(2,1)}, u32[]{:S(2)}) copy-start(bf16[2,96,4,128]{3,1,2,0:T(8,128)(2,1)} %fusion.68) | copy-start | bytes 589828
  179.2 3.8 %copy-start.4 = (bf16[2,1024,4,128]{3,1,0,2:T(8,128)(2,1)S(1)}, bf16[2,1024,4,128]{3,1,0,2:T(8,128)(2,1)}, u32[]{:S(2)}) copy-start(bf16[2,1024,4,128]{3,1,0,2:T(8,128)(2,1)} %copy.88) | copy-start | bytes 6291460
  193.9 2.9 %copy-start.17 = (bf16[2,96,4,128]{3,1,2,0:T(8,128)(2,1)S(1)}, bf16[2,96,4,128]{3,1,2,0:T(8,128)(2,1)}, u32[]{:S(2)}) copy-start(bf16[2,96,4,128]{3,1,2,0:T(8,128)(2,1)} %convolution_convert_fusion) | copy-start | bytes 589828
  196.8 2.6 %copy-start.3 = (bf16[2,1024,4,128]{3,1,0,2:T(8,128)(2,1)S(1)}, bf16[2,1024,4,128]{3,1,0,2:T(8,128)(2,1)}, u32[]{:S(2)}) copy-start(bf16[2,1024,4,128]{3,1,0,2:T(8,128)(2,1)} %copy.84) | copy-start | bytes 6291460
  196.8 3.3 %copy-start.20 = (f32[2,3,96,1120]{3,2,1,0:T(8,128)S(1)}, f32[2,3,96,1120]{3,2,1,0:T(8,128)}, u32[]{:S(2)}) copy-start(f32[2,3,96,1120]{3,2,1,0:T(8,128)} %get-tuple-element.20) | copy-start | bytes 7741444
  200.1 1.7 copy-start.19
  201.9 1.7 copy-start.18
  203.6 1.8 copy-start.13
  204.6 2.4 %copy-start.1 = (bf16[1792,896]{1,0:T(8,128)(2,1)S(1)}, bf16[1792,896]{1,0:T(8,128)(2,1)}, u32[]{:S(2)}) copy-start(bf16[1792,896]{1,0:T(8,128)(2,1)} %param.16) | copy-start | bytes 9633796
  (3 other events, 3.6 us)
Sparse Core Ops, SparseCore 0:
  12.9 21.5 reduce-scatter.1
Sparse Core Ops, SparseCore 1:
  14.8 91.6 all-gather.1
where the time goes:
time: 215 us; the launch traced here: 214 us
  waiting for transfers between devices  92.3 us (43%)
  local copies, waits for them, and re-layouts  52.8 us (25%)
  matrix products  28.5 us (13%)
  starting transfers between devices  19.5 us (9%)
  between operations  15.2 us (7%)
  other arithmetic  6.03 us (3%)
    all_gather x1, waiting for transfers between devices, body(): piece = lax.all_gather(prompt_cache, 'sess', axis=0, tiled=True)  33.9 us
    all_to_all x1, waiting for transfers between devices, body(): lax.all_to_all(chosen.astype(jnp.bfloat16), ('inner', 'rep'), split_axis=...  28.3 us
    all_to_all x1, waiting for transfers between devices, body(): lax.all_to_all(buffer.reshape(owner_count, per_owner * slot_cap, own_colu...  24.4 us
    scatter x1, local copies, waits for them, and re-layouts, body(): compact = jnp.zeros((per_device, SLOTS, projected.shape[2]), jnp.bfloat16...  13.1 us
    sub x4, matrix products, attend(): powers = jnp.exp(scores - highest)  11.7 us
    unnamed x43, local copies, waits for them, and re-layouts  10.7 us
    all_to_all x1, starting transfers between devices, body(): lax.all_to_all(counts, ('sess', 'rep'), split_axis=0, concat_axis=0, tile...  6.33 us
    slice x2, local copies, waits for them, and re-layouts, attend(): prompts[:, :, KVH * HD:].reshape(session_total, PROMPT, KVH, HD)  5.48 us
  transfers between devices with their start and end apart: 6, of which 4 were waited for; matrix products, arithmetic and copies ran while one was open for 20% of the time, Pallas kernels for 0%

commit v1 on v0

v1 whole, which is shorter than its diff:
```python
import functools
import math

import jax
import jax.numpy as jnp
import numpy as np
from jax import lax
from jax.experimental import pallas as pl
from jax.experimental.pallas import tpu as pltpu
from jax.sharding import PartitionSpec as P

H = 12
KVH = 4
HD = 128
PROMPT = 1024
SLOTS = 96
PER_GROUP = H // KVH

EPSILON = 1e-06
ROPE_BASE = 1000000.0
NT = (((1,), (1,)), ((), ()))


def rope_tables(copies):
    half_width = HD // 2
    inverse = ROPE_BASE ** (-(np.arange(half_width, dtype=np.float64) * 2.0) / HD)
    angles = (PROMPT + np.arange(SLOTS, dtype=np.float64))[:, None] * inverse[None, :]
    cosine = np.concatenate([np.cos(angles), np.cos(angles)], axis=1)
    sine = np.concatenate([-np.sin(angles), np.sin(angles)], axis=1)
    return (
        np.tile(cosine, (copies, 1)).astype(np.float32),
        np.tile(sine, (copies, 1)).astype(np.float32),
    )


def states_kernel(code_ref, slots_ref, gain_ref, weight_ref, cos_ref, sin_ref,
                  states_ref, query_ref, key_ref, value_ref):
    halves, blocks, rows, width = slots_ref.shape
    total = states_ref.shape[0]
    place = lax.broadcasted_iota(jnp.int32, (total, blocks * rows), 0)
    pick = (place == code_ref[0]).astype(jnp.bfloat16)
    parts = [
        jnp.dot(
            pick,
            slots_ref[half].reshape(blocks * rows, width),
            preferred_element_type=jnp.float32,
        )
        for half in range(halves)
    ]
    widened = jnp.concatenate(parts, axis=1)
    states_ref[...] = widened.astype(jnp.bfloat16)
    factor = lax.rsqrt(jnp.mean(widened * widened, axis=-1, keepdims=True) + EPSILON)
    normed = (widened * factor * gain_ref[...].astype(jnp.float32)).astype(jnp.bfloat16)
    both = jnp.dot(normed, weight_ref[...], preferred_element_type=jnp.float32)
    cosine, sine = cos_ref[...], sin_ref[...]
    for head in range(PER_GROUP + 1):
        vector = both[:, head * HD : (head + 1) * HD]
        turned = vector * cosine + pltpu.roll(vector, HD // 2, 1) * sine
        if head < PER_GROUP:
            query_ref[:, head * HD : (head + 1) * HD] = turned.astype(jnp.bfloat16)
        else:
            key_ref[...] = turned.astype(jnp.bfloat16)
    value_ref[...] = both[:, (PER_GROUP + 1) * HD :].astype(jnp.bfloat16)


def attention_kernel(place_ref, length_ref, query_ref, key_ref, value_ref, prompt_ref, out_ref):
    session = pl.program_id(0)
    length = length_ref[session]
    scale = HD ** (-0.5) * math.log2(math.e)
    query = jnp.concatenate(
        [query_ref[:, h * HD : (h + 1) * HD] for h in range(PER_GROUP)], axis=0
    )
    ahead = lax.dot_general(query, prompt_ref[0, :, :HD], NT, preferred_element_type=jnp.float32)
    own = lax.dot_general(query, key_ref[...], NT, preferred_element_type=jnp.float32)
    row = lax.broadcasted_iota(jnp.int32, (SLOTS, SLOTS), 0)
    column = lax.broadcasted_iota(jnp.int32, (SLOTS, SLOTS), 1)
    allowed = (column <= row) & (column < length)
    own = jnp.where(jnp.concatenate([allowed] * PER_GROUP, axis=0), own, -1e30)
    highest = jnp.maximum(
        jnp.max(ahead, axis=-1, keepdims=True), jnp.max(own, axis=-1, keepdims=True)
    )
    powers = jnp.exp2((ahead - highest) * scale)
    own_powers = jnp.exp2((own - highest) * scale)
    total = jnp.sum(powers, axis=-1, keepdims=True) + jnp.sum(own_powers, axis=-1, keepdims=True)
    mixed = jnp.dot(
        powers.astype(jnp.bfloat16), prompt_ref[0, :, HD:], preferred_element_type=jnp.float32
    ) + jnp.dot(own_powers.astype(jnp.bfloat16), value_ref[...], preferred_element_type=jnp.float32)
    mixed = (mixed / total).astype(jnp.bfloat16)
    for h in range(PER_GROUP):
        out_ref[:, h * HD : (h + 1) * HD] = mixed[h * SLOTS : (h + 1) * SLOTS]


def make_states(code, slots, gain, weight, sessions, together):
    halves, blocks, rows, width = slots.shape
    steps = sessions // together
    model = halves * width
    cosine, sine = rope_tables(together)
    total = together * SLOTS
    out = jax.ShapeDtypeStruct
    row_spec = lambda w: pl.BlockSpec((total, w), lambda i: (i, 0))
    whole = lambda a: pl.BlockSpec(a.shape, lambda i: (0,) * a.ndim)
    gain = gain.reshape(1, model)
    return pl.pallas_call(
        states_kernel,
        grid=(steps,),
        in_specs=[
            pl.BlockSpec((1, 1, code.shape[2]), lambda i: (i, 0, 0)),
            pl.BlockSpec((halves, blocks, rows // steps, width), lambda i: (0, 0, i, 0)),
            whole(gain),
            whole(weight),
            whole(cosine),
            whole(sine),
        ],
        out_specs=[row_spec(model), row_spec(PER_GROUP * HD), row_spec(HD), row_spec(HD)],
        out_shape=[
            out((sessions * SLOTS, model), jnp.bfloat16),
            out((sessions * SLOTS, PER_GROUP * HD), jnp.bfloat16),
            out((sessions * SLOTS, HD), jnp.bfloat16),
            out((sessions * SLOTS, HD), jnp.bfloat16),
        ],
        compiler_params=pltpu.CompilerParams(vmem_limit_bytes=40 << 20),
        name="states",
    )(code, slots, gain, weight, jnp.asarray(cosine), jnp.asarray(sine))


def attend(place, lengths, query, key, value, prompts):
    sessions = place.shape[0]
    row_spec = lambda w: pl.BlockSpec((SLOTS, w), lambda i, place, length: (i, 0))
    return pl.pallas_call(
        attention_kernel,
        grid_spec=pltpu.PrefetchScalarGridSpec(
            num_scalar_prefetch=2,
            grid=(sessions,),
            in_specs=[
                row_spec(PER_GROUP * HD),
                row_spec(HD),
                row_spec(HD),
                pl.BlockSpec((1, PROMPT, 2 * HD), lambda i, place, length: (place[i], 0, 0)),
            ],
            out_specs=row_spec(PER_GROUP * HD),
        ),
        out_shape=jax.ShapeDtypeStruct((sessions * SLOTS, PER_GROUP * HD), jnp.bfloat16),
        compiler_params=pltpu.CompilerParams(vmem_limit_bytes=40 << 20),
        name="attend",
    )(place, lengths, query, key, value, prompts)


def body(
    thinker_rows,
    row_session,
    speaker_of,
    prompt_slot,
    prompt_cache,
    proj_weight,
    attn_gain,
    q_weight,
    k_weight,
    v_weight,
    o_weight,
):
    sess_count = lax.axis_size("sess")
    inner_count = lax.axis_size("inner")
    rep_count = lax.axis_size("rep")
    plane = inner_count * rep_count
    blocks = sess_count * rep_count
    session_all = speaker_of.shape[0]
    per_plane = session_all // sess_count
    per_device = per_plane // plane
    slot_cap = SLOTS // blocks
    held, tokens, channels = prompt_cache.shape
    model = proj_weight.shape[1]
    sharers = plane // KVH
    held_part = held // sharers
    sess_place = lax.axis_index("sess")
    plane_place = lax.axis_index("inner") * rep_count + lax.axis_index("rep")
    head = plane_place // sharers
    sharer = plane_place % sharers

    outgoing = jnp.transpose(
        prompt_cache.reshape(sharers, held_part, tokens, 2, KVH, HD), (4, 0, 1, 2, 3, 5)
    ).reshape(plane, held_part, tokens, 2 * HD)
    own_head = lax.all_to_all(outgoing, ("inner", "rep"), split_axis=0, concat_axis=2, tiled=True)
    own_head = own_head.reshape(held_part, plane * tokens, 2 * HD)
    prompts = lax.all_gather(own_head, "sess", axis=0, tiled=True)

    row_owner = row_session[:, 0]
    order = jnp.arange(row_owner.shape[0])
    same = row_owner[:, None] == row_owner[None, :]
    earlier = jnp.sum((same & (order[None, :] < order[:, None])).astype(jnp.int32), axis=1)
    row_slot = row_owner * slot_cap + earlier
    counts = jnp.sum(
        (row_owner[:, None] == jnp.arange(session_all)[None, :]).astype(jnp.int32), axis=0
    )
    all_counts = lax.all_gather(counts, ("sess", "rep"), axis=0, tiled=False)

    partial_sum = jnp.dot(thinker_rows, proj_weight, preferred_element_type=jnp.float32)
    width = model // inner_count
    if inner_count == 2:
        inner_place = lax.axis_index("inner")
        kept = lax.dynamic_slice_in_dim(partial_sum, inner_place * width, width, 1)
        sent = lax.dynamic_slice_in_dim(partial_sum, (1 - inner_place) * width, width, 1)
        came = lax.ppermute(sent.astype(jnp.bfloat16), "inner", [(0, 1), (1, 0)])
        own_columns = (kept + came.astype(jnp.float32)).astype(jnp.bfloat16)
    else:
        own_columns = lax.psum_scatter(
            partial_sum, "inner", scatter_dimension=1, tiled=True
        ).astype(jnp.bfloat16)
    into = (jnp.arange(session_all * slot_cap)[:, None] == row_slot[None, :]).astype(jnp.bfloat16)
    buffer = jnp.dot(into, own_columns, preferred_element_type=jnp.float32).astype(jnp.bfloat16)
    arrived = lax.all_to_all(
        buffer.reshape(sess_count, per_plane * slot_cap, width),
        "sess",
        split_axis=0,
        concat_axis=0,
        tiled=True,
    )
    spread = lax.all_gather(arrived, ("inner", "rep"), axis=0, tiled=False)
    slots = spread.reshape(inner_count, rep_count * sess_count, per_plane * slot_cap, width)

    offsets = jnp.cumsum(all_counts, axis=0) - all_counts
    lengths_all = jnp.sum(all_counts, axis=0)
    mine = lambda a: lax.dynamic_slice_in_dim(a, sess_place * per_plane, per_plane, a.ndim - 1)
    by_block = lambda a: jnp.transpose(
        mine(a).reshape(sess_count, rep_count, per_plane), (1, 0, 2)
    ).reshape(blocks, per_plane)
    lengths = mine(lengths_all)
    together = 16 // math.gcd(16, slot_cap)
    within = jnp.arange(slot_cap)
    local = (jnp.arange(per_plane) % together)[None, :, None] * SLOTS
    code = jnp.where(
        within[None, None, :] < by_block(all_counts)[:, :, None],
        by_block(offsets)[:, :, None] + within[None, None, :] + local,
        -1,
    )
    steps = per_plane // together
    code = jnp.transpose(
        code.reshape(blocks, steps, together * slot_cap), (1, 0, 2)
    ).reshape(steps, 1, blocks * together * slot_cap)

    group_width = PER_GROUP * HD
    weight = jnp.concatenate(
        [
            lax.dynamic_slice_in_dim(q_weight, head * group_width, group_width, 1),
            lax.dynamic_slice_in_dim(k_weight, head * HD, HD, 1),
            lax.dynamic_slice_in_dim(v_weight, head * HD, HD, 1),
        ],
        axis=1,
    )
    states, query, key, value = make_states(
        code, slots, attn_gain, weight, per_plane, together
    )

    wanted_slot = jnp.sum(
        jnp.where(
            mine(speaker_of)[:, None] == jnp.arange(prompt_slot.shape[0])[None, :],
            prompt_slot[None, :],
            0,
        ),
        axis=1,
    )
    place = wanted_slot // held * held_part + wanted_slot % held_part
    attended = attend(place, lengths, query, key, value, prompts)
    returned = lax.all_to_all(
        attended.reshape(plane, per_device * SLOTS, group_width),
        ("inner", "rep"),
        split_axis=0,
        concat_axis=0,
        tiled=True,
    ).reshape(KVH, sharers, per_device, SLOTS, group_width)
    first = plane_place * per_device
    if sharers > 1:
        holder = lax.dynamic_slice_in_dim(wanted_slot % held // held_part, first, per_device)
        chosen = jnp.zeros_like(returned[:, 0])
        for t in range(sharers):
            chosen = jnp.where((holder == t)[None, :, None, None], returned[:, t], chosen)
    else:
        chosen = returned[:, 0]
    gathered = jnp.transpose(chosen, (1, 2, 0, 3)).reshape(per_device * SLOTS, H * HD)
    own_states = lax.dynamic_slice_in_dim(states, first * SLOTS, per_device * SLOTS, 0)
    own_lengths = lax.dynamic_slice_in_dim(lengths, first, per_device)
    summed = own_states.astype(jnp.float32) + jnp.dot(
        gathered, o_weight, preferred_element_type=jnp.float32
    )
    live_rows = (jnp.arange(SLOTS)[None, :] < own_lengths[:, None]).reshape(-1, 1)
    return (
        jnp.where(live_rows, summed, 0.0)
        .astype(jnp.bfloat16)
        .reshape(per_device, SLOTS, model)
    )


def solution(mesh):
    in_specs = (
        P(("groups", "sess", "rep"), "inner"),
        P(("groups", "sess", "rep"), None),
        P("groups"),
        P("groups"),
        P(("groups", "sess"), ("inner", "rep"), None),
        P("inner", None),
        P(),
        P(),
        P(),
        P(),
        P(),
    )
    out_specs = P(("groups", "sess", "inner", "rep"), None, None)
    return jax.shard_map(body, mesh=mesh, in_specs=in_specs, out_specs=out_specs, check_vma=False)
```

time: 215 us -> 191 us (0.89)
  blocking collectives: 0 us -> 45.3 us
  waiting for transfers between devices: 92.3 us -> 70.4 us
  local copies, waits for them, and re-layouts: 52.8 us -> 31.1 us
  matrix products: 28.5 us -> 7.39 us
  starting transfers between devices: 19.5 us -> 7.21 us
  Pallas kernels: 0 us -> 12.2 us
  other arithmetic: 6.03 us -> 1.76 us
    all_to_all x4 -> x1, waiting for transfers between devices: 52.6 us -> 9.35 us  [body(): lax.all_to_all(attended.reshape(plane, per_device * SLOTS, group_width),...]
    all_to_all x0 -> x2, blocking collectives: none -> 36.4 us  [the longest x1 20.4 us: body(): lax.all_to_all(outgoing, ('inner', 'rep'), split_axis=0, concat_axis=2, t...]
    all_gather x1 -> x2, waiting for transfers between devices: 33.9 us -> 54.8 us  [the longest x1 54.7 us: body(): prompts = lax.all_gather(own_head, 'sess', axis=0, tiled=True)]
    scatter x2 -> x0, local copies, waits for them, and re-layouts: 15.3 us -> none  [the longest x1 13.1 us: body(): compact = jnp.zeros((per_device, SLOTS, projected.shape[2]), jnp.bfloat16...]
    all_to_all x4 -> x1, starting transfers between devices: 19.4 us -> 4.16 us  [body(): lax.all_to_all(attended.reshape(plane, per_device * SLOTS, group_width),...]
    pallas_call x0 -> x2, Pallas kernels: none -> 12.2 us  [the longest x1 8.45 us: attend(): pl.pallas_call(attention_kernel, grid_spec=pltpu.PrefetchScalarGridSpec(n...]
    sub x4 -> x0, matrix products: 11.7 us -> none  [attend(): powers = jnp.exp(scores - highest)]
    unnamed x0 -> x1, blocking collectives: none -> 8.89 us
  transfers between devices with their start and end apart: 6 -> 4, of which waited for: 4 -> 3; matrix products, arithmetic and copies ran while one was open for 20% -> 8% of each run, Pallas kernels for 0% -> 2%
where the time goes in v1:
time: 191 us; the launch traced here: 190 us
  waiting for transfers between devices  70.4 us (37%)
  blocking collectives  45.3 us (24%)
  local copies, waits for them, and re-layouts  31.1 us (16%)
  between operations  14.3 us (7%)
  Pallas kernels  12.2 us (6%)
  matrix products  7.39 us (4%)
  starting transfers between devices  7.21 us (4%)
    all_gather x1, waiting for transfers between devices, body(): prompts = lax.all_gather(own_head, 'sess', axis=0, tiled=True)  54.7 us
    all_to_all x1, blocking collectives, body(): lax.all_to_all(outgoing, ('inner', 'rep'), split_axis=0, concat_axis=2, t...  20.4 us
    all_to_all x1, blocking collectives, body(): lax.all_to_all(buffer.reshape(sess_count, per_plane * slot_cap, width), '...  16 us
    unnamed x42, local copies, waits for them, and re-layouts  15.9 us
    all_to_all x1, waiting for transfers between devices, body(): lax.all_to_all(attended.reshape(plane, per_device * SLOTS, group_width),...  9.35 us
    unnamed x1, blocking collectives  8.89 us
    pallas_call x1, Pallas kernels, attend(): pl.pallas_call(attention_kernel, grid_spec=pltpu.PrefetchScalarGridSpec(n...  8.45 us
    ppermute x1, waiting for transfers between devices, body(): came = lax.ppermute(sent.astype(jnp.bfloat16), 'inner', [(0, 1), (1, 0)])  6.22 us
  transfers between devices with their start and end apart: 4, of which 3 were waited for; matrix products, arithmetic and copies ran while one was open for 8% of the time, Pallas kernels for 2%

profile of v1, /device:TPU:0, one launch (start us, length us, event | category | flops | bytes accessed | tf_op | source)
XLA Modules:
  0.0 189.6 jit_solution(14571030711564373072)
XLA Ops:
  6.5 1.9 %copy-done = bf16[1792,896]{1,0:T(8,128)(2,1)S(1)} copy-done((bf16[1792,896]{1,0:T(8,128)(2,1)S(1)}, bf16[1792,896]{1,0:T(8,128)(2,1)}, u32[]{:S(2)}) %copy-start) | copy-done | bytes 3211288
  8.4 2.3 %fusion.9 = f32[256,896]{1,0:T(8,128)S(1)} fusion(bf16[256,1792]{1,0:T(8,128)(2,1)} %param.13, bf16[1792,896]{1,0:T(8,128)(2,1)S(1)} %copy-done), kind=kOutput, calls=%fused_computation.36 | convolution fusion | flops 822083584 | bytes 5046272 | tf_op jit(solution)/shard_map/dot_general | solution.py:196
  11.8 3.0 %collective-permute-start = (bf16[256,448]{1,0:T(8,128)(2,1)S(1)}, bf16[256,448]{1,0:T(8,128)(2,1)}, u32[]{:S(2)}, u32[]{:S(2)}) collective-permute-start(bf16[256,448]{1,0:T(8,128)(2,1)S(1)} %dynamic-slice_convert_fusion), channel_id=1, source_target_pairs={{0,2},{2,0},{1,3},{3,1},{4,6},{6,4},{5,7},{7,5},{8,10},{10,8},{9,1... | collective-permute-start | bytes 688136 | tf_op jit(solution)/shard_map/ppermute | solution.py:202
  15.0 6.2 %collective-permute-done = bf16[256,448]{1,0:T(8,128)(2,1)} collective-permute-done((bf16[256,448]{1,0:T(8,128)(2,1)S(1)}, bf16[256,448]{1,0:T(8,128)(2,1)}, u32[]{:S(2)}, u32[]{:S(2)}) %collective-permute-start) | collective-permute-done | bytes 229408 | tf_op jit(solution)/shard_map/ppermute | solution.py:202
  21.2 1.7 convolution_convert_fusion
  23.9 16.0 %all_to_all.25 = bf16[4,96,448]{2,1,0:T(8,128)(2,1)} all-to-all(bf16[4,96,448]{2,1,0:T(8,128)(2,1)} %bitcast.41), channel_id=1, replica_groups=mesh['groups'=2,'sess'=4,'inner'=2,'rep'=2] {'sess'}, dimensions={0} | all-to-all | bytes 688128 | tf_op jit(solution)/shard_map/all_to_all | solution.py:210
  40.0 2.6 %reshape.94 = bf16[1,2,256,2,4,128]{5,4,3,2,1,0:T(4,128)(2,1)} reshape(bf16[2,256,1024]{2,1,0:T(8,128)(2,1)} %param.17) | data formatting | bytes 2097152 | tf_op jit(solution)/shard_map/reshape | solution.py:180
  42.6 3.0 %copy.46 = bf16[1,2,256,2,4,128]{5,3,2,1,4,0:T(2,128)(2,1)} copy(bf16[1,2,256,2,4,128]{5,4,3,2,1,0:T(4,128)(2,1)} %reshape.94) | data formatting | bytes 2097152 | tf_op jit(solution)/shard_map/reshape | solution.py:180
  45.6 2.5 %reshape.95 = bf16[4,2,256,256]{3,2,1,0:T(8,128)(2,1)} reshape(bf16[4,1,2,256,2,128]{5,4,3,2,0,1:T(2,128)(2,1)} %bitcast.39) | data formatting | bytes 2097152 | tf_op jit(solution)/shard_map/reshape | solution.py:181
  48.2 20.4 %all_to_all.26 = bf16[4,2,256,256]{3,2,1,0:T(8,128)(2,1)S(1)} all-to-all(bf16[4,2,256,256]{3,2,1,0:T(8,128)(2,1)} %reshape.95), channel_id=1, replica_groups=mesh['groups'=2,'sess'=4,'inner'=2,'rep'=2] {'inner','rep'}, dimensions={0} | all-to-all | bytes 2097152 | tf_op jit(solution)/shard_map/all_to_all | solution.py:182
  71.4 8.9 %all-reduce = s32[256]{0:T(256)S(1)} all-reduce(s32[256]{0:T(256)S(1)} %dynamic-update-slice), channel_id=2, replica_groups=mesh['groups'=2,'sess'=4,'inner'=2,'rep'=2] {'sess','rep'}, use_global_device_ids=true, to_apply=%add | all-reduce | flops 256 | bytes 2048
  82.5 1.2 constant_dynamic-slice_fusion.2
  83.7 1.1 pad_maximum_fusion.weight_ref
  84.9 1.3 copy-done.1
  86.2 1.4 copy-done.4
  89.4 3.8 %states.1 = (bf16[768,896]{1,0:T(8,128)(2,1)S(1)}, bf16[768,384]{1,0:T(8,128)(2,1)S(1)}, bf16[768,128]{1,0:T(8,128)(2,1)S(1)}, bf16[768,128]{1,0:T(8,128)(2,1)S(1)}) custom-call(s32[2,1,384]{2,1,0:T(1,128)S(1)} %reshape.90.code_ref, bf16[2,8,96,448]{3,2,1,0:T(8,128)(2,1)S(1)} %bitcast.37, bf16[1,896]{1,0:T(2,128)(2,1)S(1)} %reshape.93.gain_ref, ...), custom_call_target="tpu_custom_call" | custom-call | tf_op jit(solution)/shard_map/states/pallas_call | solution.py:103
  94.7 1.1 copy-done.11
  95.9 54.7 %all-gather.5.cloned.1.call-done.prompt_ref = bf16[8,1024,256]{2,1,0:T(8,128)(2,1)} async-done(((bf16[2,1024,256]{2,1,0:T(8,128)(2,1)}), bf16[8,1024,256]{2,1,0:T(8,128)(2,1)}) %all-gather.5.cloned.1.call-update) | async-done | bytes 4194320 | tf_op jit(solution)/shard_map/all_gather | solution.py:184
  150.6 2.2 %copy-done.2 = bf16[8,1024,256]{2,1,0:T(8,128)(2,1)S(1)} copy-done((bf16[8,1024,256]{2,1,0:T(8,128)(2,1)S(1)}, bf16[8,1024,256]{2,1,0:T(8,128)(2,1)}, u32[]{:S(2)}) %copy-start.2) | copy-done | bytes 4194328
  154.8 8.4 %attend.1 = bf16[768,384]{1,0:T(8,128)(2,1)S(1)} custom-call(s32[8]{0:T(128)S(1)} %fusion.7.place_ref, s32[8]{0:T(128)S(1)} %dynamic_slice.46.length_ref, bf16[768,384]{1,0:T(8,128)(2,1)S(1)} %copy-done.6, bf16[768,128]{1,0:T(8,128)(2,1)S(1)} %get-tuple-element.11.key_ref, bf16[768,128]{1,0:T(8,128)(2,1)S(1)} %copy-done.8, bf16[8,1024,256]{2,1,0:T(8,128)(2,1)S(1)} %copy-done.2), custom_call_target="tpu_custom_call" | custom-call | tf_op jit(solution)/shard_map/attend/pallas_call | solution.py:129
  164.1 4.2 %all-to-all-start.2 = ((bf16[4,192,384]{2,1,0:T(8,128)(2,1)}), bf16[4,192,384]{2,1,0:T(8,128)(2,1)}, u32[]{:S(2)}, u32[]{:S(2)}) async-start(bf16[4,192,384]{2,1,0:T(8,128)(2,1)} %bitcast.36), calls=%async_computation.2 | async-start | bytes 1179648 | tf_op jit(solution)/shard_map/all_to_all | solution.py:263
  168.5 9.4 %all-to-all-done.2 = bf16[4,192,384]{2,1,0:T(8,128)(2,1)} async-done(((bf16[4,192,384]{2,1,0:T(8,128)(2,1)}), bf16[4,192,384]{2,1,0:T(8,128)(2,1)}, u32[]{:S(2)}, u32[]{:S(2)}) %all-to-all-start.2) | async-done | bytes 589856 | tf_op jit(solution)/shard_map/all_to_all | solution.py:263
  177.8 1.5 copy.43
  179.5 3.3 %fusion.1 = bf16[192,896]{1,0:T(8,128)(2,1)} fusion(bf16[192,1536]{1,0:T(8,128)(2,1)S(1)} %bitcast.42, bf16[1536,896]{1,0:T(8,128)(2,1)} %param.23, bf16[768,896]{1,0:T(8,128)(2,1)} %copy-done.11, s32[]{:T(128)S(6)} %select_n.74, pred[192]{0:T(512)(128)(4,1)S(1)} %lt.101), kind=kOutput, calls=%fused_computation.2 | convolution fusion | flops 529170432 | bytes 4030660 | tf_op jit(solution)/shard_map/dot_general | solution.py:281
  (75 shorter events, 13.1 us)
Async XLA Ops:
  6.5 1.9 %copy-start = (bf16[1792,896]{1,0:T(8,128)(2,1)S(1)}, bf16[1792,896]{1,0:T(8,128)(2,1)}, u32[]{:S(2)}) copy-start(bf16[1792,896]{1,0:T(8,128)(2,1)} %param.18) | copy-start | bytes 9633796
  6.5 78.4 %all-gather.7.cloned.1.call-start = ((), (), s32[]{:S(2)}) async-start(), calls=%async_computation.4 | async-start | bytes 1966080 | tf_op jit(solution)/shard_map/all_gather | solution.py:217
  8.4 6.4 %copy-start.13 = (s32[256,1]{0,1:T(1,128)S(1)}, s32[256,1]{0,1:T(1,128)}, u32[]{:S(2)}) copy-start(s32[256,1]{0,1:T(1,128)} %param.14) | copy-start | bytes 3076
  10.8 0.9 copy-start.12
  11.8 9.4 %collective-permute-start = (bf16[256,448]{1,0:T(8,128)(2,1)S(1)}, bf16[256,448]{1,0:T(8,128)(2,1)}, u32[]{:S(2)}, u32[]{:S(2)}) collective-permute-start(bf16[256,448]{1,0:T(8,128)(2,1)S(1)} %dynamic-slice_convert_fusion), channel_id=1, source_target_pairs={{0,2},{2,0},{1,3},{3,1},{4,6},{6,4},{5,7},{7,5},{8,10},{10,8},{9,1... | collective-permute-start | bytes 688136 | tf_op jit(solution)/shard_map/ppermute | solution.py:202
  40.0 110.6 %all-gather.5.cloned.1.call-start = ((), (), s32[]{:S(2)}) async-start(), calls=%async_computation.3 | async-start | bytes 5242880 | tf_op jit(solution)/shard_map/all_gather | solution.py:184
  48.2 21.6 %copy-start.18 = (u32[32]{0:T(128)S(1)}, u32[32]{0:T(128)}, u32[]{:S(2)}) copy-start(u32[32]{0:T(128)} %constant.109) | copy-start | bytes 388
  48.2 22.8 %copy-start.14 = (s32[256,1]{0,1:T(1,128)S(1)}, s32[256,1]{0,1:T(1,128)}, u32[]{:S(2)}) copy-start(s32[256,1]{0,1:T(1,128)} %param.14) | copy-start | bytes 3076
  48.2 32.4 %copy-start.15 = (bf16[896]{0:T(1024)(128)(2,1)S(1)}, bf16[896]{0:T(1024)(128)(2,1)}, u32[]{:S(2)}) copy-start(bf16[896]{0:T(1024)(128)(2,1)} %param.19) | copy-start | bytes 5380
  48.2 32.4 %copy-start.16 = (s32[32]{0:T(128)S(1)}, s32[32]{0:T(128)}, u32[]{:S(2)}) copy-start(s32[32]{0:T(128)} %param.15) | copy-start | bytes 388
  48.2 33.1 %copy-start.17 = (s32[8]{0:T(128)S(1)}, s32[8]{0:T(128)}, u32[]{:S(2)}) copy-start(s32[8]{0:T(128)} %param.16) | copy-start | bytes 100
  84.9 1.3 copy-start.1
  86.2 1.4 copy-start.4
  87.6 0.9 copy-start.9
  88.5 0.9 copy-start.10
  93.2 0.8 copy-start.5
  94.0 0.7 copy-start.7
  94.7 1.1 copy-start.11
  150.6 2.2 %copy-start.2 = (bf16[8,1024,256]{2,1,0:T(8,128)(2,1)S(1)}, bf16[8,1024,256]{2,1,0:T(8,128)(2,1)}, u32[]{:S(2)}) copy-start(bf16[8,1024,256]{2,1,0:T(8,128)(2,1)} %all-gather.5.cloned.1.call-done.prompt_ref) | copy-start | bytes 12582916
  152.8 1.1 copy-start.6
  153.9 0.9 copy-start.8
  163.2 0.8 copy-start.3
  164.1 13.8 %all-to-all-start.2 = ((bf16[4,192,384]{2,1,0:T(8,128)(2,1)}), bf16[4,192,384]{2,1,0:T(8,128)(2,1)}, u32[]{:S(2)}, u32[]{:S(2)}) async-start(bf16[4,192,384]{2,1,0:T(8,128)(2,1)} %bitcast.36), calls=%async_computation.2 | async-start | bytes 1179648 | tf_op jit(solution)/shard_map/all_to_all | solution.py:263
Sparse Core Ops, SparseCore 0:
  40.1 21.0 all-gather.6
  69.8 80.7 all-gather.4

commit v2 on v1

--- a/solution.py
+++ b/solution.py
@@ -145,7 +145,7 @@
     )(place, lengths, query, key, value, prompts)
 
 
-def body(
+def general_body(
     thinker_rows,
     row_session,
     speaker_of,
@@ -289,6 +289,269 @@
     )
 
 
+def session_attention(query_ref, key_ref, value_ref, kv, out_ref, session, length):
+    scale = HD ** (-0.5) * math.log2(math.e)
+    rows = pl.ds(pl.multiple_of(session * SLOTS, SLOTS), SLOTS)
+    query = jnp.concatenate(
+        [query_ref[rows, h * HD : (h + 1) * HD] for h in range(PER_GROUP)], axis=0
+    )
+    tokens = kv.reshape(PROMPT, 2 * HD)
+    ahead = lax.dot_general(query, tokens[:, :HD], NT, preferred_element_type=jnp.float32)
+    own = lax.dot_general(query, key_ref[rows, :], NT, preferred_element_type=jnp.float32)
+    row = lax.broadcasted_iota(jnp.int32, (SLOTS, SLOTS), 0)
+    column = lax.broadcasted_iota(jnp.int32, (SLOTS, SLOTS), 1)
+    allowed = (column <= row) & (column < length)
+    own = jnp.where(jnp.concatenate([allowed] * PER_GROUP, axis=0), own, -1e30)
+    highest = jnp.maximum(
+        jnp.max(ahead, axis=-1, keepdims=True), jnp.max(own, axis=-1, keepdims=True)
+    )
+    powers = jnp.exp2((ahead - highest) * scale)
+    own_powers = jnp.exp2((own - highest) * scale)
+    total = jnp.sum(powers, axis=-1, keepdims=True) + jnp.sum(own_powers, axis=-1, keepdims=True)
+    mixed = jnp.dot(
+        powers.astype(jnp.bfloat16), tokens[:, HD:], preferred_element_type=jnp.float32
+    ) + jnp.dot(own_powers.astype(jnp.bfloat16), value_ref[rows, :], preferred_element_type=jnp.float32)
+    mixed = (mixed / total).astype(jnp.bfloat16)
+    for h in range(PER_GROUP):
+        out_ref[rows, h * HD : (h + 1) * HD] = mixed[h * SLOTS : (h + 1) * SLOTS]
+
+
+def hops_kernel(hop_ref, held_ref, length_ref, query_ref, key_ref, value_ref, *refs, hops, carried):
+    if carried:
+        before_ref, *refs = refs
+    prompt_refs, (out_ref, kv, sem) = refs[: 2 * len(hops)], refs[2 * len(hops) :]
+    sessions = hop_ref.shape[0]
+
+    def copies(session, which):
+        return [
+            pltpu.make_async_copy(
+                prompt_refs[2 * which + chunk].at[:, held_ref[session]],
+                kv.at[session, chunk],
+                sem.at[session, chunk],
+            )
+            for chunk in range(2)
+        ]
+
+    def fetch(session, _):
+        for which, hop in enumerate(hops):
+            @pl.when(hop_ref[session] == hop)
+            def _():
+                for copy in copies(session, which):
+                    copy.start()
+        return 0
+
+    lax.fori_loop(0, sessions, fetch, 0)
+    if carried:
+        out_ref[...] = before_ref[...]
+
+    def work(session, _):
+        ours = hop_ref[session] == hops[0]
+        for hop in hops[1:]:
+            ours = ours | (hop_ref[session] == hop)
+
+        @pl.when(ours)
+        def _():
+            for copy in copies(session, 0):
+                copy.wait()
+            session_attention(
+                query_ref, key_ref, value_ref, kv[session], out_ref, session, length_ref[session]
+            )
+
+        return 0
+
+    lax.fori_loop(0, sessions, work, 0)
+
+
+def attend_hops(hop, held, lengths, query, key, value, prompts, hops, before):
+    sessions = hop.shape[0]
+    carried = before is not None
+    smem = pl.BlockSpec(memory_space=pltpu.SMEM)
+    vmem = pl.BlockSpec(memory_space=pltpu.VMEM)
+    anywhere = pl.BlockSpec(memory_space=pl.ANY)
+    pieces = [piece for h in hops for piece in prompts[h]]
+    work = sessions * len(hops) // 7 + 1
+    return pl.pallas_call(
+        functools.partial(hops_kernel, hops=hops, carried=carried),
+        in_specs=[smem] * 3 + [vmem] * (3 + carried) + [anywhere] * len(pieces),
+        out_specs=vmem,
+        out_shape=jax.ShapeDtypeStruct((sessions * SLOTS, PER_GROUP * HD), jnp.bfloat16),
+        scratch_shapes=[
+            pltpu.VMEM((sessions, 2, 2, PROMPT // 4, 2 * HD), jnp.bfloat16),
+            pltpu.SemaphoreType.DMA((sessions, 2)),
+        ],
+        compiler_params=pltpu.CompilerParams(vmem_limit_bytes=40 << 20),
+        cost_estimate=pl.CostEstimate(
+            flops=work * 4 * PER_GROUP * SLOTS * (PROMPT + SLOTS) * HD,
+            bytes_accessed=work * PROMPT * 4 * HD,
+            transcendentals=work * PER_GROUP * SLOTS * (PROMPT + SLOTS),
+        ),
+        name="attend",
+    )(hop, held, lengths, query, key, value, *([before] if carried else []), *pieces)
+
+
+def shifted(n, by):
+    return [(i, i + by) for i in range(n) if 0 <= i + by < n]
+
+
+def swapped(n, by):
+    return [(i, i ^ by) for i in range(n)]
+
+
+def line_body(
+    thinker_rows,
+    row_session,
+    speaker_of,
+    prompt_slot,
+    prompt_cache,
+    proj_weight,
+    attn_gain,
+    q_weight,
+    k_weight,
+    v_weight,
+    o_weight,
+):
+    planes, plane, rep_count = lax.axis_size("sess"), KVH, 2
+    blocks = planes * rep_count
+    session_all = speaker_of.shape[0]
+    per_plane = session_all // planes
+    per_device = per_plane // plane
+    slot_cap = SLOTS // blocks
+    held = prompt_cache.shape[0]
+    model = proj_weight.shape[1]
+    width = model // 2
+    z, x, c = lax.axis_index("sess"), lax.axis_index("inner"), lax.axis_index("rep")
+    head = x * rep_count + c
+    pair = ("inner", "rep")
+
+    def of_head(h):
+        parts = [
+            lax.dynamic_slice_in_dim(prompt_cache, h * HD + side * KVH * HD, HD, 2)
+            for side in range(2)
+        ]
+        return jnp.concatenate(parts, axis=2)
+
+    from_core = lax.ppermute(of_head(head ^ 1), pair, swapped(4, 1))
+    from_x = lax.ppermute(of_head(head ^ 2), pair, swapped(4, 2))
+    from_far = lax.ppermute(of_head(head ^ 3), pair, swapped(4, 3))
+    right = [jnp.stack([of_head(head), from_core]), jnp.stack([from_x, from_far])]
+    left = list(right)
+    prompts = {0: tuple(right)}
+    for hop in range(1, planes):
+        for chunk in range(2):
+            right[chunk] = lax.ppermute(right[chunk], "sess", shifted(planes, 1))
+            left[chunk] = lax.ppermute(left[chunk], "sess", shifted(planes, -1))
+        prompts[-hop], prompts[hop] = tuple(right), tuple(left)
+
+    row_owner = row_session[:, 0]
+    order = jnp.arange(row_owner.shape[0])
+    same = row_owner[:, None] == row_owner[None, :]
+    earlier = jnp.sum((same & (order[None, :] < order[:, None])).astype(jnp.int32), axis=1)
+    row_slot = row_owner * slot_cap + earlier
+    all_owners = lax.all_gather(
+        row_owner.reshape(-1, 128), ("sess", "rep"), axis=0, tiled=True
+    ).reshape(blocks, -1)
+
+    partial_sum = jnp.dot(thinker_rows, proj_weight, preferred_element_type=jnp.float32)
+    kept = lax.dynamic_slice_in_dim(partial_sum, x * width, width, 1)
+    sent = lax.dynamic_slice_in_dim(partial_sum, (1 - x) * width, width, 1)
+    came = lax.ppermute(sent.astype(jnp.bfloat16), "inner", swapped(2, 1))
+    own_columns = (kept + came.astype(jnp.float32)).astype(jnp.bfloat16)
+    into = (jnp.arange(session_all * slot_cap)[:, None] == row_slot[None, :]).astype(jnp.bfloat16)
+    buffer = jnp.dot(into, own_columns, preferred_element_type=jnp.float32).astype(jnp.bfloat16)
+    buffer = buffer.reshape(planes, per_plane * slot_cap, width)
+    arrived = [lax.dynamic_index_in_dim(buffer, z, 0, keepdims=False)]
+    for by in range(1, planes):
+        outgoing = lax.dynamic_index_in_dim(buffer, z ^ by, 0, keepdims=False)
+        arrived.append(lax.ppermute(outgoing, "sess", swapped(planes, by)))
+    arrived = jnp.stack(arrived)
+    other_x = lax.ppermute(arrived, "inner", swapped(2, 1))
+    low = jnp.where(x == 0, arrived, other_x)
+    high = jnp.where(x == 0, other_x, arrived)
+    halves = jnp.stack([low, high])
+    other_core = lax.ppermute(halves, "rep", swapped(2, 1))
+    slots = jnp.concatenate([halves, other_core], axis=1)
+
+    mine = lambda a: lax.dynamic_slice_in_dim(a, z * per_plane, per_plane, a.ndim - 1)
+    ours = z * per_plane + jnp.arange(per_plane)
+    counts = jnp.sum(
+        (all_owners[:, None, :] == ours[None, :, None]).astype(jnp.int32), axis=2
+    )
+    lengths = jnp.sum(counts, axis=0)
+    kind = jnp.arange(blocks)
+    block = (z ^ (kind % planes)) * rep_count + (c ^ (kind // planes))
+    is_block = block[:, None] == kind[None, :]
+    is_before = kind[None, :] < block[:, None]
+    here = jnp.sum(jnp.where(is_block[:, :, None], counts[None], 0), axis=1)
+    offsets = jnp.sum(jnp.where(is_before[:, :, None], counts[None], 0), axis=1)
+    together = 16 // math.gcd(16, slot_cap)
+    steps = per_plane // together
+    within = jnp.arange(slot_cap)
+    local = (jnp.arange(per_plane) % together)[None, :, None] * SLOTS
+    code = jnp.where(
+        within[None, None, :] < here[:, :, None],
+        offsets[:, :, None] + within[None, None, :] + local,
+        -1,
+    )
+    code = jnp.transpose(
+        code.reshape(blocks, steps, together * slot_cap), (1, 0, 2)
+    ).reshape(steps, 1, blocks * together * slot_cap)
+
+    group_width = PER_GROUP * HD
+    weight = jnp.concatenate(
+        [
+            lax.dynamic_slice_in_dim(q_weight, head * group_width, group_width, 1),
+            lax.dynamic_slice_in_dim(k_weight, head * HD, HD, 1),
+            lax.dynamic_slice_in_dim(v_weight, head * HD, HD, 1),
+        ],
+        axis=1,
+    )
+    states, query, key, value = make_states(
+        code, slots, attn_gain, weight, per_plane, together
+    )
+
+    wanted_slot = jnp.sum(
+        jnp.where(
+            mine(speaker_of)[:, None] == jnp.arange(prompt_slot.shape[0])[None, :],
+            prompt_slot[None, :],
+            0,
+        ),
+        axis=1,
+    )
+    hop = wanted_slot // held - z
+    which = wanted_slot % held
+    near = attend_hops(
+        hop, which, lengths, query, key, value, prompts, (0, -1, 1, -2, 2), None
+    )
+    attended = attend_hops(hop, which, lengths, query, key, value, prompts, (-3, 3), near)
+
+    attended = attended.reshape(plane, per_device * SLOTS, group_width)
+    pieces = [lax.dynamic_index_in_dim(attended, head, 0, keepdims=False)]
+    for by in (2, 3, 1):
+        outgoing = lax.dynamic_index_in_dim(attended, head ^ by, 0, keepdims=False)
+        pieces.append(lax.ppermute(outgoing, pair, swapped(4, by)))
+    o_rows = o_weight.reshape(KVH, group_width, model)
+    first = head * per_device
+    summed = lax.dynamic_slice_in_dim(states, first * SLOTS, per_device * SLOTS, 0).astype(
+        jnp.float32
+    )
+    gathered = jnp.concatenate(pieces, axis=1)
+    turned = jnp.concatenate(
+        [
+            lax.dynamic_index_in_dim(o_rows, head ^ by, 0, keepdims=False)
+            for by in (0, 2, 3, 1)
+        ],
+        axis=0,
+    )
+    summed = summed + jnp.dot(gathered, turned, preferred_element_type=jnp.float32)
+    own_lengths = lax.dynamic_slice_in_dim(lengths, first, per_device)
+    live_rows = (jnp.arange(SLOTS)[None, :] < own_lengths[:, None]).reshape(-1, 1)
+    return (
+        jnp.where(live_rows, summed, 0.0)
+        .astype(jnp.bfloat16)
+        .reshape(per_device, SLOTS, model)
+    )
+
+
 def solution(mesh):
     in_specs = (
         P(("groups", "sess", "rep"), "inner"),
@@ -304,4 +567,6 @@
         P(),
     )
     out_specs = P(("groups", "sess", "inner", "rep"), None, None)
+    sizes = tuple(mesh.shape[name] for name in ("sess", "inner", "rep"))
+    body = line_body if sizes == (4, 2, 2) else general_body
     return jax.shard_map(body, mesh=mesh, in_specs=in_specs, out_specs=out_specs, check_vma=False)

time: 191 us -> 132 us (0.69)
  the two profiles are of different devices: /device:TPU:0 before, /device:TPU:5 now
where the time goes in v2:
time: 132 us
  starting transfers between devices  50.2 us (38%)
  waiting for transfers between devices  19.2 us (15%)
  Pallas kernels  15.4 us (12%)
  other arithmetic  13.9 us (11%)
  local copies, waits for them, and re-layouts  13.8 us (10%)
  blocking collectives  12.3 us (9%)
  matrix products  6.32 us (5%)
    ppermute x6, starting transfers between devices, line_body(): right[chunk] = lax.ppermute(right[chunk], 'sess', shifted(planes, 1))  29.4 us
    all_gather x1, blocking collectives, line_body(): lax.all_gather(row_owner.reshape(-1, 128), ('sess', 'rep'), axis=0, tiled...  12.3 us
    pallas_call x2, Pallas kernels, attend_hops(): pl.pallas_call(functools.partial(hops_kernel, hops=hops, carried=carried)...  11.6 us
    ppermute x6, waiting for transfers between devices, line_body(): right[chunk] = lax.ppermute(right[chunk], 'sess', shifted(planes, 1))  8.92 us
    ppermute x6, starting transfers between devices, line_body(): left[chunk] = lax.ppermute(left[chunk], 'sess', shifted(planes, -1))  7.69 us
    ppermute x3, waiting for transfers between devices, line_body(): pieces.append(lax.ppermute(outgoing, pair, swapped(4, by)))  5.66 us
    ppermute x6, waiting for transfers between devices, line_body(): left[chunk] = lax.ppermute(left[chunk], 'sess', shifted(planes, -1))  4.6 us
    pallas_call x1, Pallas kernels, make_states(): pl.pallas_call(states_kernel, grid=(steps,), in_specs=[pl.BlockSpec((1, 1...  3.82 us
  transfers between devices with their start and end apart: 24, of which 6 were waited for; matrix products, arithmetic and copies ran while one was open for 20% of the time, Pallas kernels for 7%

profile of v2, /device:TPU:5, one launch (start us, length us, event | category | flops | bytes accessed | tf_op | source)
XLA Modules:
  0.0 131.6 jit_solution(5320415500303068429)
XLA Ops:
  0.0 1.9 %copy-done = bf16[1792,896]{1,0:T(8,128)(2,1)S(1)} copy-done((bf16[1792,896]{1,0:T(8,128)(2,1)S(1)}, bf16[1792,896]{1,0:T(8,128)(2,1)}, u32[]{:S(2)}) %copy-start) | copy-done | bytes 3211288
  1.9 2.3 %fusion.30 = f32[256,896]{1,0:T(8,128)S(1)} fusion(bf16[256,1792]{1,0:T(8,128)(2,1)} %param.13, bf16[1792,896]{1,0:T(8,128)(2,1)S(1)} %copy-done), kind=kOutput, calls=%fused_computation.91 | convolution fusion | flops 822083584 | bytes 5046272 | tf_op jit(solution)/shard_map/dot_general | solution.py:454
  7.2 2.1 %constant_dynamic-slice_fusion.3 = (bf16[2,256,128]{2,1,0:T(8,128)(2,1)S(1)}, bf16[2,256,128]{2,1,0:T(8,128)(2,1)S(1)}, bf16[2,256,128]{2,1,0:T(8,128)(2,1)S(1)}...) fusion(bf16[2,256,1024]{2,1,0:T(8,128)(2,1)} %param.17, ...), kind=kLoop, calls=%fused_computation.57 | loop fusion | bytes 2097184 | tf_op jit(solution)/shard_map/dynamic_slice | solution.py:428
  11.1 2.3 %collective-permute-start.8 = (bf16[2,256,256]{2,1,0:T(8,128)(2,1)}, bf16[2,256,256]{2,1,0:T(8,128)(2,1)}, u32[]{:S(2)}, u32[]{:S(2)}) collective-permute-start(bf16[2,256,256]{2,1,0:T(8,128)(2,1)} %pad_maximum_fusion.8), channel_id=1, source_target_pairs={{0,3},{1,2},{2,1},{3,0},{4,7},{5,6},{6,5},{7,4},{8,11},{9,10},{10,... | collective-permute-start | bytes 786440 | tf_op jit(solution)/shard_map/ppermute | solution.py:435
  14.3 12.3 %all-gather = s32[8,2,128]{2,1,0:T(2,128)S(1)} all-gather(s32[1,2,128]{2,1,0:T(2,128)S(1)} %bitcast.54), channel_id=1, replica_groups=mesh['groups'=2,'sess'=4,'inner'=2,'rep'=2] {'sess','rep'}, dimensions={0}, use_global_device_ids=true | all-gather | bytes 9216 | tf_op jit(solution)/shard_map/all_gather | solution.py:450
  26.7 2.0 %constant_dynamic-slice_fusion.10 = bf16[896,384]{1,0:T(8,128)(2,1)} fusion(bf16[896,1536]{1,0:T(8,128)(2,1)} %param.20, s32[]{:T(128)S(6)} %select_n.160), kind=kLoop, calls=%fused_computation.64 | loop fusion | bytes 1376260 | tf_op jit(solution)/shard_map/dynamic_slice | solution.py:502
  30.2 2.5 %convolution_convert_fusion = bf16[384,448]{0,1:T(8,128)(2,1)} fusion(bf16[256,448]{1,0:T(8,128)(2,1)} %collective-permute-done, f32[256,896]{1,0:T(8,128)} %copy-done.8, s32[]{:T(128)S(6)} %select_n.152, s32[256]{0:T(256)S(1)} %multiply_add_fusion), kind=kOutput, calls=%fused_computation.9 | convolution fusion | flops 88694784 | bytes 1131524 | tf_op jit(solution)/shard_map/dot_general | solution.py:460
  32.7 1.9 %copy.20 = bf16[384,448]{1,0:T(8,128)(2,1)} copy(bf16[384,448]{0,1:T(8,128)(2,1)} %convolution_convert_fusion) | data formatting | bytes 688128 | tf_op jit(solution)/shard_map/convert_element_type | solution.py:460
  36.4 3.5 %collective-permute-start.3 = (bf16[96,448]{1,0:T(8,128)(2,1)}, bf16[96,448]{1,0:T(8,128)(2,1)}, u32[]{:S(2)}, u32[]{:S(2)}) collective-permute-start(bf16[96,448]{1,0:T(8,128)(2,1)} %get-tuple-element.36), channel_id=1, source_target_pairs={{0,12},{4,8},{8,4},{12,0},{1,13},{5,9},{9,5},{13,1},{2,14},{6,10},... | collective-permute-start | bytes 258056 | tf_op jit(solution)/shard_map/ppermute | solution.py:465
  41.8 2.1 %collective-permute-start.10 = (bf16[2,2,256,256]{3,2,1,0:T(8,128)(2,1)}, bf16[2,2,256,256]{3,2,1,0:T(8,128)(2,1)}, u32[]{:S(2)}, u32[]{:S(2)}) collective-permute-start(bf16[2,2,256,256]{3,2,1,0:T(8,128)(2,1)} %pad_maximum_fusion.4.refs_1_), channel_id=1, source_target_pairs={{0,4},{4,8},{8,12},{1,5},{5,9},{9,13},{2,6},{6,10},{10,14},{3,7},{... | collective-permute-start | bytes 1572872 | tf_op jit(solution)/shard_map/ppermute | solution.py:441
  47.0 4.8 %collective-permute-start.9 = (bf16[2,2,256,256]{3,2,1,0:T(8,128)(2,1)}, bf16[2,2,256,256]{3,2,1,0:T(8,128)(2,1)}, u32[]{:S(2)}, u32[]{:S(2)}) collective-permute-start(bf16[2,2,256,256]{3,2,1,0:T(8,128)(2,1)} %pad_maximum_fusion.3.refs_0_), channel_id=1, source_target_pairs={{0,4},{4,8},{8,12},{1,5},{5,9},{9,13},{2,6},{6,10},{10,14},{3,7},{... | collective-permute-start | bytes 1572872 | tf_op jit(solution)/shard_map/ppermute | solution.py:441
  56.4 4.8 %collective-permute-start.14 = (bf16[2,2,256,256]{3,2,1,0:T(8,128)(2,1)}, bf16[2,2,256,256]{3,2,1,0:T(8,128)(2,1)}, u32[]{:S(2)}, u32[]{:S(2)}) collective-permute-start(bf16[2,2,256,256]{3,2,1,0:T(8,128)(2,1)} %collective-permute-done.10.refs_3_), channel_id=1, source_target_pairs={{0,4},{4,8},{8,12},{1,5},{5,9},{9,13},{2,6},{6,10},{10,14},{3,7},{... | collective-permute-start | bytes 1572872 | tf_op jit(solution)/shard_map/ppermute | solution.py:441
  62.5 2.6 %collective-permute-done.9.refs_2_ = bf16[2,2,256,256]{3,2,1,0:T(8,128)(2,1)} collective-permute-done((bf16[2,2,256,256]{3,2,1,0:T(8,128)(2,1)}, bf16[2,2,256,256]{3,2,1,0:T(8,128)(2,1)}, u32[]{:S(2)}, u32[]{:S(2)}) %collective-permute-start.9) | collective-permute-done | bytes 524320 | tf_op jit(solution)/shard_map/ppermute | solution.py:441
  65.1 6.3 %collective-permute-start.13 = (bf16[2,2,256,256]{3,2,1,0:T(8,128)(2,1)}, bf16[2,2,256,256]{3,2,1,0:T(8,128)(2,1)}, u32[]{:S(2)}, u32[]{:S(2)}) collective-permute-start(bf16[2,2,256,256]{3,2,1,0:T(8,128)(2,1)} %collective-permute-done.9.refs_2_), channel_id=1, source_target_pairs={{0,4},{4,8},{8,12},{1,5},{5,9},{9,13},{2,6},{6,10},{10,14},{3,7},{... | collective-permute-start | bytes 1572872 | tf_op jit(solution)/shard_map/ppermute | solution.py:441
  77.9 5.1 %collective-permute-start.18 = (bf16[2,2,256,256]{3,2,1,0:T(8,128)(2,1)}, bf16[2,2,256,256]{3,2,1,0:T(8,128)(2,1)}, u32[]{:S(2)}, u32[]{:S(2)}) collective-permute-start(bf16[2,2,256,256]{3,2,1,0:T(8,128)(2,1)} %collective-permute-done.14.refs_7_), channel_id=1, source_target_pairs={{0,4},{4,8},{8,12},{1,5},{5,9},{9,13},{2,6},{6,10},{10,14},{3,7},{... | collective-permute-start | bytes 1572872 | tf_op jit(solution)/shard_map/ppermute | solution.py:441
  84.3 3.2 %collective-permute-done.13.refs_6_ = bf16[2,2,256,256]{3,2,1,0:T(8,128)(2,1)} collective-permute-done((bf16[2,2,256,256]{3,2,1,0:T(8,128)(2,1)}, bf16[2,2,256,256]{3,2,1,0:T(8,128)(2,1)}, u32[]{:S(2)}, u32[]{:S(2)}) %collective-permute-start.13) | collective-permute-done | bytes 524320 | tf_op jit(solution)/shard_map/ppermute | solution.py:441
  87.6 6.3 %collective-permute-start.17 = (bf16[2,2,256,256]{3,2,1,0:T(8,128)(2,1)}, bf16[2,2,256,256]{3,2,1,0:T(8,128)(2,1)}, u32[]{:S(2)}, u32[]{:S(2)}) collective-permute-start(bf16[2,2,256,256]{3,2,1,0:T(8,128)(2,1)} %collective-permute-done.13.refs_6_), channel_id=1, source_target_pairs={{0,4},{4,8},{8,12},{1,5},{5,9},{9,13},{2,6},{6,10},{10,14},{3,7},{... | collective-permute-start | bytes 1572872 | tf_op jit(solution)/shard_map/ppermute | solution.py:441
  97.3 3.8 %states.1 = (bf16[768,896]{1,0:T(8,128)(2,1)S(1)}, bf16[768,384]{1,0:T(8,128)(2,1)S(1)}, bf16[768,128]{1,0:T(8,128)(2,1)S(1)}, bf16[768,128]{1,0:T(8,128)(2,1)S(1)}) custom-call(s32[2,1,384]{2,1,0:T(1,128)S(1)} %reshape.139.code_ref, bf16[2,8,96,448]{3,2,1,0:T(8,128)(2,1)S(1)} %pad_maximum_fusion.slots_ref, bf16[1,896]{1,0:T(2,128)(2,1)S(1)} %reshape.141.gain_ref, ...), custom_call_target="tpu_custom_call" | custom-call | tf_op jit(solution)/shard_map/states/pallas_call | solution.py:103
  101.2 5.8 %attend.2.refs_0_ = bf16[768,384]{1,0:T(8,128)(2,1)S(1)} custom-call(s32[8]{0:T(128)S(1)} %get-tuple-element.42.hop_ref, s32[8]{0:T(128)S(1)} %get-tuple-element.41.held_ref, s32[8]{0:T(128)S(1)} %get-tuple-element.14.length_ref, bf16[768,384]{1,0:T(8,128)(2,1)S(1)} %get-tuple-element.10.query_ref, bf16[768,128]{1,0:T(8,128)(2,1)S(1)} %get-tuple-element.11.key_ref, ...), custom_call_target="tpu_custom_call" | custom-call | flops 990904320 | bytes 3145728 | tf_op jit(solution)/shard_map/attend/pallas_call | solution.py:373
  107.0 3.1 %collective-permute-done.17.refs_1_ = bf16[2,2,256,256]{3,2,1,0:T(8,128)(2,1)} collective-permute-done((bf16[2,2,256,256]{3,2,1,0:T(8,128)(2,1)}, bf16[2,2,256,256]{3,2,1,0:T(8,128)(2,1)}, u32[]{:S(2)}, u32[]{:S(2)}) %collective-permute-start.17) | collective-permute-done | bytes 524320 | tf_op jit(solution)/shard_map/ppermute | solution.py:441
  110.0 4.6 %collective-permute-done.19.refs_3_ = bf16[2,2,256,256]{3,2,1,0:T(8,128)(2,1)} collective-permute-done((bf16[2,2,256,256]{3,2,1,0:T(8,128)(2,1)}, bf16[2,2,256,256]{3,2,1,0:T(8,128)(2,1)}, u32[]{:S(2)}, u32[]{:S(2)}) %collective-permute-start.19) | collective-permute-done | bytes 524320 | tf_op jit(solution)/shard_map/ppermute | solution.py:442
  114.6 5.8 %attend.3 = bf16[768,384]{1,0:T(8,128)(2,1)S(1)} custom-call(s32[8]{0:T(128)S(1)} %get-tuple-element.42.hop_ref, s32[8]{0:T(128)S(1)} %get-tuple-element.41.held_ref, s32[8]{0:T(128)S(1)} %get-tuple-element.14.length_ref, bf16[768,384]{1,0:T(8,128)(2,1)S(1)} %get-tuple-element.10.query_ref, bf16[768,128]{1,0:T(8,128)(2,1)S(1)} %get-tuple-element.11.key_ref, ...), custom_call_target="tpu_custom_call" | custom-call | flops 495452160 | bytes 1572864 | tf_op jit(solution)/shard_map/attend/pallas_call | solution.py:373
  120.8 3.4 %collective-permute-start.22 = (bf16[192,384]{1,0:T(8,128)(2,1)S(1)}, bf16[192,384]{1,0:T(8,128)(2,1)S(1)}, u32[]{:S(2)}, u32[]{:S(2)}) collective-permute-start(bf16[192,384]{1,0:T(8,128)(2,1)S(1)} %get-tuple-element.33), channel_id=1, source_target_pairs={{0,3},{1,2},{2,1},{3,0},{4,7},{5,6},{6,5},{7,4},{8,11},{9,10},{10,... | collective-permute-start | bytes 442376 | tf_op jit(solution)/shard_map/ppermute | solution.py:531
  124.5 5.5 %collective-permute-done.22 = bf16[192,384]{1,0:T(8,128)(2,1)S(1)} collective-permute-done((bf16[192,384]{1,0:T(8,128)(2,1)S(1)}, bf16[192,384]{1,0:T(8,128)(2,1)S(1)}, u32[]{:S(2)}, u32[]{:S(2)}) %collective-permute-start.22) | collective-permute-done | bytes 147488 | tf_op jit(solution)/shard_map/ppermute | solution.py:531
  (103 shorter events, 33.1 us)
Async XLA Ops:
  6.0 24.2 %collective-permute-start = (bf16[256,448]{1,0:T(8,128)(2,1)}, bf16[256,448]{1,0:T(8,128)(2,1)}, u32[]{:S(2)}, u32[]{:S(2)}) collective-permute-start(bf16[256,448]{1,0:T(8,128)(2,1)} %dynamic-slice_convert_fusion), channel_id=1, source_target_pairs={{0,2},{2,0},{1,3},{3,1},{4,6},{6,4},{5,7},{7,5},{8,10},{10,8},{9,1... | collective-permute-start | bytes 688136 | tf_op jit(solution)/shard_map/ppermute | solution.py:457
  10.1 26.3 %collective-permute-start.7 = (bf16[2,256,256]{2,1,0:T(8,128)(2,1)}, bf16[2,256,256]{2,1,0:T(8,128)(2,1)}, u32[]{:S(2)}, u32[]{:S(2)}) collective-permute-start(bf16[2,256,256]{2,1,0:T(8,128)(2,1)} %pad_maximum_fusion.7), channel_id=1, source_target_pairs={{0,2},{1,3},{2,0},{3,1},{4,6},{5,7},{6,4},{7,5},{8,10},{9,11},{10,... | collective-permute-start | bytes 786440 | tf_op jit(solution)/shard_map/ppermute | solution.py:434
  11.1 28.8 %collective-permute-start.8 = (bf16[2,256,256]{2,1,0:T(8,128)(2,1)}, bf16[2,256,256]{2,1,0:T(8,128)(2,1)}, u32[]{:S(2)}, u32[]{:S(2)}) collective-permute-start(bf16[2,256,256]{2,1,0:T(8,128)(2,1)} %pad_maximum_fusion.8), channel_id=1, source_target_pairs={{0,3},{1,2},{2,1},{3,0},{4,7},{5,6},{6,5},{7,4},{8,11},{9,10},{10,... | collective-permute-start | bytes 786440 | tf_op jit(solution)/shard_map/ppermute | solution.py:435
  14.1 29.7 %collective-permute-start.6 = (bf16[2,256,256]{2,1,0:T(8,128)(2,1)}, bf16[2,256,256]{2,1,0:T(8,128)(2,1)}, u32[]{:S(2)}, u32[]{:S(2)}) collective-permute-start(bf16[2,256,256]{2,1,0:T(8,128)(2,1)} %pad_maximum_fusion.6), channel_id=1, source_target_pairs={{0,1},{1,0},{2,3},{3,2},{4,5},{5,4},{6,7},{7,6},{8,9},{9,8},{10,11... | collective-permute-start | bytes 786440 | tf_op jit(solution)/shard_map/ppermute | solution.py:433
  36.4 10.6 %collective-permute-start.1 = (bf16[96,448]{1,0:T(8,128)(2,1)S(1)}, bf16[96,448]{1,0:T(8,128)(2,1)}, u32[]{:S(2)}, u32[]{:S(2)}) collective-permute-start(bf16[96,448]{1,0:T(8,128)(2,1)S(1)} %get-tuple-element.38), channel_id=1, source_target_pairs={{0,4},{4,0},{8,12},{12,8},{1,5},{5,1},{9,13},{13,9},{2,6},{6,2},{1... | collective-permute-start | bytes 258056 | tf_op jit(solution)/shard_map/ppermute | solution.py:465
  36.4 15.4 %collective-permute-start.2 = (bf16[96,448]{1,0:T(8,128)(2,1)S(1)}, bf16[96,448]{1,0:T(8,128)(2,1)}, u32[]{:S(2)}, u32[]{:S(2)}) collective-permute-start(bf16[96,448]{1,0:T(8,128)(2,1)S(1)} %get-tuple-element.37), channel_id=1, source_target_pairs={{0,8},{4,12},{8,0},{12,4},{1,9},{5,13},{9,1},{13,5},{2,10},{6,14},... | collective-permute-start | bytes 258056 | tf_op jit(solution)/shard_map/ppermute | solution.py:465
  36.4 17.4 %collective-permute-start.3 = (bf16[96,448]{1,0:T(8,128)(2,1)}, bf16[96,448]{1,0:T(8,128)(2,1)}, u32[]{:S(2)}, u32[]{:S(2)}) collective-permute-start(bf16[96,448]{1,0:T(8,128)(2,1)} %get-tuple-element.36), channel_id=1, source_target_pairs={{0,12},{4,8},{8,4},{12,0},{1,13},{5,9},{9,5},{13,1},{2,14},{6,10},... | collective-permute-start | bytes 258056 | tf_op jit(solution)/shard_map/ppermute | solution.py:465
  41.8 14.6 %collective-permute-start.10 = (bf16[2,2,256,256]{3,2,1,0:T(8,128)(2,1)}, bf16[2,2,256,256]{3,2,1,0:T(8,128)(2,1)}, u32[]{:S(2)}, u32[]{:S(2)}) collective-permute-start(bf16[2,2,256,256]{3,2,1,0:T(8,128)(2,1)} %pad_maximum_fusion.4.refs_1_), channel_id=1, source_target_pairs={{0,4},{4,8},{8,12},{1,5},{5,9},{9,13},{2,6},{6,10},{10,14},{3,7},{... | collective-permute-start | bytes 1572872 | tf_op jit(solution)/shard_map/ppermute | solution.py:441
  43.9 17.3 %collective-permute-start.12 = (bf16[2,2,256,256]{3,2,1,0:T(8,128)(2,1)}, bf16[2,2,256,256]{3,2,1,0:T(8,128)(2,1)}, u32[]{:S(2)}, u32[]{:S(2)}) collective-permute-start(bf16[2,2,256,256]{3,2,1,0:T(8,128)(2,1)} %pad_maximum_fusion.4.refs_1_), channel_id=1, source_target_pairs={{4,0},{8,4},{12,8},{5,1},{9,5},{13,9},{6,2},{10,6},{14,10},{7,3},{... | collective-permute-start | bytes 1572872 | tf_op jit(solution)/shard_map/ppermute | solution.py:442
  47.0 18.1 %collective-permute-start.9 = (bf16[2,2,256,256]{3,2,1,0:T(8,128)(2,1)}, bf16[2,2,256,256]{3,2,1,0:T(8,128)(2,1)}, u32[]{:S(2)}, u32[]{:S(2)}) collective-permute-start(bf16[2,2,256,256]{3,2,1,0:T(8,128)(2,1)} %pad_maximum_fusion.3.refs_0_), channel_id=1, source_target_pairs={{0,4},{4,8},{8,12},{1,5},{5,9},{9,13},{2,6},{6,10},{10,14},{3,7},{... | collective-permute-start | bytes 1572872 | tf_op jit(solution)/shard_map/ppermute | solution.py:441
  51.8 19.7 %collective-permute-start.11 = (bf16[2,2,256,256]{3,2,1,0:T(8,128)(2,1)}, bf16[2,2,256,256]{3,2,1,0:T(8,128)(2,1)}, u32[]{:S(2)}, u32[]{:S(2)}) collective-permute-start(bf16[2,2,256,256]{3,2,1,0:T(8,128)(2,1)} %pad_maximum_fusion.3.refs_0_), channel_id=1, source_target_pairs={{4,0},{8,4},{12,8},{5,1},{9,5},{13,9},{6,2},{10,6},{14,10},{7,3},{... | collective-permute-start | bytes 1572872 | tf_op jit(solution)/shard_map/ppermute | solution.py:442
  55.0 17.8 %collective-permute-start.4 = (bf16[4,96,448]{2,1,0:T(8,128)(2,1)S(1)}, bf16[4,96,448]{2,1,0:T(8,128)(2,1)S(1)}, u32[]{:S(2)}, u32[]{:S(2)}) collective-permute-start(bf16[4,96,448]{2,1,0:T(8,128)(2,1)S(1)} %pad_maximum_fusion.5), channel_id=1, source_target_pairs={{0,2},{2,0},{1,3},{3,1},{4,6},{6,4},{5,7},{7,5},{8,10},{10,8},{9,1... | collective-permute-start | bytes 1032200 | tf_op jit(solution)/shard_map/ppermute | solution.py:467
  56.4 21.5 %collective-permute-start.14 = (bf16[2,2,256,256]{3,2,1,0:T(8,128)(2,1)}, bf16[2,2,256,256]{3,2,1,0:T(8,128)(2,1)}, u32[]{:S(2)}, u32[]{:S(2)}) collective-permute-start(bf16[2,2,256,256]{3,2,1,0:T(8,128)(2,1)} %collective-permute-done.10.refs_3_), channel_id=1, source_target_pairs={{0,4},{4,8},{8,12},{1,5},{5,9},{9,13},{2,6},{6,10},{10,14},{3,7},{... | collective-permute-start | bytes 1572872 | tf_op jit(solution)/shard_map/ppermute | solution.py:441
  61.2 21.9 %collective-permute-start.16 = (bf16[2,2,256,256]{3,2,1,0:T(8,128)(2,1)}, bf16[2,2,256,256]{3,2,1,0:T(8,128)(2,1)}, u32[]{:S(2)}, u32[]{:S(2)}) collective-permute-start(bf16[2,2,256,256]{3,2,1,0:T(8,128)(2,1)} %collective-permute-done.12.refs_5_), channel_id=1, source_target_pairs={{4,0},{8,4},{12,8},{5,1},{9,5},{13,9},{6,2},{10,6},{14,10},{7,3},{... | collective-permute-start | bytes 1572872 | tf_op jit(solution)/shard_map/ppermute | solution.py:442
  65.1 22.5 %collective-permute-start.13 = (bf16[2,2,256,256]{3,2,1,0:T(8,128)(2,1)}, bf16[2,2,256,256]{3,2,1,0:T(8,128)(2,1)}, u32[]{:S(2)}, u32[]{:S(2)}) collective-permute-start(bf16[2,2,256,256]{3,2,1,0:T(8,128)(2,1)} %collective-permute-done.9.refs_2_), channel_id=1, source_target_pairs={{0,4},{4,8},{8,12},{1,5},{5,9},{9,13},{2,6},{6,10},{10,14},{3,7},{... | collective-permute-start | bytes 1572872 | tf_op jit(solution)/shard_map/ppermute | solution.py:441
  71.4 22.5 %collective-permute-start.15 = (bf16[2,2,256,256]{3,2,1,0:T(8,128)(2,1)}, bf16[2,2,256,256]{3,2,1,0:T(8,128)(2,1)}, u32[]{:S(2)}, u32[]{:S(2)}) collective-permute-start(bf16[2,2,256,256]{3,2,1,0:T(8,128)(2,1)} %collective-permute-done.11.refs_4_), channel_id=1, source_target_pairs={{4,0},{8,4},{12,8},{5,1},{9,5},{13,9},{6,2},{10,6},{14,10},{7,3},{... | collective-permute-start | bytes 1572872 | tf_op jit(solution)/shard_map/ppermute | solution.py:442
  74.9 20.7 %collective-permute-start.5 = (bf16[2,4,96,448]{3,2,1,0:T(8,128)(2,1)}, bf16[2,4,96,448]{3,2,1,0:T(8,128)(2,1)}, u32[]{:S(2)}, u32[]{:S(2)}) collective-permute-start(bf16[2,4,96,448]{3,2,1,0:T(8,128)(2,1)} %pad_maximum_fusion.2), channel_id=1, source_target_pairs={{0,1},{1,0},{2,3},{3,2},{4,5},{5,4},{6,7},{7,6},{8,9},{9,8},{10,11... | collective-permute-start | bytes 2064392 | tf_op jit(solution)/shard_map/ppermute | solution.py:471
  77.9 29.0 %collective-permute-start.18 = (bf16[2,2,256,256]{3,2,1,0:T(8,128)(2,1)}, bf16[2,2,256,256]{3,2,1,0:T(8,128)(2,1)}, u32[]{:S(2)}, u32[]{:S(2)}) collective-permute-start(bf16[2,2,256,256]{3,2,1,0:T(8,128)(2,1)} %collective-permute-done.14.refs_7_), channel_id=1, source_target_pairs={{0,4},{4,8},{8,12},{1,5},{5,9},{9,13},{2,6},{6,10},{10,14},{3,7},{... | collective-permute-start | bytes 1572872 | tf_op jit(solution)/shard_map/ppermute | solution.py:441
  83.0 23.9 %collective-permute-start.20 = (bf16[2,2,256,256]{3,2,1,0:T(8,128)(2,1)}, bf16[2,2,256,256]{3,2,1,0:T(8,128)(2,1)}, u32[]{:S(2)}, u32[]{:S(2)}) collective-permute-start(bf16[2,2,256,256]{3,2,1,0:T(8,128)(2,1)} %collective-permute-done.16.refs_9_), channel_id=1, source_target_pairs={{4,0},{8,4},{12,8},{5,1},{9,5},{13,9},{6,2},{10,6},{14,10},{7,3},{... | collective-permute-start | bytes 1572872 | tf_op jit(solution)/shard_map/ppermute | solution.py:442
  87.6 22.5 %collective-permute-start.17 = (bf16[2,2,256,256]{3,2,1,0:T(8,128)(2,1)}, bf16[2,2,256,256]{3,2,1,0:T(8,128)(2,1)}, u32[]{:S(2)}, u32[]{:S(2)}) collective-permute-start(bf16[2,2,256,256]{3,2,1,0:T(8,128)(2,1)} %collective-permute-done.13.refs_6_), channel_id=1, source_target_pairs={{0,4},{4,8},{8,12},{1,5},{5,9},{9,13},{2,6},{6,10},{10,14},{3,7},{... | collective-permute-start | bytes 1572872 | tf_op jit(solution)/shard_map/ppermute | solution.py:441
  93.9 20.7 %collective-permute-start.19 = (bf16[2,2,256,256]{3,2,1,0:T(8,128)(2,1)}, bf16[2,2,256,256]{3,2,1,0:T(8,128)(2,1)}, u32[]{:S(2)}, u32[]{:S(2)}) collective-permute-start(bf16[2,2,256,256]{3,2,1,0:T(8,128)(2,1)} %collective-permute-done.15.refs_8_), channel_id=1, source_target_pairs={{4,0},{8,4},{12,8},{5,1},{9,5},{13,9},{6,2},{10,6},{14,10},{7,3},{... | collective-permute-start | bytes 1572872 | tf_op jit(solution)/shard_map/ppermute | solution.py:442
  120.5 4.1 %collective-permute-start.21 = (bf16[192,384]{1,0:T(8,128)(2,1)S(1)}, bf16[192,384]{1,0:T(8,128)(2,1)S(1)}, u32[]{:S(2)}, u32[]{:S(2)}) collective-permute-start(bf16[192,384]{1,0:T(8,128)(2,1)S(1)} %get-tuple-element.34), channel_id=1, source_target_pairs={{0,2},{1,3},{2,0},{3,1},{4,6},{5,7},{6,4},{7,5},{8,10},{9,11},{10,... | collective-permute-start | bytes 442376 | tf_op jit(solution)/shard_map/ppermute | solution.py:531
  120.8 9.3 %collective-permute-start.22 = (bf16[192,384]{1,0:T(8,128)(2,1)S(1)}, bf16[192,384]{1,0:T(8,128)(2,1)S(1)}, u32[]{:S(2)}, u32[]{:S(2)}) collective-permute-start(bf16[192,384]{1,0:T(8,128)(2,1)S(1)} %get-tuple-element.33), channel_id=1, source_target_pairs={{0,3},{1,2},{2,1},{3,0},{4,7},{5,6},{6,5},{7,4},{8,11},{9,10},{10,... | collective-permute-start | bytes 442376 | tf_op jit(solution)/shard_map/ppermute | solution.py:531
  124.1 5.9 %collective-permute-start.23 = (bf16[192,384]{1,0:T(8,128)(2,1)S(1)}, bf16[192,384]{1,0:T(8,128)(2,1)S(1)}, u32[]{:S(2)}, u32[]{:S(2)}) collective-permute-start(bf16[192,384]{1,0:T(8,128)(2,1)S(1)} %get-tuple-element.32), channel_id=1, source_target_pairs={{0,1},{1,0},{2,3},{3,2},{4,5},{5,4},{6,7},{7,6},{8,9},{9,8},{10,11... | collective-permute-start | bytes 442376 | tf_op jit(solution)/shard_map/ppermute | solution.py:531
  (13 other events, 148.1 us)

commit v3 on v2

--- a/solution.py
+++ b/solution.py
@@ -289,7 +289,217 @@
     )
 
 
-def session_attention(query_ref, key_ref, value_ref, kv, out_ref, session, length):
+EXTRA = 16
+SMEM = pl.BlockSpec(memory_space=pltpu.SMEM)
+VMEM = pl.BlockSpec(memory_space=pltpu.VMEM)
+ANY = pl.BlockSpec(memory_space=pl.ANY)
+
+
+def split_heads_kernel(head_ref, cache_ref, *refs):
+    out_refs, sem = refs[:-1], refs[-1]
+    copies = []
+    for by, out_ref in enumerate(out_refs):
+        for side in range(2):
+            start = pl.multiple_of((head_ref[0] ^ by) * HD + side * KVH * HD, HD)
+            copies.append(
+                pltpu.make_async_copy(
+                    cache_ref.at[:, :, pl.ds(start, HD)],
+                    out_ref.at[:, :, side * HD : (side + 1) * HD],
+                    sem.at[by, side],
+                )
+            )
+    for copy in copies:
+        copy.start()
+    for copy in copies:
+        copy.wait()
+
+
+def split_heads(head, cache):
+    held, tokens, _ = cache.shape
+    shape = jax.ShapeDtypeStruct((held, tokens, 2 * HD), cache.dtype)
+    return pl.pallas_call(
+        split_heads_kernel,
+        in_specs=[SMEM, ANY],
+        out_specs=[ANY] * KVH,
+        out_shape=[shape] * KVH,
+        scratch_shapes=[pltpu.SemaphoreType.DMA((KVH, 2))],
+        cost_estimate=pl.CostEstimate(flops=0, bytes_accessed=2 * cache.size * 2, transcendentals=0),
+        name="split_heads",
+    )(head, cache)
+
+
+def stack_kernel(*refs):
+    in_refs, (out_ref, sem) = refs[:-2], refs[-2:]
+    copies = []
+    place = 0
+    for i, in_ref in enumerate(in_refs):
+        count = in_ref.shape[0]
+        copies.append(
+            pltpu.make_async_copy(in_ref, out_ref.at[place : place + count], sem.at[i])
+        )
+        place += count
+    for copy in copies:
+        copy.start()
+    for copy in copies:
+        copy.wait()
+
+
+def stack(*arrays):
+    total = sum(a.shape[0] for a in arrays)
+    size = sum(a.size for a in arrays)
+    return pl.pallas_call(
+        stack_kernel,
+        in_specs=[ANY] * len(arrays),
+        out_specs=ANY,
+        out_shape=jax.ShapeDtypeStruct((total,) + arrays[0].shape[1:], arrays[0].dtype),
+        scratch_shapes=[pltpu.SemaphoreType.DMA((len(arrays),))],
+        cost_estimate=pl.CostEstimate(flops=0, bytes_accessed=4 * size, transcendentals=0),
+        name="stack",
+    )(*arrays)
+
+
+def route_kernel(z_ref, kept_ref, came_ref, owner_ref, owner_row_ref, *out_refs,
+                 slot_cap, per_plane):
+    rows = kept_ref.shape[0]
+    planes = len(out_refs)
+    size = out_refs[0].shape[0]
+    live = per_plane * slot_cap
+    columns = (kept_ref[...] + came_ref[...].astype(jnp.float32)).astype(jnp.bfloat16)
+    owner, owner_row = owner_ref[...], owner_row_ref[...]
+    above = lax.broadcasted_iota(jnp.int32, (rows, rows), 0)
+    beside = lax.broadcasted_iota(jnp.int32, (rows, rows), 1)
+    earlier = jnp.sum(
+        jnp.where((owner == owner_row) & (above < beside), 1.0, 0.0), axis=0, keepdims=True
+    ).astype(jnp.int32)
+    target = lax.div(owner_row, per_plane) ^ z_ref[0]
+    code = target * size + lax.rem(owner_row, per_plane) * slot_cap + earlier
+    place = lax.broadcasted_iota(jnp.int32, (planes * size, rows), 0)
+    into = (place == code).astype(jnp.bfloat16)
+    routed = jnp.dot(into, columns, preferred_element_type=jnp.float32).astype(jnp.bfloat16)
+    lane = lax.broadcasted_iota(jnp.int32, (rows, HD), 1)
+    named = (lane == owner).astype(jnp.bfloat16)
+    counts = jnp.dot(
+        jnp.ones((EXTRA, rows), jnp.bfloat16), named, preferred_element_type=jnp.float32
+    ).astype(jnp.bfloat16)
+    for k, out_ref in enumerate(out_refs):
+        out_ref[:live] = routed[k * size : k * size + live]
+        out_ref[live:] = jnp.zeros((EXTRA, out_ref.shape[1]), jnp.bfloat16)
+        out_ref[live:, :HD] = counts
+
+
+def route(z, kept, came, row_session, planes, per_plane, slot_cap):
+    width = kept.shape[1]
+    rows = row_session.shape[0]
+    size = per_plane * slot_cap + EXTRA
+    return pl.pallas_call(
+        functools.partial(route_kernel, slot_cap=slot_cap, per_plane=per_plane),
+        in_specs=[SMEM] + [VMEM] * 4,
+        out_specs=[VMEM] * planes,
+        out_shape=[jax.ShapeDtypeStruct((size, width), jnp.bfloat16)] * planes,
+        cost_estimate=pl.CostEstimate(
+            flops=2 * planes * size * rows * width, bytes_accessed=rows * width * 8, transcendentals=0
+        ),
+        name="route",
+    )(z, kept, came, row_session, row_session.reshape(1, rows))
+
+
+def place_kernel(index_ref, mine_ref, core_ref, gain_ref, weight_ref, cos_ref, sin_ref,
+                 states_ref, query_ref, key_ref, value_ref, length_ref, *, slot_cap, together):
+    z, x, c = index_ref[0], index_ref[1], index_ref[2]
+    planes = mine_ref.shape[0] // 2
+    blocks = 2 * planes
+    width = mine_ref.shape[2]
+    live = mine_ref.shape[1] - EXTRA
+    per_plane = live // slot_cap
+    steps = per_plane // together
+    window = together * slot_cap
+    total = together * SLOTS
+    counts = jnp.concatenate(
+        [ref[k, live : live + 1, :HD] for ref in (mine_ref, core_ref) for k in range(planes)],
+        axis=0,
+    ).astype(jnp.float32)
+    kind = lambda axis: lax.broadcasted_iota(jnp.int32, (blocks, blocks), axis)
+    true_block = lambda k: (z ^ (k % planes)) * 2 + (c ^ (k // planes))
+    before = (true_block(kind(1)) < true_block(kind(0))).astype(jnp.float32)
+    offsets = jnp.dot(before, counts, preferred_element_type=jnp.float32)
+    session_lane = lax.broadcasted_iota(jnp.int32, (HD, HD), 0)
+    local_lane = lax.broadcasted_iota(jnp.int32, (HD, HD), 1)
+    ours = (session_lane == z * per_plane + local_lane).astype(jnp.float32)
+    sums = jnp.dot(
+        jnp.broadcast_to(jnp.sum(counts, axis=0, keepdims=True), (8, HD)),
+        ours,
+        preferred_element_type=jnp.float32,
+    )
+    length_ref[...] = sums[:1].astype(jnp.int32)
+    cosine, sine = cos_ref[...], sin_ref[...]
+    gain = gain_ref[...].astype(jnp.float32)
+    for step in range(steps):
+        slot = lax.broadcasted_iota(jnp.int32, (blocks, blocks * window), 1)
+        in_block = slot % window
+        spread = lax.broadcasted_iota(jnp.int32, (HD, blocks * window), 1) % window // slot_cap
+        from_lane = lax.broadcasted_iota(jnp.int32, (HD, blocks * window), 0)
+        expand = (from_lane == z * per_plane + step * together + spread).astype(jnp.float32)
+        here = jnp.dot(counts, expand, preferred_element_type=jnp.float32).astype(jnp.int32)
+        start = jnp.dot(offsets, expand, preferred_element_type=jnp.float32).astype(jnp.int32)
+        within = in_block % slot_cap
+        row = jnp.where(within < here, start + within + in_block // slot_cap * SLOTS, -1)
+        block = lax.broadcasted_iota(jnp.int32, (blocks, blocks * window), 0)
+        code = jnp.max(jnp.where(slot // window == block, row, -1), axis=0, keepdims=True)
+        place = lax.broadcasted_iota(jnp.int32, (total, blocks * window), 0)
+        pick = (place == code).astype(jnp.bfloat16)
+        slots = slice(step * window, (step + 1) * window)
+        near, far = [
+            jnp.dot(
+                pick,
+                jnp.concatenate(
+                    [ref[half * planes + k, slots] for ref in (mine_ref, core_ref) for k in range(planes)],
+                    axis=0,
+                ),
+                preferred_element_type=jnp.float32,
+            )
+            for half in range(2)
+        ]
+        widened = jnp.concatenate(
+            [jnp.where(x == 0, near, far), jnp.where(x == 0, far, near)], axis=1
+        )
+        rows = slice(step * total, (step + 1) * total)
+        states_ref[rows] = widened.astype(jnp.bfloat16)
+        factor = lax.rsqrt(jnp.mean(widened * widened, axis=-1, keepdims=True) + EPSILON)
+        normed = (widened * factor * gain).astype(jnp.bfloat16)
+        both = jnp.dot(normed, weight_ref[...], preferred_element_type=jnp.float32)
+        for h in range(PER_GROUP + 1):
+            vector = both[:, h * HD : (h + 1) * HD]
+            turned = vector * cosine + pltpu.roll(vector, HD // 2, 1) * sine
+            if h < PER_GROUP:
+                query_ref[rows, h * HD : (h + 1) * HD] = turned.astype(jnp.bfloat16)
+            else:
+                key_ref[rows] = turned.astype(jnp.bfloat16)
+        value_ref[rows] = both[:, (PER_GROUP + 1) * HD :].astype(jnp.bfloat16)
+
+
+def place_rows(index, mine, core, gain, weight, sessions, slot_cap):
+    together = 16 // math.gcd(16, slot_cap)
+    cosine, sine = rope_tables(together)
+    model = 2 * mine.shape[2]
+    total = sessions * SLOTS
+    out = lambda w: jax.ShapeDtypeStruct((total, w), jnp.bfloat16)
+    return pl.pallas_call(
+        functools.partial(place_kernel, slot_cap=slot_cap, together=together),
+        in_specs=[SMEM] + [VMEM] * 6,
+        out_specs=[VMEM] * 5,
+        out_shape=[
+            out(model), out(PER_GROUP * HD), out(HD), out(HD),
+            jax.ShapeDtypeStruct((1, HD), jnp.int32),
+        ],
+        compiler_params=pltpu.CompilerParams(vmem_limit_bytes=40 << 20),
+        cost_estimate=pl.CostEstimate(
+            flops=4 * total * model * weight.shape[1], bytes_accessed=6 << 20, transcendentals=0
+        ),
+        name="place_rows",
+    )(index, mine, core, gain.reshape(1, model), weight, jnp.asarray(cosine), jnp.asarray(sine))
+
+
+def session_attention(query_ref, key_ref, value_ref, kv, session, length):
     scale = HD ** (-0.5) * math.log2(math.e)
     rows = pl.ds(pl.multiple_of(session * SLOTS, SLOTS), SLOTS)
     query = jnp.concatenate(
@@ -311,16 +521,18 @@
     mixed = jnp.dot(
         powers.astype(jnp.bfloat16), tokens[:, HD:], preferred_element_type=jnp.float32
     ) + jnp.dot(own_powers.astype(jnp.bfloat16), value_ref[rows, :], preferred_element_type=jnp.float32)
-    mixed = (mixed / total).astype(jnp.bfloat16)
-    for h in range(PER_GROUP):
-        out_ref[rows, h * HD : (h + 1) * HD] = mixed[h * SLOTS : (h + 1) * SLOTS]
-
-
-def hops_kernel(hop_ref, held_ref, length_ref, query_ref, key_ref, value_ref, *refs, hops, carried):
+    return (mixed / total).astype(jnp.bfloat16)
+
+
+def hops_kernel(index_ref, hop_ref, held_ref, length_ref, query_ref, key_ref, value_ref, *refs,
+                hops, carried):
     if carried:
         before_ref, *refs = refs
-    prompt_refs, (out_ref, kv, sem) = refs[: 2 * len(hops)], refs[2 * len(hops) :]
+    count = KVH if carried else 1
+    prompt_refs, out_refs = refs[: 2 * len(hops)], refs[2 * len(hops) : 2 * len(hops) + count]
+    kv, sem = refs[-2:]
     sessions = hop_ref.shape[0]
+    per_device = sessions // KVH
 
     def copies(session, which):
         return [
@@ -340,21 +552,44 @@
                     copy.start()
         return 0
 
+    def store(session, block):
+        def into(out_ref, first):
+            rows = pl.ds(pl.multiple_of(first * SLOTS, SLOTS), SLOTS)
+            if block.shape[0] == SLOTS:
+                out_ref[rows] = block
+            else:
+                for h in range(PER_GROUP):
+                    out_ref[rows, h * HD : (h + 1) * HD] = block[h * SLOTS : (h + 1) * SLOTS]
+
+        if not carried:
+            into(out_refs[0], session)
+            return
+        for by, out_ref in enumerate(out_refs):
+            @pl.when((lax.div(session, per_device) ^ index_ref[3]) == by)
+            def _():
+                into(out_ref, lax.rem(session, per_device))
+
     lax.fori_loop(0, sessions, fetch, 0)
-    if carried:
-        out_ref[...] = before_ref[...]
 
     def work(session, _):
         ours = hop_ref[session] == hops[0]
         for hop in hops[1:]:
             ours = ours | (hop_ref[session] == hop)
+        if carried:
+            @pl.when(jnp.logical_not(ours))
+            def _():
+                rows = pl.ds(pl.multiple_of(session * SLOTS, SLOTS), SLOTS)
+                store(session, before_ref[rows])
 
         @pl.when(ours)
         def _():
             for copy in copies(session, 0):
                 copy.wait()
-            session_attention(
-                query_ref, key_ref, value_ref, kv[session], out_ref, session, length_ref[session]
+            store(
+                session,
+                session_attention(
+                    query_ref, key_ref, value_ref, kv[session], session, length_ref[0, session]
+                ),
             )
 
         return 0
@@ -362,19 +597,21 @@
     lax.fori_loop(0, sessions, work, 0)
 
 
-def attend_hops(hop, held, lengths, query, key, value, prompts, hops, before):
+def attend_hops(index, hop, held, lengths, query, key, value, prompts, hops, before):
     sessions = hop.shape[0]
     carried = before is not None
-    smem = pl.BlockSpec(memory_space=pltpu.SMEM)
-    vmem = pl.BlockSpec(memory_space=pltpu.VMEM)
-    anywhere = pl.BlockSpec(memory_space=pl.ANY)
     pieces = [piece for h in hops for piece in prompts[h]]
     work = sessions * len(hops) // 7 + 1
+    width = PER_GROUP * HD
+    if carried:
+        out_shape = [jax.ShapeDtypeStruct((sessions // KVH * SLOTS, width), jnp.bfloat16)] * KVH
+    else:
+        out_shape = jax.ShapeDtypeStruct((sessions * SLOTS, width), jnp.bfloat16)
     return pl.pallas_call(
         functools.partial(hops_kernel, hops=hops, carried=carried),
-        in_specs=[smem] * 3 + [vmem] * (3 + carried) + [anywhere] * len(pieces),
-        out_specs=vmem,
-        out_shape=jax.ShapeDtypeStruct((sessions * SLOTS, PER_GROUP * HD), jnp.bfloat16),
+        in_specs=[SMEM] * 4 + [VMEM] * (3 + carried) + [ANY] * len(pieces),
+        out_specs=[VMEM] * KVH if carried else VMEM,
+        out_shape=out_shape,
         scratch_shapes=[
             pltpu.VMEM((sessions, 2, 2, PROMPT // 4, 2 * HD), jnp.bfloat16),
             pltpu.SemaphoreType.DMA((sessions, 2)),
@@ -386,7 +623,41 @@
             transcendentals=work * PER_GROUP * SLOTS * (PROMPT + SLOTS),
         ),
         name="attend",
-    )(hop, held, lengths, query, key, value, *([before] if carried else []), *pieces)
+    )(index, hop, held, lengths, query, key, value, *([before] if carried else []), *pieces)
+
+
+def output_kernel(index_ref, length_ref, states_ref, weight_ref, *refs):
+    piece_refs, out_ref = refs[:-1], refs[-1]
+    head = index_ref[3]
+    group_width = PER_GROUP * HD
+    per_device = out_ref.shape[0]
+    total = per_device * SLOTS
+    summed = states_ref[pl.ds(pl.multiple_of(head * total, SLOTS), total)].astype(jnp.float32)
+    for by, piece_ref in enumerate(piece_refs):
+        start = pl.multiple_of((head ^ by) * group_width, group_width)
+        summed = summed + jnp.dot(
+            piece_ref[...], weight_ref[pl.ds(start, group_width)], preferred_element_type=jnp.float32
+        )
+    row = lax.broadcasted_iota(jnp.int32, (SLOTS, 1), 0)
+    for i in range(per_device):
+        live = row < length_ref[0, head * per_device + i]
+        part = summed[i * SLOTS : (i + 1) * SLOTS]
+        out_ref[i] = jnp.where(live, part, 0.0).astype(jnp.bfloat16)
+
+
+def output(index, lengths, states, o_weight, pieces, per_device):
+    model = o_weight.shape[1]
+    return pl.pallas_call(
+        output_kernel,
+        in_specs=[SMEM] * 2 + [VMEM] * (2 + len(pieces)),
+        out_specs=VMEM,
+        out_shape=jax.ShapeDtypeStruct((per_device, SLOTS, model), jnp.bfloat16),
+        compiler_params=pltpu.CompilerParams(vmem_limit_bytes=40 << 20),
+        cost_estimate=pl.CostEstimate(
+            flops=2 * per_device * SLOTS * o_weight.size, bytes_accessed=o_weight.size * 2, transcendentals=0
+        ),
+        name="output",
+    )(index, lengths, states, o_weight, *pieces)
 
 
 def shifted(n, by):
@@ -421,80 +692,39 @@
     width = model // 2
     z, x, c = lax.axis_index("sess"), lax.axis_index("inner"), lax.axis_index("rep")
     head = x * rep_count + c
+    index = jnp.stack([z, x, c, head]).astype(jnp.int32)
     pair = ("inner", "rep")
 
-    def of_head(h):
-        parts = [
-            lax.dynamic_slice_in_dim(prompt_cache, h * HD + side * KVH * HD, HD, 2)
-            for side in range(2)
-        ]
-        return jnp.concatenate(parts, axis=2)
-
-    from_core = lax.ppermute(of_head(head ^ 1), pair, swapped(4, 1))
-    from_x = lax.ppermute(of_head(head ^ 2), pair, swapped(4, 2))
-    from_far = lax.ppermute(of_head(head ^ 3), pair, swapped(4, 3))
-    right = [jnp.stack([of_head(head), from_core]), jnp.stack([from_x, from_far])]
-    left = list(right)
-    prompts = {0: tuple(right)}
+    own, to_core, to_x, to_far = split_heads(head.reshape(1), prompt_cache)
+    from_core = lax.ppermute(to_core, pair, swapped(4, 1))
+    from_x = lax.ppermute(to_x, pair, swapped(4, 2))
+    from_far = lax.ppermute(to_far, pair, swapped(4, 3))
+    first = stack(own[None], from_core[None])
+    second = stack(from_x[None], from_far[None])
+    right = [first, second]
+    left = [first, second]
+    prompts = {0: (first, second)}
     for hop in range(1, planes):
         for chunk in range(2):
             right[chunk] = lax.ppermute(right[chunk], "sess", shifted(planes, 1))
             left[chunk] = lax.ppermute(left[chunk], "sess", shifted(planes, -1))
         prompts[-hop], prompts[hop] = tuple(right), tuple(left)
 
-    row_owner = row_session[:, 0]
-    order = jnp.arange(row_owner.shape[0])
-    same = row_owner[:, None] == row_owner[None, :]
-    earlier = jnp.sum((same & (order[None, :] < order[:, None])).astype(jnp.int32), axis=1)
-    row_slot = row_owner * slot_cap + earlier
-    all_owners = lax.all_gather(
-        row_owner.reshape(-1, 128), ("sess", "rep"), axis=0, tiled=True
-    ).reshape(blocks, -1)
-
+    thinker_rows, _ = lax.optimization_barrier((thinker_rows, (prompts[-1][0], prompts[1][0])))
     partial_sum = jnp.dot(thinker_rows, proj_weight, preferred_element_type=jnp.float32)
     kept = lax.dynamic_slice_in_dim(partial_sum, x * width, width, 1)
     sent = lax.dynamic_slice_in_dim(partial_sum, (1 - x) * width, width, 1)
     came = lax.ppermute(sent.astype(jnp.bfloat16), "inner", swapped(2, 1))
-    own_columns = (kept + came.astype(jnp.float32)).astype(jnp.bfloat16)
-    into = (jnp.arange(session_all * slot_cap)[:, None] == row_slot[None, :]).astype(jnp.bfloat16)
-    buffer = jnp.dot(into, own_columns, preferred_element_type=jnp.float32).astype(jnp.bfloat16)
-    buffer = buffer.reshape(planes, per_plane * slot_cap, width)
-    arrived = [lax.dynamic_index_in_dim(buffer, z, 0, keepdims=False)]
-    for by in range(1, planes):
-        outgoing = lax.dynamic_index_in_dim(buffer, z ^ by, 0, keepdims=False)
-        arrived.append(lax.ppermute(outgoing, "sess", swapped(planes, by)))
-    arrived = jnp.stack(arrived)
-    other_x = lax.ppermute(arrived, "inner", swapped(2, 1))
-    low = jnp.where(x == 0, arrived, other_x)
-    high = jnp.where(x == 0, other_x, arrived)
-    halves = jnp.stack([low, high])
-    other_core = lax.ppermute(halves, "rep", swapped(2, 1))
-    slots = jnp.concatenate([halves, other_core], axis=1)
-
-    mine = lambda a: lax.dynamic_slice_in_dim(a, z * per_plane, per_plane, a.ndim - 1)
-    ours = z * per_plane + jnp.arange(per_plane)
-    counts = jnp.sum(
-        (all_owners[:, None, :] == ours[None, :, None]).astype(jnp.int32), axis=2
-    )
-    lengths = jnp.sum(counts, axis=0)
-    kind = jnp.arange(blocks)
-    block = (z ^ (kind % planes)) * rep_count + (c ^ (kind // planes))
-    is_block = block[:, None] == kind[None, :]
-    is_before = kind[None, :] < block[:, None]
-    here = jnp.sum(jnp.where(is_block[:, :, None], counts[None], 0), axis=1)
-    offsets = jnp.sum(jnp.where(is_before[:, :, None], counts[None], 0), axis=1)
-    together = 16 // math.gcd(16, slot_cap)
-    steps = per_plane // together
-    within = jnp.arange(slot_cap)
-    local = (jnp.arange(per_plane) % together)[None, :, None] * SLOTS
-    code = jnp.where(
-        within[None, None, :] < here[:, :, None],
-        offsets[:, :, None] + within[None, None, :] + local,
-        -1,
-    )
-    code = jnp.transpose(
-        code.reshape(blocks, steps, together * slot_cap), (1, 0, 2)
-    ).reshape(steps, 1, blocks * together * slot_cap)
+    came, _ = lax.optimization_barrier((came, (prompts[-1][1], prompts[1][1])))
+    routed = route(z.reshape(1), kept, came, row_session, planes, per_plane, slot_cap)
+    routed, _ = lax.optimization_barrier((tuple(routed), (prompts[-2][0], prompts[2][0])))
+    arrived = [routed[0]] + [
+        lax.ppermute(routed[by], "sess", swapped(planes, by)) for by in range(1, planes)
+    ]
+    arrived, _ = lax.optimization_barrier((arrived, (prompts[-2][1], prompts[2][1])))
+    arrived = stack(*[a[None] for a in arrived])
+    mine = stack(arrived, lax.ppermute(arrived, "inner", swapped(2, 1)))
+    core = lax.ppermute(mine, "rep", swapped(2, 1))
 
     group_width = PER_GROUP * HD
     weight = jnp.concatenate(
@@ -505,51 +735,30 @@
         ],
         axis=1,
     )
-    states, query, key, value = make_states(
-        code, slots, attn_gain, weight, per_plane, together
-    )
-
+    states, query, key, value, lengths = place_rows(
+        index, mine, core, attn_gain, weight, per_plane, slot_cap
+    )
+
+    speakers = lax.dynamic_slice_in_dim(speaker_of, z * per_plane, per_plane)
     wanted_slot = jnp.sum(
         jnp.where(
-            mine(speaker_of)[:, None] == jnp.arange(prompt_slot.shape[0])[None, :],
-            prompt_slot[None, :],
-            0,
+            speakers[:, None] == jnp.arange(prompt_slot.shape[0])[None, :], prompt_slot[None, :], 0
         ),
         axis=1,
     )
     hop = wanted_slot // held - z
     which = wanted_slot % held
     near = attend_hops(
-        hop, which, lengths, query, key, value, prompts, (0, -1, 1, -2, 2), None
-    )
-    attended = attend_hops(hop, which, lengths, query, key, value, prompts, (-3, 3), near)
-
-    attended = attended.reshape(plane, per_device * SLOTS, group_width)
-    pieces = [lax.dynamic_index_in_dim(attended, head, 0, keepdims=False)]
-    for by in (2, 3, 1):
-        outgoing = lax.dynamic_index_in_dim(attended, head ^ by, 0, keepdims=False)
-        pieces.append(lax.ppermute(outgoing, pair, swapped(4, by)))
-    o_rows = o_weight.reshape(KVH, group_width, model)
-    first = head * per_device
-    summed = lax.dynamic_slice_in_dim(states, first * SLOTS, per_device * SLOTS, 0).astype(
-        jnp.float32
-    )
-    gathered = jnp.concatenate(pieces, axis=1)
-    turned = jnp.concatenate(
-        [
-            lax.dynamic_index_in_dim(o_rows, head ^ by, 0, keepdims=False)
-            for by in (0, 2, 3, 1)
-        ],
-        axis=0,
-    )
-    summed = summed + jnp.dot(gathered, turned, preferred_element_type=jnp.float32)
-    own_lengths = lax.dynamic_slice_in_dim(lengths, first, per_device)
-    live_rows = (jnp.arange(SLOTS)[None, :] < own_lengths[:, None]).reshape(-1, 1)
-    return (
-        jnp.where(live_rows, summed, 0.0)
-        .astype(jnp.bfloat16)
-        .reshape(per_device, SLOTS, model)
-    )
+        index, hop, which, lengths, query, key, value, prompts, (0, -1, 1, -2, 2), None
+    )
+    attended = attend_hops(
+        index, hop, which, lengths, query, key, value, prompts, (-3, 3), near
+    )
+
+    pieces = [attended[0]] + [
+        lax.ppermute(attended[by], pair, swapped(4, by)) for by in range(1, plane)
+    ]
+    return output(index, lengths, states, o_weight, pieces, per_device)
 
 
 def solution(mesh):

time: 132 us -> 232 us (1.76)
  the two profiles are of different devices: /device:TPU:5 before, /device:TPU:0 now
where the time goes in v3:
time: 232 us; the launch traced here: 231 us
  Pallas kernels  130 us (56%)
  starting transfers between devices  47.7 us (21%)
  waiting for transfers between devices  41.4 us (18%)
  local copies, waits for them, and re-layouts  8.45 us (4%)
    pallas_call x4, Pallas kernels, stack(): pl.pallas_call(stack_kernel, in_specs=[ANY] * len(arrays), out_specs=ANY,...  77.9 us
    pallas_call x1, Pallas kernels, split_heads(): pl.pallas_call(split_heads_kernel, in_specs=[SMEM, ANY], out_specs=[ANY]...  32.9 us
    ppermute x6, starting transfers between devices, line_body(): right[chunk] = lax.ppermute(right[chunk], 'sess', shifted(planes, 1))  26.4 us
    pallas_call x2, Pallas kernels, attend_hops(): pl.pallas_call(functools.partial(hops_kernel, hops=hops, carried=carried)...  10.5 us
    ppermute x6, waiting for transfers between devices, line_body(): left[chunk] = lax.ppermute(left[chunk], 'sess', shifted(planes, -1))  9.32 us
    ppermute x1, waiting for transfers between devices, line_body(): mine = stack(arrived, lax.ppermute(arrived, 'inner', swapped(2, 1)))  8.81 us
    ppermute x6, waiting for transfers between devices, line_body(): right[chunk] = lax.ppermute(right[chunk], 'sess', shifted(planes, 1))  8.54 us
    ppermute x6, starting transfers between devices, line_body(): left[chunk] = lax.ppermute(left[chunk], 'sess', shifted(planes, -1))  7.7 us
  transfers between devices with their start and end apart: 24, of which 11 were waited for; matrix products, arithmetic and copies ran while one was open for 4% of the time, Pallas kernels for 21%

profile of v3, /device:TPU:0, one launch (start us, length us, event | category | flops | bytes accessed | tf_op | source)
XLA Modules:
  0.0 231.4 jit_solution(2579231884544752008)
XLA Ops:
  0.0 32.9 %split_heads.1 = (bf16[2,256,256]{2,1,0:T(8,128)(2,1)}, bf16[2,256,256]{2,1,0:T(8,128)(2,1)}, bf16[2,256,256]{2,1,0:T(8,128)(2,1)}, bf16[2,256,256]{2,1,0:T(8,128)(2,1)}) custom-call(s32[1]{0:T(128)} %bitcast.3.head_ref, bf16[2,256,1024]{2,1,0:T(8,128)(2,1)} %cache_ref.1), custom_call_target="tpu_custom_call" | custom-call | bytes 2097152 | tf_op jit(solution)/shard_map/split_heads/pallas_call | solution.py:320
  33.5 2.6 %collective-permute-start.4 = (bf16[2,256,256]{2,1,0:T(8,128)(2,1)}, bf16[2,256,256]{2,1,0:T(8,128)(2,1)S(1)}, u32[]{:S(2)}, u32[]{:S(2)}) collective-permute-start(bf16[2,256,256]{2,1,0:T(8,128)(2,1)} %get-tuple-element.35), channel_id=1, source_target_pairs={{0,2},{1,3},{2,0},{3,1},{4,6},{5,7},{6,4},{7,5},{8,10},{9,11},{10,... | collective-permute-start | bytes 786440 | tf_op jit(solution)/shard_map/ppermute | solution.py:700
  36.1 17.0 %stack.24.refs_0_ = bf16[2,2,256,256]{3,2,1,0:T(8,128)(2,1)} custom-call(bf16[1,2,256,256]{3,2,1,0:T(8,128)(2,1)} %bitcast.16, bf16[1,2,256,256]{3,2,1,0:T(8,128)(2,1)} %bitcast.5.refs_1_), custom_call_target="tpu_custom_call" | custom-call | bytes 1048576 | tf_op jit(solution)/shard_map/stack/pallas_call | solution.py:350
  53.1 4.5 %collective-permute-start.1 = (bf16[2,2,256,256]{3,2,1,0:T(8,128)(2,1)}, bf16[2,2,256,256]{3,2,1,0:T(8,128)(2,1)}, u32[]{:S(2)}, u32[]{:S(2)}) collective-permute-start(bf16[2,2,256,256]{3,2,1,0:T(8,128)(2,1)} %stack.24.refs_0_), channel_id=1, source_target_pairs={{0,4},{4,8},{8,12},{1,5},{5,9},{9,13},{2,6},{6,10},{10,14},{3,7},{... | collective-permute-start | bytes 1572872 | tf_op jit(solution)/shard_map/ppermute | solution.py:709
  59.6 17.0 %stack.25.refs_1_ = bf16[2,2,256,256]{3,2,1,0:T(8,128)(2,1)} custom-call(bf16[1,2,256,256]{3,2,1,0:T(8,128)(2,1)} %bitcast.15, bf16[1,2,256,256]{3,2,1,0:T(8,128)(2,1)} %bitcast.7.refs_1_), custom_call_target="tpu_custom_call" | custom-call | bytes 1048576 | tf_op jit(solution)/shard_map/stack/pallas_call | solution.py:350
  76.6 5.4 %collective-permute-start.6 = (bf16[2,2,256,256]{3,2,1,0:T(8,128)(2,1)}, bf16[2,2,256,256]{3,2,1,0:T(8,128)(2,1)}, u32[]{:S(2)}, u32[]{:S(2)}) collective-permute-start(bf16[2,2,256,256]{3,2,1,0:T(8,128)(2,1)} %stack.25.refs_1_), channel_id=1, source_target_pairs={{0,4},{4,8},{8,12},{1,5},{5,9},{9,13},{2,6},{6,10},{10,14},{3,7},{... | collective-permute-start | bytes 1572872 | tf_op jit(solution)/shard_map/ppermute | solution.py:709
  83.3 5.3 %collective-permute-start.8 = (bf16[2,2,256,256]{3,2,1,0:T(8,128)(2,1)}, bf16[2,2,256,256]{3,2,1,0:T(8,128)(2,1)}, u32[]{:S(2)}, u32[]{:S(2)}) collective-permute-start(bf16[2,2,256,256]{3,2,1,0:T(8,128)(2,1)} %collective-permute-done.1.refs_2_), channel_id=1, source_target_pairs={{0,4},{4,8},{8,12},{1,5},{5,9},{9,13},{2,6},{6,10},{10,14},{3,7},{... | collective-permute-start | bytes 1572872 | tf_op jit(solution)/shard_map/ppermute | solution.py:709
  89.9 3.9 %collective-permute-done.6.refs_3_ = bf16[2,2,256,256]{3,2,1,0:T(8,128)(2,1)} collective-permute-done((bf16[2,2,256,256]{3,2,1,0:T(8,128)(2,1)}, bf16[2,2,256,256]{3,2,1,0:T(8,128)(2,1)}, u32[]{:S(2)}, u32[]{:S(2)}) %collective-permute-start.6) | collective-permute-done | bytes 524320 | tf_op jit(solution)/shard_map/ppermute | solution.py:709
  93.8 5.2 %collective-permute-start.13 = (bf16[2,2,256,256]{3,2,1,0:T(8,128)(2,1)}, bf16[2,2,256,256]{3,2,1,0:T(8,128)(2,1)}, u32[]{:S(2)}, u32[]{:S(2)}) collective-permute-start(bf16[2,2,256,256]{3,2,1,0:T(8,128)(2,1)} %collective-permute-done.6.refs_3_), channel_id=1, source_target_pairs={{0,4},{4,8},{8,12},{1,5},{5,9},{9,13},{2,6},{6,10},{10,14},{3,7},{... | collective-permute-start | bytes 1572872 | tf_op jit(solution)/shard_map/ppermute | solution.py:709
  110.3 2.3 route.1
  112.6 2.7 %collective-permute-start.10 = (bf16[112,448]{1,0:T(8,128)(2,1)}, bf16[112,448]{1,0:T(8,128)(2,1)S(1)}, u32[]{:S(2)}, u32[]{:S(2)}) collective-permute-start(bf16[112,448]{1,0:T(8,128)(2,1)} %get-tuple-element.43), channel_id=1, source_target_pairs={{0,4},{4,0},{8,12},{12,8},{1,5},{5,1},{9,13},{13,9},{2,6},{6,2},{1... | collective-permute-start | bytes 301064 | tf_op jit(solution)/shard_map/ppermute | solution.py:722
  115.3 2.6 %collective-permute-start.11 = (bf16[112,448]{1,0:T(8,128)(2,1)}, bf16[112,448]{1,0:T(8,128)(2,1)S(1)}, u32[]{:S(2)}, u32[]{:S(2)}) collective-permute-start(bf16[112,448]{1,0:T(8,128)(2,1)} %get-tuple-element.44), channel_id=1, source_target_pairs={{0,8},{4,12},{8,0},{12,4},{1,9},{5,13},{9,1},{13,5},{2,10},{6,14},... | collective-permute-start | bytes 301064 | tf_op jit(solution)/shard_map/ppermute | solution.py:722
  117.9 5.2 %collective-permute-done.14.refs_9_ = bf16[2,2,256,256]{3,2,1,0:T(8,128)(2,1)} collective-permute-done((bf16[2,2,256,256]{3,2,1,0:T(8,128)(2,1)}, bf16[2,2,256,256]{3,2,1,0:T(8,128)(2,1)}, u32[]{:S(2)}, u32[]{:S(2)}) %collective-permute-start.14) | collective-permute-done | bytes 524320 | tf_op jit(solution)/shard_map/ppermute | solution.py:710
  125.2 3.5 %collective-permute-done.12 = bf16[112,448]{1,0:T(8,128)(2,1)S(1)} collective-permute-done((bf16[112,448]{1,0:T(8,128)(2,1)}, bf16[112,448]{1,0:T(8,128)(2,1)S(1)}, u32[]{:S(2)}, u32[]{:S(2)}) %collective-permute-start.12) | collective-permute-done | bytes 100384 | tf_op jit(solution)/shard_map/ppermute | solution.py:722
  129.3 15.0 %stack.26.refs_0_ = bf16[4,112,448]{2,1,0:T(8,128)(2,1)} custom-call(bf16[1,112,448]{2,1,0:T(8,128)(2,1)} %bitcast.17, bf16[1,112,448]{2,1,0:T(8,128)(2,1)} %bitcast.18, bf16[1,112,448]{2,1,0:T(8,128)(2,1)} %bitcast.19, bf16[1,112,448]{2,1,0:T(8,128)(2,1)} %bitcast.20), custom_call_target="tpu_custom_call" | custom-call | bytes 802816 | tf_op jit(solution)/shard_map/stack/pallas_call | solution.py:350
  146.6 8.8 %collective-permute-done.15.refs_1_ = bf16[4,112,448]{2,1,0:T(8,128)(2,1)} collective-permute-done((bf16[4,112,448]{2,1,0:T(8,128)(2,1)}, bf16[4,112,448]{2,1,0:T(8,128)(2,1)}, u32[]{:S(2)}, u32[]{:S(2)}) %collective-permute-start.15) | collective-permute-done | bytes 401440 | tf_op jit(solution)/shard_map/ppermute | solution.py:726
  155.4 28.9 %stack.27.mine_ref = bf16[8,112,448]{2,1,0:T(8,128)(2,1)} custom-call(bf16[4,112,448]{2,1,0:T(8,128)(2,1)} %stack.26.refs_0_, bf16[4,112,448]{2,1,0:T(8,128)(2,1)} %collective-permute-done.15.refs_1_), custom_call_target="tpu_custom_call" | custom-call | bytes 1605632 | tf_op jit(solution)/shard_map/stack/pallas_call | solution.py:350
  190.5 4.6 %collective-permute-start.17 = (bf16[2,2,256,256]{3,2,1,0:T(8,128)(2,1)}, bf16[2,2,256,256]{3,2,1,0:T(8,128)(2,1)S(1)}, u32[]{:S(2)}, u32[]{:S(2)}) collective-permute-start(bf16[2,2,256,256]{3,2,1,0:T(8,128)(2,1)} %collective-permute-done.8.refs_6_), channel_id=1, source_target_pairs={{0,4},{4,8},{8,12},{1,5},{5,9},{9,13},{2,6},{6,10},{10,14},{3,7},{... | collective-permute-start | bytes 1572872 | tf_op jit(solution)/shard_map/ppermute | solution.py:709
  196.6 4.2 %place_rows.1 = (bf16[768,896]{1,0:T(8,128)(2,1)S(1)}, bf16[768,384]{1,0:T(8,128)(2,1)S(1)}, bf16[768,128]{1,0:T(8,128)(2,1)S(1)}, bf16[768,128]{1,0:T(8,128)(2,1)S(1)}, s32[1,128]{1,0:T(1,128)S(1)}) custom-call(s32[4]{0:T(128)S(1)} %pad_add_fusion.index_ref, bf16[8,112,448]{2,1,0:T(8,128)(2,1)S(1)} %copy-done.4, ...), custom_call_target="tpu_custom_call" | custom-call | flops 1761607680 | bytes 6291456 | tf_op jit(solution)/shard_map/place_rows/pallas_call | solution.py:486
  200.9 7.2 %attend.2.refs_0_ = bf16[768,384]{1,0:T(8,128)(2,1)S(1)} custom-call(s32[4]{0:T(128)S(1)} %pad_add_fusion.index_ref, s32[8]{0:T(128)S(1)} %get-tuple-element.60.hop_ref, s32[8]{0:T(128)S(1)} %get-tuple-element.59.held_ref, s32[1,128]{1,0:T(1,128)S(1)} %get-tuple-element.50.length_ref, bf16[768,384]{1,0:T(8,128)(2,1)S(1)} %get-tuple-element.52.query_ref, ...), custom_call_target="tpu_custom_call" | custom-call | flops 990904320 | bytes 3145728 | tf_op jit(solution)/shard_map/attend/pallas_call | solution.py:610
  208.1 4.7 %collective-permute-done.17.refs_1_ = bf16[2,2,256,256]{3,2,1,0:T(8,128)(2,1)S(1)} collective-permute-done((bf16[2,2,256,256]{3,2,1,0:T(8,128)(2,1)}, bf16[2,2,256,256]{3,2,1,0:T(8,128)(2,1)S(1)}, u32[]{:S(2)}, u32[]{:S(2)}) %collective-permute-start.17) | collective-permute-done | bytes 524320 | tf_op jit(solution)/shard_map/ppermute | solution.py:709
  212.7 4.0 %collective-permute-done.19.refs_3_ = bf16[2,2,256,256]{3,2,1,0:T(8,128)(2,1)S(1)} collective-permute-done((bf16[2,2,256,256]{3,2,1,0:T(8,128)(2,1)}, bf16[2,2,256,256]{3,2,1,0:T(8,128)(2,1)S(1)}, u32[]{:S(2)}, u32[]{:S(2)}) %collective-permute-start.19) | collective-permute-done | bytes 524320 | tf_op jit(solution)/shard_map/ppermute | solution.py:710
  216.8 3.4 %attend.3 = (bf16[192,384]{1,0:T(8,128)(2,1)S(1)}, bf16[192,384]{1,0:T(8,128)(2,1)S(1)}, bf16[192,384]{1,0:T(8,128)(2,1)S(1)}, bf16[192,384]{1,0:T(8,128)(2,1)S(1)}) custom-call(s32[4]{0:T(128)S(1)} %pad_add_fusion.index_ref, s32[8]{0:T(128)S(1)} %get-tuple-element.60.hop_ref, s32[8]{0:T(128)S(1)} %get-tuple-element.59.held_ref, ...), custom_call_target="tpu_custom_call" | custom-call | flops 495452160 | bytes 1572864 | tf_op jit(solution)/shard_map/attend/pallas_call | solution.py:610
  222.1 4.8 %collective-permute-done.22.refs_2_ = bf16[192,384]{1,0:T(8,128)(2,1)S(1)} collective-permute-done((bf16[192,384]{1,0:T(8,128)(2,1)S(1)}, bf16[192,384]{1,0:T(8,128)(2,1)S(1)}, u32[]{:S(2)}, u32[]{:S(2)}) %collective-permute-start.22) | collective-permute-done | bytes 147488 | tf_op jit(solution)/shard_map/ppermute | solution.py:759
  (74 shorter events, 35.3 us)
Async XLA Ops:
  32.9 3.2 %collective-permute-start = (bf16[2,256,256]{2,1,0:T(8,128)(2,1)}, bf16[2,256,256]{2,1,0:T(8,128)(2,1)}, u32[]{:S(2)}, u32[]{:S(2)}) collective-permute-start(bf16[2,256,256]{2,1,0:T(8,128)(2,1)} %get-tuple-element.33), channel_id=1, source_target_pairs={{0,1},{1,0},{2,3},{3,2},{4,5},{5,4},{6,7},{7,6},{8,9},{9,8},{10,11... | collective-permute-start | bytes 786440 | tf_op jit(solution)/shard_map/ppermute | solution.py:699
  33.5 25.5 %collective-permute-start.4 = (bf16[2,256,256]{2,1,0:T(8,128)(2,1)}, bf16[2,256,256]{2,1,0:T(8,128)(2,1)S(1)}, u32[]{:S(2)}, u32[]{:S(2)}) collective-permute-start(bf16[2,256,256]{2,1,0:T(8,128)(2,1)} %get-tuple-element.35), channel_id=1, source_target_pairs={{0,2},{1,3},{2,0},{3,1},{4,6},{5,7},{6,4},{7,5},{8,10},{9,11},{10,... | collective-permute-start | bytes 786440 | tf_op jit(solution)/shard_map/ppermute | solution.py:700
  36.0 22.9 %collective-permute-start.5 = (bf16[2,256,256]{2,1,0:T(8,128)(2,1)}, bf16[2,256,256]{2,1,0:T(8,128)(2,1)}, u32[]{:S(2)}, u32[]{:S(2)}) collective-permute-start(bf16[2,256,256]{2,1,0:T(8,128)(2,1)} %get-tuple-element.36), channel_id=1, source_target_pairs={{0,3},{1,2},{2,1},{3,0},{4,7},{5,6},{6,5},{7,4},{8,11},{9,10},{10,... | collective-permute-start | bytes 786440 | tf_op jit(solution)/shard_map/ppermute | solution.py:701
  53.1 30.2 %collective-permute-start.1 = (bf16[2,2,256,256]{3,2,1,0:T(8,128)(2,1)}, bf16[2,2,256,256]{3,2,1,0:T(8,128)(2,1)}, u32[]{:S(2)}, u32[]{:S(2)}) collective-permute-start(bf16[2,2,256,256]{3,2,1,0:T(8,128)(2,1)} %stack.24.refs_0_), channel_id=1, source_target_pairs={{0,4},{4,8},{8,12},{1,5},{5,9},{9,13},{2,6},{6,10},{10,14},{3,7},{... | collective-permute-start | bytes 1572872 | tf_op jit(solution)/shard_map/ppermute | solution.py:709
  57.6 25.7 %collective-permute-start.2 = (bf16[2,2,256,256]{3,2,1,0:T(8,128)(2,1)}, bf16[2,2,256,256]{3,2,1,0:T(8,128)(2,1)}, u32[]{:S(2)}, u32[]{:S(2)}) collective-permute-start(bf16[2,2,256,256]{3,2,1,0:T(8,128)(2,1)} %stack.24.refs_0_), channel_id=1, source_target_pairs={{4,0},{8,4},{12,8},{5,1},{9,5},{13,9},{6,2},{10,6},{14,10},{7,3},{... | collective-permute-start | bytes 1572872 | tf_op jit(solution)/shard_map/ppermute | solution.py:710
  76.6 17.2 %collective-permute-start.6 = (bf16[2,2,256,256]{3,2,1,0:T(8,128)(2,1)}, bf16[2,2,256,256]{3,2,1,0:T(8,128)(2,1)}, u32[]{:S(2)}, u32[]{:S(2)}) collective-permute-start(bf16[2,2,256,256]{3,2,1,0:T(8,128)(2,1)} %stack.25.refs_1_), channel_id=1, source_target_pairs={{0,4},{4,8},{8,12},{1,5},{5,9},{9,13},{2,6},{6,10},{10,14},{3,7},{... | collective-permute-start | bytes 1572872 | tf_op jit(solution)/shard_map/ppermute | solution.py:709
  82.0 17.1 %collective-permute-start.7 = (bf16[2,2,256,256]{3,2,1,0:T(8,128)(2,1)}, bf16[2,2,256,256]{3,2,1,0:T(8,128)(2,1)}, u32[]{:S(2)}, u32[]{:S(2)}) collective-permute-start(bf16[2,2,256,256]{3,2,1,0:T(8,128)(2,1)} %stack.25.refs_1_), channel_id=1, source_target_pairs={{4,0},{8,4},{12,8},{5,1},{9,5},{13,9},{6,2},{10,6},{14,10},{7,3},{... | collective-permute-start | bytes 1572872 | tf_op jit(solution)/shard_map/ppermute | solution.py:710
  83.3 29.3 %collective-permute-start.8 = (bf16[2,2,256,256]{3,2,1,0:T(8,128)(2,1)}, bf16[2,2,256,256]{3,2,1,0:T(8,128)(2,1)}, u32[]{:S(2)}, u32[]{:S(2)}) collective-permute-start(bf16[2,2,256,256]{3,2,1,0:T(8,128)(2,1)} %collective-permute-done.1.refs_2_), channel_id=1, source_target_pairs={{0,4},{4,8},{8,12},{1,5},{5,9},{9,13},{2,6},{6,10},{10,14},{3,7},{... | collective-permute-start | bytes 1572872 | tf_op jit(solution)/shard_map/ppermute | solution.py:709
  88.7 23.9 %collective-permute-start.9 = (bf16[2,2,256,256]{3,2,1,0:T(8,128)(2,1)}, bf16[2,2,256,256]{3,2,1,0:T(8,128)(2,1)}, u32[]{:S(2)}, u32[]{:S(2)}) collective-permute-start(bf16[2,2,256,256]{3,2,1,0:T(8,128)(2,1)} %collective-permute-done.2.refs_4_), channel_id=1, source_target_pairs={{4,0},{8,4},{12,8},{5,1},{9,5},{13,9},{6,2},{10,6},{14,10},{7,3},{... | collective-permute-start | bytes 1572872 | tf_op jit(solution)/shard_map/ppermute | solution.py:710
  93.8 24.1 %collective-permute-start.13 = (bf16[2,2,256,256]{3,2,1,0:T(8,128)(2,1)}, bf16[2,2,256,256]{3,2,1,0:T(8,128)(2,1)}, u32[]{:S(2)}, u32[]{:S(2)}) collective-permute-start(bf16[2,2,256,256]{3,2,1,0:T(8,128)(2,1)} %collective-permute-done.6.refs_3_), channel_id=1, source_target_pairs={{0,4},{4,8},{8,12},{1,5},{5,9},{9,13},{2,6},{6,10},{10,14},{3,7},{... | collective-permute-start | bytes 1572872 | tf_op jit(solution)/shard_map/ppermute | solution.py:709
  99.0 24.1 %collective-permute-start.14 = (bf16[2,2,256,256]{3,2,1,0:T(8,128)(2,1)}, bf16[2,2,256,256]{3,2,1,0:T(8,128)(2,1)}, u32[]{:S(2)}, u32[]{:S(2)}) collective-permute-start(bf16[2,2,256,256]{3,2,1,0:T(8,128)(2,1)} %collective-permute-done.7.refs_5_), channel_id=1, source_target_pairs={{4,0},{8,4},{12,8},{5,1},{9,5},{13,9},{6,2},{10,6},{14,10},{7,3},{... | collective-permute-start | bytes 1572872 | tf_op jit(solution)/shard_map/ppermute | solution.py:710
  103.7 6.5 %collective-permute-start.3 = (bf16[256,448]{1,0:T(8,128)(2,1)S(1)}, bf16[256,448]{1,0:T(8,128)(2,1)}, u32[]{:S(2)}, u32[]{:S(2)}) collective-permute-start(bf16[256,448]{1,0:T(8,128)(2,1)S(1)} %dynamic-slice_convert_fusion), channel_id=1, source_target_pairs={{0,2},{2,0},{1,3},{3,1},{4,6},{6,4},{5,7},{7,5},{8,10},{10,8},{9,1... | collective-permute-start | bytes 688136 | tf_op jit(solution)/shard_map/ppermute | solution.py:717
  112.6 12.3 %collective-permute-start.10 = (bf16[112,448]{1,0:T(8,128)(2,1)}, bf16[112,448]{1,0:T(8,128)(2,1)S(1)}, u32[]{:S(2)}, u32[]{:S(2)}) collective-permute-start(bf16[112,448]{1,0:T(8,128)(2,1)} %get-tuple-element.43), channel_id=1, source_target_pairs={{0,4},{4,0},{8,12},{12,8},{1,5},{5,1},{9,13},{13,9},{2,6},{6,2},{1... | collective-permute-start | bytes 301064 | tf_op jit(solution)/shard_map/ppermute | solution.py:722
  115.3 9.9 %collective-permute-start.11 = (bf16[112,448]{1,0:T(8,128)(2,1)}, bf16[112,448]{1,0:T(8,128)(2,1)S(1)}, u32[]{:S(2)}, u32[]{:S(2)}) collective-permute-start(bf16[112,448]{1,0:T(8,128)(2,1)} %get-tuple-element.44), channel_id=1, source_target_pairs={{0,8},{4,12},{8,0},{12,4},{1,9},{5,13},{9,1},{13,5},{2,10},{6,14},... | collective-permute-start | bytes 301064 | tf_op jit(solution)/shard_map/ppermute | solution.py:722
  117.9 10.7 %collective-permute-start.12 = (bf16[112,448]{1,0:T(8,128)(2,1)}, bf16[112,448]{1,0:T(8,128)(2,1)S(1)}, u32[]{:S(2)}, u32[]{:S(2)}) collective-permute-start(bf16[112,448]{1,0:T(8,128)(2,1)} %get-tuple-element.45), channel_id=1, source_target_pairs={{0,12},{4,8},{8,4},{12,0},{1,13},{5,9},{9,5},{13,1},{2,14},{6,10},... | collective-permute-start | bytes 301064 | tf_op jit(solution)/shard_map/ppermute | solution.py:722
  144.3 11.1 %collective-permute-start.15 = (bf16[4,112,448]{2,1,0:T(8,128)(2,1)}, bf16[4,112,448]{2,1,0:T(8,128)(2,1)}, u32[]{:S(2)}, u32[]{:S(2)}) collective-permute-start(bf16[4,112,448]{2,1,0:T(8,128)(2,1)} %stack.26.refs_0_), channel_id=1, source_target_pairs={{0,2},{2,0},{1,3},{3,1},{4,6},{6,4},{5,7},{7,5},{8,10},{10,8},{9,1... | collective-permute-start | bytes 1204232 | tf_op jit(solution)/shard_map/ppermute | solution.py:726
  184.3 12.2 %collective-permute-start.16 = (bf16[8,112,448]{2,1,0:T(8,128)(2,1)}, bf16[8,112,448]{2,1,0:T(8,128)(2,1)S(1)}, u32[]{:S(2)}, u32[]{:S(2)}) collective-permute-start(bf16[8,112,448]{2,1,0:T(8,128)(2,1)} %stack.27.mine_ref), channel_id=1, source_target_pairs={{0,1},{1,0},{2,3},{3,2},{4,5},{5,4},{6,7},{7,6},{8,9},{9,8},{10,11... | collective-permute-start | bytes 2408456 | tf_op jit(solution)/shard_map/ppermute | solution.py:727
  187.8 20.3 %collective-permute-start.18 = (bf16[2,2,256,256]{3,2,1,0:T(8,128)(2,1)}, bf16[2,2,256,256]{3,2,1,0:T(8,128)(2,1)S(1)}, u32[]{:S(2)}, u32[]{:S(2)}) collective-permute-start(bf16[2,2,256,256]{3,2,1,0:T(8,128)(2,1)} %collective-permute-done.13.refs_7_), channel_id=1, source_target_pairs={{0,4},{4,8},{8,12},{1,5},{5,9},{9,13},{2,6},{6,10},{10,14},{3,7},{... | collective-permute-start | bytes 1572872 | tf_op jit(solution)/shard_map/ppermute | solution.py:709
  189.2 18.8 %collective-permute-start.20 = (bf16[2,2,256,256]{3,2,1,0:T(8,128)(2,1)}, bf16[2,2,256,256]{3,2,1,0:T(8,128)(2,1)S(1)}, u32[]{:S(2)}, u32[]{:S(2)}) collective-permute-start(bf16[2,2,256,256]{3,2,1,0:T(8,128)(2,1)} %collective-permute-done.14.refs_9_), channel_id=1, source_target_pairs={{4,0},{8,4},{12,8},{5,1},{9,5},{13,9},{6,2},{10,6},{14,10},{7,3},{... | collective-permute-start | bytes 1572872 | tf_op jit(solution)/shard_map/ppermute | solution.py:710
  190.5 22.2 %collective-permute-start.17 = (bf16[2,2,256,256]{3,2,1,0:T(8,128)(2,1)}, bf16[2,2,256,256]{3,2,1,0:T(8,128)(2,1)S(1)}, u32[]{:S(2)}, u32[]{:S(2)}) collective-permute-start(bf16[2,2,256,256]{3,2,1,0:T(8,128)(2,1)} %collective-permute-done.8.refs_6_), channel_id=1, source_target_pairs={{0,4},{4,8},{8,12},{1,5},{5,9},{9,13},{2,6},{6,10},{10,14},{3,7},{... | collective-permute-start | bytes 1572872 | tf_op jit(solution)/shard_map/ppermute | solution.py:709
  195.1 21.6 %collective-permute-start.19 = (bf16[2,2,256,256]{3,2,1,0:T(8,128)(2,1)}, bf16[2,2,256,256]{3,2,1,0:T(8,128)(2,1)S(1)}, u32[]{:S(2)}, u32[]{:S(2)}) collective-permute-start(bf16[2,2,256,256]{3,2,1,0:T(8,128)(2,1)} %collective-permute-done.9.refs_8_), channel_id=1, source_target_pairs={{4,0},{8,4},{12,8},{5,1},{9,5},{13,9},{6,2},{10,6},{14,10},{7,3},{... | collective-permute-start | bytes 1572872 | tf_op jit(solution)/shard_map/ppermute | solution.py:710
  220.2 1.9 collective-permute-start.21
  220.2 6.7 %collective-permute-start.22 = (bf16[192,384]{1,0:T(8,128)(2,1)S(1)}, bf16[192,384]{1,0:T(8,128)(2,1)S(1)}, u32[]{:S(2)}, u32[]{:S(2)}) collective-permute-start(bf16[192,384]{1,0:T(8,128)(2,1)S(1)} %get-tuple-element.57), channel_id=1, source_target_pairs={{0,2},{1,3},{2,0},{3,1},{4,6},{5,7},{6,4},{7,5},{8,10},{9,11},{10,... | collective-permute-start | bytes 442376 | tf_op jit(solution)/shard_map/ppermute | solution.py:759
  221.8 7.4 %collective-permute-start.23 = (bf16[192,384]{1,0:T(8,128)(2,1)S(1)}, bf16[192,384]{1,0:T(8,128)(2,1)S(1)}, u32[]{:S(2)}, u32[]{:S(2)}) collective-permute-start(bf16[192,384]{1,0:T(8,128)(2,1)S(1)} %get-tuple-element.58), channel_id=1, source_target_pairs={{0,3},{1,2},{2,1},{3,0},{4,7},{5,6},{6,5},{7,4},{8,11},{9,10},{10,... | collective-permute-start | bytes 442376 | tf_op jit(solution)/shard_map/ppermute | solution.py:759
  (14 other events, 206.9 us)

commit v4 on v3

--- a/solution.py
+++ b/solution.py
@@ -295,23 +295,11 @@
 ANY = pl.BlockSpec(memory_space=pl.ANY)
 
 
-def split_heads_kernel(head_ref, cache_ref, *refs):
-    out_refs, sem = refs[:-1], refs[-1]
-    copies = []
+def split_heads_kernel(head_ref, cache_ref, *out_refs):
     for by, out_ref in enumerate(out_refs):
         for side in range(2):
             start = pl.multiple_of((head_ref[0] ^ by) * HD + side * KVH * HD, HD)
-            copies.append(
-                pltpu.make_async_copy(
-                    cache_ref.at[:, :, pl.ds(start, HD)],
-                    out_ref.at[:, :, side * HD : (side + 1) * HD],
-                    sem.at[by, side],
-                )
-            )
-    for copy in copies:
-        copy.start()
-    for copy in copies:
-        copy.wait()
+            out_ref[:, :, side * HD : (side + 1) * HD] = cache_ref[:, :, pl.ds(start, HD)]
 
 
 def split_heads(head, cache):
@@ -319,29 +307,21 @@
     shape = jax.ShapeDtypeStruct((held, tokens, 2 * HD), cache.dtype)
     return pl.pallas_call(
         split_heads_kernel,
-        in_specs=[SMEM, ANY],
-        out_specs=[ANY] * KVH,
+        in_specs=[SMEM, VMEM],
+        out_specs=[VMEM] * KVH,
         out_shape=[shape] * KVH,
-        scratch_shapes=[pltpu.SemaphoreType.DMA((KVH, 2))],
         cost_estimate=pl.CostEstimate(flops=0, bytes_accessed=2 * cache.size * 2, transcendentals=0),
         name="split_heads",
     )(head, cache)
 
 
 def stack_kernel(*refs):
-    in_refs, (out_ref, sem) = refs[:-2], refs[-2:]
-    copies = []
+    in_refs, out_ref = refs[:-1], refs[-1]
     place = 0
-    for i, in_ref in enumerate(in_refs):
+    for in_ref in in_refs:
         count = in_ref.shape[0]
-        copies.append(
-            pltpu.make_async_copy(in_ref, out_ref.at[place : place + count], sem.at[i])
-        )
+        out_ref[place : place + count] = in_ref[...]
         place += count
-    for copy in copies:
-        copy.start()
-    for copy in copies:
-        copy.wait()
 
 
 def stack(*arrays):
@@ -349,10 +329,9 @@
     size = sum(a.size for a in arrays)
     return pl.pallas_call(
         stack_kernel,
-        in_specs=[ANY] * len(arrays),
-        out_specs=ANY,
+        in_specs=[VMEM] * len(arrays),
+        out_specs=VMEM,
         out_shape=jax.ShapeDtypeStruct((total,) + arrays[0].shape[1:], arrays[0].dtype),
-        scratch_shapes=[pltpu.SemaphoreType.DMA((len(arrays),))],
         cost_estimate=pl.CostEstimate(flops=0, bytes_accessed=4 * size, transcendentals=0),
         name="stack",
     )(*arrays)

time: 232 us -> 141 us (0.61)
  Pallas kernels: 130 us -> 29.6 us
  waiting for transfers between devices: 41.4 us -> 51.1 us
    pallas_call x5, Pallas kernels: 111 us -> 10.4 us  [the longest x4 7.77 us: stack(): pl.pallas_call(stack_kernel, in_specs=[VMEM] * len(arrays), out_specs=VME...]
    ppermute x1, waiting for transfers between devices: 0.01 us -> 4.89 us  [line_body(): from_far = lax.ppermute(to_far, pair, swapped(4, 3))]
  transfers between devices with their start and end apart: 24 -> 24, of which waited for: 11 -> 12; matrix products, arithmetic and copies ran while one was open for 4% -> 7% of each run, Pallas kernels for 21% -> 12%
where the time goes in v4:
time: 141 us; the launch traced here: 139 us
  waiting for transfers between devices  51.1 us (36%)
  starting transfers between devices  46.8 us (33%)
  Pallas kernels  29.6 us (21%)
  local copies, waits for them, and re-layouts  7.77 us (6%)
  matrix products  2.29 us (2%)
    ppermute x6, starting transfers between devices, line_body(): right[chunk] = lax.ppermute(right[chunk], 'sess', shifted(planes, 1))  26 us
    ppermute x6, waiting for transfers between devices, line_body(): left[chunk] = lax.ppermute(left[chunk], 'sess', shifted(planes, -1))  11.6 us
    pallas_call x2, Pallas kernels, attend_hops(): pl.pallas_call(functools.partial(hops_kernel, hops=hops, carried=carried)...  10.5 us
    ppermute x1, waiting for transfers between devices, line_body(): mine = stack(arrived, lax.ppermute(arrived, 'inner', swapped(2, 1)))  9.87 us
    ppermute x6, waiting for transfers between devices, line_body(): right[chunk] = lax.ppermute(right[chunk], 'sess', shifted(planes, 1))  8.94 us
    pallas_call x4, Pallas kernels, stack(): pl.pallas_call(stack_kernel, in_specs=[VMEM] * len(arrays), out_specs=VME...  7.77 us
    ppermute x6, starting transfers between devices, line_body(): left[chunk] = lax.ppermute(left[chunk], 'sess', shifted(planes, -1))  7.7 us
    ppermute x3, waiting for transfers between devices, line_body(): lax.ppermute(attended[by], pair, swapped(4, by))  7.11 us
  transfers between devices with their start and end apart: 24, of which 12 were waited for; matrix products, arithmetic and copies ran while one was open for 7% of the time, Pallas kernels for 12%

profile of v4, /device:TPU:0, one launch (start us, length us, event | category | flops | bytes accessed | tf_op | source)
XLA Modules:
  0.0 139.0 jit_solution(8926884858593571256)
XLA Ops:
  0.0 2.6 %split_heads.1 = (bf16[2,256,256]{2,1,0:T(8,128)(2,1)}, bf16[2,256,256]{2,1,0:T(8,128)(2,1)}, bf16[2,256,256]{2,1,0:T(8,128)(2,1)}, bf16[2,256,256]{2,1,0:T(8,128)(2,1)}) custom-call(s32[1]{0:T(128)} %bitcast.3.head_ref, bf16[2,256,1024]{2,1,0:T(8,128)(2,1)} %cache_ref.1), custom_call_target="tpu_custom_call" | custom-call | bytes 2097152 | tf_op jit(solution)/shard_map/split_heads/pallas_call | solution.py:308
  3.1 2.5 %collective-permute-start.4 = (bf16[2,256,256]{2,1,0:T(8,128)(2,1)}, bf16[2,256,256]{2,1,0:T(8,128)(2,1)S(1)}, u32[]{:S(2)}, u32[]{:S(2)}) collective-permute-start(bf16[2,256,256]{2,1,0:T(8,128)(2,1)} %get-tuple-element.35), channel_id=1, source_target_pairs={{0,2},{1,3},{2,0},{3,1},{4,6},{5,7},{6,4},{7,5},{8,10},{9,11},{10,... | collective-permute-start | bytes 786440 | tf_op jit(solution)/shard_map/ppermute | solution.py:679
  7.6 4.5 %collective-permute-start.1 = (bf16[2,2,256,256]{3,2,1,0:T(8,128)(2,1)}, bf16[2,2,256,256]{3,2,1,0:T(8,128)(2,1)}, u32[]{:S(2)}, u32[]{:S(2)}) collective-permute-start(bf16[2,2,256,256]{3,2,1,0:T(8,128)(2,1)} %stack.24.refs_0_), channel_id=1, source_target_pairs={{0,4},{4,8},{8,12},{1,5},{5,9},{9,13},{2,6},{6,10},{10,14},{3,7},{... | collective-permute-start | bytes 1572872 | tf_op jit(solution)/shard_map/ppermute | solution.py:688
  13.4 4.9 %collective-permute-done.5 = bf16[2,256,256]{2,1,0:T(8,128)(2,1)} collective-permute-done((bf16[2,256,256]{2,1,0:T(8,128)(2,1)}, bf16[2,256,256]{2,1,0:T(8,128)(2,1)}, u32[]{:S(2)}, u32[]{:S(2)}) %collective-permute-start.5) | collective-permute-done | bytes 262176 | tf_op jit(solution)/shard_map/ppermute | solution.py:680
  20.1 4.3 %collective-permute-start.6 = (bf16[2,2,256,256]{3,2,1,0:T(8,128)(2,1)}, bf16[2,2,256,256]{3,2,1,0:T(8,128)(2,1)}, u32[]{:S(2)}, u32[]{:S(2)}) collective-permute-start(bf16[2,2,256,256]{3,2,1,0:T(8,128)(2,1)} %stack.25.refs_1_), channel_id=1, source_target_pairs={{0,4},{4,8},{8,12},{1,5},{5,9},{9,13},{2,6},{6,10},{10,14},{3,7},{... | collective-permute-start | bytes 1572872 | tf_op jit(solution)/shard_map/ppermute | solution.py:688
  25.8 2.3 %collective-permute-done.2.refs_4_ = bf16[2,2,256,256]{3,2,1,0:T(8,128)(2,1)} collective-permute-done((bf16[2,2,256,256]{3,2,1,0:T(8,128)(2,1)}, bf16[2,2,256,256]{3,2,1,0:T(8,128)(2,1)}, u32[]{:S(2)}, u32[]{:S(2)}) %collective-permute-start.2) | collective-permute-done | bytes 524320 | tf_op jit(solution)/shard_map/ppermute | solution.py:689
  28.1 3.5 %collective-permute-start.8 = (bf16[2,2,256,256]{3,2,1,0:T(8,128)(2,1)}, bf16[2,2,256,256]{3,2,1,0:T(8,128)(2,1)}, u32[]{:S(2)}, u32[]{:S(2)}) collective-permute-start(bf16[2,2,256,256]{3,2,1,0:T(8,128)(2,1)} %collective-permute-done.1.refs_2_), channel_id=1, source_target_pairs={{0,4},{4,8},{8,12},{1,5},{5,9},{9,13},{2,6},{6,10},{10,14},{3,7},{... | collective-permute-start | bytes 1572872 | tf_op jit(solution)/shard_map/ppermute | solution.py:688
  32.9 3.3 %collective-permute-done.6.refs_3_ = bf16[2,2,256,256]{3,2,1,0:T(8,128)(2,1)} collective-permute-done((bf16[2,2,256,256]{3,2,1,0:T(8,128)(2,1)}, bf16[2,2,256,256]{3,2,1,0:T(8,128)(2,1)}, u32[]{:S(2)}, u32[]{:S(2)}) %collective-permute-start.6) | collective-permute-done | bytes 524320 | tf_op jit(solution)/shard_map/ppermute | solution.py:688
  36.2 5.2 %collective-permute-start.13 = (bf16[2,2,256,256]{3,2,1,0:T(8,128)(2,1)}, bf16[2,2,256,256]{3,2,1,0:T(8,128)(2,1)}, u32[]{:S(2)}, u32[]{:S(2)}) collective-permute-start(bf16[2,2,256,256]{3,2,1,0:T(8,128)(2,1)} %collective-permute-done.6.refs_3_), channel_id=1, source_target_pairs={{0,4},{4,8},{8,12},{1,5},{5,9},{9,13},{2,6},{6,10},{10,14},{3,7},{... | collective-permute-start | bytes 1572872 | tf_op jit(solution)/shard_map/ppermute | solution.py:688
  50.6 3.0 %collective-permute-done.3.came_ref = bf16[256,448]{1,0:T(8,128)(2,1)} collective-permute-done((bf16[256,448]{1,0:T(8,128)(2,1)S(1)}, bf16[256,448]{1,0:T(8,128)(2,1)}, u32[]{:S(2)}, u32[]{:S(2)}) %collective-permute-start.3) | collective-permute-done | bytes 229408 | tf_op jit(solution)/shard_map/ppermute | solution.py:696
  53.5 2.3 %route.1 = (bf16[112,448]{1,0:T(8,128)(2,1)}, bf16[112,448]{1,0:T(8,128)(2,1)}, bf16[112,448]{1,0:T(8,128)(2,1)}, bf16[112,448]{1,0:T(8,128)(2,1)}) custom-call(s32[1]{0:T(128)} %bitcast.z_ref, f32[256,448]{1,0:T(8,128)} %constant_dynamic-slice_fusion.3.kept_ref, bf16[256,448]{1,0:T(8,128)(2,1)} %collective-permute-done.3.came_ref, ...), custom_call_target="tpu_custom_call" | custom-call | flops 102760448 | bytes 917504 | tf_op jit(solution)/shard_map/route/pallas_call | solution.py:373
  55.8 2.4 %collective-permute-start.10 = (bf16[112,448]{1,0:T(8,128)(2,1)}, bf16[112,448]{1,0:T(8,128)(2,1)S(1)}, u32[]{:S(2)}, u32[]{:S(2)}) collective-permute-start(bf16[112,448]{1,0:T(8,128)(2,1)} %get-tuple-element.43), channel_id=1, source_target_pairs={{0,4},{4,0},{8,12},{12,8},{1,5},{5,1},{9,13},{13,9},{2,6},{6,2},{1... | collective-permute-start | bytes 301064 | tf_op jit(solution)/shard_map/ppermute | solution.py:701
  58.2 2.6 %collective-permute-start.11 = (bf16[112,448]{1,0:T(8,128)(2,1)}, bf16[112,448]{1,0:T(8,128)(2,1)S(1)}, u32[]{:S(2)}, u32[]{:S(2)}) collective-permute-start(bf16[112,448]{1,0:T(8,128)(2,1)} %get-tuple-element.44), channel_id=1, source_target_pairs={{0,8},{4,12},{8,0},{12,4},{1,9},{5,13},{9,1},{13,5},{2,10},{6,14},... | collective-permute-start | bytes 301064 | tf_op jit(solution)/shard_map/ppermute | solution.py:701
  60.8 5.2 %collective-permute-done.14.refs_9_ = bf16[2,2,256,256]{3,2,1,0:T(8,128)(2,1)} collective-permute-done((bf16[2,2,256,256]{3,2,1,0:T(8,128)(2,1)}, bf16[2,2,256,256]{3,2,1,0:T(8,128)(2,1)}, u32[]{:S(2)}, u32[]{:S(2)}) %collective-permute-start.14) | collective-permute-done | bytes 524320 | tf_op jit(solution)/shard_map/ppermute | solution.py:689
  68.0 3.8 %collective-permute-done.12 = bf16[112,448]{1,0:T(8,128)(2,1)S(1)} collective-permute-done((bf16[112,448]{1,0:T(8,128)(2,1)}, bf16[112,448]{1,0:T(8,128)(2,1)S(1)}, u32[]{:S(2)}, u32[]{:S(2)}) %collective-permute-start.12) | collective-permute-done | bytes 100384 | tf_op jit(solution)/shard_map/ppermute | solution.py:701
  76.6 9.9 %collective-permute-done.15.refs_1_ = bf16[4,112,448]{2,1,0:T(8,128)(2,1)} collective-permute-done((bf16[4,112,448]{2,1,0:T(8,128)(2,1)}, bf16[4,112,448]{2,1,0:T(8,128)(2,1)}, u32[]{:S(2)}, u32[]{:S(2)}) %collective-permute-start.15) | collective-permute-done | bytes 401440 | tf_op jit(solution)/shard_map/ppermute | solution.py:705
  92.0 3.9 %collective-permute-start.18 = (bf16[2,2,256,256]{3,2,1,0:T(8,128)(2,1)}, bf16[2,2,256,256]{3,2,1,0:T(8,128)(2,1)S(1)}, u32[]{:S(2)}, u32[]{:S(2)}) collective-permute-start(bf16[2,2,256,256]{3,2,1,0:T(8,128)(2,1)} %collective-permute-done.13.refs_7_), channel_id=1, source_target_pairs={{0,4},{4,8},{8,12},{1,5},{5,9},{9,13},{2,6},{6,10},{10,14},{3,7},{... | collective-permute-start | bytes 1572872 | tf_op jit(solution)/shard_map/ppermute | solution.py:688
  97.2 4.6 %collective-permute-start.17 = (bf16[2,2,256,256]{3,2,1,0:T(8,128)(2,1)}, bf16[2,2,256,256]{3,2,1,0:T(8,128)(2,1)S(1)}, u32[]{:S(2)}, u32[]{:S(2)}) collective-permute-start(bf16[2,2,256,256]{3,2,1,0:T(8,128)(2,1)} %collective-permute-done.8.refs_6_), channel_id=1, source_target_pairs={{0,4},{4,8},{8,12},{1,5},{5,9},{9,13},{2,6},{6,10},{10,14},{3,7},{... | collective-permute-start | bytes 1572872 | tf_op jit(solution)/shard_map/ppermute | solution.py:688
  103.3 4.3 %place_rows.1 = (bf16[768,896]{1,0:T(8,128)(2,1)S(1)}, bf16[768,384]{1,0:T(8,128)(2,1)S(1)}, bf16[768,128]{1,0:T(8,128)(2,1)S(1)}, bf16[768,128]{1,0:T(8,128)(2,1)S(1)}, s32[1,128]{1,0:T(1,128)S(1)}) custom-call(s32[4]{0:T(128)S(1)} %pad_add_fusion.index_ref, bf16[8,112,448]{2,1,0:T(8,128)(2,1)S(1)} %copy-done.4, ...), custom_call_target="tpu_custom_call" | custom-call | flops 1761607680 | bytes 6291456 | tf_op jit(solution)/shard_map/place_rows/pallas_call | solution.py:465
  107.5 6.1 %attend.2.refs_0_ = bf16[768,384]{1,0:T(8,128)(2,1)S(1)} custom-call(s32[4]{0:T(128)S(1)} %pad_add_fusion.index_ref, s32[8]{0:T(128)S(1)} %get-tuple-element.60.hop_ref, s32[8]{0:T(128)S(1)} %get-tuple-element.59.held_ref, s32[1,128]{1,0:T(1,128)S(1)} %get-tuple-element.50.length_ref, bf16[768,384]{1,0:T(8,128)(2,1)S(1)} %get-tuple-element.52.query_ref, ...), custom_call_target="tpu_custom_call" | custom-call | flops 990904320 | bytes 3145728 | tf_op jit(solution)/shard_map/attend/pallas_call | solution.py:589
  113.7 5.6 %collective-permute-done.17.refs_1_ = bf16[2,2,256,256]{3,2,1,0:T(8,128)(2,1)S(1)} collective-permute-done((bf16[2,2,256,256]{3,2,1,0:T(8,128)(2,1)}, bf16[2,2,256,256]{3,2,1,0:T(8,128)(2,1)S(1)}, u32[]{:S(2)}, u32[]{:S(2)}) %collective-permute-start.17) | collective-permute-done | bytes 524320 | tf_op jit(solution)/shard_map/ppermute | solution.py:688
  119.3 4.0 %collective-permute-done.19.refs_3_ = bf16[2,2,256,256]{3,2,1,0:T(8,128)(2,1)S(1)} collective-permute-done((bf16[2,2,256,256]{3,2,1,0:T(8,128)(2,1)}, bf16[2,2,256,256]{3,2,1,0:T(8,128)(2,1)S(1)}, u32[]{:S(2)}, u32[]{:S(2)}) %collective-permute-start.19) | collective-permute-done | bytes 524320 | tf_op jit(solution)/shard_map/ppermute | solution.py:689
  123.3 4.4 %attend.3 = (bf16[192,384]{1,0:T(8,128)(2,1)S(1)}, bf16[192,384]{1,0:T(8,128)(2,1)S(1)}, bf16[192,384]{1,0:T(8,128)(2,1)S(1)}, bf16[192,384]{1,0:T(8,128)(2,1)S(1)}) custom-call(s32[4]{0:T(128)S(1)} %pad_add_fusion.index_ref, s32[8]{0:T(128)S(1)} %get-tuple-element.60.hop_ref, s32[8]{0:T(128)S(1)} %get-tuple-element.59.held_ref, ...), custom_call_target="tpu_custom_call" | custom-call | flops 495452160 | bytes 1572864 | tf_op jit(solution)/shard_map/attend/pallas_call | solution.py:589
  129.6 4.8 %collective-permute-done.22.refs_2_ = bf16[192,384]{1,0:T(8,128)(2,1)S(1)} collective-permute-done((bf16[192,384]{1,0:T(8,128)(2,1)S(1)}, bf16[192,384]{1,0:T(8,128)(2,1)S(1)}, u32[]{:S(2)}, u32[]{:S(2)}) %collective-permute-start.22) | collective-permute-done | bytes 147488 | tf_op jit(solution)/shard_map/ppermute | solution.py:738
  (74 shorter events, 38.6 us)
Async XLA Ops:
  2.6 3.1 %collective-permute-start = (bf16[2,256,256]{2,1,0:T(8,128)(2,1)}, bf16[2,256,256]{2,1,0:T(8,128)(2,1)}, u32[]{:S(2)}, u32[]{:S(2)}) collective-permute-start(bf16[2,256,256]{2,1,0:T(8,128)(2,1)} %get-tuple-element.33), channel_id=1, source_target_pairs={{0,1},{1,0},{2,3},{3,2},{4,5},{5,4},{6,7},{7,6},{8,9},{9,8},{10,11... | collective-permute-start | bytes 786440 | tf_op jit(solution)/shard_map/ppermute | solution.py:678
  3.1 10.3 %collective-permute-start.4 = (bf16[2,256,256]{2,1,0:T(8,128)(2,1)}, bf16[2,256,256]{2,1,0:T(8,128)(2,1)S(1)}, u32[]{:S(2)}, u32[]{:S(2)}) collective-permute-start(bf16[2,256,256]{2,1,0:T(8,128)(2,1)} %get-tuple-element.35), channel_id=1, source_target_pairs={{0,2},{1,3},{2,0},{3,1},{4,6},{5,7},{6,4},{7,5},{8,10},{9,11},{10,... | collective-permute-start | bytes 786440 | tf_op jit(solution)/shard_map/ppermute | solution.py:679
  5.5 12.7 %collective-permute-start.5 = (bf16[2,256,256]{2,1,0:T(8,128)(2,1)}, bf16[2,256,256]{2,1,0:T(8,128)(2,1)}, u32[]{:S(2)}, u32[]{:S(2)}) collective-permute-start(bf16[2,256,256]{2,1,0:T(8,128)(2,1)} %get-tuple-element.36), channel_id=1, source_target_pairs={{0,3},{1,2},{2,1},{3,0},{4,7},{5,6},{6,5},{7,4},{8,11},{9,10},{10,... | collective-permute-start | bytes 786440 | tf_op jit(solution)/shard_map/ppermute | solution.py:680
  7.6 18.2 %collective-permute-start.1 = (bf16[2,2,256,256]{3,2,1,0:T(8,128)(2,1)}, bf16[2,2,256,256]{3,2,1,0:T(8,128)(2,1)}, u32[]{:S(2)}, u32[]{:S(2)}) collective-permute-start(bf16[2,2,256,256]{3,2,1,0:T(8,128)(2,1)} %stack.24.refs_0_), channel_id=1, source_target_pairs={{0,4},{4,8},{8,12},{1,5},{5,9},{9,13},{2,6},{6,10},{10,14},{3,7},{... | collective-permute-start | bytes 1572872 | tf_op jit(solution)/shard_map/ppermute | solution.py:688
  12.1 16.0 %collective-permute-start.2 = (bf16[2,2,256,256]{3,2,1,0:T(8,128)(2,1)}, bf16[2,2,256,256]{3,2,1,0:T(8,128)(2,1)}, u32[]{:S(2)}, u32[]{:S(2)}) collective-permute-start(bf16[2,2,256,256]{3,2,1,0:T(8,128)(2,1)} %stack.24.refs_0_), channel_id=1, source_target_pairs={{4,0},{8,4},{12,8},{5,1},{9,5},{13,9},{6,2},{10,6},{14,10},{7,3},{... | collective-permute-start | bytes 1572872 | tf_op jit(solution)/shard_map/ppermute | solution.py:689
  20.1 16.1 %collective-permute-start.6 = (bf16[2,2,256,256]{3,2,1,0:T(8,128)(2,1)}, bf16[2,2,256,256]{3,2,1,0:T(8,128)(2,1)}, u32[]{:S(2)}, u32[]{:S(2)}) collective-permute-start(bf16[2,2,256,256]{3,2,1,0:T(8,128)(2,1)} %stack.25.refs_1_), channel_id=1, source_target_pairs={{0,4},{4,8},{8,12},{1,5},{5,9},{9,13},{2,6},{6,10},{10,14},{3,7},{... | collective-permute-start | bytes 1572872 | tf_op jit(solution)/shard_map/ppermute | solution.py:688
  24.5 17.0 %collective-permute-start.7 = (bf16[2,2,256,256]{3,2,1,0:T(8,128)(2,1)}, bf16[2,2,256,256]{3,2,1,0:T(8,128)(2,1)}, u32[]{:S(2)}, u32[]{:S(2)}) collective-permute-start(bf16[2,2,256,256]{3,2,1,0:T(8,128)(2,1)} %stack.25.refs_1_), channel_id=1, source_target_pairs={{4,0},{8,4},{12,8},{5,1},{9,5},{13,9},{6,2},{10,6},{14,10},{7,3},{... | collective-permute-start | bytes 1572872 | tf_op jit(solution)/shard_map/ppermute | solution.py:689
  28.1 27.7 %collective-permute-start.8 = (bf16[2,2,256,256]{3,2,1,0:T(8,128)(2,1)}, bf16[2,2,256,256]{3,2,1,0:T(8,128)(2,1)}, u32[]{:S(2)}, u32[]{:S(2)}) collective-permute-start(bf16[2,2,256,256]{3,2,1,0:T(8,128)(2,1)} %collective-permute-done.1.refs_2_), channel_id=1, source_target_pairs={{0,4},{4,8},{8,12},{1,5},{5,9},{9,13},{2,6},{6,10},{10,14},{3,7},{... | collective-permute-start | bytes 1572872 | tf_op jit(solution)/shard_map/ppermute | solution.py:688
  31.6 24.3 %collective-permute-start.9 = (bf16[2,2,256,256]{3,2,1,0:T(8,128)(2,1)}, bf16[2,2,256,256]{3,2,1,0:T(8,128)(2,1)}, u32[]{:S(2)}, u32[]{:S(2)}) collective-permute-start(bf16[2,2,256,256]{3,2,1,0:T(8,128)(2,1)} %collective-permute-done.2.refs_4_), channel_id=1, source_target_pairs={{4,0},{8,4},{12,8},{5,1},{9,5},{13,9},{6,2},{10,6},{14,10},{7,3},{... | collective-permute-start | bytes 1572872 | tf_op jit(solution)/shard_map/ppermute | solution.py:689
  36.2 24.6 %collective-permute-start.13 = (bf16[2,2,256,256]{3,2,1,0:T(8,128)(2,1)}, bf16[2,2,256,256]{3,2,1,0:T(8,128)(2,1)}, u32[]{:S(2)}, u32[]{:S(2)}) collective-permute-start(bf16[2,2,256,256]{3,2,1,0:T(8,128)(2,1)} %collective-permute-done.6.refs_3_), channel_id=1, source_target_pairs={{0,4},{4,8},{8,12},{1,5},{5,9},{9,13},{2,6},{6,10},{10,14},{3,7},{... | collective-permute-start | bytes 1572872 | tf_op jit(solution)/shard_map/ppermute | solution.py:688
  41.4 24.6 %collective-permute-start.14 = (bf16[2,2,256,256]{3,2,1,0:T(8,128)(2,1)}, bf16[2,2,256,256]{3,2,1,0:T(8,128)(2,1)}, u32[]{:S(2)}, u32[]{:S(2)}) collective-permute-start(bf16[2,2,256,256]{3,2,1,0:T(8,128)(2,1)} %collective-permute-done.7.refs_5_), channel_id=1, source_target_pairs={{4,0},{8,4},{12,8},{5,1},{9,5},{13,9},{6,2},{10,6},{14,10},{7,3},{... | collective-permute-start | bytes 1572872 | tf_op jit(solution)/shard_map/ppermute | solution.py:689
  46.1 7.4 %collective-permute-start.3 = (bf16[256,448]{1,0:T(8,128)(2,1)S(1)}, bf16[256,448]{1,0:T(8,128)(2,1)}, u32[]{:S(2)}, u32[]{:S(2)}) collective-permute-start(bf16[256,448]{1,0:T(8,128)(2,1)S(1)} %dynamic-slice_convert_fusion), channel_id=1, source_target_pairs={{0,2},{2,0},{1,3},{3,1},{4,6},{6,4},{5,7},{7,5},{8,10},{10,8},{9,1... | collective-permute-start | bytes 688136 | tf_op jit(solution)/shard_map/ppermute | solution.py:696
  55.8 12.2 %collective-permute-start.10 = (bf16[112,448]{1,0:T(8,128)(2,1)}, bf16[112,448]{1,0:T(8,128)(2,1)S(1)}, u32[]{:S(2)}, u32[]{:S(2)}) collective-permute-start(bf16[112,448]{1,0:T(8,128)(2,1)} %get-tuple-element.43), channel_id=1, source_target_pairs={{0,4},{4,0},{8,12},{12,8},{1,5},{5,1},{9,13},{13,9},{2,6},{6,2},{1... | collective-permute-start | bytes 301064 | tf_op jit(solution)/shard_map/ppermute | solution.py:701
  58.2 9.8 %collective-permute-start.11 = (bf16[112,448]{1,0:T(8,128)(2,1)}, bf16[112,448]{1,0:T(8,128)(2,1)S(1)}, u32[]{:S(2)}, u32[]{:S(2)}) collective-permute-start(bf16[112,448]{1,0:T(8,128)(2,1)} %get-tuple-element.44), channel_id=1, source_target_pairs={{0,8},{4,12},{8,0},{12,4},{1,9},{5,13},{9,1},{13,5},{2,10},{6,14},... | collective-permute-start | bytes 301064 | tf_op jit(solution)/shard_map/ppermute | solution.py:701
  60.8 11.0 %collective-permute-start.12 = (bf16[112,448]{1,0:T(8,128)(2,1)}, bf16[112,448]{1,0:T(8,128)(2,1)S(1)}, u32[]{:S(2)}, u32[]{:S(2)}) collective-permute-start(bf16[112,448]{1,0:T(8,128)(2,1)} %get-tuple-element.45), channel_id=1, source_target_pairs={{0,12},{4,8},{8,4},{12,0},{1,13},{5,9},{9,5},{13,1},{2,14},{6,10},... | collective-permute-start | bytes 301064 | tf_op jit(solution)/shard_map/ppermute | solution.py:701
  74.3 12.1 %collective-permute-start.15 = (bf16[4,112,448]{2,1,0:T(8,128)(2,1)}, bf16[4,112,448]{2,1,0:T(8,128)(2,1)}, u32[]{:S(2)}, u32[]{:S(2)}) collective-permute-start(bf16[4,112,448]{2,1,0:T(8,128)(2,1)} %stack.26.refs_0_), channel_id=1, source_target_pairs={{0,2},{2,0},{1,3},{3,1},{4,6},{6,4},{5,7},{7,5},{8,10},{10,8},{9,1... | collective-permute-start | bytes 1204232 | tf_op jit(solution)/shard_map/ppermute | solution.py:705
  88.6 14.7 %collective-permute-start.16 = (bf16[8,112,448]{2,1,0:T(8,128)(2,1)}, bf16[8,112,448]{2,1,0:T(8,128)(2,1)S(1)}, u32[]{:S(2)}, u32[]{:S(2)}) collective-permute-start(bf16[8,112,448]{2,1,0:T(8,128)(2,1)} %stack.27.mine_ref), channel_id=1, source_target_pairs={{0,1},{1,0},{2,3},{3,2},{4,5},{5,4},{6,7},{7,6},{8,9},{9,8},{10,11... | collective-permute-start | bytes 2408456 | tf_op jit(solution)/shard_map/ppermute | solution.py:706
  92.0 21.7 %collective-permute-start.18 = (bf16[2,2,256,256]{3,2,1,0:T(8,128)(2,1)}, bf16[2,2,256,256]{3,2,1,0:T(8,128)(2,1)S(1)}, u32[]{:S(2)}, u32[]{:S(2)}) collective-permute-start(bf16[2,2,256,256]{3,2,1,0:T(8,128)(2,1)} %collective-permute-done.13.refs_7_), channel_id=1, source_target_pairs={{0,4},{4,8},{8,12},{1,5},{5,9},{9,13},{2,6},{6,10},{10,14},{3,7},{... | collective-permute-start | bytes 1572872 | tf_op jit(solution)/shard_map/ppermute | solution.py:688
  95.9 17.8 %collective-permute-start.20 = (bf16[2,2,256,256]{3,2,1,0:T(8,128)(2,1)}, bf16[2,2,256,256]{3,2,1,0:T(8,128)(2,1)S(1)}, u32[]{:S(2)}, u32[]{:S(2)}) collective-permute-start(bf16[2,2,256,256]{3,2,1,0:T(8,128)(2,1)} %collective-permute-done.14.refs_9_), channel_id=1, source_target_pairs={{4,0},{8,4},{12,8},{5,1},{9,5},{13,9},{6,2},{10,6},{14,10},{7,3},{... | collective-permute-start | bytes 1572872 | tf_op jit(solution)/shard_map/ppermute | solution.py:689
  97.2 22.1 %collective-permute-start.17 = (bf16[2,2,256,256]{3,2,1,0:T(8,128)(2,1)}, bf16[2,2,256,256]{3,2,1,0:T(8,128)(2,1)S(1)}, u32[]{:S(2)}, u32[]{:S(2)}) collective-permute-start(bf16[2,2,256,256]{3,2,1,0:T(8,128)(2,1)} %collective-permute-done.8.refs_6_), channel_id=1, source_target_pairs={{0,4},{4,8},{8,12},{1,5},{5,9},{9,13},{2,6},{6,10},{10,14},{3,7},{... | collective-permute-start | bytes 1572872 | tf_op jit(solution)/shard_map/ppermute | solution.py:688
  101.8 21.5 %collective-permute-start.19 = (bf16[2,2,256,256]{3,2,1,0:T(8,128)(2,1)}, bf16[2,2,256,256]{3,2,1,0:T(8,128)(2,1)S(1)}, u32[]{:S(2)}, u32[]{:S(2)}) collective-permute-start(bf16[2,2,256,256]{3,2,1,0:T(8,128)(2,1)} %collective-permute-done.9.refs_8_), channel_id=1, source_target_pairs={{4,0},{8,4},{12,8},{5,1},{9,5},{13,9},{6,2},{10,6},{14,10},{7,3},{... | collective-permute-start | bytes 1572872 | tf_op jit(solution)/shard_map/ppermute | solution.py:689
  127.7 1.9 %collective-permute-start.21 = (bf16[192,384]{1,0:T(8,128)(2,1)S(1)}, bf16[192,384]{1,0:T(8,128)(2,1)S(1)}, u32[]{:S(2)}, u32[]{:S(2)}) collective-permute-start(bf16[192,384]{1,0:T(8,128)(2,1)S(1)} %get-tuple-element.56), channel_id=1, source_target_pairs={{0,1},{1,0},{2,3},{3,2},{4,5},{5,4},{6,7},{7,6},{8,9},{9,8},{10,11... | collective-permute-start | bytes 442376 | tf_op jit(solution)/shard_map/ppermute | solution.py:738
  127.8 6.7 %collective-permute-start.22 = (bf16[192,384]{1,0:T(8,128)(2,1)S(1)}, bf16[192,384]{1,0:T(8,128)(2,1)S(1)}, u32[]{:S(2)}, u32[]{:S(2)}) collective-permute-start(bf16[192,384]{1,0:T(8,128)(2,1)S(1)} %get-tuple-element.57), channel_id=1, source_target_pairs={{0,2},{1,3},{2,0},{3,1},{4,6},{5,7},{6,4},{7,5},{8,10},{9,11},{10,... | collective-permute-start | bytes 442376 | tf_op jit(solution)/shard_map/ppermute | solution.py:738
  129.3 7.4 %collective-permute-start.23 = (bf16[192,384]{1,0:T(8,128)(2,1)S(1)}, bf16[192,384]{1,0:T(8,128)(2,1)S(1)}, u32[]{:S(2)}, u32[]{:S(2)}) collective-permute-start(bf16[192,384]{1,0:T(8,128)(2,1)S(1)} %get-tuple-element.58), channel_id=1, source_target_pairs={{0,3},{1,2},{2,1},{3,0},{4,7},{5,6},{6,5},{7,4},{8,11},{9,10},{10,... | collective-permute-start | bytes 442376 | tf_op jit(solution)/shard_map/ppermute | solution.py:738
  (14 other events, 165.7 us)

commit v5 on v4

--- a/solution.py
+++ b/solution.py
@@ -702,7 +702,9 @@
     ]
     arrived, _ = lax.optimization_barrier((arrived, (prompts[-2][1], prompts[2][1])))
     arrived = stack(*[a[None] for a in arrived])
-    mine = stack(arrived, lax.ppermute(arrived, "inner", swapped(2, 1)))
+    other = lax.ppermute(arrived, "inner", swapped(2, 1))
+    other, _ = lax.optimization_barrier((other, (prompts[-3][0], prompts[3][0])))
+    mine = stack(arrived, other)
     core = lax.ppermute(mine, "rep", swapped(2, 1))
 
     group_width = PER_GROUP * HD

time: 141 us -> 139 us (0.986); the launches traced: 139 us -> 139 us
  waiting for transfers between devices: 51.1 us -> 49.1 us
    ppermute x3, waiting for transfers between devices: 5.74 us -> 18.3 us  [line_body(): lax.ppermute(routed[by], 'sess', swapped(planes, by))]
    ppermute x6, waiting for transfers between devices: 11.6 us -> 5.61 us  [line_body(): left[chunk] = lax.ppermute(left[chunk], 'sess', shifted(planes, -1))]
    ppermute x6, waiting for transfers between devices: 8.94 us -> 3.34 us  [line_body(): right[chunk] = lax.ppermute(right[chunk], 'sess', shifted(planes, 1))]
    ppermute x1, waiting for transfers between devices: 2.96 us -> 0.01 us  [line_body(): came = lax.ppermute(sent.astype(jnp.bfloat16), 'inner', swapped(2, 1))]
  transfers between devices with their start and end apart: 24 -> 24, of which waited for: 12 -> 9; matrix products, arithmetic and copies ran while one was open for 7% -> 7% of each run, Pallas kernels for 12% -> 14%
where the time goes in v5:
time: 139 us
  waiting for transfers between devices  49.1 us (35%)
  starting transfers between devices  47.8 us (34%)
  Pallas kernels  30.3 us (22%)
  local copies, waits for them, and re-layouts  7.79 us (6%)
  matrix products  2.29 us (2%)
    ppermute x6, starting transfers between devices, line_body(): right[chunk] = lax.ppermute(right[chunk], 'sess', shifted(planes, 1))  26.8 us
    ppermute x3, waiting for transfers between devices, line_body(): lax.ppermute(routed[by], 'sess', swapped(planes, by))  18.3 us
    pallas_call x2, Pallas kernels, attend_hops(): pl.pallas_call(functools.partial(hops_kernel, hops=hops, carried=carried)...  11.2 us
    ppermute x1, waiting for transfers between devices, line_body(): other = lax.ppermute(arrived, 'inner', swapped(2, 1))  9.87 us
    pallas_call x4, Pallas kernels, stack(): pl.pallas_call(stack_kernel, in_specs=[VMEM] * len(arrays), out_specs=VME...  7.76 us
    ppermute x6, starting transfers between devices, line_body(): left[chunk] = lax.ppermute(left[chunk], 'sess', shifted(planes, -1))  7.69 us
    ppermute x3, waiting for transfers between devices, line_body(): lax.ppermute(attended[by], pair, swapped(4, by))  7.11 us
    ppermute x6, waiting for transfers between devices, line_body(): left[chunk] = lax.ppermute(left[chunk], 'sess', shifted(planes, -1))  5.61 us
  transfers between devices with their start and end apart: 24, of which 9 were waited for; matrix products, arithmetic and copies ran while one was open for 7% of the time, Pallas kernels for 14%

profile of v5, /device:TPU:0, one launch (start us, length us, event | category | flops | bytes accessed | tf_op | source)
XLA Modules:
  0.0 138.6 jit_solution(3974854735710081784)
XLA Ops:
  0.0 2.6 %split_heads.1 = (bf16[2,256,256]{2,1,0:T(8,128)(2,1)}, bf16[2,256,256]{2,1,0:T(8,128)(2,1)}, bf16[2,256,256]{2,1,0:T(8,128)(2,1)}, bf16[2,256,256]{2,1,0:T(8,128)(2,1)}) custom-call(s32[1]{0:T(128)} %bitcast.3.head_ref, bf16[2,256,1024]{2,1,0:T(8,128)(2,1)} %cache_ref.1), custom_call_target="tpu_custom_call" | custom-call | bytes 2097152 | tf_op jit(solution)/shard_map/split_heads/pallas_call | solution.py:308
  3.1 2.5 %collective-permute-start.4 = (bf16[2,256,256]{2,1,0:T(8,128)(2,1)}, bf16[2,256,256]{2,1,0:T(8,128)(2,1)S(1)}, u32[]{:S(2)}, u32[]{:S(2)}) collective-permute-start(bf16[2,256,256]{2,1,0:T(8,128)(2,1)} %get-tuple-element.36), channel_id=1, source_target_pairs={{0,2},{1,3},{2,0},{3,1},{4,6},{5,7},{6,4},{7,5},{8,10},{9,11},{10,... | collective-permute-start | bytes 786440 | tf_op jit(solution)/shard_map/ppermute | solution.py:679
  7.6 4.5 %collective-permute-start.1 = (bf16[2,2,256,256]{3,2,1,0:T(8,128)(2,1)}, bf16[2,2,256,256]{3,2,1,0:T(8,128)(2,1)}, u32[]{:S(2)}, u32[]{:S(2)}) collective-permute-start(bf16[2,2,256,256]{3,2,1,0:T(8,128)(2,1)} %stack.24.refs_0_), channel_id=1, source_target_pairs={{0,4},{4,8},{8,12},{1,5},{5,9},{9,13},{2,6},{6,10},{10,14},{3,7},{... | collective-permute-start | bytes 1572872 | tf_op jit(solution)/shard_map/ppermute | solution.py:688
  13.4 4.9 %collective-permute-done.5 = bf16[2,256,256]{2,1,0:T(8,128)(2,1)} collective-permute-done((bf16[2,256,256]{2,1,0:T(8,128)(2,1)}, bf16[2,256,256]{2,1,0:T(8,128)(2,1)}, u32[]{:S(2)}, u32[]{:S(2)}) %collective-permute-start.5) | collective-permute-done | bytes 262176 | tf_op jit(solution)/shard_map/ppermute | solution.py:680
  20.1 4.3 %collective-permute-start.6 = (bf16[2,2,256,256]{3,2,1,0:T(8,128)(2,1)}, bf16[2,2,256,256]{3,2,1,0:T(8,128)(2,1)}, u32[]{:S(2)}, u32[]{:S(2)}) collective-permute-start(bf16[2,2,256,256]{3,2,1,0:T(8,128)(2,1)} %stack.25.refs_1_), channel_id=1, source_target_pairs={{0,4},{4,8},{8,12},{1,5},{5,9},{9,13},{2,6},{6,10},{10,14},{3,7},{... | collective-permute-start | bytes 1572872 | tf_op jit(solution)/shard_map/ppermute | solution.py:688
  25.8 2.3 %collective-permute-done.2.refs_4_ = bf16[2,2,256,256]{3,2,1,0:T(8,128)(2,1)} collective-permute-done((bf16[2,2,256,256]{3,2,1,0:T(8,128)(2,1)}, bf16[2,2,256,256]{3,2,1,0:T(8,128)(2,1)}, u32[]{:S(2)}, u32[]{:S(2)}) %collective-permute-start.2) | collective-permute-done | bytes 524320 | tf_op jit(solution)/shard_map/ppermute | solution.py:689
  28.1 3.5 %collective-permute-start.8 = (bf16[2,2,256,256]{3,2,1,0:T(8,128)(2,1)}, bf16[2,2,256,256]{3,2,1,0:T(8,128)(2,1)}, u32[]{:S(2)}, u32[]{:S(2)}) collective-permute-start(bf16[2,2,256,256]{3,2,1,0:T(8,128)(2,1)} %collective-permute-done.1.refs_2_), channel_id=1, source_target_pairs={{0,4},{4,8},{8,12},{1,5},{5,9},{9,13},{2,6},{6,10},{10,14},{3,7},{... | collective-permute-start | bytes 1572872 | tf_op jit(solution)/shard_map/ppermute | solution.py:688
  32.9 3.3 %collective-permute-done.6.refs_3_ = bf16[2,2,256,256]{3,2,1,0:T(8,128)(2,1)} collective-permute-done((bf16[2,2,256,256]{3,2,1,0:T(8,128)(2,1)}, bf16[2,2,256,256]{3,2,1,0:T(8,128)(2,1)}, u32[]{:S(2)}, u32[]{:S(2)}) %collective-permute-start.6) | collective-permute-done | bytes 524320 | tf_op jit(solution)/shard_map/ppermute | solution.py:688
  36.2 5.2 %collective-permute-start.13 = (bf16[2,2,256,256]{3,2,1,0:T(8,128)(2,1)}, bf16[2,2,256,256]{3,2,1,0:T(8,128)(2,1)}, u32[]{:S(2)}, u32[]{:S(2)}) collective-permute-start(bf16[2,2,256,256]{3,2,1,0:T(8,128)(2,1)} %collective-permute-done.6.refs_3_), channel_id=1, source_target_pairs={{0,4},{4,8},{8,12},{1,5},{5,9},{9,13},{2,6},{6,10},{10,14},{3,7},{... | collective-permute-start | bytes 1572872 | tf_op jit(solution)/shard_map/ppermute | solution.py:688
  42.7 2.3 %fusion.1 = f32[256,896]{1,0:T(8,128)S(1)} fusion(bf16[256,1792]{1,0:T(8,128)(2,1)} %param.13, bf16[1792,896]{1,0:T(8,128)(2,1)S(1)} %copy-done), kind=kOutput, calls=%fused_computation.15 | convolution fusion | flops 822083584 | bytes 5046272 | tf_op jit(solution)/shard_map/dot_general | solution.py:693
  48.4 5.4 %collective-permute-start.16 = (bf16[2,2,256,256]{3,2,1,0:T(8,128)(2,1)}, bf16[2,2,256,256]{3,2,1,0:T(8,128)(2,1)}, u32[]{:S(2)}, u32[]{:S(2)}) collective-permute-start(bf16[2,2,256,256]{3,2,1,0:T(8,128)(2,1)} %collective-permute-done.8.refs_6_), channel_id=1, source_target_pairs={{0,4},{4,8},{8,12},{1,5},{5,9},{9,13},{2,6},{6,10},{10,14},{3,7},{... | collective-permute-start | bytes 1572872 | tf_op jit(solution)/shard_map/ppermute | solution.py:688
  57.2 2.3 %route.1 = (bf16[112,448]{1,0:T(8,128)(2,1)}, bf16[112,448]{1,0:T(8,128)(2,1)}, bf16[112,448]{1,0:T(8,128)(2,1)}, bf16[112,448]{1,0:T(8,128)(2,1)}) custom-call(s32[1]{0:T(128)} %bitcast.z_ref, f32[256,448]{1,0:T(8,128)} %constant_dynamic-slice_fusion.3.kept_ref, bf16[256,448]{1,0:T(8,128)(2,1)} %collective-permute-done.3.came_ref, ...), custom_call_target="tpu_custom_call" | custom-call | flops 102760448 | bytes 917504 | tf_op jit(solution)/shard_map/route/pallas_call | solution.py:373
  59.5 2.7 %collective-permute-start.10 = (bf16[112,448]{1,0:T(8,128)(2,1)}, bf16[112,448]{1,0:T(8,128)(2,1)S(1)}, u32[]{:S(2)}, u32[]{:S(2)}) collective-permute-start(bf16[112,448]{1,0:T(8,128)(2,1)} %get-tuple-element.44), channel_id=1, source_target_pairs={{0,4},{4,0},{8,12},{12,8},{1,5},{5,1},{9,13},{13,9},{2,6},{6,2},{1... | collective-permute-start | bytes 301064 | tf_op jit(solution)/shard_map/ppermute | solution.py:701
  62.2 2.6 %collective-permute-start.11 = (bf16[112,448]{1,0:T(8,128)(2,1)}, bf16[112,448]{1,0:T(8,128)(2,1)S(1)}, u32[]{:S(2)}, u32[]{:S(2)}) collective-permute-start(bf16[112,448]{1,0:T(8,128)(2,1)} %get-tuple-element.45), channel_id=1, source_target_pairs={{0,8},{4,12},{8,0},{12,4},{1,9},{5,13},{9,1},{13,5},{2,10},{6,14},... | collective-permute-start | bytes 301064 | tf_op jit(solution)/shard_map/ppermute | solution.py:701
  64.7 14.5 %collective-permute-done.10 = bf16[112,448]{1,0:T(8,128)(2,1)S(1)} collective-permute-done((bf16[112,448]{1,0:T(8,128)(2,1)}, bf16[112,448]{1,0:T(8,128)(2,1)S(1)}, u32[]{:S(2)}, u32[]{:S(2)}) %collective-permute-start.10) | collective-permute-done | bytes 100384 | tf_op jit(solution)/shard_map/ppermute | solution.py:701
  79.2 3.8 %collective-permute-done.12 = bf16[112,448]{1,0:T(8,128)(2,1)S(1)} collective-permute-done((bf16[112,448]{1,0:T(8,128)(2,1)}, bf16[112,448]{1,0:T(8,128)(2,1)S(1)}, u32[]{:S(2)}, u32[]{:S(2)}) %collective-permute-start.12) | collective-permute-done | bytes 100384 | tf_op jit(solution)/shard_map/ppermute | solution.py:701
  87.8 9.9 %collective-permute-done.15.refs_1_ = bf16[4,112,448]{2,1,0:T(8,128)(2,1)} collective-permute-done((bf16[4,112,448]{2,1,0:T(8,128)(2,1)}, bf16[4,112,448]{2,1,0:T(8,128)(2,1)}, u32[]{:S(2)}, u32[]{:S(2)}) %collective-permute-start.15) | collective-permute-done | bytes 401440 | tf_op jit(solution)/shard_map/ppermute | solution.py:705
  103.2 3.9 %collective-permute-start.19 = (bf16[2,2,256,256]{3,2,1,0:T(8,128)(2,1)}, bf16[2,2,256,256]{3,2,1,0:T(8,128)(2,1)S(1)}, u32[]{:S(2)}, u32[]{:S(2)}) collective-permute-start(bf16[2,2,256,256]{3,2,1,0:T(8,128)(2,1)} %collective-permute-done.13.refs_7_), channel_id=1, source_target_pairs={{0,4},{4,8},{8,12},{1,5},{5,9},{9,13},{2,6},{6,10},{10,14},{3,7},{... | collective-permute-start | bytes 1572872 | tf_op jit(solution)/shard_map/ppermute | solution.py:688
  108.6 4.2 %place_rows.1 = (bf16[768,896]{1,0:T(8,128)(2,1)S(1)}, bf16[768,384]{1,0:T(8,128)(2,1)S(1)}, bf16[768,128]{1,0:T(8,128)(2,1)S(1)}, bf16[768,128]{1,0:T(8,128)(2,1)S(1)}, s32[1,128]{1,0:T(1,128)S(1)}) custom-call(s32[4]{0:T(128)S(1)} %pad_add_fusion.index_ref, bf16[8,112,448]{2,1,0:T(8,128)(2,1)S(1)} %copy-done.4, ...), custom_call_target="tpu_custom_call" | custom-call | flops 1761607680 | bytes 6291456 | tf_op jit(solution)/shard_map/place_rows/pallas_call | solution.py:465
  112.9 7.1 %attend.2.refs_0_ = bf16[768,384]{1,0:T(8,128)(2,1)S(1)} custom-call(s32[4]{0:T(128)S(1)} %pad_add_fusion.index_ref, s32[8]{0:T(128)S(1)} %get-tuple-element.62.hop_ref, s32[8]{0:T(128)S(1)} %get-tuple-element.61.held_ref, s32[1,128]{1,0:T(1,128)S(1)} %get-tuple-element.52.length_ref, bf16[768,384]{1,0:T(8,128)(2,1)S(1)} %get-tuple-element.54.query_ref, ...), custom_call_target="tpu_custom_call" | custom-call | flops 990904320 | bytes 3145728 | tf_op jit(solution)/shard_map/attend/pallas_call | solution.py:589
  120.0 3.3 %collective-permute-done.20.refs_4_ = bf16[2,2,256,256]{3,2,1,0:T(8,128)(2,1)S(1)} collective-permute-done((bf16[2,2,256,256]{3,2,1,0:T(8,128)(2,1)}, bf16[2,2,256,256]{3,2,1,0:T(8,128)(2,1)S(1)}, u32[]{:S(2)}, u32[]{:S(2)}) %collective-permute-start.20) | collective-permute-done | bytes 524320 | tf_op jit(solution)/shard_map/ppermute | solution.py:689
  123.3 4.1 %attend.3 = (bf16[192,384]{1,0:T(8,128)(2,1)S(1)}, bf16[192,384]{1,0:T(8,128)(2,1)S(1)}, bf16[192,384]{1,0:T(8,128)(2,1)S(1)}, bf16[192,384]{1,0:T(8,128)(2,1)S(1)}) custom-call(s32[4]{0:T(128)S(1)} %pad_add_fusion.index_ref, s32[8]{0:T(128)S(1)} %get-tuple-element.62.hop_ref, s32[8]{0:T(128)S(1)} %get-tuple-element.61.held_ref, ...), custom_call_target="tpu_custom_call" | custom-call | flops 495452160 | bytes 1572864 | tf_op jit(solution)/shard_map/attend/pallas_call | solution.py:589
  129.3 4.8 %collective-permute-done.22.refs_2_ = bf16[192,384]{1,0:T(8,128)(2,1)S(1)} collective-permute-done((bf16[192,384]{1,0:T(8,128)(2,1)S(1)}, bf16[192,384]{1,0:T(8,128)(2,1)S(1)}, u32[]{:S(2)}, u32[]{:S(2)}) %collective-permute-start.22) | collective-permute-done | bytes 147488 | tf_op jit(solution)/shard_map/ppermute | solution.py:740
  134.2 2.3 %collective-permute-done.23.refs_3_ = bf16[192,384]{1,0:T(8,128)(2,1)S(1)} collective-permute-done((bf16[192,384]{1,0:T(8,128)(2,1)S(1)}, bf16[192,384]{1,0:T(8,128)(2,1)S(1)}, u32[]{:S(2)}, u32[]{:S(2)}) %collective-permute-start.23) | collective-permute-done | bytes 147488 | tf_op jit(solution)/shard_map/ppermute | solution.py:740
  (74 shorter events, 32.2 us)
Async XLA Ops:
  2.6 3.1 %collective-permute-start = (bf16[2,256,256]{2,1,0:T(8,128)(2,1)}, bf16[2,256,256]{2,1,0:T(8,128)(2,1)}, u32[]{:S(2)}, u32[]{:S(2)}) collective-permute-start(bf16[2,256,256]{2,1,0:T(8,128)(2,1)} %get-tuple-element.34), channel_id=1, source_target_pairs={{0,1},{1,0},{2,3},{3,2},{4,5},{5,4},{6,7},{7,6},{8,9},{9,8},{10,11... | collective-permute-start | bytes 786440 | tf_op jit(solution)/shard_map/ppermute | solution.py:678
  3.1 10.3 %collective-permute-start.4 = (bf16[2,256,256]{2,1,0:T(8,128)(2,1)}, bf16[2,256,256]{2,1,0:T(8,128)(2,1)S(1)}, u32[]{:S(2)}, u32[]{:S(2)}) collective-permute-start(bf16[2,256,256]{2,1,0:T(8,128)(2,1)} %get-tuple-element.36), channel_id=1, source_target_pairs={{0,2},{1,3},{2,0},{3,1},{4,6},{5,7},{6,4},{7,5},{8,10},{9,11},{10,... | collective-permute-start | bytes 786440 | tf_op jit(solution)/shard_map/ppermute | solution.py:679
  5.5 12.7 %collective-permute-start.5 = (bf16[2,256,256]{2,1,0:T(8,128)(2,1)}, bf16[2,256,256]{2,1,0:T(8,128)(2,1)}, u32[]{:S(2)}, u32[]{:S(2)}) collective-permute-start(bf16[2,256,256]{2,1,0:T(8,128)(2,1)} %get-tuple-element.37), channel_id=1, source_target_pairs={{0,3},{1,2},{2,1},{3,0},{4,7},{5,6},{6,5},{7,4},{8,11},{9,10},{10,... | collective-permute-start | bytes 786440 | tf_op jit(solution)/shard_map/ppermute | solution.py:680
  7.6 18.2 %collective-permute-start.1 = (bf16[2,2,256,256]{3,2,1,0:T(8,128)(2,1)}, bf16[2,2,256,256]{3,2,1,0:T(8,128)(2,1)}, u32[]{:S(2)}, u32[]{:S(2)}) collective-permute-start(bf16[2,2,256,256]{3,2,1,0:T(8,128)(2,1)} %stack.24.refs_0_), channel_id=1, source_target_pairs={{0,4},{4,8},{8,12},{1,5},{5,9},{9,13},{2,6},{6,10},{10,14},{3,7},{... | collective-permute-start | bytes 1572872 | tf_op jit(solution)/shard_map/ppermute | solution.py:688
  12.1 16.0 %collective-permute-start.2 = (bf16[2,2,256,256]{3,2,1,0:T(8,128)(2,1)}, bf16[2,2,256,256]{3,2,1,0:T(8,128)(2,1)}, u32[]{:S(2)}, u32[]{:S(2)}) collective-permute-start(bf16[2,2,256,256]{3,2,1,0:T(8,128)(2,1)} %stack.24.refs_0_), channel_id=1, source_target_pairs={{4,0},{8,4},{12,8},{5,1},{9,5},{13,9},{6,2},{10,6},{14,10},{7,3},{... | collective-permute-start | bytes 1572872 | tf_op jit(solution)/shard_map/ppermute | solution.py:689
  20.1 16.1 %collective-permute-start.6 = (bf16[2,2,256,256]{3,2,1,0:T(8,128)(2,1)}, bf16[2,2,256,256]{3,2,1,0:T(8,128)(2,1)}, u32[]{:S(2)}, u32[]{:S(2)}) collective-permute-start(bf16[2,2,256,256]{3,2,1,0:T(8,128)(2,1)} %stack.25.refs_1_), channel_id=1, source_target_pairs={{0,4},{4,8},{8,12},{1,5},{5,9},{9,13},{2,6},{6,10},{10,14},{3,7},{... | collective-permute-start | bytes 1572872 | tf_op jit(solution)/shard_map/ppermute | solution.py:688
  24.4 17.0 %collective-permute-start.7 = (bf16[2,2,256,256]{3,2,1,0:T(8,128)(2,1)}, bf16[2,2,256,256]{3,2,1,0:T(8,128)(2,1)}, u32[]{:S(2)}, u32[]{:S(2)}) collective-permute-start(bf16[2,2,256,256]{3,2,1,0:T(8,128)(2,1)} %stack.25.refs_1_), channel_id=1, source_target_pairs={{4,0},{8,4},{12,8},{5,1},{9,5},{13,9},{6,2},{10,6},{14,10},{7,3},{... | collective-permute-start | bytes 1572872 | tf_op jit(solution)/shard_map/ppermute | solution.py:689
  28.1 20.4 %collective-permute-start.8 = (bf16[2,2,256,256]{3,2,1,0:T(8,128)(2,1)}, bf16[2,2,256,256]{3,2,1,0:T(8,128)(2,1)}, u32[]{:S(2)}, u32[]{:S(2)}) collective-permute-start(bf16[2,2,256,256]{3,2,1,0:T(8,128)(2,1)} %collective-permute-done.1.refs_2_), channel_id=1, source_target_pairs={{0,4},{4,8},{8,12},{1,5},{5,9},{9,13},{2,6},{6,10},{10,14},{3,7},{... | collective-permute-start | bytes 1572872 | tf_op jit(solution)/shard_map/ppermute | solution.py:688
  31.6 22.2 %collective-permute-start.9 = (bf16[2,2,256,256]{3,2,1,0:T(8,128)(2,1)}, bf16[2,2,256,256]{3,2,1,0:T(8,128)(2,1)}, u32[]{:S(2)}, u32[]{:S(2)}) collective-permute-start(bf16[2,2,256,256]{3,2,1,0:T(8,128)(2,1)} %collective-permute-done.2.refs_4_), channel_id=1, source_target_pairs={{4,0},{8,4},{12,8},{5,1},{9,5},{13,9},{6,2},{10,6},{14,10},{7,3},{... | collective-permute-start | bytes 1572872 | tf_op jit(solution)/shard_map/ppermute | solution.py:689
  36.2 26.0 %collective-permute-start.13 = (bf16[2,2,256,256]{3,2,1,0:T(8,128)(2,1)}, bf16[2,2,256,256]{3,2,1,0:T(8,128)(2,1)}, u32[]{:S(2)}, u32[]{:S(2)}) collective-permute-start(bf16[2,2,256,256]{3,2,1,0:T(8,128)(2,1)} %collective-permute-done.6.refs_3_), channel_id=1, source_target_pairs={{0,4},{4,8},{8,12},{1,5},{5,9},{9,13},{2,6},{6,10},{10,14},{3,7},{... | collective-permute-start | bytes 1572872 | tf_op jit(solution)/shard_map/ppermute | solution.py:688
  41.4 23.3 %collective-permute-start.14 = (bf16[2,2,256,256]{3,2,1,0:T(8,128)(2,1)}, bf16[2,2,256,256]{3,2,1,0:T(8,128)(2,1)}, u32[]{:S(2)}, u32[]{:S(2)}) collective-permute-start(bf16[2,2,256,256]{3,2,1,0:T(8,128)(2,1)} %collective-permute-done.7.refs_5_), channel_id=1, source_target_pairs={{4,0},{8,4},{12,8},{5,1},{9,5},{13,9},{6,2},{10,6},{14,10},{7,3},{... | collective-permute-start | bytes 1572872 | tf_op jit(solution)/shard_map/ppermute | solution.py:689
  46.1 11.1 %collective-permute-start.3 = (bf16[256,448]{1,0:T(8,128)(2,1)S(1)}, bf16[256,448]{1,0:T(8,128)(2,1)}, u32[]{:S(2)}, u32[]{:S(2)}) collective-permute-start(bf16[256,448]{1,0:T(8,128)(2,1)S(1)} %dynamic-slice_convert_fusion), channel_id=1, source_target_pairs={{0,2},{2,0},{1,3},{3,1},{4,6},{6,4},{5,7},{7,5},{8,10},{10,8},{9,1... | collective-permute-start | bytes 688136 | tf_op jit(solution)/shard_map/ppermute | solution.py:696
  48.4 49.2 %collective-permute-start.16 = (bf16[2,2,256,256]{3,2,1,0:T(8,128)(2,1)}, bf16[2,2,256,256]{3,2,1,0:T(8,128)(2,1)}, u32[]{:S(2)}, u32[]{:S(2)}) collective-permute-start(bf16[2,2,256,256]{3,2,1,0:T(8,128)(2,1)} %collective-permute-done.8.refs_6_), channel_id=1, source_target_pairs={{0,4},{4,8},{8,12},{1,5},{5,9},{9,13},{2,6},{6,10},{10,14},{3,7},{... | collective-permute-start | bytes 1572872 | tf_op jit(solution)/shard_map/ppermute | solution.py:688
  53.8 43.8 %collective-permute-start.17 = (bf16[2,2,256,256]{3,2,1,0:T(8,128)(2,1)}, bf16[2,2,256,256]{3,2,1,0:T(8,128)(2,1)}, u32[]{:S(2)}, u32[]{:S(2)}) collective-permute-start(bf16[2,2,256,256]{3,2,1,0:T(8,128)(2,1)} %collective-permute-done.9.refs_8_), channel_id=1, source_target_pairs={{4,0},{8,4},{12,8},{5,1},{9,5},{13,9},{6,2},{10,6},{14,10},{7,3},{... | collective-permute-start | bytes 1572872 | tf_op jit(solution)/shard_map/ppermute | solution.py:689
  59.5 19.7 %collective-permute-start.10 = (bf16[112,448]{1,0:T(8,128)(2,1)}, bf16[112,448]{1,0:T(8,128)(2,1)S(1)}, u32[]{:S(2)}, u32[]{:S(2)}) collective-permute-start(bf16[112,448]{1,0:T(8,128)(2,1)} %get-tuple-element.44), channel_id=1, source_target_pairs={{0,4},{4,0},{8,12},{12,8},{1,5},{5,1},{9,13},{13,9},{2,6},{6,2},{1... | collective-permute-start | bytes 301064 | tf_op jit(solution)/shard_map/ppermute | solution.py:701
  62.2 17.1 %collective-permute-start.11 = (bf16[112,448]{1,0:T(8,128)(2,1)}, bf16[112,448]{1,0:T(8,128)(2,1)S(1)}, u32[]{:S(2)}, u32[]{:S(2)}) collective-permute-start(bf16[112,448]{1,0:T(8,128)(2,1)} %get-tuple-element.45), channel_id=1, source_target_pairs={{0,8},{4,12},{8,0},{12,4},{1,9},{5,13},{9,1},{13,5},{2,10},{6,14},... | collective-permute-start | bytes 301064 | tf_op jit(solution)/shard_map/ppermute | solution.py:701
  64.7 18.3 %collective-permute-start.12 = (bf16[112,448]{1,0:T(8,128)(2,1)}, bf16[112,448]{1,0:T(8,128)(2,1)S(1)}, u32[]{:S(2)}, u32[]{:S(2)}) collective-permute-start(bf16[112,448]{1,0:T(8,128)(2,1)} %get-tuple-element.46), channel_id=1, source_target_pairs={{0,12},{4,8},{8,4},{12,0},{1,13},{5,9},{9,5},{13,1},{2,14},{6,10},... | collective-permute-start | bytes 301064 | tf_op jit(solution)/shard_map/ppermute | solution.py:701
  85.6 12.1 %collective-permute-start.15 = (bf16[4,112,448]{2,1,0:T(8,128)(2,1)}, bf16[4,112,448]{2,1,0:T(8,128)(2,1)}, u32[]{:S(2)}, u32[]{:S(2)}) collective-permute-start(bf16[4,112,448]{2,1,0:T(8,128)(2,1)} %stack.26.refs_0_), channel_id=1, source_target_pairs={{0,2},{2,0},{1,3},{3,1},{4,6},{6,4},{5,7},{7,5},{8,10},{10,8},{9,1... | collective-permute-start | bytes 1204232 | tf_op jit(solution)/shard_map/ppermute | solution.py:705
  99.8 8.8 %collective-permute-start.18 = (bf16[8,112,448]{2,1,0:T(8,128)(2,1)}, bf16[8,112,448]{2,1,0:T(8,128)(2,1)S(1)}, u32[]{:S(2)}, u32[]{:S(2)}) collective-permute-start(bf16[8,112,448]{2,1,0:T(8,128)(2,1)} %stack.27.mine_ref), channel_id=1, source_target_pairs={{0,1},{1,0},{2,3},{3,2},{4,5},{5,4},{6,7},{7,6},{8,9},{9,8},{10,11... | collective-permute-start | bytes 2408456 | tf_op jit(solution)/shard_map/ppermute | solution.py:708
  103.2 16.8 %collective-permute-start.19 = (bf16[2,2,256,256]{3,2,1,0:T(8,128)(2,1)}, bf16[2,2,256,256]{3,2,1,0:T(8,128)(2,1)S(1)}, u32[]{:S(2)}, u32[]{:S(2)}) collective-permute-start(bf16[2,2,256,256]{3,2,1,0:T(8,128)(2,1)} %collective-permute-done.13.refs_7_), channel_id=1, source_target_pairs={{0,4},{4,8},{8,12},{1,5},{5,9},{9,13},{2,6},{6,10},{10,14},{3,7},{... | collective-permute-start | bytes 1572872 | tf_op jit(solution)/shard_map/ppermute | solution.py:688
  107.1 16.2 %collective-permute-start.20 = (bf16[2,2,256,256]{3,2,1,0:T(8,128)(2,1)}, bf16[2,2,256,256]{3,2,1,0:T(8,128)(2,1)S(1)}, u32[]{:S(2)}, u32[]{:S(2)}) collective-permute-start(bf16[2,2,256,256]{3,2,1,0:T(8,128)(2,1)} %collective-permute-done.14.refs_9_), channel_id=1, source_target_pairs={{4,0},{8,4},{12,8},{5,1},{9,5},{13,9},{6,2},{10,6},{14,10},{7,3},{... | collective-permute-start | bytes 1572872 | tf_op jit(solution)/shard_map/ppermute | solution.py:689
  127.4 1.9 %collective-permute-start.21 = (bf16[192,384]{1,0:T(8,128)(2,1)S(1)}, bf16[192,384]{1,0:T(8,128)(2,1)S(1)}, u32[]{:S(2)}, u32[]{:S(2)}) collective-permute-start(bf16[192,384]{1,0:T(8,128)(2,1)S(1)} %get-tuple-element.58), channel_id=1, source_target_pairs={{0,1},{1,0},{2,3},{3,2},{4,5},{5,4},{6,7},{7,6},{8,9},{9,8},{10,11... | collective-permute-start | bytes 442376 | tf_op jit(solution)/shard_map/ppermute | solution.py:740
  127.5 6.7 %collective-permute-start.22 = (bf16[192,384]{1,0:T(8,128)(2,1)S(1)}, bf16[192,384]{1,0:T(8,128)(2,1)S(1)}, u32[]{:S(2)}, u32[]{:S(2)}) collective-permute-start(bf16[192,384]{1,0:T(8,128)(2,1)S(1)} %get-tuple-element.59), channel_id=1, source_target_pairs={{0,2},{1,3},{2,0},{3,1},{4,6},{5,7},{6,4},{7,5},{8,10},{9,11},{10,... | collective-permute-start | bytes 442376 | tf_op jit(solution)/shard_map/ppermute | solution.py:740
  129.0 7.4 %collective-permute-start.23 = (bf16[192,384]{1,0:T(8,128)(2,1)S(1)}, bf16[192,384]{1,0:T(8,128)(2,1)S(1)}, u32[]{:S(2)}, u32[]{:S(2)}) collective-permute-start(bf16[192,384]{1,0:T(8,128)(2,1)S(1)} %get-tuple-element.60), channel_id=1, source_target_pairs={{0,3},{1,2},{2,1},{3,0},{4,7},{5,6},{6,5},{7,4},{8,11},{9,10},{10,... | collective-permute-start | bytes 442376 | tf_op jit(solution)/shard_map/ppermute | solution.py:740
  (14 other events, 135.5 us)

commit v6 on v5

--- a/solution.py
+++ b/solution.py
@@ -478,15 +478,11 @@
     )(index, mine, core, gain.reshape(1, model), weight, jnp.asarray(cosine), jnp.asarray(sine))
 
 
-def session_attention(query_ref, key_ref, value_ref, kv, session, length):
+def session_attention(query, key, value, tokens, length):
     scale = HD ** (-0.5) * math.log2(math.e)
-    rows = pl.ds(pl.multiple_of(session * SLOTS, SLOTS), SLOTS)
-    query = jnp.concatenate(
-        [query_ref[rows, h * HD : (h + 1) * HD] for h in range(PER_GROUP)], axis=0
-    )
-    tokens = kv.reshape(PROMPT, 2 * HD)
+    query = jnp.concatenate([query[:, h * HD : (h + 1) * HD] for h in range(PER_GROUP)], axis=0)
     ahead = lax.dot_general(query, tokens[:, :HD], NT, preferred_element_type=jnp.float32)
-    own = lax.dot_general(query, key_ref[rows, :], NT, preferred_element_type=jnp.float32)
+    own = lax.dot_general(query, key, NT, preferred_element_type=jnp.float32)
     row = lax.broadcasted_iota(jnp.int32, (SLOTS, SLOTS), 0)
     column = lax.broadcasted_iota(jnp.int32, (SLOTS, SLOTS), 1)
     allowed = (column <= row) & (column < length)
@@ -499,101 +495,72 @@
     total = jnp.sum(powers, axis=-1, keepdims=True) + jnp.sum(own_powers, axis=-1, keepdims=True)
     mixed = jnp.dot(
         powers.astype(jnp.bfloat16), tokens[:, HD:], preferred_element_type=jnp.float32
-    ) + jnp.dot(own_powers.astype(jnp.bfloat16), value_ref[rows, :], preferred_element_type=jnp.float32)
+    ) + jnp.dot(own_powers.astype(jnp.bfloat16), value, preferred_element_type=jnp.float32)
     return (mixed / total).astype(jnp.bfloat16)
 
 
-def hops_kernel(index_ref, hop_ref, held_ref, length_ref, query_ref, key_ref, value_ref, *refs,
-                hops, carried):
-    if carried:
-        before_ref, *refs = refs
-    count = KVH if carried else 1
-    prompt_refs, out_refs = refs[: 2 * len(hops)], refs[2 * len(hops) : 2 * len(hops) + count]
-    kv, sem = refs[-2:]
-    sessions = hop_ref.shape[0]
-    per_device = sessions // KVH
-
-    def copies(session, which):
-        return [
-            pltpu.make_async_copy(
-                prompt_refs[2 * which + chunk].at[:, held_ref[session]],
-                kv.at[session, chunk],
-                sem.at[session, chunk],
-            )
-            for chunk in range(2)
-        ]
-
-    def fetch(session, _):
+def attend_kernel(index_ref, hop_ref, held_ref, length_ref, query_ref, key_ref, value_ref,
+                  gathered_ref, *refs, targets, hops):
+    chain_refs, refs = refs[: len(hops)], refs[len(hops) :]
+    out_refs, (kv, sem) = refs[: len(targets)], refs[len(targets) :]
+    z, head = index_ref[0], index_ref[3]
+    per_device = out_refs[0].shape[0] // SLOTS
+    places = [(t, j) for t in range(len(targets)) for j in range(per_device)]
+
+    def session_of(i):
+        t, j = places[i]
+        return (head ^ targets[t]) * per_device + j
+
+    def from_gathered(i):
+        session = session_of(i)
+        plane = z + hop_ref[session]
+        return pltpu.make_async_copy(
+            gathered_ref.at[pl.ds(2 * plane, 2), held_ref[session]], kv.at[i, 0], sem.at[i, 0]
+        )
+
+    def from_chain(i, which):
+        return pltpu.make_async_copy(
+            chain_refs[which].at[:, held_ref[session_of(i)]], kv.at[i, 1], sem.at[i, 1]
+        )
+
+    for i in range(len(places)):
+        from_gathered(i).start()
         for which, hop in enumerate(hops):
-            @pl.when(hop_ref[session] == hop)
+            @pl.when(hop_ref[session_of(i)] == hop)
             def _():
-                for copy in copies(session, which):
-                    copy.start()
-        return 0
-
-    def store(session, block):
-        def into(out_ref, first):
-            rows = pl.ds(pl.multiple_of(first * SLOTS, SLOTS), SLOTS)
-            if block.shape[0] == SLOTS:
-                out_ref[rows] = block
-            else:
-                for h in range(PER_GROUP):
-                    out_ref[rows, h * HD : (h + 1) * HD] = block[h * SLOTS : (h + 1) * SLOTS]
-
-        if not carried:
-            into(out_refs[0], session)
-            return
-        for by, out_ref in enumerate(out_refs):
-            @pl.when((lax.div(session, per_device) ^ index_ref[3]) == by)
-            def _():
-                into(out_ref, lax.rem(session, per_device))
-
-    lax.fori_loop(0, sessions, fetch, 0)
-
-    def work(session, _):
-        ours = hop_ref[session] == hops[0]
-        for hop in hops[1:]:
-            ours = ours | (hop_ref[session] == hop)
-        if carried:
-            @pl.when(jnp.logical_not(ours))
-            def _():
-                rows = pl.ds(pl.multiple_of(session * SLOTS, SLOTS), SLOTS)
-                store(session, before_ref[rows])
-
-        @pl.when(ours)
-        def _():
-            for copy in copies(session, 0):
-                copy.wait()
-            store(
-                session,
-                session_attention(
-                    query_ref, key_ref, value_ref, kv[session], session, length_ref[0, session]
-                ),
-            )
-
-        return 0
-
-    lax.fori_loop(0, sessions, work, 0)
-
-
-def attend_hops(index, hop, held, lengths, query, key, value, prompts, hops, before):
-    sessions = hop.shape[0]
-    carried = before is not None
-    pieces = [piece for h in hops for piece in prompts[h]]
-    work = sessions * len(hops) // 7 + 1
+                from_chain(i, which).start()
+    for i in range(len(places)):
+        from_gathered(i).wait()
+        from_chain(i, 0).wait()
+    for i, (t, j) in enumerate(places):
+        session = session_of(i)
+        rows = pl.ds(pl.multiple_of(session * SLOTS, SLOTS), SLOTS)
+        mixed = session_attention(
+            query_ref[rows],
+            key_ref[rows],
+            value_ref[rows],
+            kv[i].reshape(PROMPT, 2 * HD),
+            length_ref[0, session],
+        )
+        for h in range(PER_GROUP):
+            out_refs[t][j * SLOTS : (j + 1) * SLOTS, h * HD : (h + 1) * HD] = mixed[
+                h * SLOTS : (h + 1) * SLOTS
+            ]
+
+
+def attend_for(index, hop, held, lengths, query, key, value, gathered, chain, targets):
+    per_device = hop.shape[0] // KVH
+    hops = tuple(sorted(chain))
+    work = per_device * len(targets)
     width = PER_GROUP * HD
-    if carried:
-        out_shape = [jax.ShapeDtypeStruct((sessions // KVH * SLOTS, width), jnp.bfloat16)] * KVH
-    else:
-        out_shape = jax.ShapeDtypeStruct((sessions * SLOTS, width), jnp.bfloat16)
     return pl.pallas_call(
-        functools.partial(hops_kernel, hops=hops, carried=carried),
-        in_specs=[SMEM] * 4 + [VMEM] * (3 + carried) + [ANY] * len(pieces),
-        out_specs=[VMEM] * KVH if carried else VMEM,
-        out_shape=out_shape,
+        functools.partial(attend_kernel, targets=targets, hops=hops),
+        in_specs=[SMEM] * 4 + [VMEM] * 3 + [ANY] * (1 + len(hops)),
+        out_specs=[VMEM] * len(targets),
+        out_shape=[jax.ShapeDtypeStruct((per_device * SLOTS, width), jnp.bfloat16)] * len(targets),
         scratch_shapes=[
-            pltpu.VMEM((sessions, 2, 2, PROMPT // 4, 2 * HD), jnp.bfloat16),
-            pltpu.SemaphoreType.DMA((sessions, 2)),
+            pltpu.VMEM((work, 2, 2, PROMPT // 4, 2 * HD), jnp.bfloat16),
+            pltpu.SemaphoreType.DMA((work, 2)),
         ],
         compiler_params=pltpu.CompilerParams(vmem_limit_bytes=40 << 20),
         cost_estimate=pl.CostEstimate(
@@ -602,7 +569,7 @@
             transcendentals=work * PER_GROUP * SLOTS * (PROMPT + SLOTS),
         ),
         name="attend",
-    )(index, hop, held, lengths, query, key, value, *([before] if carried else []), *pieces)
+    )(index, hop, held, lengths, query, key, value, gathered, *[chain[h] for h in hops])
 
 
 def output_kernel(index_ref, length_ref, states_ref, weight_ref, *refs):
@@ -680,32 +647,30 @@
     from_far = lax.ppermute(to_far, pair, swapped(4, 3))
     first = stack(own[None], from_core[None])
     second = stack(from_x[None], from_far[None])
-    right = [first, second]
-    left = [first, second]
-    prompts = {0: (first, second)}
+    gathered = lax.all_gather(first, "sess", axis=0, tiled=True)
+    right = left = second
+    chain = {0: second}
     for hop in range(1, planes):
-        for chunk in range(2):
-            right[chunk] = lax.ppermute(right[chunk], "sess", shifted(planes, 1))
-            left[chunk] = lax.ppermute(left[chunk], "sess", shifted(planes, -1))
-        prompts[-hop], prompts[hop] = tuple(right), tuple(left)
-
-    thinker_rows, _ = lax.optimization_barrier((thinker_rows, (prompts[-1][0], prompts[1][0])))
+        right = lax.ppermute(right, "sess", shifted(planes, 1))
+        left = lax.ppermute(left, "sess", shifted(planes, -1))
+        chain[-hop], chain[hop] = right, left
+
+    thinker_rows, _ = lax.optimization_barrier((thinker_rows, first))
     partial_sum = jnp.dot(thinker_rows, proj_weight, preferred_element_type=jnp.float32)
     kept = lax.dynamic_slice_in_dim(partial_sum, x * width, width, 1)
     sent = lax.dynamic_slice_in_dim(partial_sum, (1 - x) * width, width, 1)
     came = lax.ppermute(sent.astype(jnp.bfloat16), "inner", swapped(2, 1))
-    came, _ = lax.optimization_barrier((came, (prompts[-1][1], prompts[1][1])))
+    came, _ = lax.optimization_barrier((came, second))
     routed = route(z.reshape(1), kept, came, row_session, planes, per_plane, slot_cap)
-    routed, _ = lax.optimization_barrier((tuple(routed), (prompts[-2][0], prompts[2][0])))
     arrived = [routed[0]] + [
         lax.ppermute(routed[by], "sess", swapped(planes, by)) for by in range(1, planes)
     ]
-    arrived, _ = lax.optimization_barrier((arrived, (prompts[-2][1], prompts[2][1])))
     arrived = stack(*[a[None] for a in arrived])
     other = lax.ppermute(arrived, "inner", swapped(2, 1))
-    other, _ = lax.optimization_barrier((other, (prompts[-3][0], prompts[3][0])))
+    other, _ = lax.optimization_barrier((other, (chain[-1], chain[1])))
     mine = stack(arrived, other)
     core = lax.ppermute(mine, "rep", swapped(2, 1))
+    core, _ = lax.optimization_barrier((core, (chain[-2], chain[2])))
 
     group_width = PER_GROUP * HD
     weight = jnp.concatenate(
@@ -729,13 +694,11 @@
     )
     hop = wanted_slot // held - z
     which = wanted_slot % held
-    near = attend_hops(
-        index, hop, which, lengths, query, key, value, prompts, (0, -1, 1, -2, 2), None
-    )
-    attended = attend_hops(
-        index, hop, which, lengths, query, key, value, prompts, (-3, 3), near
-    )
-
+    run = functools.partial(attend_for, index, hop, which, lengths)
+    attended = {}
+    attended[2], attended[3] = run(query, key, value, gathered, chain, (2, 3))
+    query, _ = lax.optimization_barrier((query, attended[2]))
+    attended[0], attended[1] = run(query, key, value, gathered, chain, (0, 1))
     pieces = [attended[0]] + [
         lax.ppermute(attended[by], pair, swapped(4, by)) for by in range(1, plane)
     ]

time: 139 us -> 156 us (1.12)
  starting transfers between devices: 47.8 us -> 32.9 us
  between operations: 0.32 us -> 13.6 us
  local copies, waits for them, and re-layouts: 7.79 us -> 20.1 us
  waiting for transfers between devices: 49.1 us -> 58 us
  Pallas kernels: 30.3 us -> 27.3 us
    ppermute x3, waiting for transfers between devices: 18.3 us -> 34.2 us  [line_body(): lax.ppermute(routed[by], 'sess', swapped(planes, by))]
    ppermute x12 -> x6, starting transfers between devices: 34.5 us -> 18.8 us  [the longest x3 14.9 us: line_body(): right = lax.ppermute(right, 'sess', shifted(planes, 1))]
    unnamed x29 -> x49, local copies, waits for them, and re-layouts: 2.43 us -> 14.1 us
    ppermute x1, waiting for transfers between devices: 9.87 us -> 2.97 us  [line_body(): other = lax.ppermute(arrived, 'inner', swapped(2, 1))]
    pallas_call x2, Pallas kernels: 11.2 us -> 8.16 us  [attend_for(): pl.pallas_call(functools.partial(attend_kernel, targets=targets, hops=hop...]
    ppermute x12 -> x6, waiting for transfers between devices: 8.95 us -> 7.04 us  [the longest x3 3.83 us: line_body(): right = lax.ppermute(right, 'sess', shifted(planes, 1))]
    ppermute x1, waiting for transfers between devices: 0.01 us -> 1.66 us  [line_body(): from_x = lax.ppermute(to_x, pair, swapped(4, 2))]
  transfers between devices with their start and end apart: 24 -> 19, of which waited for: 9 -> 10; matrix products, arithmetic and copies ran while one was open for 7% -> 7% of each run, Pallas kernels for 14% -> 11%
where the time goes in v6:
time: 156 us; the launch traced here: 155 us
  waiting for transfers between devices  58 us (37%)
  starting transfers between devices  32.9 us (21%)
  Pallas kernels  27.3 us (18%)
  local copies, waits for them, and re-layouts  20.1 us (13%)
  between operations  13.6 us (9%)
  matrix products  2.31 us (1%)
    ppermute x3, waiting for transfers between devices, line_body(): lax.ppermute(routed[by], 'sess', swapped(planes, by))  34.2 us
    ppermute x3, starting transfers between devices, line_body(): right = lax.ppermute(right, 'sess', shifted(planes, 1))  14.9 us
    unnamed x49, local copies, waits for them, and re-layouts  14.1 us
    pallas_call x2, Pallas kernels, attend_for(): pl.pallas_call(functools.partial(attend_kernel, targets=targets, hops=hop...  8.16 us
    pallas_call x4, Pallas kernels, stack(): pl.pallas_call(stack_kernel, in_specs=[VMEM] * len(arrays), out_specs=VME...  7.76 us
    ppermute x3, waiting for transfers between devices, line_body(): lax.ppermute(attended[by], pair, swapped(4, by))  5.56 us
    ppermute x3, starting transfers between devices, line_body(): lax.ppermute(routed[by], 'sess', swapped(planes, by))  5.2 us
    ppermute x1, waiting for transfers between devices, line_body(): from_far = lax.ppermute(to_far, pair, swapped(4, 3))  5.19 us
  transfers between devices with their start and end apart: 19, of which 10 were waited for; matrix products, arithmetic and copies ran while one was open for 7% of the time, Pallas kernels for 11%

profile of v6, /device:TPU:0, one launch (start us, length us, event | category | flops | bytes accessed | tf_op | source)
XLA Modules:
  0.0 155.3 jit_solution(14251010052349493602)
XLA Ops:
  6.5 2.6 %split_heads.1 = (bf16[2,256,256]{2,1,0:T(8,128)(2,1)}, bf16[2,256,256]{2,1,0:T(8,128)(2,1)}, bf16[2,256,256]{2,1,0:T(8,128)(2,1)}, bf16[2,256,256]{2,1,0:T(8,128)(2,1)}) custom-call(s32[1]{0:T(128)} %bitcast.3.head_ref, bf16[2,256,1024]{2,1,0:T(8,128)(2,1)} %cache_ref.1), custom_call_target="tpu_custom_call" | custom-call | bytes 2097152 | tf_op jit(solution)/shard_map/split_heads/pallas_call | solution.py:308
  13.5 2.9 %collective-permute-start.2 = (bf16[2,256,256]{2,1,0:T(8,128)(2,1)}, bf16[2,256,256]{2,1,0:T(8,128)(2,1)}, u32[]{:S(2)}, u32[]{:S(2)}) collective-permute-start(bf16[2,256,256]{2,1,0:T(8,128)(2,1)} %get-tuple-element.30), channel_id=1, source_target_pairs={{0,2},{1,3},{2,0},{3,1},{4,6},{5,7},{6,4},{7,5},{8,10},{9,11},{10,... | collective-permute-start | bytes 786440 | tf_op jit(solution)/shard_map/ppermute | solution.py:646
  16.5 2.3 %fusion.1 = f32[256,896]{1,0:T(8,128)S(1)} fusion(bf16[256,1792]{1,0:T(8,128)(2,1)} %param.13, bf16[1792,896]{1,0:T(8,128)(2,1)S(1)} %copy-done), kind=kOutput, calls=%fused_computation.15 | convolution fusion | flops 822083584 | bytes 5046272 | tf_op jit(solution)/shard_map/dot_general | solution.py:659
  23.9 5.2 %collective-permute-done.3 = bf16[2,256,256]{2,1,0:T(8,128)(2,1)} collective-permute-done((bf16[2,256,256]{2,1,0:T(8,128)(2,1)}, bf16[2,256,256]{2,1,0:T(8,128)(2,1)}, u32[]{:S(2)}, u32[]{:S(2)}) %collective-permute-start.3) | collective-permute-done | bytes 262176 | tf_op jit(solution)/shard_map/ppermute | solution.py:647
  29.1 1.9 %stack.25.refs_3_ = bf16[2,2,256,256]{3,2,1,0:T(8,128)(2,1)} custom-call(bf16[1,2,256,256]{3,2,1,0:T(8,128)(2,1)} %bitcast.6.refs_0_, bf16[1,2,256,256]{3,2,1,0:T(8,128)(2,1)} %bitcast.7.refs_1_), custom_call_target="tpu_custom_call" | custom-call | bytes 1048576 | tf_op jit(solution)/shard_map/stack/pallas_call | solution.py:330
  31.0 4.3 %collective-permute-start.8 = (bf16[2,2,256,256]{3,2,1,0:T(8,128)(2,1)}, bf16[2,2,256,256]{3,2,1,0:T(8,128)(2,1)}, u32[]{:S(2)}, u32[]{:S(2)}) collective-permute-start(bf16[2,2,256,256]{3,2,1,0:T(8,128)(2,1)} %stack.25.refs_3_), channel_id=1, source_target_pairs={{0,4},{4,8},{8,12},{1,5},{5,9},{9,13},{2,6},{6,10},{10,14},{3,7},{... | collective-permute-start | bytes 1572872 | tf_op jit(solution)/shard_map/ppermute | solution.py:654
  36.6 2.1 %constant_dynamic-slice_fusion.3.kept_ref = f32[256,448]{1,0:T(8,128)} fusion(f32[256,896]{1,0:T(8,128)} %copy-done.18, s32[]{:T(128)S(6)} %select_n.32), kind=kLoop, calls=%fused_computation.9 | loop fusion | bytes 917508 | tf_op jit(solution)/shard_map/dynamic_slice | solution.py:660
  38.7 2.3 %route.1 = (bf16[112,448]{1,0:T(8,128)(2,1)}, bf16[112,448]{1,0:T(8,128)(2,1)}, bf16[112,448]{1,0:T(8,128)(2,1)}, bf16[112,448]{1,0:T(8,128)(2,1)}) custom-call(s32[1]{0:T(128)} %bitcast.z_ref, f32[256,448]{1,0:T(8,128)} %constant_dynamic-slice_fusion.3.kept_ref, bf16[256,448]{1,0:T(8,128)(2,1)} %collective-permute-done.1.came_ref, ...), custom_call_target="tpu_custom_call" | custom-call | flops 102760448 | bytes 917504 | tf_op jit(solution)/shard_map/route/pallas_call | solution.py:373
  41.0 2.6 %collective-permute-start.4 = (bf16[112,448]{1,0:T(8,128)(2,1)}, bf16[112,448]{1,0:T(8,128)(2,1)S(1)}, u32[]{:S(2)}, u32[]{:S(2)}) collective-permute-start(bf16[112,448]{1,0:T(8,128)(2,1)} %get-tuple-element.34), channel_id=1, source_target_pairs={{0,4},{4,0},{8,12},{12,8},{1,5},{5,1},{9,13},{13,9},{2,6},{6,2},{1... | collective-permute-start | bytes 301064 | tf_op jit(solution)/shard_map/ppermute | solution.py:666
  43.6 2.6 %collective-permute-start.5 = (bf16[112,448]{1,0:T(8,128)(2,1)}, bf16[112,448]{1,0:T(8,128)(2,1)S(1)}, u32[]{:S(2)}, u32[]{:S(2)}) collective-permute-start(bf16[112,448]{1,0:T(8,128)(2,1)} %get-tuple-element.35), channel_id=1, source_target_pairs={{0,8},{4,12},{8,0},{12,4},{1,9},{5,13},{9,1},{13,5},{2,10},{6,14},... | collective-permute-start | bytes 301064 | tf_op jit(solution)/shard_map/ppermute | solution.py:666
  46.2 30.7 %collective-permute-done.4 = bf16[112,448]{1,0:T(8,128)(2,1)S(1)} collective-permute-done((bf16[112,448]{1,0:T(8,128)(2,1)}, bf16[112,448]{1,0:T(8,128)(2,1)S(1)}, u32[]{:S(2)}, u32[]{:S(2)}) %collective-permute-start.4) | collective-permute-done | bytes 100384 | tf_op jit(solution)/shard_map/ppermute | solution.py:666
  76.9 3.5 %collective-permute-done.5 = bf16[112,448]{1,0:T(8,128)(2,1)S(1)} collective-permute-done((bf16[112,448]{1,0:T(8,128)(2,1)}, bf16[112,448]{1,0:T(8,128)(2,1)S(1)}, u32[]{:S(2)}, u32[]{:S(2)}) %collective-permute-start.5) | collective-permute-done | bytes 100384 | tf_op jit(solution)/shard_map/ppermute | solution.py:666
  84.4 5.7 %collective-permute-start.11 = (bf16[2,2,256,256]{3,2,1,0:T(8,128)(2,1)}, bf16[2,2,256,256]{3,2,1,0:T(8,128)(2,1)}, u32[]{:S(2)}, u32[]{:S(2)}) collective-permute-start(bf16[2,2,256,256]{3,2,1,0:T(8,128)(2,1)} %collective-permute-done.8.refs_2_), channel_id=1, source_target_pairs={{0,4},{4,8},{8,12},{1,5},{5,9},{9,13},{2,6},{6,10},{10,14},{3,7},{... | collective-permute-start | bytes 1572872 | tf_op jit(solution)/shard_map/ppermute | solution.py:654
  92.8 3.0 %collective-permute-done.7.refs_1_ = bf16[4,112,448]{2,1,0:T(8,128)(2,1)} collective-permute-done((bf16[4,112,448]{2,1,0:T(8,128)(2,1)}, bf16[4,112,448]{2,1,0:T(8,128)(2,1)}, u32[]{:S(2)}, u32[]{:S(2)}) %collective-permute-start.7) | collective-permute-done | bytes 401440 | tf_op jit(solution)/shard_map/ppermute | solution.py:669
  95.7 2.1 %stack.27.mine_ref = bf16[8,112,448]{2,1,0:T(8,128)(2,1)} custom-call(bf16[4,112,448]{2,1,0:T(8,128)(2,1)} %stack.26.refs_0_, bf16[4,112,448]{2,1,0:T(8,128)(2,1)} %collective-permute-done.7.refs_1_), custom_call_target="tpu_custom_call" | custom-call | bytes 1605632 | tf_op jit(solution)/shard_map/stack/pallas_call | solution.py:330
  101.2 4.9 %collective-permute-start.13 = (bf16[2,2,256,256]{3,2,1,0:T(8,128)(2,1)}, bf16[2,2,256,256]{3,2,1,0:T(8,128)(2,1)S(1)}, u32[]{:S(2)}, u32[]{:S(2)}) collective-permute-start(bf16[2,2,256,256]{3,2,1,0:T(8,128)(2,1)} %collective-permute-done.11.refs_1_), channel_id=1, source_target_pairs={{0,4},{4,8},{8,12},{1,5},{5,9},{9,13},{2,6},{6,10},{10,14},{3,7},{... | collective-permute-start | bytes 1572872 | tf_op jit(solution)/shard_map/ppermute | solution.py:654
  107.7 4.2 %place_rows.1 = (bf16[768,896]{1,0:T(8,128)(2,1)S(1)}, bf16[768,384]{1,0:T(8,128)(2,1)S(1)}, bf16[768,128]{1,0:T(8,128)(2,1)S(1)}, bf16[768,128]{1,0:T(8,128)(2,1)S(1)}, s32[1,128]{1,0:T(1,128)S(1)}) custom-call(s32[4]{0:T(128)S(1)} %pad_add_fusion.index_ref, bf16[8,112,448]{2,1,0:T(8,128)(2,1)S(1)} %copy-done.12, ...), custom_call_target="tpu_custom_call" | custom-call | flops 1761607680 | bytes 6291456 | tf_op jit(solution)/shard_map/place_rows/pallas_call | solution.py:465
  114.5 3.8 %collective-permute-done.13.refs_0_ = bf16[2,2,256,256]{3,2,1,0:T(8,128)(2,1)S(1)} collective-permute-done((bf16[2,2,256,256]{3,2,1,0:T(8,128)(2,1)}, bf16[2,2,256,256]{3,2,1,0:T(8,128)(2,1)S(1)}, u32[]{:S(2)}, u32[]{:S(2)}) %collective-permute-start.13) | collective-permute-done | bytes 524320 | tf_op jit(solution)/shard_map/ppermute | solution.py:654
  119.1 3.2 %collective-permute-done.14.refs_6_ = bf16[2,2,256,256]{3,2,1,0:T(8,128)(2,1)S(1)} collective-permute-done((bf16[2,2,256,256]{3,2,1,0:T(8,128)(2,1)}, bf16[2,2,256,256]{3,2,1,0:T(8,128)(2,1)S(1)}, u32[]{:S(2)}, u32[]{:S(2)}) %collective-permute-start.14) | collective-permute-done | bytes 524320 | tf_op jit(solution)/shard_map/ppermute | solution.py:655
  129.9 3.6 %attend.2 = (bf16[192,384]{1,0:T(8,128)(2,1)S(1)}, bf16[192,384]{1,0:T(8,128)(2,1)S(1)}) custom-call(s32[4]{0:T(128)S(1)} %pad_add_fusion.index_ref, s32[8]{0:T(128)S(1)} %get-tuple-element.50.hop_ref, s32[8]{0:T(128)S(1)} %get-tuple-element.49.held_ref, s32[1,128]{1,0:T(1,128)S(1)} %get-tuple-element.39.length_ref, bf16[768,384]{1,0:T(8,128)(2,1)S(1)} %copy-done.5, ...), custom_call_target="tpu_custom_call" | custom-call | flops 660602880 | bytes 2097152 | tf_op jit(solution)/shard_map/attend/pallas_call | solution.py:556
  133.6 2.4 %collective-permute-start.16 = (bf16[192,384]{1,0:T(8,128)(2,1)S(1)}, bf16[192,384]{1,0:T(8,128)(2,1)S(1)}, u32[]{:S(2)}, u32[]{:S(2)}) collective-permute-start(bf16[192,384]{1,0:T(8,128)(2,1)S(1)} %get-tuple-element.44), channel_id=1, source_target_pairs={{0,2},{1,3},{2,0},{3,1},{4,6},{5,7},{6,4},{7,5},{8,10},{9,11},{10,... | collective-permute-start | bytes 442376 | tf_op jit(solution)/shard_map/ppermute | solution.py:703
  136.0 4.5 %attend.3 = (bf16[192,384]{1,0:T(8,128)(2,1)S(1)}, bf16[192,384]{1,0:T(8,128)(2,1)S(1)}) custom-call(s32[4]{0:T(128)S(1)} %pad_add_fusion.index_ref, s32[8]{0:T(128)S(1)} %get-tuple-element.50.hop_ref, s32[8]{0:T(128)S(1)} %get-tuple-element.49.held_ref, s32[1,128]{1,0:T(1,128)S(1)} %get-tuple-element.39.length_ref, bf16[768,384]{1,0:T(8,128)(2,1)S(1)} %copy-done.5, ...), custom_call_target="tpu_custom_call" | custom-call | flops 660602880 | bytes 2097152 | tf_op jit(solution)/shard_map/attend/pallas_call | solution.py:556
  141.9 4.3 %collective-permute-done.17.refs_3_ = bf16[192,384]{1,0:T(8,128)(2,1)S(1)} collective-permute-done((bf16[192,384]{1,0:T(8,128)(2,1)S(1)}, bf16[192,384]{1,0:T(8,128)(2,1)S(1)}, u32[]{:S(2)}, u32[]{:S(2)}) %collective-permute-start.17) | collective-permute-done | bytes 147488 | tf_op jit(solution)/shard_map/ppermute | solution.py:703
  146.2 2.2 %output.1 = bf16[2,96,896]{2,1,0:T(8,128)(2,1)} custom-call(s32[4]{0:T(128)S(1)} %pad_add_fusion.index_ref, s32[1,128]{1,0:T(1,128)S(1)} %get-tuple-element.39.length_ref, bf16[768,896]{1,0:T(8,128)(2,1)S(1)} %copy-done.11, bf16[1536,896]{1,0:T(8,128)(2,1)S(1)} %copy-done.3, bf16[192,384]{1,0:T(8,128)(2,1)S(1)} %get-tuple-element.46.refs_0_, ...), custom_call_target="tpu_custom_call" | custom-call | flops 528482304 | bytes 2752512 | tf_op jit(solution)/shard_map/output/pallas_call | solution.py:596
  (85 shorter events, 34.6 us)
Async XLA Ops:
  6.5 9.9 %copy-start = (bf16[1792,896]{1,0:T(8,128)(2,1)S(1)}, bf16[1792,896]{1,0:T(8,128)(2,1)}, u32[]{:S(2)}) copy-start(bf16[1792,896]{1,0:T(8,128)(2,1)} %param.18) | copy-start | bytes 9633796
  6.5 116.6 %all-gather.2.cloned.1.call-start = ((), (), s32[]{:S(2)}) async-start(), calls=%async_computation | async-start | bytes 2621440 | tf_op jit(solution)/shard_map/all_gather | solution.py:650
  9.1 1.8 %collective-permute-start = (bf16[2,256,256]{2,1,0:T(8,128)(2,1)}, bf16[2,256,256]{2,1,0:T(8,128)(2,1)S(1)}, u32[]{:S(2)}, u32[]{:S(2)}) collective-permute-start(bf16[2,256,256]{2,1,0:T(8,128)(2,1)} %get-tuple-element.28), channel_id=1, source_target_pairs={{0,1},{1,0},{2,3},{3,2},{4,5},{5,4},{6,7},{7,6},{8,9},{9,8},{10,11... | collective-permute-start | bytes 786440 | tf_op jit(solution)/shard_map/ppermute | solution.py:645
  13.5 10.3 %collective-permute-start.2 = (bf16[2,256,256]{2,1,0:T(8,128)(2,1)}, bf16[2,256,256]{2,1,0:T(8,128)(2,1)}, u32[]{:S(2)}, u32[]{:S(2)}) collective-permute-start(bf16[2,256,256]{2,1,0:T(8,128)(2,1)} %get-tuple-element.30), channel_id=1, source_target_pairs={{0,2},{1,3},{2,0},{3,1},{4,6},{5,7},{6,4},{7,5},{8,10},{9,11},{10,... | collective-permute-start | bytes 786440 | tf_op jit(solution)/shard_map/ppermute | solution.py:646
  16.5 12.6 %collective-permute-start.3 = (bf16[2,256,256]{2,1,0:T(8,128)(2,1)}, bf16[2,256,256]{2,1,0:T(8,128)(2,1)}, u32[]{:S(2)}, u32[]{:S(2)}) collective-permute-start(bf16[2,256,256]{2,1,0:T(8,128)(2,1)} %get-tuple-element.31), channel_id=1, source_target_pairs={{0,3},{1,2},{2,1},{3,0},{4,7},{5,6},{6,5},{7,4},{8,11},{9,10},{10,... | collective-permute-start | bytes 786440 | tf_op jit(solution)/shard_map/ppermute | solution.py:647
  19.9 18.8 %collective-permute-start.1 = (bf16[256,448]{1,0:T(8,128)(2,1)S(1)}, bf16[256,448]{1,0:T(8,128)(2,1)}, u32[]{:S(2)}, u32[]{:S(2)}) collective-permute-start(bf16[256,448]{1,0:T(8,128)(2,1)S(1)} %dynamic-slice_convert_fusion), channel_id=1, source_target_pairs={{0,2},{2,0},{1,3},{3,1},{4,6},{6,4},{5,7},{7,5},{8,10},{10,8},{9,1... | collective-permute-start | bytes 688136 | tf_op jit(solution)/shard_map/ppermute | solution.py:662
  31.0 53.4 %collective-permute-start.8 = (bf16[2,2,256,256]{3,2,1,0:T(8,128)(2,1)}, bf16[2,2,256,256]{3,2,1,0:T(8,128)(2,1)}, u32[]{:S(2)}, u32[]{:S(2)}) collective-permute-start(bf16[2,2,256,256]{3,2,1,0:T(8,128)(2,1)} %stack.25.refs_3_), channel_id=1, source_target_pairs={{0,4},{4,8},{8,12},{1,5},{5,9},{9,13},{2,6},{6,10},{10,14},{3,7},{... | collective-permute-start | bytes 1572872 | tf_op jit(solution)/shard_map/ppermute | solution.py:654
  35.3 54.8 %collective-permute-start.9 = (bf16[2,2,256,256]{3,2,1,0:T(8,128)(2,1)}, bf16[2,2,256,256]{3,2,1,0:T(8,128)(2,1)}, u32[]{:S(2)}, u32[]{:S(2)}) collective-permute-start(bf16[2,2,256,256]{3,2,1,0:T(8,128)(2,1)} %stack.25.refs_3_), channel_id=1, source_target_pairs={{4,0},{8,4},{12,8},{5,1},{9,5},{13,9},{6,2},{10,6},{14,10},{7,3},{... | collective-permute-start | bytes 1572872 | tf_op jit(solution)/shard_map/ppermute | solution.py:655
  41.0 35.9 %collective-permute-start.4 = (bf16[112,448]{1,0:T(8,128)(2,1)}, bf16[112,448]{1,0:T(8,128)(2,1)S(1)}, u32[]{:S(2)}, u32[]{:S(2)}) collective-permute-start(bf16[112,448]{1,0:T(8,128)(2,1)} %get-tuple-element.34), channel_id=1, source_target_pairs={{0,4},{4,0},{8,12},{12,8},{1,5},{5,1},{9,13},{13,9},{2,6},{6,2},{1... | collective-permute-start | bytes 301064 | tf_op jit(solution)/shard_map/ppermute | solution.py:666
  43.6 36.8 %collective-permute-start.5 = (bf16[112,448]{1,0:T(8,128)(2,1)}, bf16[112,448]{1,0:T(8,128)(2,1)S(1)}, u32[]{:S(2)}, u32[]{:S(2)}) collective-permute-start(bf16[112,448]{1,0:T(8,128)(2,1)} %get-tuple-element.35), channel_id=1, source_target_pairs={{0,8},{4,12},{8,0},{12,4},{1,9},{5,13},{9,1},{13,5},{2,10},{6,14},... | collective-permute-start | bytes 301064 | tf_op jit(solution)/shard_map/ppermute | solution.py:666
  46.2 34.2 %collective-permute-start.6 = (bf16[112,448]{1,0:T(8,128)(2,1)}, bf16[112,448]{1,0:T(8,128)(2,1)S(1)}, u32[]{:S(2)}, u32[]{:S(2)}) collective-permute-start(bf16[112,448]{1,0:T(8,128)(2,1)} %get-tuple-element.36), channel_id=1, source_target_pairs={{0,12},{4,8},{8,4},{12,0},{1,13},{5,9},{9,5},{13,1},{2,14},{6,10},... | collective-permute-start | bytes 301064 | tf_op jit(solution)/shard_map/ppermute | solution.py:666
  82.9 12.8 %collective-permute-start.7 = (bf16[4,112,448]{2,1,0:T(8,128)(2,1)}, bf16[4,112,448]{2,1,0:T(8,128)(2,1)}, u32[]{:S(2)}, u32[]{:S(2)}) collective-permute-start(bf16[4,112,448]{2,1,0:T(8,128)(2,1)} %stack.26.refs_0_), channel_id=1, source_target_pairs={{0,2},{2,0},{1,3},{3,1},{4,6},{6,4},{5,7},{7,5},{8,10},{10,8},{9,1... | collective-permute-start | bytes 1204232 | tf_op jit(solution)/shard_map/ppermute | solution.py:669
  84.4 16.8 %collective-permute-start.11 = (bf16[2,2,256,256]{3,2,1,0:T(8,128)(2,1)}, bf16[2,2,256,256]{3,2,1,0:T(8,128)(2,1)}, u32[]{:S(2)}, u32[]{:S(2)}) collective-permute-start(bf16[2,2,256,256]{3,2,1,0:T(8,128)(2,1)} %collective-permute-done.8.refs_2_), channel_id=1, source_target_pairs={{0,4},{4,8},{8,12},{1,5},{5,9},{9,13},{2,6},{6,10},{10,14},{3,7},{... | collective-permute-start | bytes 1572872 | tf_op jit(solution)/shard_map/ppermute | solution.py:654
  90.1 16.1 %collective-permute-start.12 = (bf16[2,2,256,256]{3,2,1,0:T(8,128)(2,1)}, bf16[2,2,256,256]{3,2,1,0:T(8,128)(2,1)}, u32[]{:S(2)}, u32[]{:S(2)}) collective-permute-start(bf16[2,2,256,256]{3,2,1,0:T(8,128)(2,1)} %collective-permute-done.9.refs_4_), channel_id=1, source_target_pairs={{4,0},{8,4},{12,8},{5,1},{9,5},{13,9},{6,2},{10,6},{14,10},{7,3},{... | collective-permute-start | bytes 1572872 | tf_op jit(solution)/shard_map/ppermute | solution.py:655
  97.9 9.7 %collective-permute-start.10 = (bf16[8,112,448]{2,1,0:T(8,128)(2,1)}, bf16[8,112,448]{2,1,0:T(8,128)(2,1)S(1)}, u32[]{:S(2)}, u32[]{:S(2)}) collective-permute-start(bf16[8,112,448]{2,1,0:T(8,128)(2,1)} %stack.27.mine_ref), channel_id=1, source_target_pairs={{0,1},{1,0},{2,3},{3,2},{4,5},{5,4},{6,7},{7,6},{8,9},{9,8},{10,11... | collective-permute-start | bytes 2408456 | tf_op jit(solution)/shard_map/ppermute | solution.py:672
  98.8 8.8 %copy-start.16 = (f32[384,128]{1,0:T(8,128)S(1)}, f32[384,128]{1,0:T(8,128)}, u32[]{:S(2)}) copy-start(f32[384,128]{1,0:T(8,128)} %constant.59.clone.cos_ref) | copy-start | bytes 589828
  98.8 8.8 %copy-start.17 = (f32[384,128]{1,0:T(8,128)S(1)}, f32[384,128]{1,0:T(8,128)}, u32[]{:S(2)}) copy-start(f32[384,128]{1,0:T(8,128)} %constant.60.clone.sin_ref) | copy-start | bytes 589828
  101.2 17.0 %collective-permute-start.13 = (bf16[2,2,256,256]{3,2,1,0:T(8,128)(2,1)}, bf16[2,2,256,256]{3,2,1,0:T(8,128)(2,1)S(1)}, u32[]{:S(2)}, u32[]{:S(2)}) collective-permute-start(bf16[2,2,256,256]{3,2,1,0:T(8,128)(2,1)} %collective-permute-done.11.refs_1_), channel_id=1, source_target_pairs={{0,4},{4,8},{8,12},{1,5},{5,9},{9,13},{2,6},{6,10},{10,14},{3,7},{... | collective-permute-start | bytes 1572872 | tf_op jit(solution)/shard_map/ppermute | solution.py:654
  106.2 16.2 %collective-permute-start.14 = (bf16[2,2,256,256]{3,2,1,0:T(8,128)(2,1)}, bf16[2,2,256,256]{3,2,1,0:T(8,128)(2,1)S(1)}, u32[]{:S(2)}, u32[]{:S(2)}) collective-permute-start(bf16[2,2,256,256]{3,2,1,0:T(8,128)(2,1)} %collective-permute-done.12.refs_5_), channel_id=1, source_target_pairs={{4,0},{8,4},{12,8},{5,1},{9,5},{13,9},{6,2},{10,6},{14,10},{7,3},{... | collective-permute-start | bytes 1572872 | tf_op jit(solution)/shard_map/ppermute | solution.py:655
  133.5 12.7 %copy-start.3 = (bf16[1536,896]{1,0:T(8,128)(2,1)S(1)}, bf16[1536,896]{1,0:T(8,128)(2,1)}, u32[]{:S(2)}) copy-start(bf16[1536,896]{1,0:T(8,128)(2,1)} %weight_ref.1) | copy-start | bytes 8257540
  133.6 12.7 %copy-start.11 = (bf16[768,896]{1,0:T(8,128)(2,1)S(1)}, bf16[768,896]{1,0:T(8,128)(2,1)}, u32[]{:S(2)}) copy-start(bf16[768,896]{1,0:T(8,128)(2,1)} %copy-done.10) | copy-start | bytes 4128772
  133.6 8.4 %collective-permute-start.16 = (bf16[192,384]{1,0:T(8,128)(2,1)S(1)}, bf16[192,384]{1,0:T(8,128)(2,1)S(1)}, u32[]{:S(2)}, u32[]{:S(2)}) collective-permute-start(bf16[192,384]{1,0:T(8,128)(2,1)S(1)} %get-tuple-element.44), channel_id=1, source_target_pairs={{0,2},{1,3},{2,0},{3,1},{4,6},{5,7},{6,4},{7,5},{8,10},{9,11},{10,... | collective-permute-start | bytes 442376 | tf_op jit(solution)/shard_map/ppermute | solution.py:703
  140.5 1.4 collective-permute-start.15
  140.6 5.6 %collective-permute-start.17 = (bf16[192,384]{1,0:T(8,128)(2,1)S(1)}, bf16[192,384]{1,0:T(8,128)(2,1)S(1)}, u32[]{:S(2)}, u32[]{:S(2)}) collective-permute-start(bf16[192,384]{1,0:T(8,128)(2,1)S(1)} %get-tuple-element.48), channel_id=1, source_target_pairs={{0,3},{1,2},{2,1},{3,0},{4,7},{5,6},{6,5},{7,4},{8,11},{9,10},{10,... | collective-permute-start | bytes 442376 | tf_op jit(solution)/shard_map/ppermute | solution.py:703
  (19 other events, 37.2 us)
Sparse Core Ops, SparseCore 0:
  13.7 63.4 all-gather.1

commit v7 on v6

--- a/solution.py
+++ b/solution.py
@@ -499,77 +499,126 @@
     return (mixed / total).astype(jnp.bfloat16)
 
 
-def attend_kernel(index_ref, hop_ref, held_ref, length_ref, query_ref, key_ref, value_ref,
-                  gathered_ref, *refs, targets, hops):
-    chain_refs, refs = refs[: len(hops)], refs[len(hops) :]
+def fetches(hop, refs, held, kv, sem, hops, start):
+    for which, source in enumerate(hops):
+        copies = [
+            pltpu.make_async_copy(refs[2 * which + chunk].at[:, held], kv.at[chunk], sem.at[chunk])
+            for chunk in range(2)
+        ]
+        if start:
+            @pl.when(hop == source)
+            def _():
+                for copy in copies:
+                    copy.start()
+        elif which == 0:
+            for copy in copies:
+                copy.wait()
+
+
+def among(hop, hops):
+    ours = hop == hops[0]
+    for other in hops[1:]:
+        ours = ours | (hop == other)
+    return ours
+
+
+def near_kernel(hop_ref, held_ref, length_ref, query_ref, key_ref, value_ref, *refs, hops):
+    prompt_refs, (out_ref, kv, sem) = refs[: 2 * len(hops)], refs[2 * len(hops) :]
+    sessions = hop_ref.shape[0]
+    for i in range(sessions):
+        fetches(hop_ref[i], prompt_refs, held_ref[i], kv.at[i], sem.at[i], hops, True)
+
+    def work(i, _):
+        @pl.when(among(hop_ref[i], hops))
+        def _():
+            fetches(hop_ref[i], prompt_refs, held_ref[i], kv.at[i], sem.at[i], hops, False)
+            rows = pl.ds(pl.multiple_of(i * SLOTS, SLOTS), SLOTS)
+            mixed = session_attention(
+                query_ref[rows], key_ref[rows], value_ref[rows],
+                kv[i].reshape(PROMPT, 2 * HD), length_ref[0, i],
+            )
+            for h in range(PER_GROUP):
+                out_ref[rows, h * HD : (h + 1) * HD] = mixed[h * SLOTS : (h + 1) * SLOTS]
+
+        return 0
+
+    lax.fori_loop(0, sessions, work, 0)
+
+
+def far_kernel(index_ref, hop_ref, held_ref, length_ref, query_ref, key_ref, value_ref, near_ref,
+               *refs, targets, hops):
+    prompt_refs, refs = refs[: 2 * len(hops)], refs[2 * len(hops) :]
     out_refs, (kv, sem) = refs[: len(targets)], refs[len(targets) :]
-    z, head = index_ref[0], index_ref[3]
+    head = index_ref[3]
     per_device = out_refs[0].shape[0] // SLOTS
     places = [(t, j) for t in range(len(targets)) for j in range(per_device)]
-
-    def session_of(i):
-        t, j = places[i]
-        return (head ^ targets[t]) * per_device + j
-
-    def from_gathered(i):
-        session = session_of(i)
-        plane = z + hop_ref[session]
-        return pltpu.make_async_copy(
-            gathered_ref.at[pl.ds(2 * plane, 2), held_ref[session]], kv.at[i, 0], sem.at[i, 0]
+    sessions = [(head ^ targets[t]) * per_device + j for t, j in places]
+    for i, session in enumerate(sessions):
+        fetches(
+            hop_ref[session], prompt_refs, held_ref[session], kv.at[i], sem.at[i], hops, True
         )
-
-    def from_chain(i, which):
-        return pltpu.make_async_copy(
-            chain_refs[which].at[:, held_ref[session_of(i)]], kv.at[i, 1], sem.at[i, 1]
-        )
-
-    for i in range(len(places)):
-        from_gathered(i).start()
-        for which, hop in enumerate(hops):
-            @pl.when(hop_ref[session_of(i)] == hop)
-            def _():
-                from_chain(i, which).start()
-    for i in range(len(places)):
-        from_gathered(i).wait()
-        from_chain(i, 0).wait()
-    for i, (t, j) in enumerate(places):
-        session = session_of(i)
+    for i, (session, (t, j)) in enumerate(zip(sessions, places)):
         rows = pl.ds(pl.multiple_of(session * SLOTS, SLOTS), SLOTS)
-        mixed = session_attention(
-            query_ref[rows],
-            key_ref[rows],
-            value_ref[rows],
-            kv[i].reshape(PROMPT, 2 * HD),
-            length_ref[0, session],
-        )
-        for h in range(PER_GROUP):
-            out_refs[t][j * SLOTS : (j + 1) * SLOTS, h * HD : (h + 1) * HD] = mixed[
-                h * SLOTS : (h + 1) * SLOTS
-            ]
-
-
-def attend_for(index, hop, held, lengths, query, key, value, gathered, chain, targets):
-    per_device = hop.shape[0] // KVH
-    hops = tuple(sorted(chain))
-    work = per_device * len(targets)
-    width = PER_GROUP * HD
+        target = slice(j * SLOTS, (j + 1) * SLOTS)
+        ours = among(hop_ref[session], hops)
+
+        @pl.when(jnp.logical_not(ours))
+        def _():
+            out_refs[t][target] = near_ref[rows]
+
+        @pl.when(ours)
+        def _():
+            fetches(
+                hop_ref[session], prompt_refs, held_ref[session], kv.at[i], sem.at[i], hops, False
+            )
+            mixed = session_attention(
+                query_ref[rows], key_ref[rows], value_ref[rows],
+                kv[i].reshape(PROMPT, 2 * HD), length_ref[0, session],
+            )
+            for h in range(PER_GROUP):
+                out_refs[t][target, h * HD : (h + 1) * HD] = mixed[h * SLOTS : (h + 1) * SLOTS]
+
+
+HBM = pl.BlockSpec(memory_space=pltpu.HBM)
+
+
+def attention_call(kernel, out_specs, out_shape, places, name, scalars, arrays, prompts, hops):
+    pieces = [piece for h in hops for piece in prompts[h]]
+    work = places * PER_GROUP * SLOTS * (PROMPT + SLOTS) // 2
     return pl.pallas_call(
-        functools.partial(attend_kernel, targets=targets, hops=hops),
-        in_specs=[SMEM] * 4 + [VMEM] * 3 + [ANY] * (1 + len(hops)),
-        out_specs=[VMEM] * len(targets),
-        out_shape=[jax.ShapeDtypeStruct((per_device * SLOTS, width), jnp.bfloat16)] * len(targets),
+        kernel,
+        in_specs=[SMEM] * len(scalars) + [VMEM] * len(arrays) + [HBM] * len(pieces),
+        out_specs=out_specs,
+        out_shape=out_shape,
         scratch_shapes=[
-            pltpu.VMEM((work, 2, 2, PROMPT // 4, 2 * HD), jnp.bfloat16),
-            pltpu.SemaphoreType.DMA((work, 2)),
+            pltpu.VMEM((places, 2, 2, PROMPT // 4, 2 * HD), jnp.bfloat16),
+            pltpu.SemaphoreType.DMA((places, 2)),
         ],
         compiler_params=pltpu.CompilerParams(vmem_limit_bytes=40 << 20),
         cost_estimate=pl.CostEstimate(
-            flops=work * 4 * PER_GROUP * SLOTS * (PROMPT + SLOTS) * HD,
-            bytes_accessed=work * PROMPT * 4 * HD,
-            transcendentals=work * PER_GROUP * SLOTS * (PROMPT + SLOTS),
+            flops=4 * work * HD, bytes_accessed=places * PROMPT * 2 * HD, transcendentals=work
         ),
-        name="attend",
-    )(index, hop, held, lengths, query, key, value, gathered, *[chain[h] for h in hops])
+        name=name,
+    )(*scalars, *arrays, *pieces)
+
+
+def attend_near(hop, held, lengths, query, key, value, prompts, hops):
+    out_shape = jax.ShapeDtypeStruct(query.shape, jnp.bfloat16)
+    return attention_call(
+        functools.partial(near_kernel, hops=hops),
+        VMEM, out_shape, hop.shape[0], "near", (hop, held, lengths), (query, key, value),
+        prompts, hops,
+    )
+
+
+def attend_far(index, hop, held, lengths, query, key, value, near, prompts, hops, targets):
+    per_device = hop.shape[0] // KVH
+    out_shape = jax.ShapeDtypeStruct((per_device * SLOTS, query.shape[1]), jnp.bfloat16)
+    return attention_call(
+        functools.partial(far_kernel, hops=hops, targets=targets),
+        [VMEM] * len(targets), [out_shape] * len(targets), per_device * len(targets), "far",
+        (index, hop, held, lengths), (query, key, value, near), prompts, hops,
+    )
 
 
 def output_kernel(index_ref, length_ref, states_ref, weight_ref, *refs):
@@ -647,30 +696,37 @@
     from_far = lax.ppermute(to_far, pair, swapped(4, 3))
     first = stack(own[None], from_core[None])
     second = stack(from_x[None], from_far[None])
-    gathered = lax.all_gather(first, "sess", axis=0, tiled=True)
-    right = left = second
-    chain = {0: second}
-    for hop in range(1, planes):
-        right = lax.ppermute(right, "sess", shifted(planes, 1))
-        left = lax.ppermute(left, "sess", shifted(planes, -1))
-        chain[-hop], chain[hop] = right, left
-
-    thinker_rows, _ = lax.optimization_barrier((thinker_rows, first))
+    thinker_rows, _ = lax.optimization_barrier((thinker_rows, to_core))
     partial_sum = jnp.dot(thinker_rows, proj_weight, preferred_element_type=jnp.float32)
     kept = lax.dynamic_slice_in_dim(partial_sum, x * width, width, 1)
     sent = lax.dynamic_slice_in_dim(partial_sum, (1 - x) * width, width, 1)
-    came = lax.ppermute(sent.astype(jnp.bfloat16), "inner", swapped(2, 1))
-    came, _ = lax.optimization_barrier((came, second))
+    sent = sent.astype(jnp.bfloat16)
+    came = lax.ppermute(sent, "inner", swapped(2, 1))
     routed = route(z.reshape(1), kept, came, row_session, planes, per_plane, slot_cap)
+    first, _ = lax.optimization_barrier((first, sent))
+    second, _ = lax.optimization_barrier((second, routed[0]))
+    right, left = [first, second], [first, second]
+    prompts = {0: (first, second)}
+    for hop in range(1, planes):
+        for chunk in range(2):
+            right[chunk] = lax.ppermute(right[chunk], "sess", shifted(planes, 1))
+            left[chunk] = lax.ppermute(left[chunk], "sess", shifted(planes, -1))
+        prompts[-hop], prompts[hop] = tuple(right), tuple(left)
+
+    def after(value, hop, chunk):
+        return lax.optimization_barrier((value, prompts[-hop][chunk], prompts[hop][chunk]))[0]
+
+    routed = after(tuple(routed), 1, 0)
     arrived = [routed[0]] + [
         lax.ppermute(routed[by], "sess", swapped(planes, by)) for by in range(1, planes)
     ]
+    arrived = after(arrived, 1, 1)
     arrived = stack(*[a[None] for a in arrived])
     other = lax.ppermute(arrived, "inner", swapped(2, 1))
-    other, _ = lax.optimization_barrier((other, (chain[-1], chain[1])))
+    other = after(other, 2, 0)
     mine = stack(arrived, other)
     core = lax.ppermute(mine, "rep", swapped(2, 1))
-    core, _ = lax.optimization_barrier((core, (chain[-2], chain[2])))
+    core = after(core, 2, 1)
 
     group_width = PER_GROUP * HD
     weight = jnp.concatenate(
@@ -694,11 +750,14 @@
     )
     hop = wanted_slot // held - z
     which = wanted_slot % held
-    run = functools.partial(attend_for, index, hop, which, lengths)
+    near = attend_near(
+        hop, which, lengths, after(query, 3, 0), key, value, prompts, (0, -1, 1, -2, 2)
+    )
+    run = functools.partial(attend_far, index, hop, which, lengths)
     attended = {}
-    attended[2], attended[3] = run(query, key, value, gathered, chain, (2, 3))
-    query, _ = lax.optimization_barrier((query, attended[2]))
-    attended[0], attended[1] = run(query, key, value, gathered, chain, (0, 1))
+    attended[2], attended[3] = run(query, key, value, near, prompts, (-3, 3), (2, 3))
+    near, _ = lax.optimization_barrier((near, attended[2]))
+    attended[0], attended[1] = run(query, key, value, near, prompts, (-3, 3), (0, 1))
     pieces = [attended[0]] + [
         lax.ppermute(attended[by], pair, swapped(4, by)) for by in range(1, plane)
     ]

time: 156 us -> 131 us (0.84)
  waiting for transfers between devices: 58 us -> 32.7 us
  starting transfers between devices: 32.9 us -> 54.4 us
  between operations: 13.6 us -> 0.29 us
  local copies, waits for them, and re-layouts: 20.1 us -> 7.91 us
  Pallas kernels: 27.3 us -> 30.5 us
    ppermute x3, waiting for transfers between devices: 34.2 us -> 12.7 us  [line_body(): lax.ppermute(routed[by], 'sess', swapped(planes, by))]
    ppermute x7 -> x13, starting transfers between devices: 20.3 us -> 38 us  [the longest x6 28.5 us: line_body(): right[chunk] = lax.ppermute(right[chunk], 'sess', shifted(planes, 1))]
    unnamed x49 -> x27, local copies, waits for them, and re-layouts: 14.1 us -> 1.53 us
    ppermute x1, waiting for transfers between devices: 5.19 us -> 0.01 us  [line_body(): from_far = lax.ppermute(to_far, pair, swapped(4, 3))]
    ppermute x7 -> x13, waiting for transfers between devices: 7.04 us -> 12.2 us  [the longest x6 9.69 us: line_body(): left[chunk] = lax.ppermute(left[chunk], 'sess', shifted(planes, -1))]
    ppermute x3, starting transfers between devices: 5.2 us -> 9.1 us  [line_body(): lax.ppermute(routed[by], 'sess', swapped(planes, by))]
    pallas_call x2 -> x3, Pallas kernels: 8.16 us -> 11.4 us  [attention_call(): pl.pallas_call(kernel, in_specs=[SMEM] * len(scalars) + [VMEM] * len(arra...]
    ppermute x1, waiting for transfers between devices: 1.66 us -> 0.01 us  [line_body(): from_x = lax.ppermute(to_x, pair, swapped(4, 2))]
  transfers between devices with their start and end apart: 19 -> 24, of which waited for: 10 -> 11; matrix products, arithmetic and copies ran while one was open for 7% -> 8% of each run, Pallas kernels for 11% -> 19%
where the time goes in v7:
time: 131 us; the launch traced here: 129 us
  starting transfers between devices  54.4 us (42%)
  waiting for transfers between devices  32.7 us (25%)
  Pallas kernels  30.5 us (23%)
  local copies, waits for them, and re-layouts  7.91 us (6%)
  matrix products  3.23 us (2%)
    ppermute x6, starting transfers between devices, line_body(): right[chunk] = lax.ppermute(right[chunk], 'sess', shifted(planes, 1))  28.5 us
    ppermute x3, waiting for transfers between devices, line_body(): lax.ppermute(routed[by], 'sess', swapped(planes, by))  12.7 us
    pallas_call x3, Pallas kernels, attention_call(): pl.pallas_call(kernel, in_specs=[SMEM] * len(scalars) + [VMEM] * len(arra...  11.4 us
    ppermute x6, waiting for transfers between devices, line_body(): left[chunk] = lax.ppermute(left[chunk], 'sess', shifted(planes, -1))  9.69 us
    ppermute x3, starting transfers between devices, line_body(): lax.ppermute(routed[by], 'sess', swapped(planes, by))  9.1 us
    pallas_call x4, Pallas kernels, stack(): pl.pallas_call(stack_kernel, in_specs=[VMEM] * len(arrays), out_specs=VME...  7.75 us
    ppermute x6, starting transfers between devices, line_body(): left[chunk] = lax.ppermute(left[chunk], 'sess', shifted(planes, -1))  7.71 us
    ppermute x3, waiting for transfers between devices, line_body(): lax.ppermute(attended[by], pair, swapped(4, by))  5.56 us
  transfers between devices with their start and end apart: 24, of which 11 were waited for; matrix products, arithmetic and copies ran while one was open for 8% of the time, Pallas kernels for 19%

profile of v7, /device:TPU:0, one launch (start us, length us, event | category | flops | bytes accessed | tf_op | source)
XLA Modules:
  0.0 129.4 jit_solution(2355625473030632244)
XLA Ops:
  0.0 2.6 %split_heads.1 = (bf16[2,256,256]{2,1,0:T(8,128)(2,1)}, bf16[2,256,256]{2,1,0:T(8,128)(2,1)}, bf16[2,256,256]{2,1,0:T(8,128)(2,1)}, bf16[2,256,256]{2,1,0:T(8,128)(2,1)}) custom-call(s32[1]{0:T(128)} %bitcast.3.head_ref, bf16[2,256,1024]{2,1,0:T(8,128)(2,1)} %cache_ref.1), custom_call_target="tpu_custom_call" | custom-call | bytes 2097152 | tf_op jit(solution)/shard_map/split_heads/pallas_call | solution.py:308
  3.1 2.5 %collective-permute-start.7 = (bf16[2,256,256]{2,1,0:T(8,128)(2,1)}, bf16[2,256,256]{2,1,0:T(8,128)(2,1)}, u32[]{:S(2)}, u32[]{:S(2)}) collective-permute-start(bf16[2,256,256]{2,1,0:T(8,128)(2,1)} %get-tuple-element.49), channel_id=1, source_target_pairs={{0,2},{1,3},{2,0},{3,1},{4,6},{5,7},{6,4},{7,5},{8,10},{9,11},{10,... | collective-permute-start | bytes 786440 | tf_op jit(solution)/shard_map/ppermute | solution.py:695
  5.7 3.2 %fusion.1 = f32[256,896]{1,0:T(8,128)} fusion(bf16[256,1792]{1,0:T(8,128)(2,1)} %param.13, bf16[1792,896]{1,0:T(8,128)(2,1)S(1)} %copy-done), kind=kOutput, calls=%fused_computation.15 | convolution fusion | flops 822083584 | bytes 5046272 | tf_op jit(solution)/shard_map/dot_general | solution.py:700
  13.8 4.3 %collective-permute-start.2 = (bf16[2,2,256,256]{3,2,1,0:T(8,128)(2,1)}, bf16[2,2,256,256]{3,2,1,0:T(8,128)(2,1)}, u32[]{:S(2)}, u32[]{:S(2)}) collective-permute-start(bf16[2,2,256,256]{3,2,1,0:T(8,128)(2,1)} %stack.24.refs_0_), channel_id=1, source_target_pairs={{0,4},{4,8},{8,12},{1,5},{5,9},{9,13},{2,6},{6,10},{10,14},{3,7},{... | collective-permute-start | bytes 1572872 | tf_op jit(solution)/shard_map/ppermute | solution.py:712
  24.1 2.3 %route.1 = (bf16[112,448]{1,0:T(8,128)(2,1)}, bf16[112,448]{1,0:T(8,128)(2,1)}, bf16[112,448]{1,0:T(8,128)(2,1)}, bf16[112,448]{1,0:T(8,128)(2,1)}) custom-call(s32[1]{0:T(128)} %bitcast.z_ref, f32[256,448]{1,0:T(8,128)} %constant_dynamic-slice_fusion.3.kept_ref, bf16[256,448]{1,0:T(8,128)(2,1)} %collective-permute-done.came_ref, s32[256,1]{1,0:T(8,128)} %copy.15.owner_ref, ...), custom_call_target="tpu_custom_call" | custom-call | flops 102760448 | bytes 917504 | tf_op jit(solution)/shard_map/route/pallas_call | solution.py:373
  29.5 5.4 %collective-permute-start.9 = (bf16[2,2,256,256]{3,2,1,0:T(8,128)(2,1)}, bf16[2,2,256,256]{3,2,1,0:T(8,128)(2,1)}, u32[]{:S(2)}, u32[]{:S(2)}) collective-permute-start(bf16[2,2,256,256]{3,2,1,0:T(8,128)(2,1)} %stack.25.refs_1_), channel_id=1, source_target_pairs={{0,4},{4,8},{8,12},{1,5},{5,9},{9,13},{2,6},{6,10},{10,14},{3,7},{... | collective-permute-start | bytes 1572872 | tf_op jit(solution)/shard_map/ppermute | solution.py:712
  34.9 3.8 %collective-permute-start.12 = (bf16[2,2,256,256]{3,2,1,0:T(8,128)(2,1)}, bf16[2,2,256,256]{3,2,1,0:T(8,128)(2,1)}, u32[]{:S(2)}, u32[]{:S(2)}) collective-permute-start(bf16[2,2,256,256]{3,2,1,0:T(8,128)(2,1)} %collective-permute-done.2.refs_2_), channel_id=1, source_target_pairs={{0,4},{4,8},{8,12},{1,5},{5,9},{9,13},{2,6},{6,10},{10,14},{3,7},{... | collective-permute-start | bytes 1572872 | tf_op jit(solution)/shard_map/ppermute | solution.py:712
  39.9 2.7 %collective-permute-start.4 = (bf16[112,448]{1,0:T(8,128)(2,1)}, bf16[112,448]{1,0:T(8,128)(2,1)S(1)}, u32[]{:S(2)}, u32[]{:S(2)}) collective-permute-start(bf16[112,448]{1,0:T(8,128)(2,1)} %get-tuple-element.46), channel_id=1, source_target_pairs={{0,4},{4,0},{8,12},{12,8},{1,5},{5,1},{9,13},{13,9},{2,6},{6,2},{1... | collective-permute-start | bytes 301064 | tf_op jit(solution)/shard_map/ppermute | solution.py:721
  42.6 3.3 %collective-permute-done.10.refs_5_ = bf16[2,2,256,256]{3,2,1,0:T(8,128)(2,1)} collective-permute-done((bf16[2,2,256,256]{3,2,1,0:T(8,128)(2,1)}, bf16[2,2,256,256]{3,2,1,0:T(8,128)(2,1)}, u32[]{:S(2)}, u32[]{:S(2)}) %collective-permute-start.10) | collective-permute-done | bytes 524320 | tf_op jit(solution)/shard_map/ppermute | solution.py:713
  45.9 2.2 %collective-permute-start.5 = (bf16[112,448]{1,0:T(8,128)(2,1)}, bf16[112,448]{1,0:T(8,128)(2,1)S(1)}, u32[]{:S(2)}, u32[]{:S(2)}) collective-permute-start(bf16[112,448]{1,0:T(8,128)(2,1)} %get-tuple-element.47), channel_id=1, source_target_pairs={{0,8},{4,12},{8,0},{12,4},{1,9},{5,13},{9,1},{13,5},{2,10},{6,14},... | collective-permute-start | bytes 301064 | tf_op jit(solution)/shard_map/ppermute | solution.py:721
  48.1 4.2 %collective-permute-start.6 = (bf16[112,448]{1,0:T(8,128)(2,1)}, bf16[112,448]{1,0:T(8,128)(2,1)S(1)}, u32[]{:S(2)}, u32[]{:S(2)}) collective-permute-start(bf16[112,448]{1,0:T(8,128)(2,1)} %get-tuple-element.48), channel_id=1, source_target_pairs={{0,12},{4,8},{8,4},{12,0},{1,13},{5,9},{9,5},{13,1},{2,14},{6,10},... | collective-permute-start | bytes 301064 | tf_op jit(solution)/shard_map/ppermute | solution.py:721
  52.3 8.7 %collective-permute-done.4 = bf16[112,448]{1,0:T(8,128)(2,1)S(1)} collective-permute-done((bf16[112,448]{1,0:T(8,128)(2,1)}, bf16[112,448]{1,0:T(8,128)(2,1)S(1)}, u32[]{:S(2)}, u32[]{:S(2)}) %collective-permute-start.4) | collective-permute-done | bytes 100384 | tf_op jit(solution)/shard_map/ppermute | solution.py:721
  61.0 4.0 %collective-permute-done.5 = bf16[112,448]{1,0:T(8,128)(2,1)S(1)} collective-permute-done((bf16[112,448]{1,0:T(8,128)(2,1)}, bf16[112,448]{1,0:T(8,128)(2,1)S(1)}, u32[]{:S(2)}, u32[]{:S(2)}) %collective-permute-start.5) | collective-permute-done | bytes 100384 | tf_op jit(solution)/shard_map/ppermute | solution.py:721
  69.0 5.7 %collective-permute-start.15 = (bf16[2,2,256,256]{3,2,1,0:T(8,128)(2,1)}, bf16[2,2,256,256]{3,2,1,0:T(8,128)(2,1)}, u32[]{:S(2)}, u32[]{:S(2)}) collective-permute-start(bf16[2,2,256,256]{3,2,1,0:T(8,128)(2,1)} %collective-permute-done.9.refs_3_), channel_id=1, source_target_pairs={{0,4},{4,8},{8,12},{1,5},{5,9},{9,13},{2,6},{6,10},{10,14},{3,7},{... | collective-permute-start | bytes 1572872 | tf_op jit(solution)/shard_map/ppermute | solution.py:712
  76.8 2.2 %collective-permute-done.11.refs_1_ = bf16[4,112,448]{2,1,0:T(8,128)(2,1)} collective-permute-done((bf16[4,112,448]{2,1,0:T(8,128)(2,1)}, bf16[4,112,448]{2,1,0:T(8,128)(2,1)}, u32[]{:S(2)}, u32[]{:S(2)}) %collective-permute-start.11) | collective-permute-done | bytes 401440 | tf_op jit(solution)/shard_map/ppermute | solution.py:725
  79.0 2.2 %stack.27.mine_ref = bf16[8,112,448]{2,1,0:T(8,128)(2,1)} custom-call(bf16[4,112,448]{2,1,0:T(8,128)(2,1)} %stack.26.refs_0_, bf16[4,112,448]{2,1,0:T(8,128)(2,1)} %collective-permute-done.11.refs_1_), custom_call_target="tpu_custom_call" | custom-call | bytes 1605632 | tf_op jit(solution)/shard_map/stack/pallas_call | solution.py:330
  83.8 4.8 %collective-permute-start.17 = (bf16[2,2,256,256]{3,2,1,0:T(8,128)(2,1)}, bf16[2,2,256,256]{3,2,1,0:T(8,128)(2,1)S(1)}, u32[]{:S(2)}, u32[]{:S(2)}) collective-permute-start(bf16[2,2,256,256]{3,2,1,0:T(8,128)(2,1)} %collective-permute-done.12.refs_6_), channel_id=1, source_target_pairs={{0,4},{4,8},{8,12},{1,5},{5,9},{9,13},{2,6},{6,10},{10,14},{3,7},{... | collective-permute-start | bytes 1572872 | tf_op jit(solution)/shard_map/ppermute | solution.py:712
  90.1 4.6 %collective-permute-start.19 = (bf16[2,2,256,256]{3,2,1,0:T(8,128)(2,1)}, bf16[2,2,256,256]{3,2,1,0:T(8,128)(2,1)S(1)}, u32[]{:S(2)}, u32[]{:S(2)}) collective-permute-start(bf16[2,2,256,256]{3,2,1,0:T(8,128)(2,1)} %collective-permute-done.15.refs_7_), channel_id=1, source_target_pairs={{0,4},{4,8},{8,12},{1,5},{5,9},{9,13},{2,6},{6,10},{10,14},{3,7},{... | collective-permute-start | bytes 1572872 | tf_op jit(solution)/shard_map/ppermute | solution.py:712
  96.2 4.2 %place_rows.1 = (bf16[768,896]{1,0:T(8,128)(2,1)S(1)}, bf16[768,384]{1,0:T(8,128)(2,1)S(1)}, bf16[768,128]{1,0:T(8,128)(2,1)S(1)}, bf16[768,128]{1,0:T(8,128)(2,1)S(1)}, s32[1,128]{1,0:T(1,128)S(1)}) custom-call(s32[4]{0:T(128)S(1)} %pad_add_fusion.index_ref, bf16[8,112,448]{2,1,0:T(8,128)(2,1)S(1)} %copy-done.4, ...), custom_call_target="tpu_custom_call" | custom-call | flops 1761607680 | bytes 6291456 | tf_op jit(solution)/shard_map/place_rows/pallas_call | solution.py:465
  101.1 4.4 %collective-permute-done.18.refs_2_ = bf16[2,2,256,256]{3,2,1,0:T(8,128)(2,1)S(1)} collective-permute-done((bf16[2,2,256,256]{3,2,1,0:T(8,128)(2,1)}, bf16[2,2,256,256]{3,2,1,0:T(8,128)(2,1)S(1)}, u32[]{:S(2)}, u32[]{:S(2)}) %collective-permute-start.18) | collective-permute-done | bytes 524320 | tf_op jit(solution)/shard_map/ppermute | solution.py:713
  105.4 8.7 %near.1.near_ref = bf16[768,384]{1,0:T(8,128)(2,1)S(1)} custom-call(s32[8]{0:T(128)S(1)} %get-tuple-element.70.hop_ref, s32[8]{0:T(128)S(1)} %get-tuple-element.69.held_ref, s32[1,128]{1,0:T(1,128)S(1)} %get-tuple-element.58.length_ref, bf16[768,384]{1,0:T(8,128)(2,1)S(1)} %get-tuple-element.63.query_ref, bf16[768,128]{1,0:T(8,128)(2,1)S(1)} %get-tuple-element.61.key_ref, ...), custom_call_target="tpu_custom_call" | custom-call | flops 660602880 | bytes 2097152 | tf_op jit(solution)/shard_map/near/pallas_call | solution.py:588
  117.2 2.6 %collective-permute-start.22 = (bf16[192,384]{1,0:T(8,128)(2,1)S(1)}, bf16[192,384]{1,0:T(8,128)(2,1)S(1)}, u32[]{:S(2)}, u32[]{:S(2)}) collective-permute-start(bf16[192,384]{1,0:T(8,128)(2,1)S(1)} %get-tuple-element.64), channel_id=1, source_target_pairs={{0,2},{1,3},{2,0},{3,1},{4,6},{5,7},{6,4},{7,5},{8,10},{9,11},{10,... | collective-permute-start | bytes 442376 | tf_op jit(solution)/shard_map/ppermute | solution.py:762
  123.4 3.9 %collective-permute-done.23.refs_3_ = bf16[192,384]{1,0:T(8,128)(2,1)S(1)} collective-permute-done((bf16[192,384]{1,0:T(8,128)(2,1)S(1)}, bf16[192,384]{1,0:T(8,128)(2,1)S(1)}, u32[]{:S(2)}, u32[]{:S(2)}) %collective-permute-start.23) | collective-permute-done | bytes 147488 | tf_op jit(solution)/shard_map/ppermute | solution.py:762
  127.2 2.2 %output.1 = bf16[2,96,896]{2,1,0:T(8,128)(2,1)} custom-call(s32[4]{0:T(128)S(1)} %pad_add_fusion.index_ref, s32[1,128]{1,0:T(1,128)S(1)} %get-tuple-element.58.length_ref, bf16[768,896]{1,0:T(8,128)(2,1)S(1)} %get-tuple-element.59.states_ref, bf16[1536,896]{1,0:T(8,128)(2,1)S(1)} %copy-done.1, bf16[192,384]{1,0:T(8,128)(2,1)S(1)} %get-tuple-element.66.refs_0_, ...), custom_call_target="tpu_custom_call" | custom-call | flops 528482304 | bytes 2752512 | tf_op jit(solution)/shard_map/output/pallas_call | solution.py:645
  (73 shorter events, 34.7 us)
Async XLA Ops:
  2.6 9.3 %collective-permute-start.1 = (bf16[2,256,256]{2,1,0:T(8,128)(2,1)}, bf16[2,256,256]{2,1,0:T(8,128)(2,1)}, u32[]{:S(2)}, u32[]{:S(2)}) collective-permute-start(bf16[2,256,256]{2,1,0:T(8,128)(2,1)} %get-tuple-element.37), channel_id=1, source_target_pairs={{0,1},{1,0},{2,3},{3,2},{4,5},{5,4},{6,7},{7,6},{8,9},{9,8},{10,11... | collective-permute-start | bytes 786440 | tf_op jit(solution)/shard_map/ppermute | solution.py:694
  3.1 23.3 %collective-permute-start.7 = (bf16[2,256,256]{2,1,0:T(8,128)(2,1)}, bf16[2,256,256]{2,1,0:T(8,128)(2,1)}, u32[]{:S(2)}, u32[]{:S(2)}) collective-permute-start(bf16[2,256,256]{2,1,0:T(8,128)(2,1)} %get-tuple-element.49), channel_id=1, source_target_pairs={{0,2},{1,3},{2,0},{3,1},{4,6},{5,7},{6,4},{7,5},{8,10},{9,11},{10,... | collective-permute-start | bytes 786440 | tf_op jit(solution)/shard_map/ppermute | solution.py:695
  5.6 20.8 %collective-permute-start.8 = (bf16[2,256,256]{2,1,0:T(8,128)(2,1)}, bf16[2,256,256]{2,1,0:T(8,128)(2,1)}, u32[]{:S(2)}, u32[]{:S(2)}) collective-permute-start(bf16[2,256,256]{2,1,0:T(8,128)(2,1)} %get-tuple-element.50), channel_id=1, source_target_pairs={{0,3},{1,2},{2,1},{3,0},{4,7},{5,6},{6,5},{7,4},{8,11},{9,10},{10,... | collective-permute-start | bytes 786440 | tf_op jit(solution)/shard_map/ppermute | solution.py:696
  10.1 13.9 %collective-permute-start = (bf16[256,448]{1,0:T(8,128)(2,1)S(1)}, bf16[256,448]{1,0:T(8,128)(2,1)}, u32[]{:S(2)}, u32[]{:S(2)}) collective-permute-start(bf16[256,448]{1,0:T(8,128)(2,1)S(1)} %dynamic-slice_convert_fusion), channel_id=1, source_target_pairs={{0,2},{2,0},{1,3},{3,1},{4,6},{6,4},{5,7},{7,5},{8,10},{10,8},{9,1... | collective-permute-start | bytes 688136 | tf_op jit(solution)/shard_map/ppermute | solution.py:704
  13.8 21.1 %collective-permute-start.2 = (bf16[2,2,256,256]{3,2,1,0:T(8,128)(2,1)}, bf16[2,2,256,256]{3,2,1,0:T(8,128)(2,1)}, u32[]{:S(2)}, u32[]{:S(2)}) collective-permute-start(bf16[2,2,256,256]{3,2,1,0:T(8,128)(2,1)} %stack.24.refs_0_), channel_id=1, source_target_pairs={{0,4},{4,8},{8,12},{1,5},{5,9},{9,13},{2,6},{6,10},{10,14},{3,7},{... | collective-permute-start | bytes 1572872 | tf_op jit(solution)/shard_map/ppermute | solution.py:712
  18.1 20.6 %collective-permute-start.3 = (bf16[2,2,256,256]{3,2,1,0:T(8,128)(2,1)}, bf16[2,2,256,256]{3,2,1,0:T(8,128)(2,1)}, u32[]{:S(2)}, u32[]{:S(2)}) collective-permute-start(bf16[2,2,256,256]{3,2,1,0:T(8,128)(2,1)} %stack.24.refs_0_), channel_id=1, source_target_pairs={{4,0},{8,4},{12,8},{5,1},{9,5},{13,9},{6,2},{10,6},{14,10},{7,3},{... | collective-permute-start | bytes 1572872 | tf_op jit(solution)/shard_map/ppermute | solution.py:713
  28.2 17.7 %collective-permute-start.10 = (bf16[2,2,256,256]{3,2,1,0:T(8,128)(2,1)}, bf16[2,2,256,256]{3,2,1,0:T(8,128)(2,1)}, u32[]{:S(2)}, u32[]{:S(2)}) collective-permute-start(bf16[2,2,256,256]{3,2,1,0:T(8,128)(2,1)} %stack.25.refs_1_), channel_id=1, source_target_pairs={{4,0},{8,4},{12,8},{5,1},{9,5},{13,9},{6,2},{10,6},{14,10},{7,3},{... | collective-permute-start | bytes 1572872 | tf_op jit(solution)/shard_map/ppermute | solution.py:713
  29.5 18.6 %collective-permute-start.9 = (bf16[2,2,256,256]{3,2,1,0:T(8,128)(2,1)}, bf16[2,2,256,256]{3,2,1,0:T(8,128)(2,1)}, u32[]{:S(2)}, u32[]{:S(2)}) collective-permute-start(bf16[2,2,256,256]{3,2,1,0:T(8,128)(2,1)} %stack.25.refs_1_), channel_id=1, source_target_pairs={{0,4},{4,8},{8,12},{1,5},{5,9},{9,13},{2,6},{6,10},{10,14},{3,7},{... | collective-permute-start | bytes 1572872 | tf_op jit(solution)/shard_map/ppermute | solution.py:712
  34.9 44.2 %collective-permute-start.12 = (bf16[2,2,256,256]{3,2,1,0:T(8,128)(2,1)}, bf16[2,2,256,256]{3,2,1,0:T(8,128)(2,1)}, u32[]{:S(2)}, u32[]{:S(2)}) collective-permute-start(bf16[2,2,256,256]{3,2,1,0:T(8,128)(2,1)} %collective-permute-done.2.refs_2_), channel_id=1, source_target_pairs={{0,4},{4,8},{8,12},{1,5},{5,9},{9,13},{2,6},{6,10},{10,14},{3,7},{... | collective-permute-start | bytes 1572872 | tf_op jit(solution)/shard_map/ppermute | solution.py:712
  38.6 40.4 %collective-permute-start.13 = (bf16[2,2,256,256]{3,2,1,0:T(8,128)(2,1)}, bf16[2,2,256,256]{3,2,1,0:T(8,128)(2,1)}, u32[]{:S(2)}, u32[]{:S(2)}) collective-permute-start(bf16[2,2,256,256]{3,2,1,0:T(8,128)(2,1)} %collective-permute-done.3.refs_4_), channel_id=1, source_target_pairs={{4,0},{8,4},{12,8},{5,1},{9,5},{13,9},{6,2},{10,6},{14,10},{7,3},{... | collective-permute-start | bytes 1572872 | tf_op jit(solution)/shard_map/ppermute | solution.py:713
  39.9 21.1 %collective-permute-start.4 = (bf16[112,448]{1,0:T(8,128)(2,1)}, bf16[112,448]{1,0:T(8,128)(2,1)S(1)}, u32[]{:S(2)}, u32[]{:S(2)}) collective-permute-start(bf16[112,448]{1,0:T(8,128)(2,1)} %get-tuple-element.46), channel_id=1, source_target_pairs={{0,4},{4,0},{8,12},{12,8},{1,5},{5,1},{9,13},{13,9},{2,6},{6,2},{1... | collective-permute-start | bytes 301064 | tf_op jit(solution)/shard_map/ppermute | solution.py:721
  45.9 19.1 %collective-permute-start.5 = (bf16[112,448]{1,0:T(8,128)(2,1)}, bf16[112,448]{1,0:T(8,128)(2,1)S(1)}, u32[]{:S(2)}, u32[]{:S(2)}) collective-permute-start(bf16[112,448]{1,0:T(8,128)(2,1)} %get-tuple-element.47), channel_id=1, source_target_pairs={{0,8},{4,12},{8,0},{12,4},{1,9},{5,13},{9,1},{13,5},{2,10},{6,14},... | collective-permute-start | bytes 301064 | tf_op jit(solution)/shard_map/ppermute | solution.py:721
  48.1 16.9 %collective-permute-start.6 = (bf16[112,448]{1,0:T(8,128)(2,1)}, bf16[112,448]{1,0:T(8,128)(2,1)S(1)}, u32[]{:S(2)}, u32[]{:S(2)}) collective-permute-start(bf16[112,448]{1,0:T(8,128)(2,1)} %get-tuple-element.48), channel_id=1, source_target_pairs={{0,12},{4,8},{8,4},{12,0},{1,13},{5,9},{9,5},{13,1},{2,14},{6,10},... | collective-permute-start | bytes 301064 | tf_op jit(solution)/shard_map/ppermute | solution.py:721
  67.6 11.4 %collective-permute-start.11 = (bf16[4,112,448]{2,1,0:T(8,128)(2,1)}, bf16[4,112,448]{2,1,0:T(8,128)(2,1)}, u32[]{:S(2)}, u32[]{:S(2)}) collective-permute-start(bf16[4,112,448]{2,1,0:T(8,128)(2,1)} %stack.26.refs_0_), channel_id=1, source_target_pairs={{0,2},{2,0},{1,3},{3,1},{4,6},{6,4},{5,7},{7,5},{8,10},{10,8},{9,1... | collective-permute-start | bytes 1204232 | tf_op jit(solution)/shard_map/ppermute | solution.py:725
  69.0 21.0 %collective-permute-start.15 = (bf16[2,2,256,256]{3,2,1,0:T(8,128)(2,1)}, bf16[2,2,256,256]{3,2,1,0:T(8,128)(2,1)}, u32[]{:S(2)}, u32[]{:S(2)}) collective-permute-start(bf16[2,2,256,256]{3,2,1,0:T(8,128)(2,1)} %collective-permute-done.9.refs_3_), channel_id=1, source_target_pairs={{0,4},{4,8},{8,12},{1,5},{5,9},{9,13},{2,6},{6,10},{10,14},{3,7},{... | collective-permute-start | bytes 1572872 | tf_op jit(solution)/shard_map/ppermute | solution.py:712
  74.8 19.9 %collective-permute-start.16 = (bf16[2,2,256,256]{3,2,1,0:T(8,128)(2,1)}, bf16[2,2,256,256]{3,2,1,0:T(8,128)(2,1)}, u32[]{:S(2)}, u32[]{:S(2)}) collective-permute-start(bf16[2,2,256,256]{3,2,1,0:T(8,128)(2,1)} %collective-permute-done.10.refs_5_), channel_id=1, source_target_pairs={{4,0},{8,4},{12,8},{5,1},{9,5},{13,9},{6,2},{10,6},{14,10},{7,3},{... | collective-permute-start | bytes 1572872 | tf_op jit(solution)/shard_map/ppermute | solution.py:713
  81.2 14.9 %collective-permute-start.14 = (bf16[8,112,448]{2,1,0:T(8,128)(2,1)}, bf16[8,112,448]{2,1,0:T(8,128)(2,1)S(1)}, u32[]{:S(2)}, u32[]{:S(2)}) collective-permute-start(bf16[8,112,448]{2,1,0:T(8,128)(2,1)} %stack.27.mine_ref), channel_id=1, source_target_pairs={{0,1},{1,0},{2,3},{3,2},{4,5},{5,4},{6,7},{7,6},{8,9},{9,8},{10,11... | collective-permute-start | bytes 2408456 | tf_op jit(solution)/shard_map/ppermute | solution.py:728
  83.8 17.3 %collective-permute-start.17 = (bf16[2,2,256,256]{3,2,1,0:T(8,128)(2,1)}, bf16[2,2,256,256]{3,2,1,0:T(8,128)(2,1)S(1)}, u32[]{:S(2)}, u32[]{:S(2)}) collective-permute-start(bf16[2,2,256,256]{3,2,1,0:T(8,128)(2,1)} %collective-permute-done.12.refs_6_), channel_id=1, source_target_pairs={{0,4},{4,8},{8,12},{1,5},{5,9},{9,13},{2,6},{6,10},{10,14},{3,7},{... | collective-permute-start | bytes 1572872 | tf_op jit(solution)/shard_map/ppermute | solution.py:712
  88.6 16.9 %collective-permute-start.18 = (bf16[2,2,256,256]{3,2,1,0:T(8,128)(2,1)}, bf16[2,2,256,256]{3,2,1,0:T(8,128)(2,1)S(1)}, u32[]{:S(2)}, u32[]{:S(2)}) collective-permute-start(bf16[2,2,256,256]{3,2,1,0:T(8,128)(2,1)} %collective-permute-done.13.refs_8_), channel_id=1, source_target_pairs={{4,0},{8,4},{12,8},{5,1},{9,5},{13,9},{6,2},{10,6},{14,10},{7,3},{... | collective-permute-start | bytes 1572872 | tf_op jit(solution)/shard_map/ppermute | solution.py:713
  90.1 24.0 %collective-permute-start.19 = (bf16[2,2,256,256]{3,2,1,0:T(8,128)(2,1)}, bf16[2,2,256,256]{3,2,1,0:T(8,128)(2,1)S(1)}, u32[]{:S(2)}, u32[]{:S(2)}) collective-permute-start(bf16[2,2,256,256]{3,2,1,0:T(8,128)(2,1)} %collective-permute-done.15.refs_7_), channel_id=1, source_target_pairs={{0,4},{4,8},{8,12},{1,5},{5,9},{9,13},{2,6},{6,10},{10,14},{3,7},{... | collective-permute-start | bytes 1572872 | tf_op jit(solution)/shard_map/ppermute | solution.py:712
  94.7 21.5 %collective-permute-start.20 = (bf16[2,2,256,256]{3,2,1,0:T(8,128)(2,1)}, bf16[2,2,256,256]{3,2,1,0:T(8,128)(2,1)S(1)}, u32[]{:S(2)}, u32[]{:S(2)}) collective-permute-start(bf16[2,2,256,256]{3,2,1,0:T(8,128)(2,1)} %collective-permute-done.16.refs_9_), channel_id=1, source_target_pairs={{4,0},{8,4},{12,8},{5,1},{9,5},{13,9},{6,2},{10,6},{14,10},{7,3},{... | collective-permute-start | bytes 1572872 | tf_op jit(solution)/shard_map/ppermute | solution.py:713
  117.2 6.2 %collective-permute-start.22 = (bf16[192,384]{1,0:T(8,128)(2,1)S(1)}, bf16[192,384]{1,0:T(8,128)(2,1)S(1)}, u32[]{:S(2)}, u32[]{:S(2)}) collective-permute-start(bf16[192,384]{1,0:T(8,128)(2,1)S(1)} %get-tuple-element.64), channel_id=1, source_target_pairs={{0,2},{1,3},{2,0},{3,1},{4,6},{5,7},{6,4},{7,5},{8,10},{9,11},{10,... | collective-permute-start | bytes 442376 | tf_op jit(solution)/shard_map/ppermute | solution.py:762
  121.5 1.4 %collective-permute-start.21 = (bf16[192,384]{1,0:T(8,128)(2,1)S(1)}, bf16[192,384]{1,0:T(8,128)(2,1)S(1)}, u32[]{:S(2)}, u32[]{:S(2)}) collective-permute-start(bf16[192,384]{1,0:T(8,128)(2,1)S(1)} %get-tuple-element.67), channel_id=1, source_target_pairs={{0,1},{1,0},{2,3},{3,2},{4,5},{5,4},{6,7},{7,6},{8,9},{9,8},{10,11... | collective-permute-start | bytes 442376 | tf_op jit(solution)/shard_map/ppermute | solution.py:762
  121.6 5.6 %collective-permute-start.23 = (bf16[192,384]{1,0:T(8,128)(2,1)S(1)}, bf16[192,384]{1,0:T(8,128)(2,1)S(1)}, u32[]{:S(2)}, u32[]{:S(2)}) collective-permute-start(bf16[192,384]{1,0:T(8,128)(2,1)S(1)} %get-tuple-element.68), channel_id=1, source_target_pairs={{0,3},{1,2},{2,1},{3,0},{4,7},{5,6},{6,5},{7,4},{8,11},{9,10},{10,... | collective-permute-start | bytes 442376 | tf_op jit(solution)/shard_map/ppermute | solution.py:762
  (13 other events, 114.7 us)

commit v8 on v7

--- a/solution.py
+++ b/solution.py
@@ -704,7 +704,10 @@
     came = lax.ppermute(sent, "inner", swapped(2, 1))
     routed = route(z.reshape(1), kept, came, row_session, planes, per_plane, slot_cap)
     first, _ = lax.optimization_barrier((first, sent))
-    second, _ = lax.optimization_barrier((second, routed[0]))
+    arrived = [routed[0]] + [
+        lax.ppermute(routed[by], "sess", swapped(planes, by)) for by in range(1, planes)
+    ]
+    second, arrived = lax.optimization_barrier((second, arrived))
     right, left = [first, second], [first, second]
     prompts = {0: (first, second)}
     for hop in range(1, planes):
@@ -716,17 +719,12 @@
     def after(value, hop, chunk):
         return lax.optimization_barrier((value, prompts[-hop][chunk], prompts[hop][chunk]))[0]
 
-    routed = after(tuple(routed), 1, 0)
-    arrived = [routed[0]] + [
-        lax.ppermute(routed[by], "sess", swapped(planes, by)) for by in range(1, planes)
-    ]
-    arrived = after(arrived, 1, 1)
     arrived = stack(*[a[None] for a in arrived])
     other = lax.ppermute(arrived, "inner", swapped(2, 1))
-    other = after(other, 2, 0)
+    other = after(other, 1, 1)
     mine = stack(arrived, other)
     core = lax.ppermute(mine, "rep", swapped(2, 1))
-    core = after(core, 2, 1)
+    core = after(core, 2, 0)
 
     group_width = PER_GROUP * HD
     weight = jnp.concatenate(

time: 131 us -> 117 us (0.89)
  waiting for transfers between devices: 32.7 us -> 25.6 us
  starting transfers between devices: 54.4 us -> 48.6 us
    ppermute x3, starting transfers between devices: 9.1 us -> 4.41 us  [line_body(): lax.ppermute(routed[by], 'sess', swapped(planes, by))]
    ppermute x1, waiting for transfers between devices: 2.23 us -> 0.01 us  [line_body(): other = lax.ppermute(arrived, 'inner', swapped(2, 1))]
    ppermute x3, waiting for transfers between devices: 12.7 us -> 10.6 us  [line_body(): lax.ppermute(routed[by], 'sess', swapped(planes, by))]
    ppermute x3, waiting for transfers between devices: 5.56 us -> 3.98 us  [line_body(): lax.ppermute(attended[by], pair, swapped(4, by))]
    ppermute x6, waiting for transfers between devices: 9.69 us -> 8.12 us  [line_body(): left[chunk] = lax.ppermute(left[chunk], 'sess', shifted(planes, -1))]
    ppermute x6, waiting for transfers between devices: 0.67 us -> 2.02 us  [line_body(): right[chunk] = lax.ppermute(right[chunk], 'sess', shifted(planes, 1))]
  transfers between devices with their start and end apart: 24 -> 24, of which waited for: 11 -> 9; matrix products, arithmetic and copies ran while one was open for 8% -> 9% of each run, Pallas kernels for 19% -> 20%
where the time goes in v8:
time: 117 us; the launch traced here: 116 us
  starting transfers between devices  48.6 us (42%)
  Pallas kernels  30.5 us (26%)
  waiting for transfers between devices  25.6 us (22%)
  local copies, waits for them, and re-layouts  7.23 us (6%)
  matrix products  3.23 us (3%)
    ppermute x6, starting transfers between devices, line_body(): right[chunk] = lax.ppermute(right[chunk], 'sess', shifted(planes, 1))  28.5 us
    pallas_call x3, Pallas kernels, attention_call(): pl.pallas_call(kernel, in_specs=[SMEM] * len(scalars) + [VMEM] * len(arra...  11.4 us
    ppermute x3, waiting for transfers between devices, line_body(): lax.ppermute(routed[by], 'sess', swapped(planes, by))  10.6 us
    ppermute x6, waiting for transfers between devices, line_body(): left[chunk] = lax.ppermute(left[chunk], 'sess', shifted(planes, -1))  8.12 us
    pallas_call x4, Pallas kernels, stack(): pl.pallas_call(stack_kernel, in_specs=[VMEM] * len(arrays), out_specs=VME...  7.75 us
    ppermute x6, starting transfers between devices, line_body(): left[chunk] = lax.ppermute(left[chunk], 'sess', shifted(planes, -1))  7.69 us
    ppermute x3, starting transfers between devices, line_body(): lax.ppermute(routed[by], 'sess', swapped(planes, by))  4.41 us
    pallas_call x1, Pallas kernels, place_rows(): pl.pallas_call(functools.partial(place_kernel, slot_cap=slot_cap, togethe...  4.25 us
  transfers between devices with their start and end apart: 24, of which 9 were waited for; matrix products, arithmetic and copies ran while one was open for 9% of the time, Pallas kernels for 20%

profile of v8, /device:TPU:0, one launch (start us, length us, event | category | flops | bytes accessed | tf_op | source)
XLA Modules:
  0.0 115.9 jit_solution(12138812983416845159)
XLA Ops:
  0.0 2.6 %split_heads.1 = (bf16[2,256,256]{2,1,0:T(8,128)(2,1)}, bf16[2,256,256]{2,1,0:T(8,128)(2,1)}, bf16[2,256,256]{2,1,0:T(8,128)(2,1)}, bf16[2,256,256]{2,1,0:T(8,128)(2,1)}) custom-call(s32[1]{0:T(128)} %bitcast.3.head_ref, bf16[2,256,1024]{2,1,0:T(8,128)(2,1)} %cache_ref.1), custom_call_target="tpu_custom_call" | custom-call | bytes 2097152 | tf_op jit(solution)/shard_map/split_heads/pallas_call | solution.py:308
  2.6 2.9 %collective-permute-start = (bf16[2,256,256]{2,1,0:T(8,128)(2,1)}, bf16[2,256,256]{2,1,0:T(8,128)(2,1)}, u32[]{:S(2)}, u32[]{:S(2)}) collective-permute-start(bf16[2,256,256]{2,1,0:T(8,128)(2,1)} %get-tuple-element.33), channel_id=1, source_target_pairs={{0,2},{1,3},{2,0},{3,1},{4,6},{5,7},{6,4},{7,5},{8,10},{9,11},{10,... | collective-permute-start | bytes 786440 | tf_op jit(solution)/shard_map/ppermute | solution.py:695
  5.7 3.2 %fusion.1 = f32[256,896]{1,0:T(8,128)} fusion(bf16[256,1792]{1,0:T(8,128)(2,1)} %param.13, bf16[1792,896]{1,0:T(8,128)(2,1)S(1)} %copy-done), kind=kOutput, calls=%fused_computation.15 | convolution fusion | flops 822083584 | bytes 5046272 | tf_op jit(solution)/shard_map/dot_general | solution.py:700
  10.1 2.1 %collective-permute-start.2 = (bf16[256,448]{1,0:T(8,128)(2,1)S(1)}, bf16[256,448]{1,0:T(8,128)(2,1)}, u32[]{:S(2)}, u32[]{:S(2)}) collective-permute-start(bf16[256,448]{1,0:T(8,128)(2,1)S(1)} %dynamic-slice_convert_fusion), channel_id=1, source_target_pairs={{0,2},{2,0},{1,3},{3,1},{4,6},{6,4},{5,7},{7,5},{8,10},{10,8},{9,1... | collective-permute-start | bytes 688136 | tf_op jit(solution)/shard_map/ppermute | solution.py:704
  14.1 4.3 %collective-permute-start.11 = (bf16[2,2,256,256]{3,2,1,0:T(8,128)(2,1)}, bf16[2,2,256,256]{3,2,1,0:T(8,128)(2,1)}, u32[]{:S(2)}, u32[]{:S(2)}) collective-permute-start(bf16[2,2,256,256]{3,2,1,0:T(8,128)(2,1)} %stack.27.refs_0_), channel_id=1, source_target_pairs={{0,4},{4,8},{8,12},{1,5},{5,9},{9,13},{2,6},{6,10},{10,14},{3,7},{... | collective-permute-start | bytes 1572872 | tf_op jit(solution)/shard_map/ppermute | solution.py:715
  19.7 2.1 %constant_dynamic-slice_fusion.3.kept_ref = f32[256,448]{1,0:T(8,128)} fusion(f32[256,896]{1,0:T(8,128)} %fusion.1, s32[]{:T(128)S(6)} %select_n.32), kind=kLoop, calls=%fused_computation.9 | loop fusion | bytes 917508 | tf_op jit(solution)/shard_map/dynamic_slice | solution.py:701
  23.4 2.3 %route.1 = (bf16[112,448]{1,0:T(8,128)(2,1)}, bf16[112,448]{1,0:T(8,128)(2,1)}, bf16[112,448]{1,0:T(8,128)(2,1)}, bf16[112,448]{1,0:T(8,128)(2,1)}) custom-call(s32[1]{0:T(128)} %bitcast.z_ref, f32[256,448]{1,0:T(8,128)} %constant_dynamic-slice_fusion.3.kept_ref, bf16[256,448]{1,0:T(8,128)(2,1)} %collective-permute-done.2.came_ref, ...), custom_call_target="tpu_custom_call" | custom-call | flops 102760448 | bytes 917504 | tf_op jit(solution)/shard_map/route/pallas_call | solution.py:373
  27.5 2.6 %collective-permute-start.4 = (bf16[112,448]{1,0:T(8,128)(2,1)}, bf16[112,448]{1,0:T(8,128)(2,1)S(1)}, u32[]{:S(2)}, u32[]{:S(2)}) collective-permute-start(bf16[112,448]{1,0:T(8,128)(2,1)} %get-tuple-element.39), channel_id=1, source_target_pairs={{0,8},{4,12},{8,0},{12,4},{1,9},{5,13},{9,1},{13,5},{2,10},{6,14},... | collective-permute-start | bytes 301064 | tf_op jit(solution)/shard_map/ppermute | solution.py:708
  32.0 6.2 %collective-permute-done.3 = bf16[112,448]{1,0:T(8,128)(2,1)S(1)} collective-permute-done((bf16[112,448]{1,0:T(8,128)(2,1)}, bf16[112,448]{1,0:T(8,128)(2,1)S(1)}, u32[]{:S(2)}, u32[]{:S(2)}) %collective-permute-start.3) | collective-permute-done | bytes 100384 | tf_op jit(solution)/shard_map/ppermute | solution.py:708
  38.1 4.4 %collective-permute-done.4 = bf16[112,448]{1,0:T(8,128)(2,1)S(1)} collective-permute-done((bf16[112,448]{1,0:T(8,128)(2,1)}, bf16[112,448]{1,0:T(8,128)(2,1)S(1)}, u32[]{:S(2)}, u32[]{:S(2)}) %collective-permute-start.4) | collective-permute-done | bytes 100384 | tf_op jit(solution)/shard_map/ppermute | solution.py:708
  42.6 4.5 %collective-permute-start.7 = (bf16[2,2,256,256]{3,2,1,0:T(8,128)(2,1)}, bf16[2,2,256,256]{3,2,1,0:T(8,128)(2,1)}, u32[]{:S(2)}, u32[]{:S(2)}) collective-permute-start(bf16[2,2,256,256]{3,2,1,0:T(8,128)(2,1)} %stack.24.refs_1_), channel_id=1, source_target_pairs={{0,4},{4,8},{8,12},{1,5},{5,9},{9,13},{2,6},{6,10},{10,14},{3,7},{... | collective-permute-start | bytes 1572872 | tf_op jit(solution)/shard_map/ppermute | solution.py:715
  48.4 1.9 %stack.25.refs_0_ = bf16[4,112,448]{2,1,0:T(8,128)(2,1)} custom-call(bf16[1,112,448]{2,1,0:T(8,128)(2,1)} %bitcast.16, bf16[1,112,448]{2,1,0:T(8,128)(2,1)} %bitcast.17, bf16[1,112,448]{2,1,0:T(8,128)(2,1)} %bitcast.18, bf16[1,112,448]{2,1,0:T(8,128)(2,1)} %bitcast.19), custom_call_target="tpu_custom_call" | custom-call | bytes 802816 | tf_op jit(solution)/shard_map/stack/pallas_call | solution.py:330
  50.8 5.4 %collective-permute-start.12 = (bf16[2,2,256,256]{3,2,1,0:T(8,128)(2,1)}, bf16[2,2,256,256]{3,2,1,0:T(8,128)(2,1)}, u32[]{:S(2)}, u32[]{:S(2)}) collective-permute-start(bf16[2,2,256,256]{3,2,1,0:T(8,128)(2,1)} %collective-permute-done.11.refs_2_), channel_id=1, source_target_pairs={{0,4},{4,8},{8,12},{1,5},{5,9},{9,13},{2,6},{6,10},{10,14},{3,7},{... | collective-permute-start | bytes 1572872 | tf_op jit(solution)/shard_map/ppermute | solution.py:715
  57.4 5.4 %collective-permute-start.17 = (bf16[2,2,256,256]{3,2,1,0:T(8,128)(2,1)}, bf16[2,2,256,256]{3,2,1,0:T(8,128)(2,1)}, u32[]{:S(2)}, u32[]{:S(2)}) collective-permute-start(bf16[2,2,256,256]{3,2,1,0:T(8,128)(2,1)} %collective-permute-done.7.refs_3_), channel_id=1, source_target_pairs={{0,4},{4,8},{8,12},{1,5},{5,9},{9,13},{2,6},{6,10},{10,14},{3,7},{... | collective-permute-start | bytes 1572872 | tf_op jit(solution)/shard_map/ppermute | solution.py:715
  64.8 2.2 %stack.26.mine_ref = bf16[8,112,448]{2,1,0:T(8,128)(2,1)} custom-call(bf16[4,112,448]{2,1,0:T(8,128)(2,1)} %stack.25.refs_0_, bf16[4,112,448]{2,1,0:T(8,128)(2,1)} %collective-permute-done.6.refs_1_), custom_call_target="tpu_custom_call" | custom-call | bytes 1605632 | tf_op jit(solution)/shard_map/stack/pallas_call | solution.py:330
  69.6 4.6 %collective-permute-start.15 = (bf16[2,2,256,256]{3,2,1,0:T(8,128)(2,1)}, bf16[2,2,256,256]{3,2,1,0:T(8,128)(2,1)S(1)}, u32[]{:S(2)}, u32[]{:S(2)}) collective-permute-start(bf16[2,2,256,256]{3,2,1,0:T(8,128)(2,1)} %collective-permute-done.12.refs_6_), channel_id=1, source_target_pairs={{0,4},{4,8},{8,12},{1,5},{5,9},{9,13},{2,6},{6,10},{10,14},{3,7},{... | collective-permute-start | bytes 1572872 | tf_op jit(solution)/shard_map/ppermute | solution.py:715
  75.7 2.0 %collective-permute-done.17.refs_7_ = bf16[2,2,256,256]{3,2,1,0:T(8,128)(2,1)} collective-permute-done((bf16[2,2,256,256]{3,2,1,0:T(8,128)(2,1)}, bf16[2,2,256,256]{3,2,1,0:T(8,128)(2,1)}, u32[]{:S(2)}, u32[]{:S(2)}) %collective-permute-start.17) | collective-permute-done | bytes 524320 | tf_op jit(solution)/shard_map/ppermute | solution.py:715
  77.7 4.4 %collective-permute-start.19 = (bf16[2,2,256,256]{3,2,1,0:T(8,128)(2,1)}, bf16[2,2,256,256]{3,2,1,0:T(8,128)(2,1)S(1)}, u32[]{:S(2)}, u32[]{:S(2)}) collective-permute-start(bf16[2,2,256,256]{3,2,1,0:T(8,128)(2,1)} %collective-permute-done.17.refs_7_), channel_id=1, source_target_pairs={{0,4},{4,8},{8,12},{1,5},{5,9},{9,13},{2,6},{6,10},{10,14},{3,7},{... | collective-permute-start | bytes 1572872 | tf_op jit(solution)/shard_map/ppermute | solution.py:715
  84.8 4.2 %place_rows.1 = (bf16[768,896]{1,0:T(8,128)(2,1)S(1)}, bf16[768,384]{1,0:T(8,128)(2,1)S(1)}, bf16[768,128]{1,0:T(8,128)(2,1)S(1)}, bf16[768,128]{1,0:T(8,128)(2,1)S(1)}, s32[1,128]{1,0:T(1,128)S(1)}) custom-call(s32[4]{0:T(128)S(1)} %pad_add_fusion.index_ref, bf16[8,112,448]{2,1,0:T(8,128)(2,1)S(1)} %copy-done.4, ...), custom_call_target="tpu_custom_call" | custom-call | flops 1761607680 | bytes 6291456 | tf_op jit(solution)/shard_map/place_rows/pallas_call | solution.py:465
  89.1 5.4 %collective-permute-done.16.refs_2_ = bf16[2,2,256,256]{3,2,1,0:T(8,128)(2,1)S(1)} collective-permute-done((bf16[2,2,256,256]{3,2,1,0:T(8,128)(2,1)}, bf16[2,2,256,256]{3,2,1,0:T(8,128)(2,1)S(1)}, u32[]{:S(2)}, u32[]{:S(2)}) %collective-permute-start.16) | collective-permute-done | bytes 524320 | tf_op jit(solution)/shard_map/ppermute | solution.py:716
  94.5 7.7 %near.1.near_ref = bf16[768,384]{1,0:T(8,128)(2,1)S(1)} custom-call(s32[8]{0:T(128)S(1)} %get-tuple-element.62.hop_ref, s32[8]{0:T(128)S(1)} %get-tuple-element.61.held_ref, s32[1,128]{1,0:T(1,128)S(1)} %get-tuple-element.50.length_ref, bf16[768,384]{1,0:T(8,128)(2,1)S(1)} %get-tuple-element.55.query_ref, bf16[768,128]{1,0:T(8,128)(2,1)S(1)} %get-tuple-element.53.key_ref, ...), custom_call_target="tpu_custom_call" | custom-call | flops 660602880 | bytes 2097152 | tf_op jit(solution)/shard_map/near/pallas_call | solution.py:588
  103.6 1.9 %far.2 = (bf16[192,384]{1,0:T(8,128)(2,1)S(1)}, bf16[192,384]{1,0:T(8,128)(2,1)S(1)}) custom-call(s32[4]{0:T(128)S(1)} %pad_add_fusion.index_ref, s32[8]{0:T(128)S(1)} %get-tuple-element.62.hop_ref, s32[8]{0:T(128)S(1)} %get-tuple-element.61.held_ref, s32[1,128]{1,0:T(1,128)S(1)} %get-tuple-element.50.length_ref, ...), custom_call_target="tpu_custom_call" | custom-call | flops 330301440 | bytes 1048576 | tf_op jit(solution)/shard_map/far/pallas_call | solution.py:588
  110.8 2.8 %collective-permute-done.23.refs_3_ = bf16[192,384]{1,0:T(8,128)(2,1)S(1)} collective-permute-done((bf16[192,384]{1,0:T(8,128)(2,1)S(1)}, bf16[192,384]{1,0:T(8,128)(2,1)S(1)}, u32[]{:S(2)}, u32[]{:S(2)}) %collective-permute-start.23) | collective-permute-done | bytes 147488 | tf_op jit(solution)/shard_map/ppermute | solution.py:760
  113.7 2.2 %output.1 = bf16[2,96,896]{2,1,0:T(8,128)(2,1)} custom-call(s32[4]{0:T(128)S(1)} %pad_add_fusion.index_ref, s32[1,128]{1,0:T(1,128)S(1)} %get-tuple-element.50.length_ref, bf16[768,896]{1,0:T(8,128)(2,1)S(1)} %get-tuple-element.51.states_ref, bf16[1536,896]{1,0:T(8,128)(2,1)S(1)} %copy-done.1, bf16[192,384]{1,0:T(8,128)(2,1)S(1)} %get-tuple-element.58.refs_0_, ...), custom_call_target="tpu_custom_call" | custom-call | flops 528482304 | bytes 2752512 | tf_op jit(solution)/shard_map/output/pallas_call | solution.py:645
  (73 shorter events, 28.2 us)
Async XLA Ops:
  2.6 24.9 %collective-permute-start = (bf16[2,256,256]{2,1,0:T(8,128)(2,1)}, bf16[2,256,256]{2,1,0:T(8,128)(2,1)}, u32[]{:S(2)}, u32[]{:S(2)}) collective-permute-start(bf16[2,256,256]{2,1,0:T(8,128)(2,1)} %get-tuple-element.33), channel_id=1, source_target_pairs={{0,2},{1,3},{2,0},{3,1},{4,6},{5,7},{6,4},{7,5},{8,10},{9,11},{10,... | collective-permute-start | bytes 786440 | tf_op jit(solution)/shard_map/ppermute | solution.py:695
  5.6 24.6 %collective-permute-start.1 = (bf16[2,256,256]{2,1,0:T(8,128)(2,1)}, bf16[2,256,256]{2,1,0:T(8,128)(2,1)}, u32[]{:S(2)}, u32[]{:S(2)}) collective-permute-start(bf16[2,256,256]{2,1,0:T(8,128)(2,1)} %get-tuple-element.34), channel_id=1, source_target_pairs={{0,3},{1,2},{2,1},{3,0},{4,7},{5,6},{6,5},{7,4},{8,11},{9,10},{10,... | collective-permute-start | bytes 786440 | tf_op jit(solution)/shard_map/ppermute | solution.py:696
  5.6 6.7 %collective-permute-start.10 = (bf16[2,256,256]{2,1,0:T(8,128)(2,1)}, bf16[2,256,256]{2,1,0:T(8,128)(2,1)}, u32[]{:S(2)}, u32[]{:S(2)}) collective-permute-start(bf16[2,256,256]{2,1,0:T(8,128)(2,1)} %get-tuple-element.35), channel_id=1, source_target_pairs={{0,1},{1,0},{2,3},{3,2},{4,5},{5,4},{6,7},{7,6},{8,9},{9,8},{10,11... | collective-permute-start | bytes 786440 | tf_op jit(solution)/shard_map/ppermute | solution.py:694
  10.1 13.3 %collective-permute-start.2 = (bf16[256,448]{1,0:T(8,128)(2,1)S(1)}, bf16[256,448]{1,0:T(8,128)(2,1)}, u32[]{:S(2)}, u32[]{:S(2)}) collective-permute-start(bf16[256,448]{1,0:T(8,128)(2,1)S(1)} %dynamic-slice_convert_fusion), channel_id=1, source_target_pairs={{0,2},{2,0},{1,3},{3,1},{4,6},{6,4},{5,7},{7,5},{8,10},{10,8},{9,1... | collective-permute-start | bytes 688136 | tf_op jit(solution)/shard_map/ppermute | solution.py:704
  14.1 36.7 %collective-permute-start.11 = (bf16[2,2,256,256]{3,2,1,0:T(8,128)(2,1)}, bf16[2,2,256,256]{3,2,1,0:T(8,128)(2,1)}, u32[]{:S(2)}, u32[]{:S(2)}) collective-permute-start(bf16[2,2,256,256]{3,2,1,0:T(8,128)(2,1)} %stack.27.refs_0_), channel_id=1, source_target_pairs={{0,4},{4,8},{8,12},{1,5},{5,9},{9,13},{2,6},{6,10},{10,14},{3,7},{... | collective-permute-start | bytes 1572872 | tf_op jit(solution)/shard_map/ppermute | solution.py:715
  18.4 37.8 %collective-permute-start.13 = (bf16[2,2,256,256]{3,2,1,0:T(8,128)(2,1)}, bf16[2,2,256,256]{3,2,1,0:T(8,128)(2,1)}, u32[]{:S(2)}, u32[]{:S(2)}) collective-permute-start(bf16[2,2,256,256]{3,2,1,0:T(8,128)(2,1)} %stack.27.refs_0_), channel_id=1, source_target_pairs={{4,0},{8,4},{12,8},{5,1},{9,5},{13,9},{6,2},{10,6},{14,10},{7,3},{... | collective-permute-start | bytes 1572872 | tf_op jit(solution)/shard_map/ppermute | solution.py:716
  25.7 12.4 %collective-permute-start.3 = (bf16[112,448]{1,0:T(8,128)(2,1)}, bf16[112,448]{1,0:T(8,128)(2,1)S(1)}, u32[]{:S(2)}, u32[]{:S(2)}) collective-permute-start(bf16[112,448]{1,0:T(8,128)(2,1)} %get-tuple-element.38), channel_id=1, source_target_pairs={{0,4},{4,0},{8,12},{12,8},{1,5},{5,1},{9,13},{13,9},{2,6},{6,2},{1... | collective-permute-start | bytes 301064 | tf_op jit(solution)/shard_map/ppermute | solution.py:708
  27.5 15.1 %collective-permute-start.4 = (bf16[112,448]{1,0:T(8,128)(2,1)}, bf16[112,448]{1,0:T(8,128)(2,1)S(1)}, u32[]{:S(2)}, u32[]{:S(2)}) collective-permute-start(bf16[112,448]{1,0:T(8,128)(2,1)} %get-tuple-element.39), channel_id=1, source_target_pairs={{0,8},{4,12},{8,0},{12,4},{1,9},{5,13},{9,1},{13,5},{2,10},{6,14},... | collective-permute-start | bytes 301064 | tf_op jit(solution)/shard_map/ppermute | solution.py:708
  30.1 12.5 %collective-permute-start.5 = (bf16[112,448]{1,0:T(8,128)(2,1)}, bf16[112,448]{1,0:T(8,128)(2,1)S(1)}, u32[]{:S(2)}, u32[]{:S(2)}) collective-permute-start(bf16[112,448]{1,0:T(8,128)(2,1)} %get-tuple-element.40), channel_id=1, source_target_pairs={{0,12},{4,8},{8,4},{12,0},{1,13},{5,9},{9,5},{13,1},{2,14},{6,10},... | collective-permute-start | bytes 301064 | tf_op jit(solution)/shard_map/ppermute | solution.py:708
  42.6 14.8 %collective-permute-start.7 = (bf16[2,2,256,256]{3,2,1,0:T(8,128)(2,1)}, bf16[2,2,256,256]{3,2,1,0:T(8,128)(2,1)}, u32[]{:S(2)}, u32[]{:S(2)}) collective-permute-start(bf16[2,2,256,256]{3,2,1,0:T(8,128)(2,1)} %stack.24.refs_1_), channel_id=1, source_target_pairs={{0,4},{4,8},{8,12},{1,5},{5,9},{9,13},{2,6},{6,10},{10,14},{3,7},{... | collective-permute-start | bytes 1572872 | tf_op jit(solution)/shard_map/ppermute | solution.py:715
  47.1 15.7 %collective-permute-start.8 = (bf16[2,2,256,256]{3,2,1,0:T(8,128)(2,1)}, bf16[2,2,256,256]{3,2,1,0:T(8,128)(2,1)}, u32[]{:S(2)}, u32[]{:S(2)}) collective-permute-start(bf16[2,2,256,256]{3,2,1,0:T(8,128)(2,1)} %stack.24.refs_1_), channel_id=1, source_target_pairs={{4,0},{8,4},{12,8},{5,1},{9,5},{13,9},{6,2},{10,6},{14,10},{7,3},{... | collective-permute-start | bytes 1572872 | tf_op jit(solution)/shard_map/ppermute | solution.py:716
  50.3 14.5 %collective-permute-start.6 = (bf16[4,112,448]{2,1,0:T(8,128)(2,1)}, bf16[4,112,448]{2,1,0:T(8,128)(2,1)}, u32[]{:S(2)}, u32[]{:S(2)}) collective-permute-start(bf16[4,112,448]{2,1,0:T(8,128)(2,1)} %stack.25.refs_0_), channel_id=1, source_target_pairs={{0,2},{2,0},{1,3},{3,1},{4,6},{6,4},{5,7},{7,5},{8,10},{10,8},{9,1... | collective-permute-start | bytes 1204232 | tf_op jit(solution)/shard_map/ppermute | solution.py:723
  50.8 18.8 %collective-permute-start.12 = (bf16[2,2,256,256]{3,2,1,0:T(8,128)(2,1)}, bf16[2,2,256,256]{3,2,1,0:T(8,128)(2,1)}, u32[]{:S(2)}, u32[]{:S(2)}) collective-permute-start(bf16[2,2,256,256]{3,2,1,0:T(8,128)(2,1)} %collective-permute-done.11.refs_2_), channel_id=1, source_target_pairs={{0,4},{4,8},{8,12},{1,5},{5,9},{9,13},{2,6},{6,10},{10,14},{3,7},{... | collective-permute-start | bytes 1572872 | tf_op jit(solution)/shard_map/ppermute | solution.py:715
  56.1 18.1 %collective-permute-start.14 = (bf16[2,2,256,256]{3,2,1,0:T(8,128)(2,1)}, bf16[2,2,256,256]{3,2,1,0:T(8,128)(2,1)}, u32[]{:S(2)}, u32[]{:S(2)}) collective-permute-start(bf16[2,2,256,256]{3,2,1,0:T(8,128)(2,1)} %collective-permute-done.13.refs_4_), channel_id=1, source_target_pairs={{4,0},{8,4},{12,8},{5,1},{9,5},{13,9},{6,2},{10,6},{14,10},{7,3},{... | collective-permute-start | bytes 1572872 | tf_op jit(solution)/shard_map/ppermute | solution.py:716
  57.4 20.3 %collective-permute-start.17 = (bf16[2,2,256,256]{3,2,1,0:T(8,128)(2,1)}, bf16[2,2,256,256]{3,2,1,0:T(8,128)(2,1)}, u32[]{:S(2)}, u32[]{:S(2)}) collective-permute-start(bf16[2,2,256,256]{3,2,1,0:T(8,128)(2,1)} %collective-permute-done.7.refs_3_), channel_id=1, source_target_pairs={{0,4},{4,8},{8,12},{1,5},{5,9},{9,13},{2,6},{6,10},{10,14},{3,7},{... | collective-permute-start | bytes 1572872 | tf_op jit(solution)/shard_map/ppermute | solution.py:715
  62.8 20.6 %collective-permute-start.18 = (bf16[2,2,256,256]{3,2,1,0:T(8,128)(2,1)}, bf16[2,2,256,256]{3,2,1,0:T(8,128)(2,1)}, u32[]{:S(2)}, u32[]{:S(2)}) collective-permute-start(bf16[2,2,256,256]{3,2,1,0:T(8,128)(2,1)} %collective-permute-done.8.refs_5_), channel_id=1, source_target_pairs={{4,0},{8,4},{12,8},{5,1},{9,5},{13,9},{6,2},{10,6},{14,10},{7,3},{... | collective-permute-start | bytes 1572872 | tf_op jit(solution)/shard_map/ppermute | solution.py:716
  67.0 17.8 %collective-permute-start.9 = (bf16[8,112,448]{2,1,0:T(8,128)(2,1)}, bf16[8,112,448]{2,1,0:T(8,128)(2,1)S(1)}, u32[]{:S(2)}, u32[]{:S(2)}) collective-permute-start(bf16[8,112,448]{2,1,0:T(8,128)(2,1)} %stack.26.mine_ref), channel_id=1, source_target_pairs={{0,1},{1,0},{2,3},{3,2},{4,5},{5,4},{6,7},{7,6},{8,9},{9,8},{10,11... | collective-permute-start | bytes 2408456 | tf_op jit(solution)/shard_map/ppermute | solution.py:726
  69.6 19.5 %collective-permute-start.15 = (bf16[2,2,256,256]{3,2,1,0:T(8,128)(2,1)}, bf16[2,2,256,256]{3,2,1,0:T(8,128)(2,1)S(1)}, u32[]{:S(2)}, u32[]{:S(2)}) collective-permute-start(bf16[2,2,256,256]{3,2,1,0:T(8,128)(2,1)} %collective-permute-done.12.refs_6_), channel_id=1, source_target_pairs={{0,4},{4,8},{8,12},{1,5},{5,9},{9,13},{2,6},{6,10},{10,14},{3,7},{... | collective-permute-start | bytes 1572872 | tf_op jit(solution)/shard_map/ppermute | solution.py:715
  74.2 20.3 %collective-permute-start.16 = (bf16[2,2,256,256]{3,2,1,0:T(8,128)(2,1)}, bf16[2,2,256,256]{3,2,1,0:T(8,128)(2,1)S(1)}, u32[]{:S(2)}, u32[]{:S(2)}) collective-permute-start(bf16[2,2,256,256]{3,2,1,0:T(8,128)(2,1)} %collective-permute-done.14.refs_8_), channel_id=1, source_target_pairs={{4,0},{8,4},{12,8},{5,1},{9,5},{13,9},{6,2},{10,6},{14,10},{7,3},{... | collective-permute-start | bytes 1572872 | tf_op jit(solution)/shard_map/ppermute | solution.py:716
  77.7 24.5 %collective-permute-start.19 = (bf16[2,2,256,256]{3,2,1,0:T(8,128)(2,1)}, bf16[2,2,256,256]{3,2,1,0:T(8,128)(2,1)S(1)}, u32[]{:S(2)}, u32[]{:S(2)}) collective-permute-start(bf16[2,2,256,256]{3,2,1,0:T(8,128)(2,1)} %collective-permute-done.17.refs_7_), channel_id=1, source_target_pairs={{0,4},{4,8},{8,12},{1,5},{5,9},{9,13},{2,6},{6,10},{10,14},{3,7},{... | collective-permute-start | bytes 1572872 | tf_op jit(solution)/shard_map/ppermute | solution.py:715
  83.4 20.3 %collective-permute-start.20 = (bf16[2,2,256,256]{3,2,1,0:T(8,128)(2,1)}, bf16[2,2,256,256]{3,2,1,0:T(8,128)(2,1)S(1)}, u32[]{:S(2)}, u32[]{:S(2)}) collective-permute-start(bf16[2,2,256,256]{3,2,1,0:T(8,128)(2,1)} %collective-permute-done.18.refs_9_), channel_id=1, source_target_pairs={{4,0},{8,4},{12,8},{5,1},{9,5},{13,9},{6,2},{10,6},{14,10},{7,3},{... | collective-permute-start | bytes 1572872 | tf_op jit(solution)/shard_map/ppermute | solution.py:716
  105.6 5.2 %collective-permute-start.22 = (bf16[192,384]{1,0:T(8,128)(2,1)S(1)}, bf16[192,384]{1,0:T(8,128)(2,1)S(1)}, u32[]{:S(2)}, u32[]{:S(2)}) collective-permute-start(bf16[192,384]{1,0:T(8,128)(2,1)S(1)} %get-tuple-element.56), channel_id=1, source_target_pairs={{0,2},{1,3},{2,0},{3,1},{4,6},{5,7},{6,4},{7,5},{8,10},{9,11},{10,... | collective-permute-start | bytes 442376 | tf_op jit(solution)/shard_map/ppermute | solution.py:760
  107.9 1.7 %collective-permute-start.21 = (bf16[192,384]{1,0:T(8,128)(2,1)S(1)}, bf16[192,384]{1,0:T(8,128)(2,1)S(1)}, u32[]{:S(2)}, u32[]{:S(2)}) collective-permute-start(bf16[192,384]{1,0:T(8,128)(2,1)S(1)} %get-tuple-element.59), channel_id=1, source_target_pairs={{0,1},{1,0},{2,3},{3,2},{4,5},{5,4},{6,7},{7,6},{8,9},{9,8},{10,11... | collective-permute-start | bytes 442376 | tf_op jit(solution)/shard_map/ppermute | solution.py:760
  108.0 5.6 %collective-permute-start.23 = (bf16[192,384]{1,0:T(8,128)(2,1)S(1)}, bf16[192,384]{1,0:T(8,128)(2,1)S(1)}, u32[]{:S(2)}, u32[]{:S(2)}) collective-permute-start(bf16[192,384]{1,0:T(8,128)(2,1)S(1)} %get-tuple-element.60), channel_id=1, source_target_pairs={{0,3},{1,2},{2,1},{3,0},{4,7},{5,6},{6,5},{7,4},{8,11},{9,10},{10,... | collective-permute-start | bytes 442376 | tf_op jit(solution)/shard_map/ppermute | solution.py:760
  (13 other events, 138.5 us)

commit v9 on v8

--- a/solution.py
+++ b/solution.py
@@ -337,20 +337,48 @@
     )(*arrays)
 
 
-def route_kernel(z_ref, kept_ref, came_ref, owner_ref, owner_row_ref, *out_refs,
+def project_kernel(index_ref, rows_ref, weight_ref, kept_ref, sent_ref):
+    width = kept_ref.shape[1]
+    partial_sum = jnp.dot(rows_ref[...], weight_ref[...], preferred_element_type=jnp.float32)
+    low, high = partial_sum[:, :width], partial_sum[:, width:]
+    is_low = index_ref[1] == 0
+    kept_ref[...] = jnp.where(is_low, low, high)
+    sent_ref[...] = jnp.where(is_low, high, low).astype(jnp.bfloat16)
+
+
+def project(index, rows, weight):
+    count, width = rows.shape[0], weight.shape[1] // 2
+    return pl.pallas_call(
+        project_kernel,
+        in_specs=[SMEM, VMEM, VMEM],
+        out_specs=[VMEM] * 2,
+        out_shape=[
+            jax.ShapeDtypeStruct((count, width), jnp.float32),
+            jax.ShapeDtypeStruct((count, width), jnp.bfloat16),
+        ],
+        compiler_params=pltpu.CompilerParams(vmem_limit_bytes=40 << 20),
+        cost_estimate=pl.CostEstimate(
+            flops=2 * count * weight.size, bytes_accessed=2 * (rows.size + weight.size), transcendentals=0
+        ),
+        name="project",
+    )(index, rows, weight)
+
+
+def route_kernel(index_ref, kept_ref, came_ref, owner_ref, *out_refs,
                  slot_cap, per_plane):
     rows = kept_ref.shape[0]
     planes = len(out_refs)
     size = out_refs[0].shape[0]
     live = per_plane * slot_cap
     columns = (kept_ref[...] + came_ref[...].astype(jnp.float32)).astype(jnp.bfloat16)
-    owner, owner_row = owner_ref[...], owner_row_ref[...]
+    owner_row = owner_ref[...]
     above = lax.broadcasted_iota(jnp.int32, (rows, rows), 0)
     beside = lax.broadcasted_iota(jnp.int32, (rows, rows), 1)
+    owner = jnp.sum(jnp.where(above == beside, owner_row, 0), axis=1, keepdims=True)
     earlier = jnp.sum(
         jnp.where((owner == owner_row) & (above < beside), 1.0, 0.0), axis=0, keepdims=True
     ).astype(jnp.int32)
-    target = lax.div(owner_row, per_plane) ^ z_ref[0]
+    target = lax.div(owner_row, per_plane) ^ index_ref[0]
     code = target * size + lax.rem(owner_row, per_plane) * slot_cap + earlier
     place = lax.broadcasted_iota(jnp.int32, (planes * size, rows), 0)
     into = (place == code).astype(jnp.bfloat16)
@@ -366,35 +394,36 @@
         out_ref[live:, :HD] = counts
 
 
-def route(z, kept, came, row_session, planes, per_plane, slot_cap):
+def route(index, kept, came, row_session, planes, per_plane, slot_cap):
     width = kept.shape[1]
     rows = row_session.shape[0]
     size = per_plane * slot_cap + EXTRA
     return pl.pallas_call(
         functools.partial(route_kernel, slot_cap=slot_cap, per_plane=per_plane),
-        in_specs=[SMEM] + [VMEM] * 4,
+        in_specs=[SMEM] + [VMEM] * 3,
         out_specs=[VMEM] * planes,
         out_shape=[jax.ShapeDtypeStruct((size, width), jnp.bfloat16)] * planes,
         cost_estimate=pl.CostEstimate(
             flops=2 * planes * size * rows * width, bytes_accessed=rows * width * 8, transcendentals=0
         ),
         name="route",
-    )(z, kept, came, row_session, row_session.reshape(1, rows))
-
-
-def place_kernel(index_ref, mine_ref, core_ref, gain_ref, weight_ref, cos_ref, sin_ref,
-                 states_ref, query_ref, key_ref, value_ref, length_ref, *, slot_cap, together):
-    z, x, c = index_ref[0], index_ref[1], index_ref[2]
-    planes = mine_ref.shape[0] // 2
+    )(index, kept, came, row_session.reshape(1, rows))
+
+
+def place_kernel(index_ref, near_ref, far_ref, near_core_ref, far_core_ref, gain_ref,
+                 q_ref, k_ref, v_ref, cos_ref, sin_ref, states_ref, query_ref, key_ref, value_ref, length_ref, *, slot_cap, together):
+    z, x, c, head = [index_ref[i] for i in range(4)]
+    planes, live, width = near_ref.shape
     blocks = 2 * planes
-    width = mine_ref.shape[2]
-    live = mine_ref.shape[1] - EXTRA
+    live = live - EXTRA
+    columns = pl.ds(pl.multiple_of(head * HD, HD), HD)
+    group_columns = pl.ds(pl.multiple_of(head * PER_GROUP * HD, HD), PER_GROUP * HD)
     per_plane = live // slot_cap
     steps = per_plane // together
     window = together * slot_cap
     total = together * SLOTS
     counts = jnp.concatenate(
-        [ref[k, live : live + 1, :HD] for ref in (mine_ref, core_ref) for k in range(planes)],
+        [ref[k, live : live + 1, :HD] for ref in (near_ref, near_core_ref) for k in range(planes)],
         axis=0,
     ).astype(jnp.float32)
     kind = lambda axis: lax.broadcasted_iota(jnp.int32, (blocks, blocks), axis)
@@ -431,12 +460,11 @@
             jnp.dot(
                 pick,
                 jnp.concatenate(
-                    [ref[half * planes + k, slots] for ref in (mine_ref, core_ref) for k in range(planes)],
-                    axis=0,
+                    [ref[k, slots] for ref in refs for k in range(planes)], axis=0
                 ),
                 preferred_element_type=jnp.float32,
             )
-            for half in range(2)
+            for refs in ((near_ref, near_core_ref), (far_ref, far_core_ref))
         ]
         widened = jnp.concatenate(
             [jnp.where(x == 0, near, far), jnp.where(x == 0, far, near)], axis=1
@@ -445,26 +473,28 @@
         states_ref[rows] = widened.astype(jnp.bfloat16)
         factor = lax.rsqrt(jnp.mean(widened * widened, axis=-1, keepdims=True) + EPSILON)
         normed = (widened * factor * gain).astype(jnp.bfloat16)
-        both = jnp.dot(normed, weight_ref[...], preferred_element_type=jnp.float32)
+        queries = jnp.dot(normed, q_ref[:, group_columns], preferred_element_type=jnp.float32)
+        keys = jnp.dot(normed, k_ref[:, columns], preferred_element_type=jnp.float32)
         for h in range(PER_GROUP + 1):
-            vector = both[:, h * HD : (h + 1) * HD]
+            vector = keys if h == PER_GROUP else queries[:, h * HD : (h + 1) * HD]
             turned = vector * cosine + pltpu.roll(vector, HD // 2, 1) * sine
             if h < PER_GROUP:
                 query_ref[rows, h * HD : (h + 1) * HD] = turned.astype(jnp.bfloat16)
             else:
                 key_ref[rows] = turned.astype(jnp.bfloat16)
-        value_ref[rows] = both[:, (PER_GROUP + 1) * HD :].astype(jnp.bfloat16)
-
-
-def place_rows(index, mine, core, gain, weight, sessions, slot_cap):
+        values = jnp.dot(normed, v_ref[:, columns], preferred_element_type=jnp.float32)
+        value_ref[rows] = values.astype(jnp.bfloat16)
+
+
+def place_rows(index, slots, gain, weights, sessions, slot_cap):
     together = 16 // math.gcd(16, slot_cap)
     cosine, sine = rope_tables(together)
-    model = 2 * mine.shape[2]
+    model = 2 * slots[0].shape[2]
     total = sessions * SLOTS
     out = lambda w: jax.ShapeDtypeStruct((total, w), jnp.bfloat16)
     return pl.pallas_call(
         functools.partial(place_kernel, slot_cap=slot_cap, together=together),
-        in_specs=[SMEM] + [VMEM] * 6,
+        in_specs=[SMEM] + [VMEM] * 10,
         out_specs=[VMEM] * 5,
         out_shape=[
             out(model), out(PER_GROUP * HD), out(HD), out(HD),
@@ -472,10 +502,10 @@
         ],
         compiler_params=pltpu.CompilerParams(vmem_limit_bytes=40 << 20),
         cost_estimate=pl.CostEstimate(
-            flops=4 * total * model * weight.shape[1], bytes_accessed=6 << 20, transcendentals=0
+            flops=4 * total * model * 5 * HD, bytes_accessed=6 << 20, transcendentals=0
         ),
         name="place_rows",
-    )(index, mine, core, gain.reshape(1, model), weight, jnp.asarray(cosine), jnp.asarray(sine))
+    )(index, *slots, gain.reshape(1, model), *weights, jnp.asarray(cosine), jnp.asarray(sine))
 
 
 def session_attention(query, key, value, tokens, length):
@@ -690,20 +720,18 @@
     index = jnp.stack([z, x, c, head]).astype(jnp.int32)
     pair = ("inner", "rep")
 
+    kept, sent = project(index, thinker_rows, proj_weight)
+    came = lax.ppermute(sent, "inner", swapped(2, 1))
+
     own, to_core, to_x, to_far = split_heads(head.reshape(1), prompt_cache)
     from_core = lax.ppermute(to_core, pair, swapped(4, 1))
     from_x = lax.ppermute(to_x, pair, swapped(4, 2))
     from_far = lax.ppermute(to_far, pair, swapped(4, 3))
     first = stack(own[None], from_core[None])
     second = stack(from_x[None], from_far[None])
-    thinker_rows, _ = lax.optimization_barrier((thinker_rows, to_core))
-    partial_sum = jnp.dot(thinker_rows, proj_weight, preferred_element_type=jnp.float32)
-    kept = lax.dynamic_slice_in_dim(partial_sum, x * width, width, 1)
-    sent = lax.dynamic_slice_in_dim(partial_sum, (1 - x) * width, width, 1)
-    sent = sent.astype(jnp.bfloat16)
-    came = lax.ppermute(sent, "inner", swapped(2, 1))
-    routed = route(z.reshape(1), kept, came, row_session, planes, per_plane, slot_cap)
-    first, _ = lax.optimization_barrier((first, sent))
+
+    routed = route(index, kept, came, row_session, planes, per_plane, slot_cap)
+    first, _ = lax.optimization_barrier((first, routed[0]))
     arrived = [routed[0]] + [
         lax.ppermute(routed[by], "sess", swapped(planes, by)) for by in range(1, planes)
     ]
@@ -722,21 +750,12 @@
     arrived = stack(*[a[None] for a in arrived])
     other = lax.ppermute(arrived, "inner", swapped(2, 1))
     other = after(other, 1, 1)
-    mine = stack(arrived, other)
-    core = lax.ppermute(mine, "rep", swapped(2, 1))
-    core = after(core, 2, 0)
-
-    group_width = PER_GROUP * HD
-    weight = jnp.concatenate(
-        [
-            lax.dynamic_slice_in_dim(q_weight, head * group_width, group_width, 1),
-            lax.dynamic_slice_in_dim(k_weight, head * HD, HD, 1),
-            lax.dynamic_slice_in_dim(v_weight, head * HD, HD, 1),
-        ],
-        axis=1,
-    )
+    slots = (
+        arrived, other, lax.ppermute(arrived, "rep", swapped(2, 1)), lax.ppermute(other, "rep", swapped(2, 1))
+    )
+    slots = after(slots, 2, 0)
     states, query, key, value, lengths = place_rows(
-        index, mine, core, attn_gain, weight, per_plane, slot_cap
+        index, slots, attn_gain, (q_weight, k_weight, v_weight), per_plane, slot_cap
     )
 
     speakers = lax.dynamic_slice_in_dim(speaker_of, z * per_plane, per_plane)

time: 117 us -> 121 us (1.034)
  starting transfers between devices: 48.6 us -> 57.7 us
  waiting for transfers between devices: 25.6 us -> 17.3 us
  local copies, waits for them, and re-layouts: 7.23 us -> 11.7 us
  matrix products: 3.23 us -> 0 us
  Pallas kernels: 30.5 us -> 31.8 us
    unnamed x27 -> x44, local copies, waits for them, and re-layouts: 0.86 us -> 11.6 us
    ppermute x3, waiting for transfers between devices: 10.6 us -> 1.13 us  [line_body(): lax.ppermute(routed[by], 'sess', swapped(planes, by))]
    ppermute x6, waiting for transfers between devices: 8.12 us -> 0.02 us  [line_body(): left[chunk] = lax.ppermute(left[chunk], 'sess', shifted(planes, -1))]
    ppermute x6, starting transfers between devices: 28.5 us -> 35 us  [line_body(): right[chunk] = lax.ppermute(right[chunk], 'sess', shifted(planes, 1))]
    ppermute x1, waiting for transfers between devices: 0.85 us -> 5.57 us  [line_body(): came = lax.ppermute(sent, 'inner', swapped(2, 1))]
    dynamic_slice x3 -> x0, local copies, waits for them, and re-layouts: 4.45 us -> none  [the longest x1 2.09 us: line_body(): kept = lax.dynamic_slice_in_dim(partial_sum, x * width, width, 1)]
    dot_general x1 -> x0, matrix products: 3.23 us -> none  [line_body(): jnp.dot(thinker_rows, proj_weight, preferred_element_type=jnp.float32)]
    ppermute x1, starting transfers between devices: 2.94 us -> 0.08 us  [line_body(): from_x = lax.ppermute(to_x, pair, swapped(4, 2))]
  transfers between devices with their start and end apart: 24 -> 25, of which waited for: 9 -> 7; matrix products, arithmetic and copies ran while one was open for 9% -> 0% of each run, Pallas kernels for 20% -> 20%
where the time goes in v9:
time: 121 us; the launch traced here: 119 us
  starting transfers between devices  57.7 us (48%)
  Pallas kernels  31.8 us (26%)
  waiting for transfers between devices  17.3 us (14%)
  local copies, waits for them, and re-layouts  11.7 us (10%)
    ppermute x6, starting transfers between devices, line_body(): right[chunk] = lax.ppermute(right[chunk], 'sess', shifted(planes, 1))  35 us
    pallas_call x3, Pallas kernels, attention_call(): pl.pallas_call(kernel, in_specs=[SMEM] * len(scalars) + [VMEM] * len(arra...  12.2 us
    unnamed x44, local copies, waits for them, and re-layouts  11.6 us
    ppermute x6, starting transfers between devices, line_body(): left[chunk] = lax.ppermute(left[chunk], 'sess', shifted(planes, -1))  7.72 us
    pallas_call x3, Pallas kernels, stack(): pl.pallas_call(stack_kernel, in_specs=[VMEM] * len(arrays), out_specs=VME...  5.63 us
    ppermute x1, waiting for transfers between devices, line_body(): came = lax.ppermute(sent, 'inner', swapped(2, 1))  5.57 us
    pallas_call x1, Pallas kernels, place_rows(): pl.pallas_call(functools.partial(place_kernel, slot_cap=slot_cap, togethe...  5.07 us
    ppermute x3, starting transfers between devices, line_body(): lax.ppermute(routed[by], 'sess', swapped(planes, by))  4.62 us
  transfers between devices with their start and end apart: 25, of which 7 were waited for; matrix products, arithmetic and copies ran while one was open for 0% of the time, Pallas kernels for 20%

profile of v9, /device:TPU:0, one launch (start us, length us, event | category | flops | bytes accessed | tf_op | source)
XLA Modules:
  0.0 119.2 jit_solution(17723807228157078463)
XLA Ops:
  0.0 2.5 %split_heads.1 = (bf16[2,256,256]{2,1,0:T(8,128)(2,1)}, bf16[2,256,256]{2,1,0:T(8,128)(2,1)}, bf16[2,256,256]{2,1,0:T(8,128)(2,1)}, bf16[2,256,256]{2,1,0:T(8,128)(2,1)}) custom-call(s32[1]{0:T(128)} %bitcast.3.head_ref, bf16[2,256,1024]{2,1,0:T(8,128)(2,1)} %cache_ref.1), custom_call_target="tpu_custom_call" | custom-call | bytes 2097152 | tf_op jit(solution)/shard_map/split_heads/pallas_call | solution.py:308
  3.0 1.9 %copy-done = bf16[1792,896]{1,0:T(8,128)(2,1)S(1)} copy-done((bf16[1792,896]{1,0:T(8,128)(2,1)S(1)}, bf16[1792,896]{1,0:T(8,128)(2,1)}, u32[]{:S(2)}) %copy-start) | copy-done | bytes 3211288
  8.8 2.6 %collective-permute-start.2 = (bf16[256,448]{1,0:T(8,128)(2,1)S(1)}, bf16[256,448]{1,0:T(8,128)(2,1)S(1)}, u32[]{:S(2)}, u32[]{:S(2)}) collective-permute-start(bf16[256,448]{1,0:T(8,128)(2,1)S(1)} %get-tuple-element.40), channel_id=1, source_target_pairs={{0,2},{2,0},{1,3},{3,1},{4,6},{6,4},{5,7},{7,5},{8,10},{10,8},{9,1... | collective-permute-start | bytes 688136 | tf_op jit(solution)/shard_map/ppermute | solution.py:724
  13.0 5.6 %collective-permute-done.2.came_ref = bf16[256,448]{1,0:T(8,128)(2,1)S(1)} collective-permute-done((bf16[256,448]{1,0:T(8,128)(2,1)S(1)}, bf16[256,448]{1,0:T(8,128)(2,1)S(1)}, u32[]{:S(2)}, u32[]{:S(2)}) %collective-permute-start.2) | collective-permute-done | bytes 229408 | tf_op jit(solution)/shard_map/ppermute | solution.py:724
  19.2 2.3 %route.1 = (bf16[112,448]{1,0:T(8,128)(2,1)}, bf16[112,448]{1,0:T(8,128)(2,1)}, bf16[112,448]{1,0:T(8,128)(2,1)}, bf16[112,448]{1,0:T(8,128)(2,1)}) custom-call(s32[4]{0:T(128)} %copy-done.16, f32[256,448]{1,0:T(8,128)} %copy-done.11, bf16[256,448]{1,0:T(8,128)(2,1)} %copy-done.18, s32[1,256]{1,0:T(1,128)} %bitcast.15), custom_call_target="tpu_custom_call" | custom-call | flops 102760448 | bytes 917504 | tf_op jit(solution)/shard_map/route/pallas_call | solution.py:401
  21.6 2.0 %collective-permute-start.3 = (bf16[112,448]{1,0:T(8,128)(2,1)}, bf16[112,448]{1,0:T(8,128)(2,1)}, u32[]{:S(2)}, u32[]{:S(2)}) collective-permute-start(bf16[112,448]{1,0:T(8,128)(2,1)} %get-tuple-element.42), channel_id=1, source_target_pairs={{0,4},{4,0},{8,12},{12,8},{1,5},{5,1},{9,13},{13,9},{2,6},{6,2},{1... | collective-permute-start | bytes 301064 | tf_op jit(solution)/shard_map/ppermute | solution.py:736
  23.6 2.6 %collective-permute-start.4 = (bf16[112,448]{1,0:T(8,128)(2,1)}, bf16[112,448]{1,0:T(8,128)(2,1)}, u32[]{:S(2)}, u32[]{:S(2)}) collective-permute-start(bf16[112,448]{1,0:T(8,128)(2,1)} %get-tuple-element.43), channel_id=1, source_target_pairs={{0,8},{4,12},{8,0},{12,4},{1,9},{5,13},{9,1},{13,5},{2,10},{6,14},... | collective-permute-start | bytes 301064 | tf_op jit(solution)/shard_map/ppermute | solution.py:736
  26.2 1.9 %stack.25.refs_0_ = bf16[2,2,256,256]{3,2,1,0:T(8,128)(2,1)} custom-call(bf16[1,2,256,256]{3,2,1,0:T(8,128)(2,1)} %bitcast.13, bf16[1,2,256,256]{3,2,1,0:T(8,128)(2,1)} %bitcast.12.refs_1_), custom_call_target="tpu_custom_call" | custom-call | bytes 1048576 | tf_op jit(solution)/shard_map/stack/pallas_call | solution.py:330
  28.0 2.8 %collective-permute-start.12 = (bf16[2,2,256,256]{3,2,1,0:T(8,128)(2,1)}, bf16[2,2,256,256]{3,2,1,0:T(8,128)(2,1)S(1)}, u32[]{:S(2)}, u32[]{:S(2)}) collective-permute-start(bf16[2,2,256,256]{3,2,1,0:T(8,128)(2,1)} %stack.25.refs_0_), channel_id=1, source_target_pairs={{0,4},{4,8},{8,12},{1,5},{5,9},{9,13},{2,6},{6,10},{10,14},{3,7},{... | collective-permute-start | bytes 1572872 | tf_op jit(solution)/shard_map/ppermute | solution.py:743
  32.2 1.9 %stack.23.refs_1_ = bf16[2,2,256,256]{3,2,1,0:T(8,128)(2,1)} custom-call(bf16[1,2,256,256]{3,2,1,0:T(8,128)(2,1)} %bitcast.4.refs_0_, bf16[1,2,256,256]{3,2,1,0:T(8,128)(2,1)} %bitcast.5.refs_1_), custom_call_target="tpu_custom_call" | custom-call | bytes 1048576 | tf_op jit(solution)/shard_map/stack/pallas_call | solution.py:330
  35.2 4.9 %collective-permute-start.7 = (bf16[2,2,256,256]{3,2,1,0:T(8,128)(2,1)}, bf16[2,2,256,256]{3,2,1,0:T(8,128)(2,1)}, u32[]{:S(2)}, u32[]{:S(2)}) collective-permute-start(bf16[2,2,256,256]{3,2,1,0:T(8,128)(2,1)} %stack.23.refs_1_), channel_id=1, source_target_pairs={{0,4},{4,8},{8,12},{1,5},{5,9},{9,13},{2,6},{6,10},{10,14},{3,7},{... | collective-permute-start | bytes 1572872 | tf_op jit(solution)/shard_map/ppermute | solution.py:743
  41.4 1.9 %stack.24.near_ref = bf16[4,112,448]{2,1,0:T(8,128)(2,1)} custom-call(bf16[1,112,448]{2,1,0:T(8,128)(2,1)} %bitcast.14, bf16[1,112,448]{2,1,0:T(8,128)(2,1)} %bitcast.8.refs_1_, bf16[1,112,448]{2,1,0:T(8,128)(2,1)} %bitcast.9.refs_2_, bf16[1,112,448]{2,1,0:T(8,128)(2,1)} %bitcast.10.refs_3_), custom_call_target="tpu_custom_call" | custom-call | bytes 802816 | tf_op jit(solution)/shard_map/stack/pallas_call | solution.py:330
  44.8 6.6 %collective-permute-start.13 = (bf16[2,2,256,256]{3,2,1,0:T(8,128)(2,1)S(1)}, bf16[2,2,256,256]{3,2,1,0:T(8,128)(2,1)}, u32[]{:S(2)}, u32[]{:S(2)}) collective-permute-start(bf16[2,2,256,256]{3,2,1,0:T(8,128)(2,1)S(1)} %collective-permute-done.12.refs_2_), channel_id=1, source_target_pairs={{0,4},{4,8},{8,12},{1,5},{5,9},{9,13},{2,6},{6,10},{10,14},{3,7},{... | collective-permute-start | bytes 1572872 | tf_op jit(solution)/shard_map/ppermute | solution.py:743
  54.9 7.7 %collective-permute-start.18 = (bf16[2,2,256,256]{3,2,1,0:T(8,128)(2,1)}, bf16[2,2,256,256]{3,2,1,0:T(8,128)(2,1)}, u32[]{:S(2)}, u32[]{:S(2)}) collective-permute-start(bf16[2,2,256,256]{3,2,1,0:T(8,128)(2,1)} %collective-permute-done.7.refs_3_), channel_id=1, source_target_pairs={{0,4},{4,8},{8,12},{1,5},{5,9},{9,13},{2,6},{6,10},{10,14},{3,7},{... | collective-permute-start | bytes 1572872 | tf_op jit(solution)/shard_map/ppermute | solution.py:743
  64.0 2.0 %collective-permute-done.9.near_core_ref = bf16[4,112,448]{2,1,0:T(8,128)(2,1)S(1)} collective-permute-done((bf16[4,112,448]{2,1,0:T(8,128)(2,1)}, bf16[4,112,448]{2,1,0:T(8,128)(2,1)S(1)}, u32[]{:S(2)}, u32[]{:S(2)}) %collective-permute-start.9) | collective-permute-done | bytes 401440 | tf_op jit(solution)/shard_map/ppermute | solution.py:754
  67.0 6.0 %collective-permute-start.16 = (bf16[2,2,256,256]{3,2,1,0:T(8,128)(2,1)}, bf16[2,2,256,256]{3,2,1,0:T(8,128)(2,1)S(1)}, u32[]{:S(2)}, u32[]{:S(2)}) collective-permute-start(bf16[2,2,256,256]{3,2,1,0:T(8,128)(2,1)} %collective-permute-done.13.refs_6_), channel_id=1, source_target_pairs={{0,4},{4,8},{8,12},{1,5},{5,9},{9,13},{2,6},{6,10},{10,14},{3,7},{... | collective-permute-start | bytes 1572872 | tf_op jit(solution)/shard_map/ppermute | solution.py:743
  74.4 3.0 %collective-permute-done.18.refs_7_ = bf16[2,2,256,256]{3,2,1,0:T(8,128)(2,1)} collective-permute-done((bf16[2,2,256,256]{3,2,1,0:T(8,128)(2,1)}, bf16[2,2,256,256]{3,2,1,0:T(8,128)(2,1)}, u32[]{:S(2)}, u32[]{:S(2)}) %collective-permute-start.18) | collective-permute-done | bytes 524320 | tf_op jit(solution)/shard_map/ppermute | solution.py:743
  77.4 6.9 %collective-permute-start.20 = (bf16[2,2,256,256]{3,2,1,0:T(8,128)(2,1)}, bf16[2,2,256,256]{3,2,1,0:T(8,128)(2,1)S(1)}, u32[]{:S(2)}, u32[]{:S(2)}) collective-permute-start(bf16[2,2,256,256]{3,2,1,0:T(8,128)(2,1)} %collective-permute-done.18.refs_7_), channel_id=1, source_target_pairs={{0,4},{4,8},{8,12},{1,5},{5,9},{9,13},{2,6},{6,10},{10,14},{3,7},{... | collective-permute-start | bytes 1572872 | tf_op jit(solution)/shard_map/ppermute | solution.py:743
  91.3 5.1 %place_rows.1 = (bf16[768,896]{1,0:T(8,128)(2,1)S(1)}, bf16[768,384]{1,0:T(8,128)(2,1)S(1)}, bf16[768,128]{1,0:T(8,128)(2,1)S(1)}, bf16[768,128]{1,0:T(8,128)(2,1)S(1)}, s32[1,128]{1,0:T(1,128)S(1)}) custom-call(s32[4]{0:T(128)S(1)} %copy-done.17, bf16[4,112,448]{2,1,0:T(8,128)(2,1)S(1)} %copy-done.5, bf16[4,112,448]{2,1,0:T(8,128)(2,1)} %collective-permute-done.6.far_ref, ...), custom_call_target="tpu_custom_call" | custom-call | flops 1761607680 | bytes 6291456 | tf_op jit(solution)/shard_map/place_rows/pallas_call | solution.py:495
  96.4 8.7 %near.1.near_ref = bf16[768,384]{1,0:T(8,128)(2,1)S(1)} custom-call(s32[8]{0:T(128)S(1)} %get-tuple-element.70.hop_ref, s32[8]{0:T(128)S(1)} %get-tuple-element.69.held_ref, s32[1,128]{1,0:T(1,128)S(1)} %get-tuple-element.58.length_ref, bf16[768,384]{1,0:T(8,128)(2,1)S(1)} %get-tuple-element.63.query_ref, bf16[768,128]{1,0:T(8,128)(2,1)S(1)} %get-tuple-element.61.key_ref, ...), custom_call_target="tpu_custom_call" | custom-call | flops 660602880 | bytes 2097152 | tf_op jit(solution)/shard_map/near/pallas_call | solution.py:618
  105.1 2.8 %far.2 = (bf16[192,384]{1,0:T(8,128)(2,1)S(1)}, bf16[192,384]{1,0:T(8,128)(2,1)S(1)}) custom-call(s32[4]{0:T(128)S(1)} %copy-done.17, s32[8]{0:T(128)S(1)} %get-tuple-element.70.hop_ref, s32[8]{0:T(128)S(1)} %get-tuple-element.69.held_ref, s32[1,128]{1,0:T(1,128)S(1)} %get-tuple-element.58.length_ref, bf16[768,384]{1,0:T(8,128)(2,1)S(1)} %get-tuple-element.63.query_ref, ...), custom_call_target="tpu_custom_call" | custom-call | flops 330301440 | bytes 1048576 | tf_op jit(solution)/shard_map/far/pallas_call | solution.py:618
  108.9 4.0 %collective-permute-start.24 = (bf16[192,384]{1,0:T(8,128)(2,1)S(1)}, bf16[192,384]{1,0:T(8,128)(2,1)S(1)}, u32[]{:S(2)}, u32[]{:S(2)}) collective-permute-start(bf16[192,384]{1,0:T(8,128)(2,1)S(1)} %get-tuple-element.68), channel_id=1, source_target_pairs={{0,3},{1,2},{2,1},{3,0},{4,7},{5,6},{6,5},{7,4},{8,11},{9,10},{10,... | collective-permute-start | bytes 442376 | tf_op jit(solution)/shard_map/ppermute | solution.py:779
  113.2 3.8 %collective-permute-done.24.refs_3_ = bf16[192,384]{1,0:T(8,128)(2,1)S(1)} collective-permute-done((bf16[192,384]{1,0:T(8,128)(2,1)S(1)}, bf16[192,384]{1,0:T(8,128)(2,1)S(1)}, u32[]{:S(2)}, u32[]{:S(2)}) %collective-permute-start.24) | collective-permute-done | bytes 147488 | tf_op jit(solution)/shard_map/ppermute | solution.py:779
  117.0 2.2 %output.1 = bf16[2,96,896]{2,1,0:T(8,128)(2,1)} custom-call(s32[4]{0:T(128)S(1)} %copy-done.17, s32[1,128]{1,0:T(1,128)S(1)} %get-tuple-element.58.length_ref, bf16[768,896]{1,0:T(8,128)(2,1)S(1)} %get-tuple-element.59.states_ref, bf16[1536,896]{1,0:T(8,128)(2,1)S(1)} %copy-done.2, bf16[192,384]{1,0:T(8,128)(2,1)S(1)} %get-tuple-element.66.refs_0_, ...), custom_call_target="tpu_custom_call" | custom-call | flops 528482304 | bytes 2752512 | tf_op jit(solution)/shard_map/output/pallas_call | solution.py:675
  (86 shorter events, 27.2 us)
Async XLA Ops:
  2.5 23.7 %collective-permute-start.11 = (bf16[2,256,256]{2,1,0:T(8,128)(2,1)}, bf16[2,256,256]{2,1,0:T(8,128)(2,1)}, u32[]{:S(2)}, u32[]{:S(2)}) collective-permute-start(bf16[2,256,256]{2,1,0:T(8,128)(2,1)} %get-tuple-element.52), channel_id=1, source_target_pairs={{0,1},{1,0},{2,3},{3,2},{4,5},{5,4},{6,7},{7,6},{8,9},{9,8},{10,11... | collective-permute-start | bytes 786440 | tf_op jit(solution)/shard_map/ppermute | solution.py:727
  8.8 9.7 %collective-permute-start.2 = (bf16[256,448]{1,0:T(8,128)(2,1)S(1)}, bf16[256,448]{1,0:T(8,128)(2,1)S(1)}, u32[]{:S(2)}, u32[]{:S(2)}) collective-permute-start(bf16[256,448]{1,0:T(8,128)(2,1)S(1)} %get-tuple-element.40), channel_id=1, source_target_pairs={{0,2},{2,0},{1,3},{3,1},{4,6},{6,4},{5,7},{7,5},{8,10},{10,8},{9,1... | collective-permute-start | bytes 688136 | tf_op jit(solution)/shard_map/ppermute | solution.py:724
  11.4 16.7 %collective-permute-start = (bf16[2,256,256]{2,1,0:T(8,128)(2,1)}, bf16[2,256,256]{2,1,0:T(8,128)(2,1)}, u32[]{:S(2)}, u32[]{:S(2)}) collective-permute-start(bf16[2,256,256]{2,1,0:T(8,128)(2,1)} %get-tuple-element.37), channel_id=1, source_target_pairs={{0,2},{1,3},{2,0},{3,1},{4,6},{5,7},{6,4},{7,5},{8,10},{9,11},{10,... | collective-permute-start | bytes 786440 | tf_op jit(solution)/shard_map/ppermute | solution.py:728
  11.4 19.4 %collective-permute-start.1 = (bf16[2,256,256]{2,1,0:T(8,128)(2,1)}, bf16[2,256,256]{2,1,0:T(8,128)(2,1)}, u32[]{:S(2)}, u32[]{:S(2)}) collective-permute-start(bf16[2,256,256]{2,1,0:T(8,128)(2,1)} %get-tuple-element.38), channel_id=1, source_target_pairs={{0,3},{1,2},{2,1},{3,0},{4,7},{5,6},{6,5},{7,4},{8,11},{9,10},{10,... | collective-permute-start | bytes 786440 | tf_op jit(solution)/shard_map/ppermute | solution.py:729
  21.6 12.5 %collective-permute-start.3 = (bf16[112,448]{1,0:T(8,128)(2,1)}, bf16[112,448]{1,0:T(8,128)(2,1)}, u32[]{:S(2)}, u32[]{:S(2)}) collective-permute-start(bf16[112,448]{1,0:T(8,128)(2,1)} %get-tuple-element.42), channel_id=1, source_target_pairs={{0,4},{4,0},{8,12},{12,8},{1,5},{5,1},{9,13},{13,9},{2,6},{6,2},{1... | collective-permute-start | bytes 301064 | tf_op jit(solution)/shard_map/ppermute | solution.py:736
  23.6 11.6 %collective-permute-start.4 = (bf16[112,448]{1,0:T(8,128)(2,1)}, bf16[112,448]{1,0:T(8,128)(2,1)}, u32[]{:S(2)}, u32[]{:S(2)}) collective-permute-start(bf16[112,448]{1,0:T(8,128)(2,1)} %get-tuple-element.43), channel_id=1, source_target_pairs={{0,8},{4,12},{8,0},{12,4},{1,9},{5,13},{9,1},{13,5},{2,10},{6,14},... | collective-permute-start | bytes 301064 | tf_op jit(solution)/shard_map/ppermute | solution.py:736
  26.2 9.0 %collective-permute-start.5 = (bf16[112,448]{1,0:T(8,128)(2,1)}, bf16[112,448]{1,0:T(8,128)(2,1)}, u32[]{:S(2)}, u32[]{:S(2)}) collective-permute-start(bf16[112,448]{1,0:T(8,128)(2,1)} %get-tuple-element.44), channel_id=1, source_target_pairs={{0,12},{4,8},{8,4},{12,0},{1,13},{5,9},{9,5},{13,1},{2,14},{6,10},... | collective-permute-start | bytes 301064 | tf_op jit(solution)/shard_map/ppermute | solution.py:736
  28.0 16.7 %collective-permute-start.12 = (bf16[2,2,256,256]{3,2,1,0:T(8,128)(2,1)}, bf16[2,2,256,256]{3,2,1,0:T(8,128)(2,1)S(1)}, u32[]{:S(2)}, u32[]{:S(2)}) collective-permute-start(bf16[2,2,256,256]{3,2,1,0:T(8,128)(2,1)} %stack.25.refs_0_), channel_id=1, source_target_pairs={{0,4},{4,8},{8,12},{1,5},{5,9},{9,13},{2,6},{6,10},{10,14},{3,7},{... | collective-permute-start | bytes 1572872 | tf_op jit(solution)/shard_map/ppermute | solution.py:743
  30.9 21.3 %collective-permute-start.14 = (bf16[2,2,256,256]{3,2,1,0:T(8,128)(2,1)}, bf16[2,2,256,256]{3,2,1,0:T(8,128)(2,1)}, u32[]{:S(2)}, u32[]{:S(2)}) collective-permute-start(bf16[2,2,256,256]{3,2,1,0:T(8,128)(2,1)} %stack.25.refs_0_), channel_id=1, source_target_pairs={{4,0},{8,4},{12,8},{5,1},{9,5},{13,9},{6,2},{10,6},{14,10},{7,3},{... | collective-permute-start | bytes 1572872 | tf_op jit(solution)/shard_map/ppermute | solution.py:744
  35.2 19.7 %collective-permute-start.7 = (bf16[2,2,256,256]{3,2,1,0:T(8,128)(2,1)}, bf16[2,2,256,256]{3,2,1,0:T(8,128)(2,1)}, u32[]{:S(2)}, u32[]{:S(2)}) collective-permute-start(bf16[2,2,256,256]{3,2,1,0:T(8,128)(2,1)} %stack.23.refs_1_), channel_id=1, source_target_pairs={{0,4},{4,8},{8,12},{1,5},{5,9},{9,13},{2,6},{6,10},{10,14},{3,7},{... | collective-permute-start | bytes 1572872 | tf_op jit(solution)/shard_map/ppermute | solution.py:743
  40.1 22.5 %collective-permute-start.8 = (bf16[2,2,256,256]{3,2,1,0:T(8,128)(2,1)}, bf16[2,2,256,256]{3,2,1,0:T(8,128)(2,1)}, u32[]{:S(2)}, u32[]{:S(2)}) collective-permute-start(bf16[2,2,256,256]{3,2,1,0:T(8,128)(2,1)} %stack.23.refs_1_), channel_id=1, source_target_pairs={{4,0},{8,4},{12,8},{5,1},{9,5},{13,9},{6,2},{10,6},{14,10},{7,3},{... | collective-permute-start | bytes 1572872 | tf_op jit(solution)/shard_map/ppermute | solution.py:744
  43.3 20.6 %collective-permute-start.6 = (bf16[4,112,448]{2,1,0:T(8,128)(2,1)}, bf16[4,112,448]{2,1,0:T(8,128)(2,1)}, u32[]{:S(2)}, u32[]{:S(2)}) collective-permute-start(bf16[4,112,448]{2,1,0:T(8,128)(2,1)} %stack.24.near_ref), channel_id=1, source_target_pairs={{0,2},{2,0},{1,3},{3,1},{4,6},{6,4},{5,7},{7,5},{8,10},{10,8},{9,1... | collective-permute-start | bytes 1204232 | tf_op jit(solution)/shard_map/ppermute | solution.py:751
  44.8 22.2 %collective-permute-start.13 = (bf16[2,2,256,256]{3,2,1,0:T(8,128)(2,1)S(1)}, bf16[2,2,256,256]{3,2,1,0:T(8,128)(2,1)}, u32[]{:S(2)}, u32[]{:S(2)}) collective-permute-start(bf16[2,2,256,256]{3,2,1,0:T(8,128)(2,1)S(1)} %collective-permute-done.12.refs_2_), channel_id=1, source_target_pairs={{0,4},{4,8},{8,12},{1,5},{5,9},{9,13},{2,6},{6,10},{10,14},{3,7},{... | collective-permute-start | bytes 1572872 | tf_op jit(solution)/shard_map/ppermute | solution.py:743
  52.2 20.8 %collective-permute-start.15 = (bf16[2,2,256,256]{3,2,1,0:T(8,128)(2,1)}, bf16[2,2,256,256]{3,2,1,0:T(8,128)(2,1)}, u32[]{:S(2)}, u32[]{:S(2)}) collective-permute-start(bf16[2,2,256,256]{3,2,1,0:T(8,128)(2,1)} %collective-permute-done.14.refs_4_), channel_id=1, source_target_pairs={{4,0},{8,4},{12,8},{5,1},{9,5},{13,9},{6,2},{10,6},{14,10},{7,3},{... | collective-permute-start | bytes 1572872 | tf_op jit(solution)/shard_map/ppermute | solution.py:744
  54.9 22.5 %collective-permute-start.18 = (bf16[2,2,256,256]{3,2,1,0:T(8,128)(2,1)}, bf16[2,2,256,256]{3,2,1,0:T(8,128)(2,1)}, u32[]{:S(2)}, u32[]{:S(2)}) collective-permute-start(bf16[2,2,256,256]{3,2,1,0:T(8,128)(2,1)} %collective-permute-done.7.refs_3_), channel_id=1, source_target_pairs={{0,4},{4,8},{8,12},{1,5},{5,9},{9,13},{2,6},{6,10},{10,14},{3,7},{... | collective-permute-start | bytes 1572872 | tf_op jit(solution)/shard_map/ppermute | solution.py:743
  62.6 21.7 %collective-permute-start.19 = (bf16[2,2,256,256]{3,2,1,0:T(8,128)(2,1)}, bf16[2,2,256,256]{3,2,1,0:T(8,128)(2,1)}, u32[]{:S(2)}, u32[]{:S(2)}) collective-permute-start(bf16[2,2,256,256]{3,2,1,0:T(8,128)(2,1)} %collective-permute-done.8.refs_5_), channel_id=1, source_target_pairs={{4,0},{8,4},{12,8},{5,1},{9,5},{13,9},{6,2},{10,6},{14,10},{7,3},{... | collective-permute-start | bytes 1572872 | tf_op jit(solution)/shard_map/ppermute | solution.py:744
  66.8 19.0 %collective-permute-start.10 = (bf16[4,112,448]{2,1,0:T(8,128)(2,1)}, bf16[4,112,448]{2,1,0:T(8,128)(2,1)}, u32[]{:S(2)}, u32[]{:S(2)}) collective-permute-start(bf16[4,112,448]{2,1,0:T(8,128)(2,1)} %collective-permute-done.6.far_ref), channel_id=1, source_target_pairs={{0,1},{1,0},{2,3},{3,2},{4,5},{5,4},{6,7},{7,6},{8,9},{9,8},{10,11... | collective-permute-start | bytes 1204232 | tf_op jit(solution)/shard_map/ppermute | solution.py:754
  67.0 29.4 %collective-permute-start.16 = (bf16[2,2,256,256]{3,2,1,0:T(8,128)(2,1)}, bf16[2,2,256,256]{3,2,1,0:T(8,128)(2,1)S(1)}, u32[]{:S(2)}, u32[]{:S(2)}) collective-permute-start(bf16[2,2,256,256]{3,2,1,0:T(8,128)(2,1)} %collective-permute-done.13.refs_6_), channel_id=1, source_target_pairs={{0,4},{4,8},{8,12},{1,5},{5,9},{9,13},{2,6},{6,10},{10,14},{3,7},{... | collective-permute-start | bytes 1572872 | tf_op jit(solution)/shard_map/ppermute | solution.py:743
  73.0 23.4 %collective-permute-start.17 = (bf16[2,2,256,256]{3,2,1,0:T(8,128)(2,1)}, bf16[2,2,256,256]{3,2,1,0:T(8,128)(2,1)}, u32[]{:S(2)}, u32[]{:S(2)}) collective-permute-start(bf16[2,2,256,256]{3,2,1,0:T(8,128)(2,1)} %collective-permute-done.15.refs_8_), channel_id=1, source_target_pairs={{4,0},{8,4},{12,8},{5,1},{9,5},{13,9},{6,2},{10,6},{14,10},{7,3},{... | collective-permute-start | bytes 1572872 | tf_op jit(solution)/shard_map/ppermute | solution.py:744
  77.4 27.7 %collective-permute-start.20 = (bf16[2,2,256,256]{3,2,1,0:T(8,128)(2,1)}, bf16[2,2,256,256]{3,2,1,0:T(8,128)(2,1)S(1)}, u32[]{:S(2)}, u32[]{:S(2)}) collective-permute-start(bf16[2,2,256,256]{3,2,1,0:T(8,128)(2,1)} %collective-permute-done.18.refs_7_), channel_id=1, source_target_pairs={{0,4},{4,8},{8,12},{1,5},{5,9},{9,13},{2,6},{6,10},{10,14},{3,7},{... | collective-permute-start | bytes 1572872 | tf_op jit(solution)/shard_map/ppermute | solution.py:743
  84.3 20.8 %collective-permute-start.21 = (bf16[2,2,256,256]{3,2,1,0:T(8,128)(2,1)}, bf16[2,2,256,256]{3,2,1,0:T(8,128)(2,1)S(1)}, u32[]{:S(2)}, u32[]{:S(2)}) collective-permute-start(bf16[2,2,256,256]{3,2,1,0:T(8,128)(2,1)} %collective-permute-done.19.refs_9_), channel_id=1, source_target_pairs={{4,0},{8,4},{12,8},{5,1},{9,5},{13,9},{6,2},{10,6},{14,10},{7,3},{... | collective-permute-start | bytes 1572872 | tf_op jit(solution)/shard_map/ppermute | solution.py:744
  108.0 5.2 %collective-permute-start.23 = (bf16[192,384]{1,0:T(8,128)(2,1)S(1)}, bf16[192,384]{1,0:T(8,128)(2,1)S(1)}, u32[]{:S(2)}, u32[]{:S(2)}) collective-permute-start(bf16[192,384]{1,0:T(8,128)(2,1)S(1)} %get-tuple-element.64), channel_id=1, source_target_pairs={{0,2},{1,3},{2,0},{3,1},{4,6},{5,7},{6,4},{7,5},{8,10},{9,11},{10,... | collective-permute-start | bytes 442376 | tf_op jit(solution)/shard_map/ppermute | solution.py:779
  108.8 4.1 %collective-permute-start.22 = (bf16[192,384]{1,0:T(8,128)(2,1)S(1)}, bf16[192,384]{1,0:T(8,128)(2,1)S(1)}, u32[]{:S(2)}, u32[]{:S(2)}) collective-permute-start(bf16[192,384]{1,0:T(8,128)(2,1)S(1)} %get-tuple-element.67), channel_id=1, source_target_pairs={{0,1},{1,0},{2,3},{3,2},{4,5},{5,4},{6,7},{7,6},{8,9},{9,8},{10,11... | collective-permute-start | bytes 442376 | tf_op jit(solution)/shard_map/ppermute | solution.py:779
  108.9 8.1 %collective-permute-start.24 = (bf16[192,384]{1,0:T(8,128)(2,1)S(1)}, bf16[192,384]{1,0:T(8,128)(2,1)S(1)}, u32[]{:S(2)}, u32[]{:S(2)}) collective-permute-start(bf16[192,384]{1,0:T(8,128)(2,1)S(1)} %get-tuple-element.68), channel_id=1, source_target_pairs={{0,3},{1,2},{2,1},{3,0},{4,7},{5,6},{6,5},{7,4},{8,11},{9,10},{10,... | collective-permute-start | bytes 442376 | tf_op jit(solution)/shard_map/ppermute | solution.py:779
  (23 other events, 487.8 us)

commit v10 on v9

--- a/solution.py
+++ b/solution.py
@@ -118,7 +118,7 @@
             out((sessions * SLOTS, HD), jnp.bfloat16),
             out((sessions * SLOTS, HD), jnp.bfloat16),
         ],
-        compiler_params=pltpu.CompilerParams(vmem_limit_bytes=40 << 20),
+        compiler_params=pltpu.CompilerParams(vmem_limit_bytes=32 << 20),
         name="states",
     )(code, slots, gain, weight, jnp.asarray(cosine), jnp.asarray(sine))
 
@@ -140,7 +140,7 @@
             out_specs=row_spec(PER_GROUP * HD),
         ),
         out_shape=jax.ShapeDtypeStruct((sessions * SLOTS, PER_GROUP * HD), jnp.bfloat16),
-        compiler_params=pltpu.CompilerParams(vmem_limit_bytes=40 << 20),
+        compiler_params=pltpu.CompilerParams(vmem_limit_bytes=32 << 20),
         name="attend",
     )(place, lengths, query, key, value, prompts)
 
@@ -292,7 +292,7 @@
 EXTRA = 16
 SMEM = pl.BlockSpec(memory_space=pltpu.SMEM)
 VMEM = pl.BlockSpec(memory_space=pltpu.VMEM)
-ANY = pl.BlockSpec(memory_space=pl.ANY)
+HBM = pl.BlockSpec(memory_space=pltpu.HBM)
 
 
 def split_heads_kernel(head_ref, cache_ref, *out_refs):
@@ -356,7 +356,7 @@
             jax.ShapeDtypeStruct((count, width), jnp.float32),
             jax.ShapeDtypeStruct((count, width), jnp.bfloat16),
         ],
-        compiler_params=pltpu.CompilerParams(vmem_limit_bytes=40 << 20),
+        compiler_params=pltpu.CompilerParams(vmem_limit_bytes=32 << 20),
         cost_estimate=pl.CostEstimate(
             flops=2 * count * weight.size, bytes_accessed=2 * (rows.size + weight.size), transcendentals=0
         ),
@@ -410,14 +410,47 @@
     )(index, kept, came, row_session.reshape(1, rows))
 
 
+def head_weights_kernel(index_ref, q_ref, k_ref, v_ref, out_ref, sem):
+    copies = []
+    for i, (ref, heads, place) in enumerate(
+        ((q_ref, PER_GROUP, 0), (k_ref, 1, PER_GROUP), (v_ref, 1, PER_GROUP + 1))
+    ):
+        start = pl.multiple_of(index_ref[3] * heads * HD, HD)
+        copies.append(
+            pltpu.make_async_copy(
+                ref.at[:, pl.ds(start, heads * HD)],
+                out_ref.at[:, place * HD : (place + heads) * HD],
+                sem.at[i],
+            )
+        )
+    for copy in copies:
+        copy.start()
+    for copy in copies:
+        copy.wait()
+
+
+def head_weights(index, q_weight, k_weight, v_weight):
+    model, width = q_weight.shape[0], (PER_GROUP + 2) * HD
+    return pl.pallas_call(
+        head_weights_kernel,
+        in_specs=[SMEM] + [HBM] * 3,
+        out_specs=VMEM,
+        out_shape=jax.ShapeDtypeStruct((model, width), q_weight.dtype),
+        scratch_shapes=[pltpu.SemaphoreType.DMA((3,))],
+        cost_estimate=pl.CostEstimate(
+            flops=0, bytes_accessed=4 * model * width, transcendentals=0
+        ),
+        name="head_weights",
+    )(index, q_weight, k_weight, v_weight)
+
+
 def place_kernel(index_ref, near_ref, far_ref, near_core_ref, far_core_ref, gain_ref,
-                 q_ref, k_ref, v_ref, cos_ref, sin_ref, states_ref, query_ref, key_ref, value_ref, length_ref, *, slot_cap, together):
+                 weight_ref, cos_ref, sin_ref, states_ref, query_ref, key_ref, value_ref, length_ref, *,
+                 slot_cap, together):
     z, x, c, head = [index_ref[i] for i in range(4)]
     planes, live, width = near_ref.shape
     blocks = 2 * planes
     live = live - EXTRA
-    columns = pl.ds(pl.multiple_of(head * HD, HD), HD)
-    group_columns = pl.ds(pl.multiple_of(head * PER_GROUP * HD, HD), PER_GROUP * HD)
     per_plane = live // slot_cap
     steps = per_plane // together
     window = together * slot_cap
@@ -439,7 +472,8 @@
         preferred_element_type=jnp.float32,
     )
     length_ref[...] = sums[:1].astype(jnp.int32)
-    cosine, sine = cos_ref[...], sin_ref[...]
+    cosine = jnp.concatenate([cos_ref[...]] * together, axis=0)
+    sine = jnp.concatenate([sin_ref[...]] * together, axis=0)
     gain = gain_ref[...].astype(jnp.float32)
     for step in range(steps):
         slot = lax.broadcasted_iota(jnp.int32, (blocks, blocks * window), 1)
@@ -473,39 +507,37 @@
         states_ref[rows] = widened.astype(jnp.bfloat16)
         factor = lax.rsqrt(jnp.mean(widened * widened, axis=-1, keepdims=True) + EPSILON)
         normed = (widened * factor * gain).astype(jnp.bfloat16)
-        queries = jnp.dot(normed, q_ref[:, group_columns], preferred_element_type=jnp.float32)
-        keys = jnp.dot(normed, k_ref[:, columns], preferred_element_type=jnp.float32)
+        both = jnp.dot(normed, weight_ref[...], preferred_element_type=jnp.float32)
         for h in range(PER_GROUP + 1):
-            vector = keys if h == PER_GROUP else queries[:, h * HD : (h + 1) * HD]
+            vector = both[:, h * HD : (h + 1) * HD]
             turned = vector * cosine + pltpu.roll(vector, HD // 2, 1) * sine
             if h < PER_GROUP:
                 query_ref[rows, h * HD : (h + 1) * HD] = turned.astype(jnp.bfloat16)
             else:
                 key_ref[rows] = turned.astype(jnp.bfloat16)
-        values = jnp.dot(normed, v_ref[:, columns], preferred_element_type=jnp.float32)
-        value_ref[rows] = values.astype(jnp.bfloat16)
-
-
-def place_rows(index, slots, gain, weights, sessions, slot_cap):
+        value_ref[rows] = both[:, (PER_GROUP + 1) * HD :].astype(jnp.bfloat16)
+
+
+def place_rows(index, slots, gain, weight, sessions, slot_cap):
     together = 16 // math.gcd(16, slot_cap)
-    cosine, sine = rope_tables(together)
+    cosine, sine = rope_tables(1)
     model = 2 * slots[0].shape[2]
     total = sessions * SLOTS
     out = lambda w: jax.ShapeDtypeStruct((total, w), jnp.bfloat16)
     return pl.pallas_call(
         functools.partial(place_kernel, slot_cap=slot_cap, together=together),
-        in_specs=[SMEM] + [VMEM] * 10,
+        in_specs=[SMEM] + [VMEM] * 8,
         out_specs=[VMEM] * 5,
         out_shape=[
             out(model), out(PER_GROUP * HD), out(HD), out(HD),
             jax.ShapeDtypeStruct((1, HD), jnp.int32),
         ],
-        compiler_params=pltpu.CompilerParams(vmem_limit_bytes=40 << 20),
+        compiler_params=pltpu.CompilerParams(vmem_limit_bytes=32 << 20),
         cost_estimate=pl.CostEstimate(
             flops=4 * total * model * 5 * HD, bytes_accessed=6 << 20, transcendentals=0
         ),
         name="place_rows",
-    )(index, *slots, gain.reshape(1, model), *weights, jnp.asarray(cosine), jnp.asarray(sine))
+    )(index, *slots, gain.reshape(1, model), weight, jnp.asarray(cosine), jnp.asarray(sine))
 
 
 def session_attention(query, key, value, tokens, length):
@@ -555,24 +587,18 @@
 def near_kernel(hop_ref, held_ref, length_ref, query_ref, key_ref, value_ref, *refs, hops):
     prompt_refs, (out_ref, kv, sem) = refs[: 2 * len(hops)], refs[2 * len(hops) :]
     sessions = hop_ref.shape[0]
+    for start in (True, False):
+        for i in range(sessions):
+            hop = jnp.where(among(hop_ref[i], hops), hop_ref[i], 0)
+            fetches(hop, prompt_refs, held_ref[i], kv.at[i], sem.at[i], hops, start)
     for i in range(sessions):
-        fetches(hop_ref[i], prompt_refs, held_ref[i], kv.at[i], sem.at[i], hops, True)
-
-    def work(i, _):
-        @pl.when(among(hop_ref[i], hops))
-        def _():
-            fetches(hop_ref[i], prompt_refs, held_ref[i], kv.at[i], sem.at[i], hops, False)
-            rows = pl.ds(pl.multiple_of(i * SLOTS, SLOTS), SLOTS)
-            mixed = session_attention(
-                query_ref[rows], key_ref[rows], value_ref[rows],
-                kv[i].reshape(PROMPT, 2 * HD), length_ref[0, i],
-            )
-            for h in range(PER_GROUP):
-                out_ref[rows, h * HD : (h + 1) * HD] = mixed[h * SLOTS : (h + 1) * SLOTS]
-
-        return 0
-
-    lax.fori_loop(0, sessions, work, 0)
+        rows = slice(i * SLOTS, (i + 1) * SLOTS)
+        mixed = session_attention(
+            query_ref[rows], key_ref[rows], value_ref[rows],
+            kv[i].reshape(PROMPT, 2 * HD), length_ref[0, i],
+        )
+        for h in range(PER_GROUP):
+            out_ref[rows, h * HD : (h + 1) * HD] = mixed[h * SLOTS : (h + 1) * SLOTS]
 
 
 def far_kernel(index_ref, hop_ref, held_ref, length_ref, query_ref, key_ref, value_ref, near_ref,
@@ -609,9 +635,6 @@
                 out_refs[t][target, h * HD : (h + 1) * HD] = mixed[h * SLOTS : (h + 1) * SLOTS]
 
 
-HBM = pl.BlockSpec(memory_space=pltpu.HBM)
-
-
 def attention_call(kernel, out_specs, out_shape, places, name, scalars, arrays, prompts, hops):
     pieces = [piece for h in hops for piece in prompts[h]]
     work = places * PER_GROUP * SLOTS * (PROMPT + SLOTS) // 2
@@ -624,7 +647,7 @@
             pltpu.VMEM((places, 2, 2, PROMPT // 4, 2 * HD), jnp.bfloat16),
             pltpu.SemaphoreType.DMA((places, 2)),
         ],
-        compiler_params=pltpu.CompilerParams(vmem_limit_bytes=40 << 20),
+        compiler_params=pltpu.CompilerParams(vmem_limit_bytes=32 << 20),
         cost_estimate=pl.CostEstimate(
             flops=4 * work * HD, bytes_accessed=places * PROMPT * 2 * HD, transcendentals=work
         ),
@@ -677,7 +700,7 @@
         in_specs=[SMEM] * 2 + [VMEM] * (2 + len(pieces)),
         out_specs=VMEM,
         out_shape=jax.ShapeDtypeStruct((per_device, SLOTS, model), jnp.bfloat16),
-        compiler_params=pltpu.CompilerParams(vmem_limit_bytes=40 << 20),
+        compiler_params=pltpu.CompilerParams(vmem_limit_bytes=32 << 20),
         cost_estimate=pl.CostEstimate(
             flops=2 * per_device * SLOTS * o_weight.size, bytes_accessed=o_weight.size * 2, transcendentals=0
         ),
@@ -730,19 +753,25 @@
     first = stack(own[None], from_core[None])
     second = stack(from_x[None], from_far[None])
 
+    weight = head_weights(index, q_weight, k_weight, v_weight)
+    came, weight = lax.optimization_barrier((came, weight))
     routed = route(index, kept, came, row_session, planes, per_plane, slot_cap)
-    first, _ = lax.optimization_barrier((first, routed[0]))
+    first, _ = lax.optimization_barrier((first, sent))
     arrived = [routed[0]] + [
         lax.ppermute(routed[by], "sess", swapped(planes, by)) for by in range(1, planes)
     ]
     second, arrived = lax.optimization_barrier((second, arrived))
     right, left = [first, second], [first, second]
     prompts = {0: (first, second)}
-    for hop in range(1, planes):
+
+    def travel(hop):
         for chunk in range(2):
             right[chunk] = lax.ppermute(right[chunk], "sess", shifted(planes, 1))
             left[chunk] = lax.ppermute(left[chunk], "sess", shifted(planes, -1))
         prompts[-hop], prompts[hop] = tuple(right), tuple(left)
+
+    travel(1)
+    travel(2)
 
     def after(value, hop, chunk):
         return lax.optimization_barrier((value, prompts[-hop][chunk], prompts[hop][chunk]))[0]
@@ -755,8 +784,10 @@
     )
     slots = after(slots, 2, 0)
     states, query, key, value, lengths = place_rows(
-        index, slots, attn_gain, (q_weight, k_weight, v_weight), per_plane, slot_cap
-    )
+        index, slots, attn_gain, weight, per_plane, slot_cap
+    )
+
+    travel(3)
 
     speakers = lax.dynamic_slice_in_dim(speaker_of, z * per_plane, per_plane)
     wanted_slot = jnp.sum(
@@ -768,7 +799,7 @@
     hop = wanted_slot // held - z
     which = wanted_slot % held
     near = attend_near(
-        hop, which, lengths, after(query, 3, 0), key, value, prompts, (0, -1, 1, -2, 2)
+        hop, which, lengths, query, key, value, prompts, (0, -1, 1, -2, 2)
     )
     run = functools.partial(attend_far, index, hop, which, lengths)
     attended = {}

time: 121 us -> 117 us (0.967)
  the two profiles are of different devices: /device:TPU:0 before, /device:TPU:29 now
where the time goes in v10:
time: 117 us; the launch traced here: 115 us
  starting transfers between devices  48.9 us (42%)
  Pallas kernels  35.2 us (30%)
  waiting for transfers between devices  21.6 us (18%)
  local copies, waits for them, and re-layouts  8.3 us (7%)
    ppermute x6, starting transfers between devices, travel(): left[chunk] = lax.ppermute(left[chunk], 'sess', shifted(planes, -1))  25.2 us
    pallas_call x3, Pallas kernels, attention_call(): pl.pallas_call(kernel, in_specs=[SMEM] * len(scalars) + [VMEM] * len(arra...  12.9 us
    ppermute x6, waiting for transfers between devices, travel(): right[chunk] = lax.ppermute(right[chunk], 'sess', shifted(planes, 1))  11 us
    unnamed x52, local copies, waits for them, and re-layouts  8.22 us
    ppermute x6, starting transfers between devices, travel(): right[chunk] = lax.ppermute(right[chunk], 'sess', shifted(planes, 1))  7.68 us
    pallas_call x3, Pallas kernels, stack(): pl.pallas_call(stack_kernel, in_specs=[VMEM] * len(arrays), out_specs=VME...  5.61 us
    ppermute x3, waiting for transfers between devices, line_body(): lax.ppermute(attended[by], pair, swapped(4, by))  5.34 us
    pallas_call x1, Pallas kernels, place_rows(): pl.pallas_call(functools.partial(place_kernel, slot_cap=slot_cap, togethe...  4.86 us
  transfers between devices with their start and end apart: 25, of which 9 were waited for; matrix products, arithmetic and copies ran while one was open for 0% of the time, Pallas kernels for 24%

profile of v10, /device:TPU:29, one launch (start us, length us, event | category | flops | bytes accessed | tf_op | source)
XLA Modules:
  0.0 114.7 jit_solution(15898204144062154142)
XLA Ops:
  0.0 2.4 %split_heads.1 = (bf16[2,256,256]{2,1,0:T(8,128)(2,1)}, bf16[2,256,256]{2,1,0:T(8,128)(2,1)}, bf16[2,256,256]{2,1,0:T(8,128)(2,1)}, bf16[2,256,256]{2,1,0:T(8,128)(2,1)}) custom-call(s32[1]{0:T(128)} %bitcast.3.head_ref, bf16[2,256,1024]{2,1,0:T(8,128)(2,1)} %cache_ref.1), custom_call_target="tpu_custom_call" | custom-call | bytes 2097152 | tf_op jit(solution)/shard_map/split_heads/pallas_call | solution.py:308
  3.2 1.9 %copy-done = bf16[1792,896]{1,0:T(8,128)(2,1)S(1)} copy-done((bf16[1792,896]{1,0:T(8,128)(2,1)S(1)}, bf16[1792,896]{1,0:T(8,128)(2,1)}, u32[]{:S(2)}) %copy-start) | copy-done | bytes 3211288
  12.1 3.0 %head_weights.1.weight_ref = bf16[896,640]{1,0:T(8,128)(2,1)} custom-call(s32[4]{0:T(128)} %copy-done.8, bf16[896,1536]{1,0:T(8,128)(2,1)} %q_ref.1, bf16[896,512]{1,0:T(8,128)(2,1)} %k_ref.1, bf16[896,512]{1,0:T(8,128)(2,1)} %v_ref.1), custom_call_target="tpu_custom_call" | custom-call | bytes 2293760 | tf_op jit(solution)/shard_map/head_weights/pallas_call | solution.py:434
  17.6 2.3 %route.1 = (bf16[112,448]{1,0:T(8,128)(2,1)}, bf16[112,448]{1,0:T(8,128)(2,1)}, bf16[112,448]{1,0:T(8,128)(2,1)}, bf16[112,448]{1,0:T(8,128)(2,1)}) custom-call(s32[4]{0:T(128)} %copy-done.8, f32[256,448]{1,0:T(8,128)} %copy-done.6, bf16[256,448]{1,0:T(8,128)(2,1)} %copy-done.14, s32[1,256]{1,0:T(1,128)} %bitcast.21), custom_call_target="tpu_custom_call" | custom-call | flops 102760448 | bytes 917504 | tf_op jit(solution)/shard_map/route/pallas_call | solution.py:401
  20.2 3.3 %collective-permute-start.5 = (bf16[112,448]{1,0:T(8,128)(2,1)}, bf16[112,448]{1,0:T(8,128)(2,1)S(1)}, u32[]{:S(2)}, u32[]{:S(2)}) collective-permute-start(bf16[112,448]{1,0:T(8,128)(2,1)} %get-tuple-element.46), channel_id=1, source_target_pairs={{0,12},{4,8},{8,4},{12,0},{1,13},{5,9},{9,5},{13,1},{2,14},{6,10},... | collective-permute-start | bytes 301064 | tf_op jit(solution)/shard_map/ppermute | solution.py:761
  26.6 1.9 %collective-permute-done.1 = bf16[2,256,256]{2,1,0:T(8,128)(2,1)S(1)} collective-permute-done((bf16[2,256,256]{2,1,0:T(8,128)(2,1)S(1)}, bf16[2,256,256]{2,1,0:T(8,128)(2,1)S(1)}, u32[]{:S(2)}, u32[]{:S(2)}) %collective-permute-start.1) | collective-permute-done | bytes 262176 | tf_op jit(solution)/shard_map/ppermute | solution.py:752
  28.5 2.2 %collective-permute-start.14 = (bf16[2,2,256,256]{3,2,1,0:T(8,128)(2,1)}, bf16[2,2,256,256]{3,2,1,0:T(8,128)(2,1)S(1)}, u32[]{:S(2)}, u32[]{:S(2)}) collective-permute-start(bf16[2,2,256,256]{3,2,1,0:T(8,128)(2,1)} %stack.25.refs_0_), channel_id=1, source_target_pairs={{4,0},{8,4},{12,8},{5,1},{9,5},{13,9},{6,2},{10,6},{14,10},{7,3},{... | collective-permute-start | bytes 1572872 | tf_op jit(solution)/shard_map/ppermute | solution.py:770
  30.7 1.9 %stack.23.refs_1_ = bf16[2,2,256,256]{3,2,1,0:T(8,128)(2,1)} custom-call(bf16[1,2,256,256]{3,2,1,0:T(8,128)(2,1)} %bitcast.15, bf16[1,2,256,256]{3,2,1,0:T(8,128)(2,1)} %bitcast.16), custom_call_target="tpu_custom_call" | custom-call | bytes 1048576 | tf_op jit(solution)/shard_map/stack/pallas_call | solution.py:330
  34.6 4.0 %collective-permute-start.8 = (bf16[2,2,256,256]{3,2,1,0:T(8,128)(2,1)}, bf16[2,2,256,256]{3,2,1,0:T(8,128)(2,1)S(1)}, u32[]{:S(2)}, u32[]{:S(2)}) collective-permute-start(bf16[2,2,256,256]{3,2,1,0:T(8,128)(2,1)} %stack.23.refs_1_), channel_id=1, source_target_pairs={{4,0},{8,4},{12,8},{5,1},{9,5},{13,9},{6,2},{10,6},{14,10},{7,3},{... | collective-permute-start | bytes 1572872 | tf_op jit(solution)/shard_map/ppermute | solution.py:770
  38.6 1.9 %stack.24.near_ref = bf16[4,112,448]{2,1,0:T(8,128)(2,1)} custom-call(bf16[1,112,448]{2,1,0:T(8,128)(2,1)} %bitcast.17, bf16[1,112,448]{2,1,0:T(8,128)(2,1)} %bitcast.18, bf16[1,112,448]{2,1,0:T(8,128)(2,1)} %bitcast.19, bf16[1,112,448]{2,1,0:T(8,128)(2,1)} %bitcast.20), custom_call_target="tpu_custom_call" | custom-call | bytes 802816 | tf_op jit(solution)/shard_map/stack/pallas_call | solution.py:330
  43.2 5.3 %collective-permute-start.15 = (bf16[2,2,256,256]{3,2,1,0:T(8,128)(2,1)S(1)}, bf16[2,2,256,256]{3,2,1,0:T(8,128)(2,1)}, u32[]{:S(2)}, u32[]{:S(2)}) collective-permute-start(bf16[2,2,256,256]{3,2,1,0:T(8,128)(2,1)S(1)} %collective-permute-done.14.refs_4_), channel_id=1, source_target_pairs={{4,0},{8,4},{12,8},{5,1},{9,5},{13,9},{6,2},{10,6},{14,10},{7,3},{... | collective-permute-start | bytes 1572872 | tf_op jit(solution)/shard_map/ppermute | solution.py:770
  48.5 4.8 %collective-permute-done.7.refs_3_ = bf16[2,2,256,256]{3,2,1,0:T(8,128)(2,1)S(1)} collective-permute-done((bf16[2,2,256,256]{3,2,1,0:T(8,128)(2,1)}, bf16[2,2,256,256]{3,2,1,0:T(8,128)(2,1)S(1)}, u32[]{:S(2)}, u32[]{:S(2)}) %collective-permute-start.7) | collective-permute-done | bytes 524320 | tf_op jit(solution)/shard_map/ppermute | solution.py:769
  54.5 5.2 %collective-permute-start.17 = (bf16[2,2,256,256]{3,2,1,0:T(8,128)(2,1)S(1)}, bf16[2,2,256,256]{3,2,1,0:T(8,128)(2,1)}, u32[]{:S(2)}, u32[]{:S(2)}) collective-permute-start(bf16[2,2,256,256]{3,2,1,0:T(8,128)(2,1)S(1)} %collective-permute-done.8.refs_5_), channel_id=1, source_target_pairs={{4,0},{8,4},{12,8},{5,1},{9,5},{13,9},{6,2},{10,6},{14,10},{7,3},{... | collective-permute-start | bytes 1572872 | tf_op jit(solution)/shard_map/ppermute | solution.py:770
  59.7 3.6 %collective-permute-start.9 = (bf16[4,112,448]{2,1,0:T(8,128)(2,1)}, bf16[4,112,448]{2,1,0:T(8,128)(2,1)S(1)}, u32[]{:S(2)}, u32[]{:S(2)}) collective-permute-start(bf16[4,112,448]{2,1,0:T(8,128)(2,1)} %stack.24.near_ref), channel_id=1, source_target_pairs={{0,1},{1,0},{2,3},{3,2},{4,5},{5,4},{6,7},{7,6},{8,9},{9,8},{10,11... | collective-permute-start | bytes 1204232 | tf_op jit(solution)/shard_map/ppermute | solution.py:783
  67.5 4.0 %collective-permute-start.20 = (bf16[2,2,256,256]{3,2,1,0:T(8,128)(2,1)}, bf16[2,2,256,256]{3,2,1,0:T(8,128)(2,1)S(1)}, u32[]{:S(2)}, u32[]{:S(2)}) collective-permute-start(bf16[2,2,256,256]{3,2,1,0:T(8,128)(2,1)} %collective-permute-done.15.refs_8_), channel_id=1, source_target_pairs={{4,0},{8,4},{12,8},{5,1},{9,5},{13,9},{6,2},{10,6},{14,10},{7,3},{... | collective-permute-start | bytes 1572872 | tf_op jit(solution)/shard_map/ppermute | solution.py:770
  71.6 4.2 %collective-permute-done.16.refs_7_ = bf16[2,2,256,256]{3,2,1,0:T(8,128)(2,1)} collective-permute-done((bf16[2,2,256,256]{3,2,1,0:T(8,128)(2,1)S(1)}, bf16[2,2,256,256]{3,2,1,0:T(8,128)(2,1)}, u32[]{:S(2)}, u32[]{:S(2)}) %collective-permute-start.16) | collective-permute-done | bytes 524320 | tf_op jit(solution)/shard_map/ppermute | solution.py:769
  77.0 4.5 %collective-permute-start.21 = (bf16[2,2,256,256]{3,2,1,0:T(8,128)(2,1)}, bf16[2,2,256,256]{3,2,1,0:T(8,128)(2,1)S(1)}, u32[]{:S(2)}, u32[]{:S(2)}) collective-permute-start(bf16[2,2,256,256]{3,2,1,0:T(8,128)(2,1)} %collective-permute-done.17.refs_9_), channel_id=1, source_target_pairs={{4,0},{8,4},{12,8},{5,1},{9,5},{13,9},{6,2},{10,6},{14,10},{7,3},{... | collective-permute-start | bytes 1572872 | tf_op jit(solution)/shard_map/ppermute | solution.py:770
  83.9 4.9 %place_rows.1 = (bf16[768,896]{1,0:T(8,128)(2,1)S(1)}, bf16[768,384]{1,0:T(8,128)(2,1)S(1)}, bf16[768,128]{1,0:T(8,128)(2,1)S(1)}, bf16[768,128]{1,0:T(8,128)(2,1)S(1)}, s32[1,128]{1,0:T(1,128)S(1)}) custom-call(s32[4]{0:T(128)S(1)} %copy-done.9, bf16[4,112,448]{2,1,0:T(8,128)(2,1)S(1)} %copy-done.7, bf16[4,112,448]{2,1,0:T(8,128)(2,1)} %collective-permute-done.6.far_ref, ...), custom_call_target="tpu_custom_call" | custom-call | flops 1761607680 | bytes 6291456 | tf_op jit(solution)/shard_map/place_rows/pallas_call | solution.py:527
  88.8 7.4 %near.1.near_ref = bf16[768,384]{1,0:T(8,128)(2,1)S(1)} custom-call(s32[8]{0:T(128)S(1)} %get-tuple-element.72.hop_ref, s32[8]{0:T(128)S(1)} %get-tuple-element.71.held_ref, s32[1,128]{1,0:T(1,128)S(1)} %get-tuple-element.61.length_ref, bf16[768,384]{1,0:T(8,128)(2,1)S(1)} %get-tuple-element.63.query_ref, bf16[768,128]{1,0:T(8,128)(2,1)S(1)} %get-tuple-element.64.key_ref, ...), custom_call_target="tpu_custom_call" | custom-call | flops 660602880 | bytes 2097152 | tf_op jit(solution)/shard_map/near/pallas_call | solution.py:641
  98.1 2.8 %far.2 = (bf16[192,384]{1,0:T(8,128)(2,1)S(1)}, bf16[192,384]{1,0:T(8,128)(2,1)S(1)}) custom-call(s32[4]{0:T(128)S(1)} %copy-done.9, s32[8]{0:T(128)S(1)} %get-tuple-element.72.hop_ref, s32[8]{0:T(128)S(1)} %get-tuple-element.71.held_ref, s32[1,128]{1,0:T(1,128)S(1)} %get-tuple-element.61.length_ref, bf16[768,384]{1,0:T(8,128)(2,1)S(1)} %get-tuple-element.63.query_ref, ...), custom_call_target="tpu_custom_call" | custom-call | flops 330301440 | bytes 1048576 | tf_op jit(solution)/shard_map/far/pallas_call | solution.py:641
  102.2 2.8 %far.3 = (bf16[192,384]{1,0:T(8,128)(2,1)S(1)}, bf16[192,384]{1,0:T(8,128)(2,1)S(1)}) custom-call(s32[4]{0:T(128)S(1)} %copy-done.9, s32[8]{0:T(128)S(1)} %get-tuple-element.72.hop_ref, s32[8]{0:T(128)S(1)} %get-tuple-element.71.held_ref, s32[1,128]{1,0:T(1,128)S(1)} %get-tuple-element.61.length_ref, bf16[768,384]{1,0:T(8,128)(2,1)S(1)} %get-tuple-element.63.query_ref, ...), custom_call_target="tpu_custom_call" | custom-call | flops 330301440 | bytes 1048576 | tf_op jit(solution)/shard_map/far/pallas_call | solution.py:641
  104.9 2.0 %collective-permute-start.22 = (bf16[192,384]{1,0:T(8,128)(2,1)S(1)}, bf16[192,384]{1,0:T(8,128)(2,1)S(1)}, u32[]{:S(2)}, u32[]{:S(2)}) collective-permute-start(bf16[192,384]{1,0:T(8,128)(2,1)S(1)} %get-tuple-element.69), channel_id=1, source_target_pairs={{0,1},{1,0},{2,3},{3,2},{4,5},{5,4},{6,7},{7,6},{8,9},{9,8},{10,11... | collective-permute-start | bytes 442376 | tf_op jit(solution)/shard_map/ppermute | solution.py:810
  108.0 4.5 %collective-permute-done.24.refs_3_ = bf16[192,384]{1,0:T(8,128)(2,1)S(1)} collective-permute-done((bf16[192,384]{1,0:T(8,128)(2,1)S(1)}, bf16[192,384]{1,0:T(8,128)(2,1)S(1)}, u32[]{:S(2)}, u32[]{:S(2)}) %collective-permute-start.24) | collective-permute-done | bytes 147488 | tf_op jit(solution)/shard_map/ppermute | solution.py:810
  112.5 2.2 %output.1 = bf16[2,96,896]{2,1,0:T(8,128)(2,1)} custom-call(s32[4]{0:T(128)S(1)} %copy-done.9, s32[1,128]{1,0:T(1,128)S(1)} %get-tuple-element.61.length_ref, bf16[768,896]{1,0:T(8,128)(2,1)S(1)} %get-tuple-element.62.states_ref, bf16[1536,896]{1,0:T(8,128)(2,1)S(1)} %copy-done.1, bf16[192,384]{1,0:T(8,128)(2,1)S(1)} %get-tuple-element.68.refs_0_, ...), custom_call_target="tpu_custom_call" | custom-call | flops 528482304 | bytes 2752512 | tf_op jit(solution)/shard_map/output/pallas_call | solution.py:698
  (95 shorter events, 31.5 us)
Async XLA Ops:
  2.4 17.7 %collective-permute-start.11 = (bf16[2,256,256]{2,1,0:T(8,128)(2,1)}, bf16[2,256,256]{2,1,0:T(8,128)(2,1)S(1)}, u32[]{:S(2)}, u32[]{:S(2)}) collective-permute-start(bf16[2,256,256]{2,1,0:T(8,128)(2,1)} %get-tuple-element.54), channel_id=1, source_target_pairs={{0,1},{1,0},{2,3},{3,2},{4,5},{5,4},{6,7},{7,6},{8,9},{9,8},{10,11... | collective-permute-start | bytes 786440 | tf_op jit(solution)/shard_map/ppermute | solution.py:750
  9.0 7.9 %collective-permute-start.2 = (bf16[256,448]{1,0:T(8,128)(2,1)S(1)}, bf16[256,448]{1,0:T(8,128)(2,1)S(1)}, u32[]{:S(2)}, u32[]{:S(2)}) collective-permute-start(bf16[256,448]{1,0:T(8,128)(2,1)S(1)} %get-tuple-element.41), channel_id=1, source_target_pairs={{0,2},{2,0},{1,3},{3,1},{4,6},{6,4},{5,7},{7,5},{8,10},{10,8},{9,1... | collective-permute-start | bytes 688136 | tf_op jit(solution)/shard_map/ppermute | solution.py:747
  10.2 15.2 %collective-permute-start = (bf16[2,256,256]{2,1,0:T(8,128)(2,1)S(1)}, bf16[2,256,256]{2,1,0:T(8,128)(2,1)S(1)}, u32[]{:S(2)}, u32[]{:S(2)}) collective-permute-start(bf16[2,256,256]{2,1,0:T(8,128)(2,1)S(1)} %copy-done.23), channel_id=1, source_target_pairs={{0,2},{1,3},{2,0},{3,1},{4,6},{5,7},{6,4},{7,5},{8,10},{9,11},{10,... | collective-permute-start | bytes 786440 | tf_op jit(solution)/shard_map/ppermute | solution.py:751
  10.4 18.1 %collective-permute-start.1 = (bf16[2,256,256]{2,1,0:T(8,128)(2,1)S(1)}, bf16[2,256,256]{2,1,0:T(8,128)(2,1)S(1)}, u32[]{:S(2)}, u32[]{:S(2)}) collective-permute-start(bf16[2,256,256]{2,1,0:T(8,128)(2,1)S(1)} %copy-done.22), channel_id=1, source_target_pairs={{0,3},{1,2},{2,1},{3,0},{4,7},{5,6},{6,5},{7,4},{8,11},{9,10},{10,... | collective-permute-start | bytes 786440 | tf_op jit(solution)/shard_map/ppermute | solution.py:752
  19.9 12.7 %collective-permute-start.3 = (bf16[112,448]{1,0:T(8,128)(2,1)}, bf16[112,448]{1,0:T(8,128)(2,1)S(1)}, u32[]{:S(2)}, u32[]{:S(2)}) collective-permute-start(bf16[112,448]{1,0:T(8,128)(2,1)} %get-tuple-element.44), channel_id=1, source_target_pairs={{0,4},{4,0},{8,12},{12,8},{1,5},{5,1},{9,13},{13,9},{2,6},{6,2},{1... | collective-permute-start | bytes 301064 | tf_op jit(solution)/shard_map/ppermute | solution.py:761
  20.1 12.5 %collective-permute-start.4 = (bf16[112,448]{1,0:T(8,128)(2,1)}, bf16[112,448]{1,0:T(8,128)(2,1)S(1)}, u32[]{:S(2)}, u32[]{:S(2)}) collective-permute-start(bf16[112,448]{1,0:T(8,128)(2,1)} %get-tuple-element.45), channel_id=1, source_target_pairs={{0,8},{4,12},{8,0},{12,4},{1,9},{5,13},{9,1},{13,5},{2,10},{6,14},... | collective-permute-start | bytes 301064 | tf_op jit(solution)/shard_map/ppermute | solution.py:761
  20.2 12.4 %collective-permute-start.5 = (bf16[112,448]{1,0:T(8,128)(2,1)}, bf16[112,448]{1,0:T(8,128)(2,1)S(1)}, u32[]{:S(2)}, u32[]{:S(2)}) collective-permute-start(bf16[112,448]{1,0:T(8,128)(2,1)} %get-tuple-element.46), channel_id=1, source_target_pairs={{0,12},{4,8},{8,4},{12,0},{1,13},{5,9},{9,5},{13,1},{2,14},{6,10},... | collective-permute-start | bytes 301064 | tf_op jit(solution)/shard_map/ppermute | solution.py:761
  25.3 16.6 %collective-permute-start.12 = (bf16[2,2,256,256]{3,2,1,0:T(8,128)(2,1)}, bf16[2,2,256,256]{3,2,1,0:T(8,128)(2,1)S(1)}, u32[]{:S(2)}, u32[]{:S(2)}) collective-permute-start(bf16[2,2,256,256]{3,2,1,0:T(8,128)(2,1)} %stack.25.refs_0_), channel_id=1, source_target_pairs={{0,4},{4,8},{8,12},{1,5},{5,9},{9,13},{2,6},{6,10},{10,14},{3,7},{... | collective-permute-start | bytes 1572872 | tf_op jit(solution)/shard_map/ppermute | solution.py:769
  28.5 14.7 %collective-permute-start.14 = (bf16[2,2,256,256]{3,2,1,0:T(8,128)(2,1)}, bf16[2,2,256,256]{3,2,1,0:T(8,128)(2,1)S(1)}, u32[]{:S(2)}, u32[]{:S(2)}) collective-permute-start(bf16[2,2,256,256]{3,2,1,0:T(8,128)(2,1)} %stack.25.refs_0_), channel_id=1, source_target_pairs={{4,0},{8,4},{12,8},{5,1},{9,5},{13,9},{6,2},{10,6},{14,10},{7,3},{... | collective-permute-start | bytes 1572872 | tf_op jit(solution)/shard_map/ppermute | solution.py:770
  33.3 20.0 %collective-permute-start.7 = (bf16[2,2,256,256]{3,2,1,0:T(8,128)(2,1)}, bf16[2,2,256,256]{3,2,1,0:T(8,128)(2,1)S(1)}, u32[]{:S(2)}, u32[]{:S(2)}) collective-permute-start(bf16[2,2,256,256]{3,2,1,0:T(8,128)(2,1)} %stack.23.refs_1_), channel_id=1, source_target_pairs={{0,4},{4,8},{8,12},{1,5},{5,9},{9,13},{2,6},{6,10},{10,14},{3,7},{... | collective-permute-start | bytes 1572872 | tf_op jit(solution)/shard_map/ppermute | solution.py:769
  34.6 20.0 %collective-permute-start.8 = (bf16[2,2,256,256]{3,2,1,0:T(8,128)(2,1)}, bf16[2,2,256,256]{3,2,1,0:T(8,128)(2,1)S(1)}, u32[]{:S(2)}, u32[]{:S(2)}) collective-permute-start(bf16[2,2,256,256]{3,2,1,0:T(8,128)(2,1)} %stack.23.refs_1_), channel_id=1, source_target_pairs={{4,0},{8,4},{12,8},{5,1},{9,5},{13,9},{6,2},{10,6},{14,10},{7,3},{... | collective-permute-start | bytes 1572872 | tf_op jit(solution)/shard_map/ppermute | solution.py:770
  40.5 19.3 %collective-permute-start.6 = (bf16[4,112,448]{2,1,0:T(8,128)(2,1)}, bf16[4,112,448]{2,1,0:T(8,128)(2,1)}, u32[]{:S(2)}, u32[]{:S(2)}) collective-permute-start(bf16[4,112,448]{2,1,0:T(8,128)(2,1)} %stack.24.near_ref), channel_id=1, source_target_pairs={{0,2},{2,0},{1,3},{3,1},{4,6},{6,4},{5,7},{7,5},{8,10},{10,8},{9,1... | collective-permute-start | bytes 1204232 | tf_op jit(solution)/shard_map/ppermute | solution.py:780
  41.9 24.3 %collective-permute-start.13 = (bf16[2,2,256,256]{3,2,1,0:T(8,128)(2,1)S(1)}, bf16[2,2,256,256]{3,2,1,0:T(8,128)(2,1)}, u32[]{:S(2)}, u32[]{:S(2)}) collective-permute-start(bf16[2,2,256,256]{3,2,1,0:T(8,128)(2,1)S(1)} %collective-permute-done.12.refs_2_), channel_id=1, source_target_pairs={{0,4},{4,8},{8,12},{1,5},{5,9},{9,13},{2,6},{6,10},{10,14},{3,7},{... | collective-permute-start | bytes 1572872 | tf_op jit(solution)/shard_map/ppermute | solution.py:769
  43.2 24.3 %collective-permute-start.15 = (bf16[2,2,256,256]{3,2,1,0:T(8,128)(2,1)S(1)}, bf16[2,2,256,256]{3,2,1,0:T(8,128)(2,1)}, u32[]{:S(2)}, u32[]{:S(2)}) collective-permute-start(bf16[2,2,256,256]{3,2,1,0:T(8,128)(2,1)S(1)} %collective-permute-done.14.refs_4_), channel_id=1, source_target_pairs={{4,0},{8,4},{12,8},{5,1},{9,5},{13,9},{6,2},{10,6},{14,10},{7,3},{... | collective-permute-start | bytes 1572872 | tf_op jit(solution)/shard_map/ppermute | solution.py:770
  53.2 22.5 %collective-permute-start.16 = (bf16[2,2,256,256]{3,2,1,0:T(8,128)(2,1)S(1)}, bf16[2,2,256,256]{3,2,1,0:T(8,128)(2,1)}, u32[]{:S(2)}, u32[]{:S(2)}) collective-permute-start(bf16[2,2,256,256]{3,2,1,0:T(8,128)(2,1)S(1)} %collective-permute-done.7.refs_3_), channel_id=1, source_target_pairs={{0,4},{4,8},{8,12},{1,5},{5,9},{9,13},{2,6},{6,10},{10,14},{3,7},{... | collective-permute-start | bytes 1572872 | tf_op jit(solution)/shard_map/ppermute | solution.py:769
  54.5 22.5 %collective-permute-start.17 = (bf16[2,2,256,256]{3,2,1,0:T(8,128)(2,1)S(1)}, bf16[2,2,256,256]{3,2,1,0:T(8,128)(2,1)}, u32[]{:S(2)}, u32[]{:S(2)}) collective-permute-start(bf16[2,2,256,256]{3,2,1,0:T(8,128)(2,1)S(1)} %collective-permute-done.8.refs_5_), channel_id=1, source_target_pairs={{4,0},{8,4},{12,8},{5,1},{9,5},{13,9},{6,2},{10,6},{14,10},{7,3},{... | collective-permute-start | bytes 1572872 | tf_op jit(solution)/shard_map/ppermute | solution.py:770
  59.7 5.2 %collective-permute-start.9 = (bf16[4,112,448]{2,1,0:T(8,128)(2,1)}, bf16[4,112,448]{2,1,0:T(8,128)(2,1)S(1)}, u32[]{:S(2)}, u32[]{:S(2)}) collective-permute-start(bf16[4,112,448]{2,1,0:T(8,128)(2,1)} %stack.24.near_ref), channel_id=1, source_target_pairs={{0,1},{1,0},{2,3},{3,2},{4,5},{5,4},{6,7},{7,6},{8,9},{9,8},{10,11... | collective-permute-start | bytes 1204232 | tf_op jit(solution)/shard_map/ppermute | solution.py:783
  65.8 16.0 %collective-permute-start.10 = (bf16[4,112,448]{2,1,0:T(8,128)(2,1)}, bf16[4,112,448]{2,1,0:T(8,128)(2,1)}, u32[]{:S(2)}, u32[]{:S(2)}) collective-permute-start(bf16[4,112,448]{2,1,0:T(8,128)(2,1)} %collective-permute-done.6.far_ref), channel_id=1, source_target_pairs={{0,1},{1,0},{2,3},{3,2},{4,5},{5,4},{6,7},{7,6},{8,9},{9,8},{10,11... | collective-permute-start | bytes 1204232 | tf_op jit(solution)/shard_map/ppermute | solution.py:783
  66.2 30.0 %collective-permute-start.18 = (bf16[2,2,256,256]{3,2,1,0:T(8,128)(2,1)}, bf16[2,2,256,256]{3,2,1,0:T(8,128)(2,1)S(1)}, u32[]{:S(2)}, u32[]{:S(2)}) collective-permute-start(bf16[2,2,256,256]{3,2,1,0:T(8,128)(2,1)} %collective-permute-done.13.refs_6_), channel_id=1, source_target_pairs={{0,4},{4,8},{8,12},{1,5},{5,9},{9,13},{2,6},{6,10},{10,14},{3,7},{... | collective-permute-start | bytes 1572872 | tf_op jit(solution)/shard_map/ppermute | solution.py:769
  67.5 28.7 %collective-permute-start.20 = (bf16[2,2,256,256]{3,2,1,0:T(8,128)(2,1)}, bf16[2,2,256,256]{3,2,1,0:T(8,128)(2,1)S(1)}, u32[]{:S(2)}, u32[]{:S(2)}) collective-permute-start(bf16[2,2,256,256]{3,2,1,0:T(8,128)(2,1)} %collective-permute-done.15.refs_8_), channel_id=1, source_target_pairs={{4,0},{8,4},{12,8},{5,1},{9,5},{13,9},{6,2},{10,6},{14,10},{7,3},{... | collective-permute-start | bytes 1572872 | tf_op jit(solution)/shard_map/ppermute | solution.py:770
  75.7 22.4 %collective-permute-start.19 = (bf16[2,2,256,256]{3,2,1,0:T(8,128)(2,1)}, bf16[2,2,256,256]{3,2,1,0:T(8,128)(2,1)S(1)}, u32[]{:S(2)}, u32[]{:S(2)}) collective-permute-start(bf16[2,2,256,256]{3,2,1,0:T(8,128)(2,1)} %collective-permute-done.16.refs_7_), channel_id=1, source_target_pairs={{0,4},{4,8},{8,12},{1,5},{5,9},{9,13},{2,6},{6,10},{10,14},{3,7},{... | collective-permute-start | bytes 1572872 | tf_op jit(solution)/shard_map/ppermute | solution.py:769
  77.0 21.1 %collective-permute-start.21 = (bf16[2,2,256,256]{3,2,1,0:T(8,128)(2,1)}, bf16[2,2,256,256]{3,2,1,0:T(8,128)(2,1)S(1)}, u32[]{:S(2)}, u32[]{:S(2)}) collective-permute-start(bf16[2,2,256,256]{3,2,1,0:T(8,128)(2,1)} %collective-permute-done.17.refs_9_), channel_id=1, source_target_pairs={{4,0},{8,4},{12,8},{5,1},{9,5},{13,9},{6,2},{10,6},{14,10},{7,3},{... | collective-permute-start | bytes 1572872 | tf_op jit(solution)/shard_map/ppermute | solution.py:770
  100.9 7.1 %collective-permute-start.23 = (bf16[192,384]{1,0:T(8,128)(2,1)S(1)}, bf16[192,384]{1,0:T(8,128)(2,1)S(1)}, u32[]{:S(2)}, u32[]{:S(2)}) collective-permute-start(bf16[192,384]{1,0:T(8,128)(2,1)S(1)} %get-tuple-element.66), channel_id=1, source_target_pairs={{0,2},{1,3},{2,0},{3,1},{4,6},{5,7},{6,4},{7,5},{8,10},{9,11},{10,... | collective-permute-start | bytes 442376 | tf_op jit(solution)/shard_map/ppermute | solution.py:810
  107.0 5.5 %collective-permute-start.24 = (bf16[192,384]{1,0:T(8,128)(2,1)S(1)}, bf16[192,384]{1,0:T(8,128)(2,1)S(1)}, u32[]{:S(2)}, u32[]{:S(2)}) collective-permute-start(bf16[192,384]{1,0:T(8,128)(2,1)S(1)} %get-tuple-element.70), channel_id=1, source_target_pairs={{0,3},{1,2},{2,1},{3,0},{4,7},{5,6},{6,5},{7,4},{8,11},{9,10},{10,... | collective-permute-start | bytes 442376 | tf_op jit(solution)/shard_map/ppermute | solution.py:810
  (27 other events, 503.5 us)

commit v11 on v10

--- a/solution.py
+++ b/solution.py
@@ -587,18 +587,24 @@
 def near_kernel(hop_ref, held_ref, length_ref, query_ref, key_ref, value_ref, *refs, hops):
     prompt_refs, (out_ref, kv, sem) = refs[: 2 * len(hops)], refs[2 * len(hops) :]
     sessions = hop_ref.shape[0]
-    for start in (True, False):
-        for i in range(sessions):
-            hop = jnp.where(among(hop_ref[i], hops), hop_ref[i], 0)
-            fetches(hop, prompt_refs, held_ref[i], kv.at[i], sem.at[i], hops, start)
     for i in range(sessions):
-        rows = slice(i * SLOTS, (i + 1) * SLOTS)
-        mixed = session_attention(
-            query_ref[rows], key_ref[rows], value_ref[rows],
-            kv[i].reshape(PROMPT, 2 * HD), length_ref[0, i],
-        )
-        for h in range(PER_GROUP):
-            out_ref[rows, h * HD : (h + 1) * HD] = mixed[h * SLOTS : (h + 1) * SLOTS]
+        fetches(hop_ref[i], prompt_refs, held_ref[i], kv.at[i], sem.at[i], hops, True)
+
+    def work(i, _):
+        @pl.when(among(hop_ref[i], hops))
+        def _():
+            fetches(hop_ref[i], prompt_refs, held_ref[i], kv.at[i], sem.at[i], hops, False)
+            rows = pl.ds(pl.multiple_of(i * SLOTS, SLOTS), SLOTS)
+            mixed = session_attention(
+                query_ref[rows], key_ref[rows], value_ref[rows],
+                kv[i].reshape(PROMPT, 2 * HD), length_ref[0, i],
+            )
+            for h in range(PER_GROUP):
+                out_ref[rows, h * HD : (h + 1) * HD] = mixed[h * SLOTS : (h + 1) * SLOTS]
+
+        return 0
+
+    lax.fori_loop(0, sessions, work, 0)
 
 
 def far_kernel(index_ref, hop_ref, held_ref, length_ref, query_ref, key_ref, value_ref, near_ref,

time: 117 us -> 117 us (level)
  the two profiles are of different devices: /device:TPU:29 before, /device:TPU:0 now
where the time goes in v11:
time: 117 us; the launch traced here: 114 us
  starting transfers between devices  55.5 us (47%)
  Pallas kernels  33 us (28%)
  waiting for transfers between devices  16.2 us (14%)
  local copies, waits for them, and re-layouts  9.01 us (8%)
    ppermute x6, starting transfers between devices, travel(): right[chunk] = lax.ppermute(right[chunk], 'sess', shifted(planes, 1))  33.6 us
    pallas_call x3, Pallas kernels, attention_call(): pl.pallas_call(kernel, in_specs=[SMEM] * len(scalars) + [VMEM] * len(arra...  10.7 us
    unnamed x52, local copies, waits for them, and re-layouts  8.93 us
    ppermute x6, starting transfers between devices, travel(): left[chunk] = lax.ppermute(left[chunk], 'sess', shifted(planes, -1))  7.73 us
    pallas_call x3, Pallas kernels, stack(): pl.pallas_call(stack_kernel, in_specs=[VMEM] * len(arrays), out_specs=VME...  5.61 us
    ppermute x6, waiting for transfers between devices, travel(): right[chunk] = lax.ppermute(right[chunk], 'sess', shifted(planes, 1))  5.45 us
    pallas_call x1, Pallas kernels, place_rows(): pl.pallas_call(functools.partial(place_kernel, slot_cap=slot_cap, togethe...  4.87 us
    ppermute x3, starting transfers between devices, line_body(): lax.ppermute(routed[by], 'sess', swapped(planes, by))  4.62 us
  transfers between devices with their start and end apart: 25, of which 8 were waited for; matrix products, arithmetic and copies ran while one was open for 0% of the time, Pallas kernels for 23%

profile of v11, /device:TPU:0, one launch (start us, length us, event | category | flops | bytes accessed | tf_op | source)
XLA Modules:
  0.0 114.4 jit_solution(16742135339527186691)
XLA Ops:
  0.0 2.4 %split_heads.1 = (bf16[2,256,256]{2,1,0:T(8,128)(2,1)}, bf16[2,256,256]{2,1,0:T(8,128)(2,1)}, bf16[2,256,256]{2,1,0:T(8,128)(2,1)}, bf16[2,256,256]{2,1,0:T(8,128)(2,1)}) custom-call(s32[1]{0:T(128)} %bitcast.3.head_ref, bf16[2,256,1024]{2,1,0:T(8,128)(2,1)} %cache_ref.1), custom_call_target="tpu_custom_call" | custom-call | bytes 2097152 | tf_op jit(solution)/shard_map/split_heads/pallas_call | solution.py:308
  3.0 1.9 %copy-done = bf16[1792,896]{1,0:T(8,128)(2,1)S(1)} copy-done((bf16[1792,896]{1,0:T(8,128)(2,1)S(1)}, bf16[1792,896]{1,0:T(8,128)(2,1)}, u32[]{:S(2)}) %copy-start) | copy-done | bytes 3211288
  8.7 2.5 %collective-permute-start.2 = (bf16[256,448]{1,0:T(8,128)(2,1)S(1)}, bf16[256,448]{1,0:T(8,128)(2,1)S(1)}, u32[]{:S(2)}, u32[]{:S(2)}) collective-permute-start(bf16[256,448]{1,0:T(8,128)(2,1)S(1)} %get-tuple-element.41), channel_id=1, source_target_pairs={{0,2},{2,0},{1,3},{3,1},{4,6},{6,4},{5,7},{7,5},{8,10},{10,8},{9,1... | collective-permute-start | bytes 688136 | tf_op jit(solution)/shard_map/ppermute | solution.py:753
  12.8 3.0 %head_weights.1.weight_ref = bf16[896,640]{1,0:T(8,128)(2,1)} custom-call(s32[4]{0:T(128)} %copy-done.8, bf16[896,1536]{1,0:T(8,128)(2,1)} %q_ref.1, bf16[896,512]{1,0:T(8,128)(2,1)} %k_ref.1, bf16[896,512]{1,0:T(8,128)(2,1)} %v_ref.1), custom_call_target="tpu_custom_call" | custom-call | bytes 2293760 | tf_op jit(solution)/shard_map/head_weights/pallas_call | solution.py:434
  15.9 2.5 %collective-permute-done.2.came_ref = bf16[256,448]{1,0:T(8,128)(2,1)S(1)} collective-permute-done((bf16[256,448]{1,0:T(8,128)(2,1)S(1)}, bf16[256,448]{1,0:T(8,128)(2,1)S(1)}, u32[]{:S(2)}, u32[]{:S(2)}) %collective-permute-start.2) | collective-permute-done | bytes 229408 | tf_op jit(solution)/shard_map/ppermute | solution.py:753
  19.1 2.3 %route.1 = (bf16[112,448]{1,0:T(8,128)(2,1)}, bf16[112,448]{1,0:T(8,128)(2,1)}, bf16[112,448]{1,0:T(8,128)(2,1)}, bf16[112,448]{1,0:T(8,128)(2,1)}) custom-call(s32[4]{0:T(128)} %copy-done.8, f32[256,448]{1,0:T(8,128)} %copy-done.6, bf16[256,448]{1,0:T(8,128)(2,1)} %copy-done.14, s32[1,256]{1,0:T(1,128)} %bitcast.21), custom_call_target="tpu_custom_call" | custom-call | flops 102760448 | bytes 917504 | tf_op jit(solution)/shard_map/route/pallas_call | solution.py:401
  21.4 2.0 %collective-permute-start.3 = (bf16[112,448]{1,0:T(8,128)(2,1)}, bf16[112,448]{1,0:T(8,128)(2,1)S(1)}, u32[]{:S(2)}, u32[]{:S(2)}) collective-permute-start(bf16[112,448]{1,0:T(8,128)(2,1)} %get-tuple-element.44), channel_id=1, source_target_pairs={{0,4},{4,0},{8,12},{12,8},{1,5},{5,1},{9,13},{13,9},{2,6},{6,2},{1... | collective-permute-start | bytes 301064 | tf_op jit(solution)/shard_map/ppermute | solution.py:767
  23.4 2.6 %collective-permute-start.4 = (bf16[112,448]{1,0:T(8,128)(2,1)}, bf16[112,448]{1,0:T(8,128)(2,1)S(1)}, u32[]{:S(2)}, u32[]{:S(2)}) collective-permute-start(bf16[112,448]{1,0:T(8,128)(2,1)} %get-tuple-element.45), channel_id=1, source_target_pairs={{0,8},{4,12},{8,0},{12,4},{1,9},{5,13},{9,1},{13,5},{2,10},{6,14},... | collective-permute-start | bytes 301064 | tf_op jit(solution)/shard_map/ppermute | solution.py:767
  28.6 2.4 %collective-permute-start.12 = (bf16[2,2,256,256]{3,2,1,0:T(8,128)(2,1)}, bf16[2,2,256,256]{3,2,1,0:T(8,128)(2,1)S(1)}, u32[]{:S(2)}, u32[]{:S(2)}) collective-permute-start(bf16[2,2,256,256]{3,2,1,0:T(8,128)(2,1)} %stack.25.refs_0_), channel_id=1, source_target_pairs={{0,4},{4,8},{8,12},{1,5},{5,9},{9,13},{2,6},{6,10},{10,14},{3,7},{... | collective-permute-start | bytes 1572872 | tf_op jit(solution)/shard_map/ppermute | solution.py:775
  35.7 4.2 %collective-permute-start.7 = (bf16[2,2,256,256]{3,2,1,0:T(8,128)(2,1)}, bf16[2,2,256,256]{3,2,1,0:T(8,128)(2,1)S(1)}, u32[]{:S(2)}, u32[]{:S(2)}) collective-permute-start(bf16[2,2,256,256]{3,2,1,0:T(8,128)(2,1)} %stack.23.refs_1_), channel_id=1, source_target_pairs={{0,4},{4,8},{8,12},{1,5},{5,9},{9,13},{2,6},{6,10},{10,14},{3,7},{... | collective-permute-start | bytes 1572872 | tf_op jit(solution)/shard_map/ppermute | solution.py:775
  41.2 1.9 %stack.24.near_ref = bf16[4,112,448]{2,1,0:T(8,128)(2,1)} custom-call(bf16[1,112,448]{2,1,0:T(8,128)(2,1)} %bitcast.17, bf16[1,112,448]{2,1,0:T(8,128)(2,1)} %bitcast.18, bf16[1,112,448]{2,1,0:T(8,128)(2,1)} %bitcast.19, bf16[1,112,448]{2,1,0:T(8,128)(2,1)} %bitcast.20), custom_call_target="tpu_custom_call" | custom-call | bytes 802816 | tf_op jit(solution)/shard_map/stack/pallas_call | solution.py:330
  44.6 6.7 %collective-permute-start.13 = (bf16[2,2,256,256]{3,2,1,0:T(8,128)(2,1)S(1)}, bf16[2,2,256,256]{3,2,1,0:T(8,128)(2,1)}, u32[]{:S(2)}, u32[]{:S(2)}) collective-permute-start(bf16[2,2,256,256]{3,2,1,0:T(8,128)(2,1)S(1)} %collective-permute-done.12.refs_2_), channel_id=1, source_target_pairs={{0,4},{4,8},{8,12},{1,5},{5,9},{9,13},{2,6},{6,10},{10,14},{3,7},{... | collective-permute-start | bytes 1572872 | tf_op jit(solution)/shard_map/ppermute | solution.py:775
  52.5 2.3 %collective-permute-done.7.refs_3_ = bf16[2,2,256,256]{3,2,1,0:T(8,128)(2,1)S(1)} collective-permute-done((bf16[2,2,256,256]{3,2,1,0:T(8,128)(2,1)}, bf16[2,2,256,256]{3,2,1,0:T(8,128)(2,1)S(1)}, u32[]{:S(2)}, u32[]{:S(2)}) %collective-permute-start.7) | collective-permute-done | bytes 524320 | tf_op jit(solution)/shard_map/ppermute | solution.py:775
  54.9 7.6 %collective-permute-start.16 = (bf16[2,2,256,256]{3,2,1,0:T(8,128)(2,1)S(1)}, bf16[2,2,256,256]{3,2,1,0:T(8,128)(2,1)}, u32[]{:S(2)}, u32[]{:S(2)}) collective-permute-start(bf16[2,2,256,256]{3,2,1,0:T(8,128)(2,1)S(1)} %collective-permute-done.7.refs_3_), channel_id=1, source_target_pairs={{0,4},{4,8},{8,12},{1,5},{5,9},{9,13},{2,6},{6,10},{10,14},{3,7},{... | collective-permute-start | bytes 1572872 | tf_op jit(solution)/shard_map/ppermute | solution.py:775
  63.9 2.0 %collective-permute-done.9.near_core_ref = bf16[4,112,448]{2,1,0:T(8,128)(2,1)S(1)} collective-permute-done((bf16[4,112,448]{2,1,0:T(8,128)(2,1)}, bf16[4,112,448]{2,1,0:T(8,128)(2,1)S(1)}, u32[]{:S(2)}, u32[]{:S(2)}) %collective-permute-start.9) | collective-permute-done | bytes 401440 | tf_op jit(solution)/shard_map/ppermute | solution.py:789
  66.9 5.9 %collective-permute-start.18 = (bf16[2,2,256,256]{3,2,1,0:T(8,128)(2,1)}, bf16[2,2,256,256]{3,2,1,0:T(8,128)(2,1)S(1)}, u32[]{:S(2)}, u32[]{:S(2)}) collective-permute-start(bf16[2,2,256,256]{3,2,1,0:T(8,128)(2,1)} %collective-permute-done.13.refs_6_), channel_id=1, source_target_pairs={{0,4},{4,8},{8,12},{1,5},{5,9},{9,13},{2,6},{6,10},{10,14},{3,7},{... | collective-permute-start | bytes 1572872 | tf_op jit(solution)/shard_map/ppermute | solution.py:775
  74.1 3.1 %collective-permute-done.16.refs_7_ = bf16[2,2,256,256]{3,2,1,0:T(8,128)(2,1)} collective-permute-done((bf16[2,2,256,256]{3,2,1,0:T(8,128)(2,1)S(1)}, bf16[2,2,256,256]{3,2,1,0:T(8,128)(2,1)}, u32[]{:S(2)}, u32[]{:S(2)}) %collective-permute-start.16) | collective-permute-done | bytes 524320 | tf_op jit(solution)/shard_map/ppermute | solution.py:775
  77.2 6.8 %collective-permute-start.19 = (bf16[2,2,256,256]{3,2,1,0:T(8,128)(2,1)}, bf16[2,2,256,256]{3,2,1,0:T(8,128)(2,1)S(1)}, u32[]{:S(2)}, u32[]{:S(2)}) collective-permute-start(bf16[2,2,256,256]{3,2,1,0:T(8,128)(2,1)} %collective-permute-done.16.refs_7_), channel_id=1, source_target_pairs={{0,4},{4,8},{8,12},{1,5},{5,9},{9,13},{2,6},{6,10},{10,14},{3,7},{... | collective-permute-start | bytes 1572872 | tf_op jit(solution)/shard_map/ppermute | solution.py:775
  87.8 4.9 %place_rows.1 = (bf16[768,896]{1,0:T(8,128)(2,1)S(1)}, bf16[768,384]{1,0:T(8,128)(2,1)S(1)}, bf16[768,128]{1,0:T(8,128)(2,1)S(1)}, bf16[768,128]{1,0:T(8,128)(2,1)S(1)}, s32[1,128]{1,0:T(1,128)S(1)}) custom-call(s32[4]{0:T(128)S(1)} %copy-done.9, bf16[4,112,448]{2,1,0:T(8,128)(2,1)S(1)} %copy-done.7, bf16[4,112,448]{2,1,0:T(8,128)(2,1)} %collective-permute-done.6.far_ref, ...), custom_call_target="tpu_custom_call" | custom-call | flops 1761607680 | bytes 6291456 | tf_op jit(solution)/shard_map/place_rows/pallas_call | solution.py:527
  92.7 8.0 %near.1.near_ref = bf16[768,384]{1,0:T(8,128)(2,1)S(1)} custom-call(s32[8]{0:T(128)S(1)} %get-tuple-element.72.hop_ref, s32[8]{0:T(128)S(1)} %get-tuple-element.71.held_ref, s32[1,128]{1,0:T(1,128)S(1)} %get-tuple-element.61.length_ref, bf16[768,384]{1,0:T(8,128)(2,1)S(1)} %get-tuple-element.63.query_ref, bf16[768,128]{1,0:T(8,128)(2,1)S(1)} %get-tuple-element.64.key_ref, ...), custom_call_target="tpu_custom_call" | custom-call | flops 660602880 | bytes 2097152 | tf_op jit(solution)/shard_map/near/pallas_call | solution.py:647
  102.0 2.0 %far.2 = (bf16[192,384]{1,0:T(8,128)(2,1)S(1)}, bf16[192,384]{1,0:T(8,128)(2,1)S(1)}) custom-call(s32[4]{0:T(128)S(1)} %copy-done.9, s32[8]{0:T(128)S(1)} %get-tuple-element.72.hop_ref, s32[8]{0:T(128)S(1)} %get-tuple-element.71.held_ref, s32[1,128]{1,0:T(1,128)S(1)} %get-tuple-element.61.length_ref, bf16[768,384]{1,0:T(8,128)(2,1)S(1)} %get-tuple-element.63.query_ref, ...), custom_call_target="tpu_custom_call" | custom-call | flops 330301440 | bytes 1048576 | tf_op jit(solution)/shard_map/far/pallas_call | solution.py:647
  105.5 2.6 %collective-permute-start.24 = (bf16[192,384]{1,0:T(8,128)(2,1)S(1)}, bf16[192,384]{1,0:T(8,128)(2,1)S(1)}, u32[]{:S(2)}, u32[]{:S(2)}) collective-permute-start(bf16[192,384]{1,0:T(8,128)(2,1)S(1)} %get-tuple-element.70), channel_id=1, source_target_pairs={{0,3},{1,2},{2,1},{3,0},{4,7},{5,6},{6,5},{7,4},{8,11},{9,10},{10,... | collective-permute-start | bytes 442376 | tf_op jit(solution)/shard_map/ppermute | solution.py:816
  109.2 3.0 %collective-permute-done.24.refs_3_ = bf16[192,384]{1,0:T(8,128)(2,1)S(1)} collective-permute-done((bf16[192,384]{1,0:T(8,128)(2,1)S(1)}, bf16[192,384]{1,0:T(8,128)(2,1)S(1)}, u32[]{:S(2)}, u32[]{:S(2)}) %collective-permute-start.24) | collective-permute-done | bytes 147488 | tf_op jit(solution)/shard_map/ppermute | solution.py:816
  112.2 2.2 %output.1 = bf16[2,96,896]{2,1,0:T(8,128)(2,1)} custom-call(s32[4]{0:T(128)S(1)} %copy-done.9, s32[1,128]{1,0:T(1,128)S(1)} %get-tuple-element.61.length_ref, bf16[768,896]{1,0:T(8,128)(2,1)S(1)} %get-tuple-element.62.states_ref, bf16[1536,896]{1,0:T(8,128)(2,1)S(1)} %copy-done.1, bf16[192,384]{1,0:T(8,128)(2,1)S(1)} %get-tuple-element.68.refs_0_, ...), custom_call_target="tpu_custom_call" | custom-call | flops 528482304 | bytes 2752512 | tf_op jit(solution)/shard_map/output/pallas_call | solution.py:704
  (95 shorter events, 29.1 us)
Async XLA Ops:
  2.4 23.6 %collective-permute-start.11 = (bf16[2,256,256]{2,1,0:T(8,128)(2,1)}, bf16[2,256,256]{2,1,0:T(8,128)(2,1)S(1)}, u32[]{:S(2)}, u32[]{:S(2)}) collective-permute-start(bf16[2,256,256]{2,1,0:T(8,128)(2,1)} %get-tuple-element.54), channel_id=1, source_target_pairs={{0,1},{1,0},{2,3},{3,2},{4,5},{5,4},{6,7},{7,6},{8,9},{9,8},{10,11... | collective-permute-start | bytes 786440 | tf_op jit(solution)/shard_map/ppermute | solution.py:756
  8.7 9.6 %collective-permute-start.2 = (bf16[256,448]{1,0:T(8,128)(2,1)S(1)}, bf16[256,448]{1,0:T(8,128)(2,1)S(1)}, u32[]{:S(2)}, u32[]{:S(2)}) collective-permute-start(bf16[256,448]{1,0:T(8,128)(2,1)S(1)} %get-tuple-element.41), channel_id=1, source_target_pairs={{0,2},{2,0},{1,3},{3,1},{4,6},{6,4},{5,7},{7,5},{8,10},{10,8},{9,1... | collective-permute-start | bytes 688136 | tf_op jit(solution)/shard_map/ppermute | solution.py:753
  11.2 17.4 %collective-permute-start = (bf16[2,256,256]{2,1,0:T(8,128)(2,1)S(1)}, bf16[2,256,256]{2,1,0:T(8,128)(2,1)S(1)}, u32[]{:S(2)}, u32[]{:S(2)}) collective-permute-start(bf16[2,256,256]{2,1,0:T(8,128)(2,1)S(1)} %copy-done.23), channel_id=1, source_target_pairs={{0,2},{1,3},{2,0},{3,1},{4,6},{5,7},{6,4},{7,5},{8,10},{9,11},{10,... | collective-permute-start | bytes 786440 | tf_op jit(solution)/shard_map/ppermute | solution.py:757
  11.3 19.7 %collective-permute-start.1 = (bf16[2,256,256]{2,1,0:T(8,128)(2,1)S(1)}, bf16[2,256,256]{2,1,0:T(8,128)(2,1)S(1)}, u32[]{:S(2)}, u32[]{:S(2)}) collective-permute-start(bf16[2,256,256]{2,1,0:T(8,128)(2,1)S(1)} %copy-done.22), channel_id=1, source_target_pairs={{0,3},{1,2},{2,1},{3,0},{4,7},{5,6},{6,5},{7,4},{8,11},{9,10},{10,... | collective-permute-start | bytes 786440 | tf_op jit(solution)/shard_map/ppermute | solution.py:758
  21.4 12.8 %collective-permute-start.3 = (bf16[112,448]{1,0:T(8,128)(2,1)}, bf16[112,448]{1,0:T(8,128)(2,1)S(1)}, u32[]{:S(2)}, u32[]{:S(2)}) collective-permute-start(bf16[112,448]{1,0:T(8,128)(2,1)} %get-tuple-element.44), channel_id=1, source_target_pairs={{0,4},{4,0},{8,12},{12,8},{1,5},{5,1},{9,13},{13,9},{2,6},{6,2},{1... | collective-permute-start | bytes 301064 | tf_op jit(solution)/shard_map/ppermute | solution.py:767
  23.4 11.5 %collective-permute-start.4 = (bf16[112,448]{1,0:T(8,128)(2,1)}, bf16[112,448]{1,0:T(8,128)(2,1)S(1)}, u32[]{:S(2)}, u32[]{:S(2)}) collective-permute-start(bf16[112,448]{1,0:T(8,128)(2,1)} %get-tuple-element.45), channel_id=1, source_target_pairs={{0,8},{4,12},{8,0},{12,4},{1,9},{5,13},{9,1},{13,5},{2,10},{6,14},... | collective-permute-start | bytes 301064 | tf_op jit(solution)/shard_map/ppermute | solution.py:767
  26.0 8.9 %collective-permute-start.5 = (bf16[112,448]{1,0:T(8,128)(2,1)}, bf16[112,448]{1,0:T(8,128)(2,1)S(1)}, u32[]{:S(2)}, u32[]{:S(2)}) collective-permute-start(bf16[112,448]{1,0:T(8,128)(2,1)} %get-tuple-element.46), channel_id=1, source_target_pairs={{0,12},{4,8},{8,4},{12,0},{1,13},{5,9},{9,5},{13,1},{2,14},{6,10},... | collective-permute-start | bytes 301064 | tf_op jit(solution)/shard_map/ppermute | solution.py:767
  28.6 15.9 %collective-permute-start.12 = (bf16[2,2,256,256]{3,2,1,0:T(8,128)(2,1)}, bf16[2,2,256,256]{3,2,1,0:T(8,128)(2,1)S(1)}, u32[]{:S(2)}, u32[]{:S(2)}) collective-permute-start(bf16[2,2,256,256]{3,2,1,0:T(8,128)(2,1)} %stack.25.refs_0_), channel_id=1, source_target_pairs={{0,4},{4,8},{8,12},{1,5},{5,9},{9,13},{2,6},{6,10},{10,14},{3,7},{... | collective-permute-start | bytes 1572872 | tf_op jit(solution)/shard_map/ppermute | solution.py:775
  31.0 20.2 %collective-permute-start.14 = (bf16[2,2,256,256]{3,2,1,0:T(8,128)(2,1)}, bf16[2,2,256,256]{3,2,1,0:T(8,128)(2,1)S(1)}, u32[]{:S(2)}, u32[]{:S(2)}) collective-permute-start(bf16[2,2,256,256]{3,2,1,0:T(8,128)(2,1)} %stack.25.refs_0_), channel_id=1, source_target_pairs={{4,0},{8,4},{12,8},{5,1},{9,5},{13,9},{6,2},{10,6},{14,10},{7,3},{... | collective-permute-start | bytes 1572872 | tf_op jit(solution)/shard_map/ppermute | solution.py:776
  35.7 19.2 %collective-permute-start.7 = (bf16[2,2,256,256]{3,2,1,0:T(8,128)(2,1)}, bf16[2,2,256,256]{3,2,1,0:T(8,128)(2,1)S(1)}, u32[]{:S(2)}, u32[]{:S(2)}) collective-permute-start(bf16[2,2,256,256]{3,2,1,0:T(8,128)(2,1)} %stack.23.refs_1_), channel_id=1, source_target_pairs={{0,4},{4,8},{8,12},{1,5},{5,9},{9,13},{2,6},{6,10},{10,14},{3,7},{... | collective-permute-start | bytes 1572872 | tf_op jit(solution)/shard_map/ppermute | solution.py:775
  39.9 22.6 %collective-permute-start.8 = (bf16[2,2,256,256]{3,2,1,0:T(8,128)(2,1)}, bf16[2,2,256,256]{3,2,1,0:T(8,128)(2,1)S(1)}, u32[]{:S(2)}, u32[]{:S(2)}) collective-permute-start(bf16[2,2,256,256]{3,2,1,0:T(8,128)(2,1)} %stack.23.refs_1_), channel_id=1, source_target_pairs={{4,0},{8,4},{12,8},{5,1},{9,5},{13,9},{6,2},{10,6},{14,10},{7,3},{... | collective-permute-start | bytes 1572872 | tf_op jit(solution)/shard_map/ppermute | solution.py:776
  43.1 20.7 %collective-permute-start.6 = (bf16[4,112,448]{2,1,0:T(8,128)(2,1)}, bf16[4,112,448]{2,1,0:T(8,128)(2,1)}, u32[]{:S(2)}, u32[]{:S(2)}) collective-permute-start(bf16[4,112,448]{2,1,0:T(8,128)(2,1)} %stack.24.near_ref), channel_id=1, source_target_pairs={{0,2},{2,0},{1,3},{3,1},{4,6},{6,4},{5,7},{7,5},{8,10},{10,8},{9,1... | collective-permute-start | bytes 1204232 | tf_op jit(solution)/shard_map/ppermute | solution.py:786
  44.6 22.3 %collective-permute-start.13 = (bf16[2,2,256,256]{3,2,1,0:T(8,128)(2,1)S(1)}, bf16[2,2,256,256]{3,2,1,0:T(8,128)(2,1)}, u32[]{:S(2)}, u32[]{:S(2)}) collective-permute-start(bf16[2,2,256,256]{3,2,1,0:T(8,128)(2,1)S(1)} %collective-permute-done.12.refs_2_), channel_id=1, source_target_pairs={{0,4},{4,8},{8,12},{1,5},{5,9},{9,13},{2,6},{6,10},{10,14},{3,7},{... | collective-permute-start | bytes 1572872 | tf_op jit(solution)/shard_map/ppermute | solution.py:775
  51.2 21.6 %collective-permute-start.15 = (bf16[2,2,256,256]{3,2,1,0:T(8,128)(2,1)S(1)}, bf16[2,2,256,256]{3,2,1,0:T(8,128)(2,1)}, u32[]{:S(2)}, u32[]{:S(2)}) collective-permute-start(bf16[2,2,256,256]{3,2,1,0:T(8,128)(2,1)S(1)} %collective-permute-done.14.refs_4_), channel_id=1, source_target_pairs={{4,0},{8,4},{12,8},{5,1},{9,5},{13,9},{6,2},{10,6},{14,10},{7,3},{... | collective-permute-start | bytes 1572872 | tf_op jit(solution)/shard_map/ppermute | solution.py:776
  54.9 22.4 %collective-permute-start.16 = (bf16[2,2,256,256]{3,2,1,0:T(8,128)(2,1)S(1)}, bf16[2,2,256,256]{3,2,1,0:T(8,128)(2,1)}, u32[]{:S(2)}, u32[]{:S(2)}) collective-permute-start(bf16[2,2,256,256]{3,2,1,0:T(8,128)(2,1)S(1)} %collective-permute-done.7.refs_3_), channel_id=1, source_target_pairs={{0,4},{4,8},{8,12},{1,5},{5,9},{9,13},{2,6},{6,10},{10,14},{3,7},{... | collective-permute-start | bytes 1572872 | tf_op jit(solution)/shard_map/ppermute | solution.py:775
  62.5 21.6 %collective-permute-start.17 = (bf16[2,2,256,256]{3,2,1,0:T(8,128)(2,1)S(1)}, bf16[2,2,256,256]{3,2,1,0:T(8,128)(2,1)}, u32[]{:S(2)}, u32[]{:S(2)}) collective-permute-start(bf16[2,2,256,256]{3,2,1,0:T(8,128)(2,1)S(1)} %collective-permute-done.8.refs_5_), channel_id=1, source_target_pairs={{4,0},{8,4},{12,8},{5,1},{9,5},{13,9},{6,2},{10,6},{14,10},{7,3},{... | collective-permute-start | bytes 1572872 | tf_op jit(solution)/shard_map/ppermute | solution.py:776
  66.6 19.0 %collective-permute-start.10 = (bf16[4,112,448]{2,1,0:T(8,128)(2,1)}, bf16[4,112,448]{2,1,0:T(8,128)(2,1)}, u32[]{:S(2)}, u32[]{:S(2)}) collective-permute-start(bf16[4,112,448]{2,1,0:T(8,128)(2,1)} %collective-permute-done.6.far_ref), channel_id=1, source_target_pairs={{0,1},{1,0},{2,3},{3,2},{4,5},{5,4},{6,7},{7,6},{8,9},{9,8},{10,11... | collective-permute-start | bytes 1204232 | tf_op jit(solution)/shard_map/ppermute | solution.py:789
  66.9 33.8 %collective-permute-start.18 = (bf16[2,2,256,256]{3,2,1,0:T(8,128)(2,1)}, bf16[2,2,256,256]{3,2,1,0:T(8,128)(2,1)S(1)}, u32[]{:S(2)}, u32[]{:S(2)}) collective-permute-start(bf16[2,2,256,256]{3,2,1,0:T(8,128)(2,1)} %collective-permute-done.13.refs_6_), channel_id=1, source_target_pairs={{0,4},{4,8},{8,12},{1,5},{5,9},{9,13},{2,6},{6,10},{10,14},{3,7},{... | collective-permute-start | bytes 1572872 | tf_op jit(solution)/shard_map/ppermute | solution.py:775
  72.8 27.9 %collective-permute-start.20 = (bf16[2,2,256,256]{3,2,1,0:T(8,128)(2,1)}, bf16[2,2,256,256]{3,2,1,0:T(8,128)(2,1)S(1)}, u32[]{:S(2)}, u32[]{:S(2)}) collective-permute-start(bf16[2,2,256,256]{3,2,1,0:T(8,128)(2,1)} %collective-permute-done.15.refs_8_), channel_id=1, source_target_pairs={{4,0},{8,4},{12,8},{5,1},{9,5},{13,9},{6,2},{10,6},{14,10},{7,3},{... | collective-permute-start | bytes 1572872 | tf_op jit(solution)/shard_map/ppermute | solution.py:776
  77.2 23.5 %collective-permute-start.19 = (bf16[2,2,256,256]{3,2,1,0:T(8,128)(2,1)}, bf16[2,2,256,256]{3,2,1,0:T(8,128)(2,1)S(1)}, u32[]{:S(2)}, u32[]{:S(2)}) collective-permute-start(bf16[2,2,256,256]{3,2,1,0:T(8,128)(2,1)} %collective-permute-done.16.refs_7_), channel_id=1, source_target_pairs={{0,4},{4,8},{8,12},{1,5},{5,9},{9,13},{2,6},{6,10},{10,14},{3,7},{... | collective-permute-start | bytes 1572872 | tf_op jit(solution)/shard_map/ppermute | solution.py:775
  84.1 17.9 %collective-permute-start.21 = (bf16[2,2,256,256]{3,2,1,0:T(8,128)(2,1)}, bf16[2,2,256,256]{3,2,1,0:T(8,128)(2,1)S(1)}, u32[]{:S(2)}, u32[]{:S(2)}) collective-permute-start(bf16[2,2,256,256]{3,2,1,0:T(8,128)(2,1)} %collective-permute-done.17.refs_9_), channel_id=1, source_target_pairs={{4,0},{8,4},{12,8},{5,1},{9,5},{13,9},{6,2},{10,6},{14,10},{7,3},{... | collective-permute-start | bytes 1572872 | tf_op jit(solution)/shard_map/ppermute | solution.py:776
  104.0 5.2 %collective-permute-start.23 = (bf16[192,384]{1,0:T(8,128)(2,1)S(1)}, bf16[192,384]{1,0:T(8,128)(2,1)S(1)}, u32[]{:S(2)}, u32[]{:S(2)}) collective-permute-start(bf16[192,384]{1,0:T(8,128)(2,1)S(1)} %get-tuple-element.66), channel_id=1, source_target_pairs={{0,2},{1,3},{2,0},{3,1},{4,6},{5,7},{6,4},{7,5},{8,10},{9,11},{10,... | collective-permute-start | bytes 442376 | tf_op jit(solution)/shard_map/ppermute | solution.py:816
  105.4 2.7 %collective-permute-start.22 = (bf16[192,384]{1,0:T(8,128)(2,1)S(1)}, bf16[192,384]{1,0:T(8,128)(2,1)S(1)}, u32[]{:S(2)}, u32[]{:S(2)}) collective-permute-start(bf16[192,384]{1,0:T(8,128)(2,1)S(1)} %get-tuple-element.69), channel_id=1, source_target_pairs={{0,1},{1,0},{2,3},{3,2},{4,5},{5,4},{6,7},{7,6},{8,9},{9,8},{10,11... | collective-permute-start | bytes 442376 | tf_op jit(solution)/shard_map/ppermute | solution.py:816
  105.5 6.7 %collective-permute-start.24 = (bf16[192,384]{1,0:T(8,128)(2,1)S(1)}, bf16[192,384]{1,0:T(8,128)(2,1)S(1)}, u32[]{:S(2)}, u32[]{:S(2)}) collective-permute-start(bf16[192,384]{1,0:T(8,128)(2,1)S(1)} %get-tuple-element.70), channel_id=1, source_target_pairs={{0,3},{1,2},{2,1},{3,0},{4,7},{5,6},{6,5},{7,4},{8,11},{9,10},{10,... | collective-permute-start | bytes 442376 | tf_op jit(solution)/shard_map/ppermute | solution.py:816
  (27 other events, 513.7 us)

commit v12 on v11

--- a/solution.py
+++ b/solution.py
@@ -808,10 +808,7 @@
         hop, which, lengths, query, key, value, prompts, (0, -1, 1, -2, 2)
     )
     run = functools.partial(attend_far, index, hop, which, lengths)
-    attended = {}
-    attended[2], attended[3] = run(query, key, value, near, prompts, (-3, 3), (2, 3))
-    near, _ = lax.optimization_barrier((near, attended[2]))
-    attended[0], attended[1] = run(query, key, value, near, prompts, (-3, 3), (0, 1))
+    attended = run(query, key, value, near, prompts, (-3, 3), tuple(range(plane)))
     pieces = [attended[0]] + [
         lax.ppermute(attended[by], pair, swapped(4, by)) for by in range(1, plane)
     ]

time: 117 us -> 117 us (level)
  waiting for transfers between devices: 16.2 us -> 18.5 us
  starting transfers between devices: 55.5 us -> 54.2 us
    ppermute x3, waiting for transfers between devices: 4.13 us -> 7.11 us  [line_body(): lax.ppermute(attended[by], pair, swapped(4, by))]
    ppermute x3, starting transfers between devices: 3.29 us -> 1.93 us  [line_body(): lax.ppermute(attended[by], pair, swapped(4, by))]
    pallas_call x3 -> x2, Pallas kernels: 10.7 us -> 10.8 us  [attention_call(): pl.pallas_call(kernel, in_specs=[SMEM] * len(scalars) + [VMEM] * len(arra...]
where the time goes in v12:
time: 117 us; the launch traced here: 115 us
  starting transfers between devices  54.2 us (46%)
  Pallas kernels  33.1 us (28%)
  waiting for transfers between devices  18.5 us (16%)
  local copies, waits for them, and re-layouts  9.01 us (8%)
    ppermute x6, starting transfers between devices, travel(): right[chunk] = lax.ppermute(right[chunk], 'sess', shifted(planes, 1))  33.7 us
    pallas_call x2, Pallas kernels, attention_call(): pl.pallas_call(kernel, in_specs=[SMEM] * len(scalars) + [VMEM] * len(arra...  10.8 us
    unnamed x52, local copies, waits for them, and re-layouts  8.92 us
    ppermute x6, starting transfers between devices, travel(): left[chunk] = lax.ppermute(left[chunk], 'sess', shifted(planes, -1))  7.73 us
    ppermute x3, waiting for transfers between devices, line_body(): lax.ppermute(attended[by], pair, swapped(4, by))  7.11 us
    pallas_call x3, Pallas kernels, stack(): pl.pallas_call(stack_kernel, in_specs=[VMEM] * len(arrays), out_specs=VME...  5.61 us
    ppermute x6, waiting for transfers between devices, travel(): right[chunk] = lax.ppermute(right[chunk], 'sess', shifted(planes, 1))  5.42 us
    pallas_call x1, Pallas kernels, place_rows(): pl.pallas_call(functools.partial(place_kernel, slot_cap=slot_cap, togethe...  4.84 us
  transfers between devices with their start and end apart: 25, of which 8 were waited for; matrix products, arithmetic and copies ran while one was open for 0% of the time, Pallas kernels for 23%

profile of v12, /device:TPU:0, one launch (start us, length us, event | category | flops | bytes accessed | tf_op | source)
XLA Modules:
  0.0 115.4 jit_solution(16304477418374480833)
XLA Ops:
  0.0 2.5 %split_heads.1 = (bf16[2,256,256]{2,1,0:T(8,128)(2,1)}, bf16[2,256,256]{2,1,0:T(8,128)(2,1)}, bf16[2,256,256]{2,1,0:T(8,128)(2,1)}, bf16[2,256,256]{2,1,0:T(8,128)(2,1)}) custom-call(s32[1]{0:T(128)} %bitcast.3.head_ref, bf16[2,256,1024]{2,1,0:T(8,128)(2,1)} %cache_ref.1), custom_call_target="tpu_custom_call" | custom-call | bytes 2097152 | tf_op jit(solution)/shard_map/split_heads/pallas_call | solution.py:308
  3.0 1.9 %copy-done = bf16[1792,896]{1,0:T(8,128)(2,1)S(1)} copy-done((bf16[1792,896]{1,0:T(8,128)(2,1)S(1)}, bf16[1792,896]{1,0:T(8,128)(2,1)}, u32[]{:S(2)}) %copy-start) | copy-done | bytes 3211288
  8.7 2.5 %collective-permute-start.2 = (bf16[256,448]{1,0:T(8,128)(2,1)S(1)}, bf16[256,448]{1,0:T(8,128)(2,1)S(1)}, u32[]{:S(2)}, u32[]{:S(2)}) collective-permute-start(bf16[256,448]{1,0:T(8,128)(2,1)S(1)} %get-tuple-element.40), channel_id=1, source_target_pairs={{0,2},{2,0},{1,3},{3,1},{4,6},{6,4},{5,7},{7,5},{8,10},{10,8},{9,1... | collective-permute-start | bytes 688136 | tf_op jit(solution)/shard_map/ppermute | solution.py:753
  12.8 3.0 %head_weights.1.weight_ref = bf16[896,640]{1,0:T(8,128)(2,1)} custom-call(s32[4]{0:T(128)} %copy-done.8, bf16[896,1536]{1,0:T(8,128)(2,1)} %q_ref.1, bf16[896,512]{1,0:T(8,128)(2,1)} %k_ref.1, bf16[896,512]{1,0:T(8,128)(2,1)} %v_ref.1), custom_call_target="tpu_custom_call" | custom-call | bytes 2293760 | tf_op jit(solution)/shard_map/head_weights/pallas_call | solution.py:434
  15.9 2.5 %collective-permute-done.2.came_ref = bf16[256,448]{1,0:T(8,128)(2,1)S(1)} collective-permute-done((bf16[256,448]{1,0:T(8,128)(2,1)S(1)}, bf16[256,448]{1,0:T(8,128)(2,1)S(1)}, u32[]{:S(2)}, u32[]{:S(2)}) %collective-permute-start.2) | collective-permute-done | bytes 229408 | tf_op jit(solution)/shard_map/ppermute | solution.py:753
  19.1 2.3 %route.1 = (bf16[112,448]{1,0:T(8,128)(2,1)}, bf16[112,448]{1,0:T(8,128)(2,1)}, bf16[112,448]{1,0:T(8,128)(2,1)}, bf16[112,448]{1,0:T(8,128)(2,1)}) custom-call(s32[4]{0:T(128)} %copy-done.8, f32[256,448]{1,0:T(8,128)} %copy-done.6, bf16[256,448]{1,0:T(8,128)(2,1)} %copy-done.14, s32[1,256]{1,0:T(1,128)} %bitcast.21), custom_call_target="tpu_custom_call" | custom-call | flops 102760448 | bytes 917504 | tf_op jit(solution)/shard_map/route/pallas_call | solution.py:401
  21.4 2.0 %collective-permute-start.3 = (bf16[112,448]{1,0:T(8,128)(2,1)}, bf16[112,448]{1,0:T(8,128)(2,1)S(1)}, u32[]{:S(2)}, u32[]{:S(2)}) collective-permute-start(bf16[112,448]{1,0:T(8,128)(2,1)} %get-tuple-element.43), channel_id=1, source_target_pairs={{0,4},{4,0},{8,12},{12,8},{1,5},{5,1},{9,13},{13,9},{2,6},{6,2},{1... | collective-permute-start | bytes 301064 | tf_op jit(solution)/shard_map/ppermute | solution.py:767
  23.4 2.6 %collective-permute-start.4 = (bf16[112,448]{1,0:T(8,128)(2,1)}, bf16[112,448]{1,0:T(8,128)(2,1)S(1)}, u32[]{:S(2)}, u32[]{:S(2)}) collective-permute-start(bf16[112,448]{1,0:T(8,128)(2,1)} %get-tuple-element.44), channel_id=1, source_target_pairs={{0,8},{4,12},{8,0},{12,4},{1,9},{5,13},{9,1},{13,5},{2,10},{6,14},... | collective-permute-start | bytes 301064 | tf_op jit(solution)/shard_map/ppermute | solution.py:767
  28.6 2.4 %collective-permute-start.12 = (bf16[2,2,256,256]{3,2,1,0:T(8,128)(2,1)}, bf16[2,2,256,256]{3,2,1,0:T(8,128)(2,1)S(1)}, u32[]{:S(2)}, u32[]{:S(2)}) collective-permute-start(bf16[2,2,256,256]{3,2,1,0:T(8,128)(2,1)} %stack.25.refs_0_), channel_id=1, source_target_pairs={{0,4},{4,8},{8,12},{1,5},{5,9},{9,13},{2,6},{6,10},{10,14},{3,7},{... | collective-permute-start | bytes 1572872 | tf_op jit(solution)/shard_map/ppermute | solution.py:775
  35.6 4.2 %collective-permute-start.7 = (bf16[2,2,256,256]{3,2,1,0:T(8,128)(2,1)}, bf16[2,2,256,256]{3,2,1,0:T(8,128)(2,1)S(1)}, u32[]{:S(2)}, u32[]{:S(2)}) collective-permute-start(bf16[2,2,256,256]{3,2,1,0:T(8,128)(2,1)} %stack.23.refs_1_), channel_id=1, source_target_pairs={{0,4},{4,8},{8,12},{1,5},{5,9},{9,13},{2,6},{6,10},{10,14},{3,7},{... | collective-permute-start | bytes 1572872 | tf_op jit(solution)/shard_map/ppermute | solution.py:775
  41.2 1.9 %stack.24.near_ref = bf16[4,112,448]{2,1,0:T(8,128)(2,1)} custom-call(bf16[1,112,448]{2,1,0:T(8,128)(2,1)} %bitcast.17, bf16[1,112,448]{2,1,0:T(8,128)(2,1)} %bitcast.18, bf16[1,112,448]{2,1,0:T(8,128)(2,1)} %bitcast.19, bf16[1,112,448]{2,1,0:T(8,128)(2,1)} %bitcast.20), custom_call_target="tpu_custom_call" | custom-call | bytes 802816 | tf_op jit(solution)/shard_map/stack/pallas_call | solution.py:330
  44.5 6.7 %collective-permute-start.13 = (bf16[2,2,256,256]{3,2,1,0:T(8,128)(2,1)S(1)}, bf16[2,2,256,256]{3,2,1,0:T(8,128)(2,1)}, u32[]{:S(2)}, u32[]{:S(2)}) collective-permute-start(bf16[2,2,256,256]{3,2,1,0:T(8,128)(2,1)S(1)} %collective-permute-done.12.refs_2_), channel_id=1, source_target_pairs={{0,4},{4,8},{8,12},{1,5},{5,9},{9,13},{2,6},{6,10},{10,14},{3,7},{... | collective-permute-start | bytes 1572872 | tf_op jit(solution)/shard_map/ppermute | solution.py:775
  52.5 2.3 %collective-permute-done.7.refs_3_ = bf16[2,2,256,256]{3,2,1,0:T(8,128)(2,1)S(1)} collective-permute-done((bf16[2,2,256,256]{3,2,1,0:T(8,128)(2,1)}, bf16[2,2,256,256]{3,2,1,0:T(8,128)(2,1)S(1)}, u32[]{:S(2)}, u32[]{:S(2)}) %collective-permute-start.7) | collective-permute-done | bytes 524320 | tf_op jit(solution)/shard_map/ppermute | solution.py:775
  54.9 7.6 %collective-permute-start.16 = (bf16[2,2,256,256]{3,2,1,0:T(8,128)(2,1)S(1)}, bf16[2,2,256,256]{3,2,1,0:T(8,128)(2,1)}, u32[]{:S(2)}, u32[]{:S(2)}) collective-permute-start(bf16[2,2,256,256]{3,2,1,0:T(8,128)(2,1)S(1)} %collective-permute-done.7.refs_3_), channel_id=1, source_target_pairs={{0,4},{4,8},{8,12},{1,5},{5,9},{9,13},{2,6},{6,10},{10,14},{3,7},{... | collective-permute-start | bytes 1572872 | tf_op jit(solution)/shard_map/ppermute | solution.py:775
  63.9 2.0 %collective-permute-done.9.near_core_ref = bf16[4,112,448]{2,1,0:T(8,128)(2,1)S(1)} collective-permute-done((bf16[4,112,448]{2,1,0:T(8,128)(2,1)}, bf16[4,112,448]{2,1,0:T(8,128)(2,1)S(1)}, u32[]{:S(2)}, u32[]{:S(2)}) %collective-permute-start.9) | collective-permute-done | bytes 401440 | tf_op jit(solution)/shard_map/ppermute | solution.py:789
  66.9 5.9 %collective-permute-start.18 = (bf16[2,2,256,256]{3,2,1,0:T(8,128)(2,1)}, bf16[2,2,256,256]{3,2,1,0:T(8,128)(2,1)S(1)}, u32[]{:S(2)}, u32[]{:S(2)}) collective-permute-start(bf16[2,2,256,256]{3,2,1,0:T(8,128)(2,1)} %collective-permute-done.13.refs_6_), channel_id=1, source_target_pairs={{0,4},{4,8},{8,12},{1,5},{5,9},{9,13},{2,6},{6,10},{10,14},{3,7},{... | collective-permute-start | bytes 1572872 | tf_op jit(solution)/shard_map/ppermute | solution.py:775
  74.1 3.1 %collective-permute-done.16.refs_7_ = bf16[2,2,256,256]{3,2,1,0:T(8,128)(2,1)} collective-permute-done((bf16[2,2,256,256]{3,2,1,0:T(8,128)(2,1)S(1)}, bf16[2,2,256,256]{3,2,1,0:T(8,128)(2,1)}, u32[]{:S(2)}, u32[]{:S(2)}) %collective-permute-start.16) | collective-permute-done | bytes 524320 | tf_op jit(solution)/shard_map/ppermute | solution.py:775
  77.2 6.8 %collective-permute-start.19 = (bf16[2,2,256,256]{3,2,1,0:T(8,128)(2,1)}, bf16[2,2,256,256]{3,2,1,0:T(8,128)(2,1)S(1)}, u32[]{:S(2)}, u32[]{:S(2)}) collective-permute-start(bf16[2,2,256,256]{3,2,1,0:T(8,128)(2,1)} %collective-permute-done.16.refs_7_), channel_id=1, source_target_pairs={{0,4},{4,8},{8,12},{1,5},{5,9},{9,13},{2,6},{6,10},{10,14},{3,7},{... | collective-permute-start | bytes 1572872 | tf_op jit(solution)/shard_map/ppermute | solution.py:775
  87.8 4.8 %place_rows.1 = (bf16[768,896]{1,0:T(8,128)(2,1)S(1)}, bf16[768,384]{1,0:T(8,128)(2,1)S(1)}, bf16[768,128]{1,0:T(8,128)(2,1)S(1)}, bf16[768,128]{1,0:T(8,128)(2,1)S(1)}, s32[1,128]{1,0:T(1,128)S(1)}) custom-call(s32[4]{0:T(128)S(1)} %copy-done.9, bf16[4,112,448]{2,1,0:T(8,128)(2,1)S(1)} %copy-done.7, bf16[4,112,448]{2,1,0:T(8,128)(2,1)} %collective-permute-done.6.far_ref, ...), custom_call_target="tpu_custom_call" | custom-call | flops 1761607680 | bytes 6291456 | tf_op jit(solution)/shard_map/place_rows/pallas_call | solution.py:527
  92.6 8.7 %near.1.near_ref = bf16[768,384]{1,0:T(8,128)(2,1)S(1)} custom-call(s32[8]{0:T(128)S(1)} %get-tuple-element.70.hop_ref, s32[8]{0:T(128)S(1)} %get-tuple-element.69.held_ref, s32[1,128]{1,0:T(1,128)S(1)} %get-tuple-element.60.length_ref, bf16[768,384]{1,0:T(8,128)(2,1)S(1)} %get-tuple-element.62.query_ref, bf16[768,128]{1,0:T(8,128)(2,1)S(1)} %get-tuple-element.63.key_ref, ...), custom_call_target="tpu_custom_call" | custom-call | flops 660602880 | bytes 2097152 | tf_op jit(solution)/shard_map/near/pallas_call | solution.py:647
  102.0 2.2 %far.1 = (bf16[192,384]{1,0:T(8,128)(2,1)S(1)}, bf16[192,384]{1,0:T(8,128)(2,1)S(1)}, bf16[192,384]{1,0:T(8,128)(2,1)S(1)}, bf16[192,384]{1,0:T(8,128)(2,1)S(1)}) custom-call(s32[4]{0:T(128)S(1)} %copy-done.9, s32[8]{0:T(128)S(1)} %get-tuple-element.70.hop_ref, s32[8]{0:T(128)S(1)} %get-tuple-element.69.held_ref, s32[1,128]{1,0:T(1,128)S(1)} %get-tuple-element.60.length_ref, ...), custom_call_target="tpu_custom_call" | custom-call | flops 660602880 | bytes 2097152 | tf_op jit(solution)/shard_map/far/pallas_call | solution.py:647
  106.1 4.8 %collective-permute-done.23.refs_2_ = bf16[192,384]{1,0:T(8,128)(2,1)S(1)} collective-permute-done((bf16[192,384]{1,0:T(8,128)(2,1)S(1)}, bf16[192,384]{1,0:T(8,128)(2,1)S(1)}, u32[]{:S(2)}, u32[]{:S(2)}) %collective-permute-start.23) | collective-permute-done | bytes 147488 | tf_op jit(solution)/shard_map/ppermute | solution.py:813
  111.0 2.3 %collective-permute-done.24.refs_3_ = bf16[192,384]{1,0:T(8,128)(2,1)S(1)} collective-permute-done((bf16[192,384]{1,0:T(8,128)(2,1)S(1)}, bf16[192,384]{1,0:T(8,128)(2,1)S(1)}, u32[]{:S(2)}, u32[]{:S(2)}) %collective-permute-start.24) | collective-permute-done | bytes 147488 | tf_op jit(solution)/shard_map/ppermute | solution.py:813
  113.2 2.2 %output.1 = bf16[2,96,896]{2,1,0:T(8,128)(2,1)} custom-call(s32[4]{0:T(128)S(1)} %copy-done.9, s32[1,128]{1,0:T(1,128)S(1)} %get-tuple-element.60.length_ref, bf16[768,896]{1,0:T(8,128)(2,1)S(1)} %get-tuple-element.61.states_ref, bf16[1536,896]{1,0:T(8,128)(2,1)S(1)} %copy-done.1, bf16[192,384]{1,0:T(8,128)(2,1)S(1)} %get-tuple-element.65.refs_0_, ...), custom_call_target="tpu_custom_call" | custom-call | flops 528482304 | bytes 2752512 | tf_op jit(solution)/shard_map/output/pallas_call | solution.py:704
  (94 shorter events, 27.8 us)
Async XLA Ops:
  2.5 23.6 %collective-permute-start.11 = (bf16[2,256,256]{2,1,0:T(8,128)(2,1)}, bf16[2,256,256]{2,1,0:T(8,128)(2,1)S(1)}, u32[]{:S(2)}, u32[]{:S(2)}) collective-permute-start(bf16[2,256,256]{2,1,0:T(8,128)(2,1)} %get-tuple-element.53), channel_id=1, source_target_pairs={{0,1},{1,0},{2,3},{3,2},{4,5},{5,4},{6,7},{7,6},{8,9},{9,8},{10,11... | collective-permute-start | bytes 786440 | tf_op jit(solution)/shard_map/ppermute | solution.py:756
  8.7 9.6 %collective-permute-start.2 = (bf16[256,448]{1,0:T(8,128)(2,1)S(1)}, bf16[256,448]{1,0:T(8,128)(2,1)S(1)}, u32[]{:S(2)}, u32[]{:S(2)}) collective-permute-start(bf16[256,448]{1,0:T(8,128)(2,1)S(1)} %get-tuple-element.40), channel_id=1, source_target_pairs={{0,2},{2,0},{1,3},{3,1},{4,6},{6,4},{5,7},{7,5},{8,10},{10,8},{9,1... | collective-permute-start | bytes 688136 | tf_op jit(solution)/shard_map/ppermute | solution.py:753
  11.2 17.4 %collective-permute-start = (bf16[2,256,256]{2,1,0:T(8,128)(2,1)S(1)}, bf16[2,256,256]{2,1,0:T(8,128)(2,1)S(1)}, u32[]{:S(2)}, u32[]{:S(2)}) collective-permute-start(bf16[2,256,256]{2,1,0:T(8,128)(2,1)S(1)} %copy-done.23), channel_id=1, source_target_pairs={{0,2},{1,3},{2,0},{3,1},{4,6},{5,7},{6,4},{7,5},{8,10},{9,11},{10,... | collective-permute-start | bytes 786440 | tf_op jit(solution)/shard_map/ppermute | solution.py:757
  11.3 19.7 %collective-permute-start.1 = (bf16[2,256,256]{2,1,0:T(8,128)(2,1)S(1)}, bf16[2,256,256]{2,1,0:T(8,128)(2,1)S(1)}, u32[]{:S(2)}, u32[]{:S(2)}) collective-permute-start(bf16[2,256,256]{2,1,0:T(8,128)(2,1)S(1)} %copy-done.22), channel_id=1, source_target_pairs={{0,3},{1,2},{2,1},{3,0},{4,7},{5,6},{6,5},{7,4},{8,11},{9,10},{10,... | collective-permute-start | bytes 786440 | tf_op jit(solution)/shard_map/ppermute | solution.py:758
  21.4 12.8 %collective-permute-start.3 = (bf16[112,448]{1,0:T(8,128)(2,1)}, bf16[112,448]{1,0:T(8,128)(2,1)S(1)}, u32[]{:S(2)}, u32[]{:S(2)}) collective-permute-start(bf16[112,448]{1,0:T(8,128)(2,1)} %get-tuple-element.43), channel_id=1, source_target_pairs={{0,4},{4,0},{8,12},{12,8},{1,5},{5,1},{9,13},{13,9},{2,6},{6,2},{1... | collective-permute-start | bytes 301064 | tf_op jit(solution)/shard_map/ppermute | solution.py:767
  23.4 11.5 %collective-permute-start.4 = (bf16[112,448]{1,0:T(8,128)(2,1)}, bf16[112,448]{1,0:T(8,128)(2,1)S(1)}, u32[]{:S(2)}, u32[]{:S(2)}) collective-permute-start(bf16[112,448]{1,0:T(8,128)(2,1)} %get-tuple-element.44), channel_id=1, source_target_pairs={{0,8},{4,12},{8,0},{12,4},{1,9},{5,13},{9,1},{13,5},{2,10},{6,14},... | collective-permute-start | bytes 301064 | tf_op jit(solution)/shard_map/ppermute | solution.py:767
  26.0 8.9 %collective-permute-start.5 = (bf16[112,448]{1,0:T(8,128)(2,1)}, bf16[112,448]{1,0:T(8,128)(2,1)S(1)}, u32[]{:S(2)}, u32[]{:S(2)}) collective-permute-start(bf16[112,448]{1,0:T(8,128)(2,1)} %get-tuple-element.45), channel_id=1, source_target_pairs={{0,12},{4,8},{8,4},{12,0},{1,13},{5,9},{9,5},{13,1},{2,14},{6,10},... | collective-permute-start | bytes 301064 | tf_op jit(solution)/shard_map/ppermute | solution.py:767
  28.6 16.0 %collective-permute-start.12 = (bf16[2,2,256,256]{3,2,1,0:T(8,128)(2,1)}, bf16[2,2,256,256]{3,2,1,0:T(8,128)(2,1)S(1)}, u32[]{:S(2)}, u32[]{:S(2)}) collective-permute-start(bf16[2,2,256,256]{3,2,1,0:T(8,128)(2,1)} %stack.25.refs_0_), channel_id=1, source_target_pairs={{0,4},{4,8},{8,12},{1,5},{5,9},{9,13},{2,6},{6,10},{10,14},{3,7},{... | collective-permute-start | bytes 1572872 | tf_op jit(solution)/shard_map/ppermute | solution.py:775
  31.0 20.2 %collective-permute-start.14 = (bf16[2,2,256,256]{3,2,1,0:T(8,128)(2,1)}, bf16[2,2,256,256]{3,2,1,0:T(8,128)(2,1)S(1)}, u32[]{:S(2)}, u32[]{:S(2)}) collective-permute-start(bf16[2,2,256,256]{3,2,1,0:T(8,128)(2,1)} %stack.25.refs_0_), channel_id=1, source_target_pairs={{4,0},{8,4},{12,8},{5,1},{9,5},{13,9},{6,2},{10,6},{14,10},{7,3},{... | collective-permute-start | bytes 1572872 | tf_op jit(solution)/shard_map/ppermute | solution.py:776
  35.6 19.2 %collective-permute-start.7 = (bf16[2,2,256,256]{3,2,1,0:T(8,128)(2,1)}, bf16[2,2,256,256]{3,2,1,0:T(8,128)(2,1)S(1)}, u32[]{:S(2)}, u32[]{:S(2)}) collective-permute-start(bf16[2,2,256,256]{3,2,1,0:T(8,128)(2,1)} %stack.23.refs_1_), channel_id=1, source_target_pairs={{0,4},{4,8},{8,12},{1,5},{5,9},{9,13},{2,6},{6,10},{10,14},{3,7},{... | collective-permute-start | bytes 1572872 | tf_op jit(solution)/shard_map/ppermute | solution.py:775
  39.9 22.6 %collective-permute-start.8 = (bf16[2,2,256,256]{3,2,1,0:T(8,128)(2,1)}, bf16[2,2,256,256]{3,2,1,0:T(8,128)(2,1)S(1)}, u32[]{:S(2)}, u32[]{:S(2)}) collective-permute-start(bf16[2,2,256,256]{3,2,1,0:T(8,128)(2,1)} %stack.23.refs_1_), channel_id=1, source_target_pairs={{4,0},{8,4},{12,8},{5,1},{9,5},{13,9},{6,2},{10,6},{14,10},{7,3},{... | collective-permute-start | bytes 1572872 | tf_op jit(solution)/shard_map/ppermute | solution.py:776
  43.1 20.7 %collective-permute-start.6 = (bf16[4,112,448]{2,1,0:T(8,128)(2,1)}, bf16[4,112,448]{2,1,0:T(8,128)(2,1)}, u32[]{:S(2)}, u32[]{:S(2)}) collective-permute-start(bf16[4,112,448]{2,1,0:T(8,128)(2,1)} %stack.24.near_ref), channel_id=1, source_target_pairs={{0,2},{2,0},{1,3},{3,1},{4,6},{6,4},{5,7},{7,5},{8,10},{10,8},{9,1... | collective-permute-start | bytes 1204232 | tf_op jit(solution)/shard_map/ppermute | solution.py:786
  44.5 22.3 %collective-permute-start.13 = (bf16[2,2,256,256]{3,2,1,0:T(8,128)(2,1)S(1)}, bf16[2,2,256,256]{3,2,1,0:T(8,128)(2,1)}, u32[]{:S(2)}, u32[]{:S(2)}) collective-permute-start(bf16[2,2,256,256]{3,2,1,0:T(8,128)(2,1)S(1)} %collective-permute-done.12.refs_2_), channel_id=1, source_target_pairs={{0,4},{4,8},{8,12},{1,5},{5,9},{9,13},{2,6},{6,10},{10,14},{3,7},{... | collective-permute-start | bytes 1572872 | tf_op jit(solution)/shard_map/ppermute | solution.py:775
  51.2 21.6 %collective-permute-start.15 = (bf16[2,2,256,256]{3,2,1,0:T(8,128)(2,1)S(1)}, bf16[2,2,256,256]{3,2,1,0:T(8,128)(2,1)}, u32[]{:S(2)}, u32[]{:S(2)}) collective-permute-start(bf16[2,2,256,256]{3,2,1,0:T(8,128)(2,1)S(1)} %collective-permute-done.14.refs_4_), channel_id=1, source_target_pairs={{4,0},{8,4},{12,8},{5,1},{9,5},{13,9},{6,2},{10,6},{14,10},{7,3},{... | collective-permute-start | bytes 1572872 | tf_op jit(solution)/shard_map/ppermute | solution.py:776
  54.9 22.4 %collective-permute-start.16 = (bf16[2,2,256,256]{3,2,1,0:T(8,128)(2,1)S(1)}, bf16[2,2,256,256]{3,2,1,0:T(8,128)(2,1)}, u32[]{:S(2)}, u32[]{:S(2)}) collective-permute-start(bf16[2,2,256,256]{3,2,1,0:T(8,128)(2,1)S(1)} %collective-permute-done.7.refs_3_), channel_id=1, source_target_pairs={{0,4},{4,8},{8,12},{1,5},{5,9},{9,13},{2,6},{6,10},{10,14},{3,7},{... | collective-permute-start | bytes 1572872 | tf_op jit(solution)/shard_map/ppermute | solution.py:775
  62.5 21.6 %collective-permute-start.17 = (bf16[2,2,256,256]{3,2,1,0:T(8,128)(2,1)S(1)}, bf16[2,2,256,256]{3,2,1,0:T(8,128)(2,1)}, u32[]{:S(2)}, u32[]{:S(2)}) collective-permute-start(bf16[2,2,256,256]{3,2,1,0:T(8,128)(2,1)S(1)} %collective-permute-done.8.refs_5_), channel_id=1, source_target_pairs={{4,0},{8,4},{12,8},{5,1},{9,5},{13,9},{6,2},{10,6},{14,10},{7,3},{... | collective-permute-start | bytes 1572872 | tf_op jit(solution)/shard_map/ppermute | solution.py:776
  63.8 2.1 %collective-permute-start.9 = (bf16[4,112,448]{2,1,0:T(8,128)(2,1)}, bf16[4,112,448]{2,1,0:T(8,128)(2,1)S(1)}, u32[]{:S(2)}, u32[]{:S(2)}) collective-permute-start(bf16[4,112,448]{2,1,0:T(8,128)(2,1)} %stack.24.near_ref), channel_id=1, source_target_pairs={{0,1},{1,0},{2,3},{3,2},{4,5},{5,4},{6,7},{7,6},{8,9},{9,8},{10,11... | collective-permute-start | bytes 1204232 | tf_op jit(solution)/shard_map/ppermute | solution.py:789
  66.7 19.0 %collective-permute-start.10 = (bf16[4,112,448]{2,1,0:T(8,128)(2,1)}, bf16[4,112,448]{2,1,0:T(8,128)(2,1)}, u32[]{:S(2)}, u32[]{:S(2)}) collective-permute-start(bf16[4,112,448]{2,1,0:T(8,128)(2,1)} %collective-permute-done.6.far_ref), channel_id=1, source_target_pairs={{0,1},{1,0},{2,3},{3,2},{4,5},{5,4},{6,7},{7,6},{8,9},{9,8},{10,11... | collective-permute-start | bytes 1204232 | tf_op jit(solution)/shard_map/ppermute | solution.py:789
  66.9 34.5 %collective-permute-start.18 = (bf16[2,2,256,256]{3,2,1,0:T(8,128)(2,1)}, bf16[2,2,256,256]{3,2,1,0:T(8,128)(2,1)S(1)}, u32[]{:S(2)}, u32[]{:S(2)}) collective-permute-start(bf16[2,2,256,256]{3,2,1,0:T(8,128)(2,1)} %collective-permute-done.13.refs_6_), channel_id=1, source_target_pairs={{0,4},{4,8},{8,12},{1,5},{5,9},{9,13},{2,6},{6,10},{10,14},{3,7},{... | collective-permute-start | bytes 1572872 | tf_op jit(solution)/shard_map/ppermute | solution.py:775
  72.8 28.5 %collective-permute-start.20 = (bf16[2,2,256,256]{3,2,1,0:T(8,128)(2,1)}, bf16[2,2,256,256]{3,2,1,0:T(8,128)(2,1)S(1)}, u32[]{:S(2)}, u32[]{:S(2)}) collective-permute-start(bf16[2,2,256,256]{3,2,1,0:T(8,128)(2,1)} %collective-permute-done.15.refs_8_), channel_id=1, source_target_pairs={{4,0},{8,4},{12,8},{5,1},{9,5},{13,9},{6,2},{10,6},{14,10},{7,3},{... | collective-permute-start | bytes 1572872 | tf_op jit(solution)/shard_map/ppermute | solution.py:776
  77.2 24.1 %collective-permute-start.19 = (bf16[2,2,256,256]{3,2,1,0:T(8,128)(2,1)}, bf16[2,2,256,256]{3,2,1,0:T(8,128)(2,1)S(1)}, u32[]{:S(2)}, u32[]{:S(2)}) collective-permute-start(bf16[2,2,256,256]{3,2,1,0:T(8,128)(2,1)} %collective-permute-done.16.refs_7_), channel_id=1, source_target_pairs={{0,4},{4,8},{8,12},{1,5},{5,9},{9,13},{2,6},{6,10},{10,14},{3,7},{... | collective-permute-start | bytes 1572872 | tf_op jit(solution)/shard_map/ppermute | solution.py:775
  84.1 17.9 %collective-permute-start.21 = (bf16[2,2,256,256]{3,2,1,0:T(8,128)(2,1)}, bf16[2,2,256,256]{3,2,1,0:T(8,128)(2,1)S(1)}, u32[]{:S(2)}, u32[]{:S(2)}) collective-permute-start(bf16[2,2,256,256]{3,2,1,0:T(8,128)(2,1)} %collective-permute-done.17.refs_9_), channel_id=1, source_target_pairs={{4,0},{8,4},{12,8},{5,1},{9,5},{13,9},{6,2},{10,6},{14,10},{7,3},{... | collective-permute-start | bytes 1572872 | tf_op jit(solution)/shard_map/ppermute | solution.py:776
  104.3 6.7 %collective-permute-start.23 = (bf16[192,384]{1,0:T(8,128)(2,1)S(1)}, bf16[192,384]{1,0:T(8,128)(2,1)S(1)}, u32[]{:S(2)}, u32[]{:S(2)}) collective-permute-start(bf16[192,384]{1,0:T(8,128)(2,1)S(1)} %get-tuple-element.67), channel_id=1, source_target_pairs={{0,2},{1,3},{2,0},{3,1},{4,6},{5,7},{6,4},{7,5},{8,10},{9,11},{10,... | collective-permute-start | bytes 442376 | tf_op jit(solution)/shard_map/ppermute | solution.py:813
  105.9 7.3 %collective-permute-start.24 = (bf16[192,384]{1,0:T(8,128)(2,1)S(1)}, bf16[192,384]{1,0:T(8,128)(2,1)S(1)}, u32[]{:S(2)}, u32[]{:S(2)}) collective-permute-start(bf16[192,384]{1,0:T(8,128)(2,1)S(1)} %get-tuple-element.68), channel_id=1, source_target_pairs={{0,3},{1,2},{2,1},{3,0},{4,7},{5,6},{6,5},{7,4},{8,11},{9,10},{10,... | collective-permute-start | bytes 442376 | tf_op jit(solution)/shard_map/ppermute | solution.py:813
  (27 other events, 517.3 us)
